TPU v7x, 32 devices: a whole 2x2x4 slice. The times are simulated.
32 devices in a mesh: dp: 16 (over z, x, core), mp: 2 (over y).
Axes of the slice: x: 2, y: 2, z: 4, core: 2. Of those that a mesh axis runs over, the one named last changes fastest.
Arguments:
- captions: bfloat16 [2048, 16, 768], P('dp'), may hold values from -6 to 6
- image_cache: bfloat16 [2048, 768], P('dp'), may hold values from -6 to 6
- send_order: int32 [16, 128], P('dp'), may hold values from 0 to 127, each once within a row
- arrive_order: int32 [16, 128], P('dp'), may hold values from 0 to 127, each once within a row
- counts: int32 [16, 2], replicated, may hold values from 4 to 64, as said below
- keep_mask: int32 [2048], replicated, may hold values 0 or 1
- end_pos: int32 [2048], P('dp'), may hold values from 4 to 15
- w_qkv: bfloat16 [768, 3, 768], P('dp', None, 'mp'), may hold values from -0.21875 to 0.21875
- w_out: bfloat16 [768, 768], P('dp', 'mp'), may hold values from -0.625 to 0.625
- w_up: bfloat16 [768, 3072], P('dp', 'mp'), may hold values from -0.21875 to 0.21875
- w_down: bfloat16 [768, 3072], P('dp', 'mp'), may hold values from -0.15625 to 0.15625
- w_proj: bfloat16 [768, 768], P('dp'), may hold values from -0.21875 to 0.21875
- ln1_gain: float32 [768], P('dp'), may hold values from 0.5 to 1.5
- ln2_gain: float32 [768], P('dp'), may hold values from 0.5 to 1.5
Outputs:
- loss: float32 [], replicated
- grad_captions: float32 [2048, 16, 768], P('dp')
- grad_qkv: float32 [768, 3, 768], P('dp', None, 'mp')
- grad_out: float32 [768, 768], P('dp', 'mp')
- grad_up: float32 [768, 3072], P('dp', 'mp')
- grad_down: float32 [768, 3072], P('dp', 'mp')
- grad_proj: float32 [768, 768], P('dp')
- grad_ln1: float32 [768], P('dp')
- grad_ln2: float32 [768], P('dp')
Inputs may be any that keep to these rules, and one draw needn't show every extreme that they name: `send_order`: each row is a permutation; entry (d, p * 8 * 8 + k) names the local cache row that index d of dp hands to index p as its k-th (8 = 1 there, so k = 0). `arrive_order`: each row is a permutation; entry (d, j) = p * 8 * 8 + k names the k-th embedding handed to index d by index p (8 = 1 there, so k = 0). `counts`: every entry is either 64 // 16 or 64; index 0 of dp fills 64 // 16 slots and the last index fills all 64 in every micro-batch.
All inputs are finite; a program needn't handle non-finite values.
Results may differ from a plain program's by a relative error of at most 0.035.
Values may be sent and summed in bfloat16 or wider, within the bound.
No kernel may reach another device: no remote copies, remote signals or barrier semaphores. Data moves between devices by JAX's collectives and lax.ppermute only.
A program may use at most 256 MiB of HBM per device.

v0:
```python
import math

import jax
import jax.numpy as jnp
from jax import lax
from jax.experimental import pallas as pl
from jax.experimental.pallas import tpu as pltpu
from jax.sharding import PartitionSpec as P

HEAD = 64
MICRO = 2
CAP_DEV = 64
LOGIT_SCALE = 40.0
SCORE_SCALE = 1.0 / math.sqrt(HEAD)
LENGTH = 16
WIDTH = 768
HEADS_HERE = 6
COLS = HEADS_HERE * HEAD
BLOCK = 16
TOKENS = BLOCK * LENGTH
STACK = HEADS_HERE * BLOCK

low = jnp.bfloat16
full = jnp.float32


def mm(a, b):
    return lax.dot_general(a, b, (((1,), (0,)), ((), ())), preferred_element_type=full)


def mm_nt(a, b):
    return lax.dot_general(a, b, (((1,), (1,)), ((), ())), preferred_element_type=full)


def mm_tn(a, b):
    return lax.dot_general(a, b, (((0,), (0,)), ((), ())), preferred_element_type=full)


def pick(flag, when_zero, when_one):
    return jnp.where(flag == 0, when_zero, when_one)


class Plane:
    def __init__(self):
        self.count = lax.axis_size("dp")
        self.index = lax.axis_index("dp")
        self.core = self.index % 2
        self.side = (self.index // 2) % 2
        self.depth = self.index // 4
        self.fast = self.count == 16

    def swap_core(self, x):
        return lax.ppermute(x, "dp", [(i, i ^ 1) for i in range(self.count)])

    def swap_side(self, x):
        return lax.ppermute(x, "dp", [(i, i ^ 2) for i in range(self.count)])

    def shift_depth(self, x, step):
        return lax.ppermute(
            x, "dp", [(i, (i + 4 * step) % self.count) for i in range(self.count)]
        )

    def gather(self, mine, send, after=None):
        if not self.fast:
            zero_all = lax.all_gather(pick(self.core, mine, send), "dp", axis=0, tiled=True)
            one_all = lax.all_gather(pick(self.core, send, mine), "dp", axis=0, tiled=True)
            return pick(self.core, zero_all, one_all)
        rows, width = mine.shape
        arrived = self.swap_core(send)
        block = jnp.zeros((2, rows, width), mine.dtype)
        block = lax.dynamic_update_slice(block, mine[None], (self.core, 0, 0))
        block = lax.dynamic_update_slice(block, arrived[None], (1 - self.core, 0, 0))
        block = block.reshape(2 * rows, width)
        if after is not None:
            block, _ = lax.optimization_barrier((block, after))
        up = self.shift_depth(block, 1)
        down = self.shift_depth(block, -1)
        far = self.shift_depth(up, 1)
        self.last = up
        whole = jnp.zeros((self.count // 2, 2 * rows, width), mine.dtype)
        for step, here in ((0, block), (1, up), (-1, down), (2, far)):
            place = ((self.depth - step) % 4) * 2
            across = self.swap_side(here)
            whole = lax.dynamic_update_slice(whole, here[None], (place + self.side, 0, 0))
            whole = lax.dynamic_update_slice(
                whole, across[None], (place + 1 - self.side, 0, 0)
            )
        return whole.reshape(rows * self.count, width)

    def scatter(self, keep, send=None):
        if not self.fast:
            if send is None:
                send = jnp.zeros_like(keep)
            halves = (pick(self.core, keep, send), pick(self.core, send, keep))
            return [
                lax.psum_scatter(half, "dp", scatter_dimension=0, tiled=True).astype(full)
                for half in halves
            ]
        rows = keep.shape[0] // self.count
        width = keep.shape[1]
        pair = keep
        if send is not None:
            pair = (keep.astype(full) + self.swap_core(send).astype(full)).astype(low)
        pair = pair.reshape(4, 2, 2 * rows, width)
        stay = lax.dynamic_index_in_dim(pair, self.side, 1, False)
        leave = lax.dynamic_index_in_dim(pair, 1 - self.side, 1, False)
        quad_sum = (stay.astype(full) + self.swap_side(leave).astype(full)).astype(low)
        total = lax.dynamic_index_in_dim(quad_sum, self.depth, 0, False).astype(full)
        for step in range(1, 4):
            leave = lax.dynamic_index_in_dim(quad_sum, (self.depth + step) % 4, 0, False)
            total = total + self.shift_depth(leave, step).astype(full)
        total = total.reshape(2, rows, width)
        mine = lax.dynamic_index_in_dim(total, self.core, 0, False)
        arrived = self.swap_core(lax.dynamic_index_in_dim(total, 1 - self.core, 0, False))
        return pick(self.core, mine, arrived), pick(self.core, arrived, mine)

    def total(self, x):
        if not self.fast:
            return lax.psum(x, "dp")
        x = (x + self.swap_core(x)) + (self.swap_side(x) + self.swap_both(x))
        return x + sum(self.shift_depth(x, step) for step in range(1, 4))

    def swap_both(self, x):
        return lax.ppermute(x, "dp", [(i, i ^ 3) for i in range(self.count)])


def swap_near(x, flip):
    size = 2 * lax.axis_size("dp")
    return lax.ppermute(x, ("dp", "mp"), [(i, i ^ flip) for i in range(size)])


def swap_group(x):
    return swap_near(x, 1)


def roll_rows(x):
    half = x.shape[0] // 2
    return jnp.concatenate([x[half:], x[:half]], 0)


def norm_rows(inputs):
    center = inputs - jnp.mean(inputs, -1, keepdims=True)
    scale = lax.rsqrt(jnp.mean(center * center, -1, keepdims=True) + 1e-05)
    return center * scale, scale


def norm_back(inner, unit, scale):
    return scale * (
        inner
        - jnp.mean(inner, -1, keepdims=True)
        - unit * jnp.mean(inner * unit, -1, keepdims=True)
    )


def gelu_parts(raised):
    cumulative = 0.5 * (1.0 + lax.erf(raised * 0.7071067811865476))
    slope = cumulative + raised * jnp.exp(-0.5 * raised * raised) * 0.3989422804014327
    return raised * cumulative, slope


def whole_block(shape):
    return pl.BlockSpec(shape, lambda *_: (0,) * len(shape))


def shapes(*items):
    return [jax.ShapeDtypeStruct(shape, kind) for shape, kind in items]


def pack_body(core_ref, mix_ref, back_ref, raise_ref, lower_ref, embed_ref, g1_ref, g2_ref, *outs):
    first = core_ref[0] == 0
    g1 = g1_ref[...]
    g2 = g2_ref[...]

    def part(index):
        return (mix_ref[:, index, :].astype(full) * g1).astype(low)

    def put(index, columns, zero, one):
        outs[index][:, columns] = jnp.where(first, zero, one)
        outs[index + 1][:, columns] = jnp.where(first, one, zero)

    put(0, slice(0, COLS), part(1), part(2))
    put(0, slice(COLS, 2 * COLS), part(0), back_ref[...])
    hidden = raise_ref.shape[1] // 2
    raised = (raise_ref[...].astype(full) * g2).astype(low)
    put(2, slice(0, hidden), raised[:, :hidden], raised[:, hidden:])
    put(2, slice(hidden, 2 * hidden), lower_ref[:, :hidden], lower_ref[:, hidden:])
    put(4, slice(0, COLS), embed_ref[:, :COLS], embed_ref[:, COLS:])


def pack(core, w_qkv, w_out, w_up, w_down, w_proj, g1, g2):
    rows, hidden = w_up.shape
    vmem = pl.BlockSpec(memory_space=pltpu.VMEM)
    return pl.pallas_call(
        pack_body,
        out_shape=shapes(
            *[((rows, 2 * COLS), low)] * 2, *[((rows, hidden), low)] * 2, *[((rows, COLS), low)] * 2
        ),
        in_specs=[pl.BlockSpec(memory_space=pltpu.SMEM)] + [vmem] * 7,
        out_specs=[vmem] * 6,
        name="pack",
    )(core, w_qkv, w_out, w_up, w_down, w_proj, g1, g2)


def end_picks(ends, copies):
    ends = jnp.concatenate([ends] * copies, 0)
    shape = (copies * BLOCK, TOKENS)
    row = lax.broadcasted_iota(jnp.int32, shape, 0) & (BLOCK - 1)
    return lax.broadcasted_iota(jnp.int32, shape, 1) == row * LENGTH + ends


def norm_body(group_ref, x_ref, ends_ref, unit_ref, scale_ref, unit_end_ref, stream_end_ref):
    x = x_ref[...]
    stream = x.astype(full)
    center = stream - jnp.sum(stream, -1, keepdims=True) * (1.0 / WIDTH)
    scale = lax.rsqrt(jnp.sum(center * center, -1, keepdims=True) * (1.0 / WIDTH) + 1e-05)
    unit = (center * scale).astype(low)
    unit_ref[...] = unit
    scale_ref[...] = jnp.broadcast_to(scale, scale_ref.shape)
    picks = end_picks(ends_ref[...], 1).astype(low)
    unit_end_ref[...] = mm(picks, unit).astype(low)
    stream_end_ref[...] = mm(picks, x).astype(low)


def norm_first(group, x, ends):
    steps = ends.shape[0] // BLOCK
    return pl.pallas_call(
        norm_body,
        out_shape=shapes(
            (x.shape, low), ((x.shape[0], 128), full), *[((ends.shape[0], WIDTH), low)] * 2
        ),
        grid_spec=pltpu.PrefetchScalarGridSpec(
            num_scalar_prefetch=1,
            grid=(steps,),
            in_specs=[
                pl.BlockSpec((TOKENS, WIDTH), lambda i, g: ((i + g[0] * (steps // 2)) % steps, 0)),
                pl.BlockSpec((BLOCK, 1), lambda i, g: (i, 0)),
            ],
            out_specs=[
                pl.BlockSpec((TOKENS, WIDTH), lambda i, g: (i, 0)),
                pl.BlockSpec((TOKENS, 128), lambda i, g: (i, 0)),
                pl.BlockSpec((BLOCK, WIDTH), lambda i, g: (i, 0)),
                pl.BlockSpec((BLOCK, WIDTH), lambda i, g: (i, 0)),
            ],
        ),
        name="norm_first",
    )(group, x, ends)


def head_mask(head):
    return lax.broadcasted_iota(jnp.int32, (BLOCK, COLS), 1) // HEAD == head


def head_stack(x):
    zero = jnp.zeros_like(x)
    return jnp.concatenate([jnp.where(head_mask(h), x, zero) for h in range(HEADS_HERE)], 0)


def head_fold(x):
    out = jnp.zeros((BLOCK, COLS), full)
    for h in range(HEADS_HERE):
        out = jnp.where(head_mask(h), x[h * BLOCK : (h + 1) * BLOCK], out)
    return out


def stack_grid():
    row = lax.broadcasted_iota(jnp.int32, (STACK, TOKENS), 0) & (BLOCK - 1)
    token = lax.broadcasted_iota(jnp.int32, (STACK, TOKENS), 1)
    return row, token


def step_rows(i):
    return pl.ds(pl.multiple_of(i * BLOCK, BLOCK), BLOCK)


def attend_body(
    unit_ref, unit_end_ref, ends_ref, kq_ref, vo_ref, k_ref, v_ref, p_ref, q_ref, att_ref, out_ref
):
    i = pl.program_id(0)

    @pl.when(i == 0)
    def _():
        q_ref[...] = mm(unit_end_ref[...], kq_ref[:, COLS:]).astype(low)

    unit = unit_ref[...]
    keys = mm(unit, kq_ref[:, :COLS]).astype(low)
    values = mm(unit, vo_ref[:, :COLS]).astype(low)
    k_ref[...] = keys
    v_ref[...] = values
    scores = mm_nt(head_stack(q_ref[step_rows(i), :]), keys) * SCORE_SCALE
    row, token = stack_grid()
    ends = jnp.concatenate([ends_ref[...]] * HEADS_HERE, 0)
    allowed = (token >= row * LENGTH) & (token <= row * LENGTH + ends)
    scores = jnp.where(allowed, scores, -1e30)
    weight = jnp.exp(scores - jnp.max(scores, 1, keepdims=True))
    probs = weight / jnp.sum(weight, 1, keepdims=True)
    p_ref[...] = probs
    att_ref[step_rows(i), :] = head_fold(mm(probs.astype(low), values)).astype(low)

    @pl.when(i == pl.num_programs(0) - 1)
    def _():
        out_ref[...] = mm_nt(att_ref[...], vo_ref[:, COLS:]).astype(low)


def attend(unit, unit_end, ends, kq, vo):
    count = ends.shape[0]
    steps = count // BLOCK
    return pl.pallas_call(
        attend_body,
        grid=(steps,),
        out_shape=shapes(
            *[((count * LENGTH, COLS), low)] * 2,
            ((steps * STACK, TOKENS), full),
            *[((count, COLS), low)] * 2,
            ((count, WIDTH), low),
        ),
        in_specs=[
            pl.BlockSpec((TOKENS, WIDTH), lambda i: (i, 0)),
            whole_block((count, WIDTH)),
            pl.BlockSpec((BLOCK, 1), lambda i: (i, 0)),
            whole_block(kq.shape),
            whole_block(vo.shape),
        ],
        out_specs=[
            pl.BlockSpec((TOKENS, COLS), lambda i: (i, 0)),
            pl.BlockSpec((TOKENS, COLS), lambda i: (i, 0)),
            pl.BlockSpec((STACK, TOKENS), lambda i: (i, 0)),
            whole_block((count, COLS)),
            whole_block((count, COLS)),
            whole_block((count, WIDTH)),
        ],
        name="attend",
    )(unit, unit_end, ends, kq, vo)


def attend_back_body(
    core_ref, d_mid_ref, unit_ref, unit_end_ref, vo_ref, k_ref, v_ref, p_ref, q_ref, att_ref,
    keep_ref, send_ref, dk_ref, dv_ref, small_ref, probs_ref,
    sum_ref, d_att_ref, dq_ref,
):
    i = pl.program_id(0)

    @pl.when(i == 0)
    def _():
        sum_ref[...] = jnp.zeros_like(sum_ref)
        d_att_ref[...] = mm(d_mid_ref[...], vo_ref[:, COLS:]).astype(low)

    values = v_ref[...]
    probs = p_ref[...]
    probs_low = probs.astype(low)
    queries = head_stack(q_ref[step_rows(i), :])
    d_att = head_stack(d_att_ref[step_rows(i), :])
    d_probs = mm_nt(d_att, values)
    d_scores = probs * (d_probs - jnp.sum(probs * d_probs, 1, keepdims=True))
    d_scores = (d_scores * SCORE_SCALE).astype(low)
    dq_ref[step_rows(i), :] = head_fold(mm(d_scores, k_ref[...])).astype(low)
    d_keys = mm_tn(d_scores, queries).astype(low)
    d_values = mm_tn(probs_low, d_att).astype(low)
    dk_ref[...] = d_keys
    dv_ref[...] = d_values
    spot = lax.broadcasted_iota(jnp.int32, (TOKENS, 128), 0) & (LENGTH - 1)
    lane = lax.broadcasted_iota(jnp.int32, (TOKENS, 128), 1)
    squeeze = (spot == lane).astype(low)
    squeeze_far = (spot + LENGTH == lane).astype(low)
    probs_ref[...] = (mm(probs_low, squeeze) + mm(d_scores, squeeze_far)).astype(low)
    sum_ref[...] += mm_tn(unit_ref[...], jnp.concatenate([d_keys, d_values], 1))

    @pl.when(i == pl.num_programs(0) - 1)
    def _():
        first = core_ref[0] == 0
        d_queries = dq_ref[...]
        small_ref[:, :COLS] = q_ref[...]
        small_ref[:, COLS : 2 * COLS] = d_att_ref[...]
        small_ref[:, 2 * COLS :] = d_queries
        g_key = sum_ref[:, :COLS].astype(low)
        g_value = sum_ref[:, COLS:].astype(low)
        g_query = mm_tn(unit_end_ref[...], d_queries).astype(low)
        g_back = mm_tn(d_mid_ref[...], att_ref[...]).astype(low)
        keep_ref[:, :COLS] = jnp.where(first, g_key, g_value)
        send_ref[:, :COLS] = jnp.where(first, g_value, g_key)
        keep_ref[:, COLS:] = jnp.where(first, g_query, g_back)
        send_ref[:, COLS:] = jnp.where(first, g_back, g_query)


def attend_back(core, d_mid, unit, unit_end, vo, keys, values, probs, queries, attended):
    count = d_mid.shape[0]
    steps = count // BLOCK
    return pl.pallas_call(
        attend_back_body,
        grid=(steps,),
        out_shape=shapes(
            *[((WIDTH, 2 * COLS), low)] * 2,
            *[((count * LENGTH, COLS), low)] * 2,
            ((count, 3 * COLS), low),
            ((steps * STACK, 128), low),
        ),
        in_specs=[
            pl.BlockSpec(memory_space=pltpu.SMEM),
            whole_block((count, WIDTH)),
            pl.BlockSpec((TOKENS, WIDTH), lambda i: (i, 0)),
            whole_block((count, WIDTH)),
            whole_block(vo.shape),
            pl.BlockSpec((TOKENS, COLS), lambda i: (i, 0)),
            pl.BlockSpec((TOKENS, COLS), lambda i: (i, 0)),
            pl.BlockSpec((STACK, TOKENS), lambda i: (i, 0)),
            whole_block((count, COLS)),
            whole_block((count, COLS)),
        ],
        out_specs=[
            whole_block((WIDTH, 2 * COLS)),
            whole_block((WIDTH, 2 * COLS)),
            pl.BlockSpec((TOKENS, COLS), lambda i: (i, 0)),
            pl.BlockSpec((TOKENS, COLS), lambda i: (i, 0)),
            whole_block((count, 3 * COLS)),
            pl.BlockSpec((STACK, 128), lambda i: (i, 0)),
        ],
        scratch_shapes=[
            pltpu.VMEM((WIDTH, 2 * COLS), full),
            pltpu.VMEM((count, COLS), low),
            pltpu.VMEM((count, COLS), low),
        ],
        name="attend_back",
    )(core, d_mid, unit, unit_end, vo, keys, values, probs, queries, attended)


def place_rows(picks, rows):
    high = rows.astype(low)
    rest = (rows - high.astype(full)).astype(low)
    return mm_tn(picks, jnp.concatenate([high, rest], 0))


def captions_body(
    group_ref, ends_ref, unit_ref, scale_ref, d_mid_ref, dk_ref, dv_ref, small_ref,
    small_far_ref, probs_far_ref, kq_ref, vo_ref, kq_far_ref, vo_far_ref, out_ref, inner_end_ref,
):
    i = pl.program_id(0)
    count = small_ref.shape[0]
    half = count // 2

    @pl.when(i == 0)
    def _():
        far = mm_nt(small_far_ref[:, 2 * COLS :], kq_far_ref[:, COLS:])
        own = mm_nt(small_ref[:, 2 * COLS :], kq_ref[:, COLS:])
        inner_end_ref[:half] = own[:half] + far[half:]
        inner_end_ref[half:] = own[half:] + far[:half]

    steps = pl.num_programs(0)
    far_rows = step_rows((i + steps // 2) % steps)
    row, token = stack_grid()
    own_caption = token // LENGTH == row
    lane = lax.broadcasted_iota(jnp.int32, (128, TOKENS), 0)
    spot = lax.broadcasted_iota(jnp.int32, (128, TOKENS), 1) & (LENGTH - 1)
    pair = probs_far_ref[...]
    probs = jnp.where(own_caption, mm(pair, (spot == lane).astype(low)), 0.0).astype(low)
    d_scores = jnp.where(
        own_caption, mm(pair, (spot + LENGTH == lane).astype(low)), 0.0
    ).astype(low)
    d_keys = mm_tn(d_scores, head_stack(small_far_ref[far_rows, :COLS])).astype(low)
    d_values = mm_tn(probs, head_stack(small_far_ref[far_rows, COLS : 2 * COLS])).astype(low)
    inner = mm_nt(dk_ref[...], kq_ref[:, :COLS]) + mm_nt(dv_ref[...], vo_ref[:, :COLS])
    inner += mm_nt(d_keys, kq_far_ref[:, :COLS]) + mm_nt(d_values, vo_far_ref[:, :COLS])
    picks = end_picks(ends_ref[...], 2).astype(low)
    inner += place_rows(picks, inner_end_ref[step_rows(i), :])
    unit = unit_ref[...].astype(full)
    flat = jnp.sum(inner, -1, keepdims=True) * (1.0 / WIDTH)
    tilt = jnp.sum(inner * unit, -1, keepdims=True) * (1.0 / WIDTH)
    out_ref[...] = place_rows(picks, d_mid_ref[...]) + scale_ref[:, :1] * (
        inner - flat - unit * tilt
    )


def captions_back(
    group, ends, unit, scale, d_mid, d_keys, d_values, small, small_far, probs_far, kq, vo,
    kq_far, vo_far,
):
    count = ends.shape[0]
    steps = count // BLOCK
    return pl.pallas_call(
        captions_body,
        out_shape=jax.ShapeDtypeStruct(unit.shape, full),
        grid_spec=pltpu.PrefetchScalarGridSpec(
            num_scalar_prefetch=1,
            grid=(steps,),
            in_specs=[
                pl.BlockSpec((BLOCK, 1), lambda i, g: (i, 0)),
                pl.BlockSpec((TOKENS, WIDTH), lambda i, g: (i, 0)),
                pl.BlockSpec((TOKENS, 128), lambda i, g: (i, 0)),
                pl.BlockSpec((BLOCK, WIDTH), lambda i, g: (i, 0)),
                pl.BlockSpec((TOKENS, COLS), lambda i, g: (i, 0)),
                pl.BlockSpec((TOKENS, COLS), lambda i, g: (i, 0)),
                whole_block(small.shape),
                whole_block(small.shape),
                pl.BlockSpec((STACK, 128), lambda i, g: ((i + steps // 2) % steps, 0)),
            ]
            + [whole_block(kq.shape)] * 4,
            out_specs=pl.BlockSpec(
                (TOKENS, WIDTH), lambda i, g: ((i + g[0] * (steps // 2)) % steps, 0)
            ),
            scratch_shapes=[pltpu.VMEM((count, WIDTH), full)],
        ),
        name="captions_back",
    )(
        group, ends, unit, scale, d_mid, d_keys, d_values, small, small_far, probs_far, kq, vo,
        kq_far, vo_far,
    )


def local(
    captions,
    image_cache,
    send_order,
    arrive_order,
    counts,
    keep_mask,
    end_pos,
    w_qkv,
    w_out,
    w_up,
    w_down,
    w_proj,
    ln1_gain,
    ln2_gain,
):
    plane = Plane()
    core = plane.core
    group = lax.axis_index("mp")
    spread = plane.count
    rows_dev, length, width = captions.shape
    rows = w_out.shape[0]
    per_peer = rows_dev // spread
    hidden = w_up.shape[1] // 2
    quarter = width // 4
    core_flag = core.reshape(1).astype(jnp.int32)
    group_flag = group.reshape(1).astype(jnp.int32)

    packed = pack(
        core_flag, w_qkv, w_out, w_up, w_down, w_proj, ln1_gain[:, None], ln2_gain[:, None]
    )
    mix_own = plane.gather(packed[0], packed[1])
    mix_other = plane.swap_core(mix_own)
    feeds = plane.gather(packed[2], packed[3], plane.last if plane.fast else None)

    cached = image_cache.astype(full)
    cached = (cached * lax.rsqrt(jnp.sum(cached * cached, -1, keepdims=True) + 1e-06)).astype(low)
    places = jnp.arange(rows_dev, dtype=jnp.int32)
    hand_out = (send_order[0][:, None] == places[None, :]).astype(low)
    outgoing = mm(hand_out, cached).astype(low).reshape(spread, per_peer, width)
    incoming = lax.all_to_all(outgoing, "dp", split_axis=0, concat_axis=0, tiled=True)
    own_arrive = lax.dynamic_slice_in_dim(arrive_order[0], group * CAP_DEV, CAP_DEV, 0)
    take_in = (own_arrive[:, None] == places[None, :]).astype(low)
    pictures = mm(take_in, incoming.reshape(rows_dev, width)).astype(low)
    wide = width // 2
    picture_mine = pick(core, pictures[:, :wide], pictures[:, wide:])
    picture_send = pick(core, pictures[:, wide:], pictures[:, :wide])
    main = rows if plane.fast else CAP_DEV
    spare = CAP_DEV - main
    if plane.fast:

        def join(embed, half):
            parts = [half[main:, i * 128 : (i + 1) * 128] for i in range(wide // 128)]
            return jnp.concatenate([embed, half[:main], jnp.concatenate(parts, 0)], 1)

        third = plane.gather(
            join(packed[4], picture_mine), join(packed[5], picture_send), plane.last
        )
        third_other = plane.swap_core(third)

        def images(x):
            extra = x[:, 2 * wide :].reshape(spread, wide // 128, spare, 128)
            extra = extra.transpose(0, 2, 1, 3).reshape(spread * spare, wide)
            return jnp.concatenate([x[:, wide : 2 * wide], extra], 0)

        image_halves = images(third), images(third_other)
        embed_halves = third[:, :wide], third_other[:, :wide]
    else:
        image_half = plane.gather(picture_mine, picture_send)
        image_halves = image_half, plane.swap_core(image_half)
        embed_half = plane.gather(packed[4], packed[5])
        embed_halves = embed_half, plane.swap_core(embed_half)

    def sides(pair):
        return jnp.concatenate([pick(core, *pair), pick(core, pair[1], pair[0])], 1)

    pictures_all = sides(image_halves)
    w_embed = sides(embed_halves)
    kq = pick(core, mix_own, mix_other)
    vo = pick(core, mix_other, mix_own)
    far_own = swap_group(mix_own)
    far_other = plane.swap_core(far_own)
    kq_far = pick(core, far_own, far_other)
    vo_far = pick(core, far_other, far_own)

    flipped = jnp.concatenate([end_pos, end_pos], 0)
    ends = lax.dynamic_slice_in_dim(flipped, group * CAP_DEV, rows_dev, 0)[:, None]
    unit, scale, unit_end, stream_end = norm_first(
        group_flag, captions.reshape(rows_dev * length, width), ends
    )
    keys, values, probs, queries, attended, attention = attend(unit, unit_end, ends, kq, vo)

    stream_near = swap_near(stream_end, 2)
    from_group, from_core, from_both = [swap_near(attention, flip) for flip in (1, 2, 3)]
    attention = jnp.concatenate([attention, from_core], 0).astype(full)
    attention = attention + jnp.concatenate(
        [roll_rows(from_group), roll_rows(from_both)], 0
    ).astype(full)
    middle = jnp.concatenate([stream_end, stream_near], 0).astype(full) + attention
    unit_second, scale_second = norm_rows(middle)
    second_low = unit_second.astype(low)
    w_raise = feeds[:, :hidden]
    w_lower = feeds[:, hidden:]
    active, slope = gelu_parts(mm(second_low, w_raise))
    active = active.astype(low)
    lowered = mm_nt(active, w_lower).astype(low)
    feed = lowered[:CAP_DEV].astype(full)
    for flip in (1, 2, 3):
        part = swap_near(lowered[flip * CAP_DEV : (flip + 1) * CAP_DEV], flip)
        feed = feed + part.astype(full)
    pooled = (middle[:CAP_DEV] + feed).astype(low)
    embedding = mm(pooled, w_embed)
    inverse = lax.rsqrt(jnp.sum(embedding * embedding, -1, keepdims=True) + 1e-06)
    unit_text = embedding * inverse
    text_low = unit_text.astype(low)

    keep_rows = keep_mask.reshape(spread, MICRO, CAP_DEV) == 1
    filled = jnp.arange(CAP_DEV, dtype=jnp.int32)[None, None, :] < counts[:, :, None]
    valid = keep_rows & filled
    total_valid = jnp.sum(valid.astype(full))
    batch_valid = lax.dynamic_index_in_dim(valid, group, 1, False)
    own_valid = lax.dynamic_index_in_dim(batch_valid, plane.index, 0, False)
    batch_valid = jnp.concatenate(
        [batch_valid[:, :main].reshape(-1), batch_valid[:, main:].reshape(-1)]
    )
    sims = LOGIT_SCALE * mm_nt(text_low, pictures_all)
    allowed = own_valid[:, None] & batch_valid[None, :]
    weight = jnp.where(allowed, jnp.exp(sims), 0.0)
    row_sum = jnp.sum(weight, 1)
    place = jnp.arange(CAP_DEV, dtype=jnp.int32)
    slot = jnp.where(
        place < main,
        plane.index * main + place,
        spread * main + plane.index * spare + place - main,
    )
    target = (
        jnp.arange(spread * CAP_DEV, dtype=jnp.int32)[None, :] == slot[:, None]
    ) & own_valid[:, None]
    row_safe = jnp.where(own_valid, row_sum, 1.0)
    row_part = 0.5 * jnp.sum(jnp.log(row_safe)) - jnp.sum(jnp.where(target, sims, 0.0))
    col_part = jnp.sum(weight, 0)
    totals = jnp.concatenate([col_part, jnp.full((128,), 1.0 / 128, full) * row_part])
    totals = plane.total(totals.reshape(-1, 128)).reshape(-1)
    col_sum = totals[: spread * CAP_DEV]
    col_safe = jnp.where(batch_valid, col_sum, 1.0)
    objective = jnp.sum(totals[spread * CAP_DEV :]) + 0.5 * jnp.sum(jnp.log(col_safe))
    objective = jnp.full((8, 128), objective)
    loss = (objective + swap_group(objective))[0, 0] / total_valid
    d_sims = (
        weight * (0.5 / row_safe[:, None] + 0.5 / col_safe[None, :]) - target.astype(full)
    ).astype(low)
    d_unit = LOGIT_SCALE * mm(d_sims, pictures_all)
    d_embed = (
        (d_unit - unit_text * jnp.sum(unit_text * d_unit, -1, keepdims=True)) * inverse
    ).astype(low)

    pooled_all = jnp.concatenate([pooled] + [swap_near(pooled, flip) for flip in (1, 2, 3)], 0)
    d_embed_all = jnp.concatenate([d_embed] + [swap_near(d_embed, flip) for flip in (1, 2, 3)], 0)
    d_pooled = mm_nt(d_embed_all, w_embed)
    d_out_low = d_pooled.astype(low)
    g_lower = mm_tn(d_out_low, active).astype(low)
    d_raised = (mm(d_out_low, w_lower) * slope).astype(low)
    g_raise = mm_tn(second_low, d_raised).astype(low)
    d_second = mm_nt(d_raised, w_raise).astype(low)
    d_embed_half = pick(group, d_embed_all[:, :wide], d_embed_all[:, wide:])
    d_embed_here = pick(core, d_embed_half[:, :quarter], d_embed_half[:, quarter:])
    g_embed = mm_tn(pooled_all, d_embed_here).astype(low)
    lower_sum = plane.scatter(jnp.concatenate([g_lower, g_embed], 1))
    raise_sum = plane.scatter(g_raise)
    inner = d_second[:rows_dev].astype(full)
    inner = inner + roll_rows(swap_near(d_second[:rows_dev], 1)).astype(full)
    inner = inner + swap_near(d_second[rows_dev:], 2).astype(full)
    inner = inner + roll_rows(swap_near(d_second[rows_dev:], 3)).astype(full)
    d_middle = d_pooled[:rows_dev] + norm_back(
        inner, unit_second[:rows_dev], scale_second[:rows_dev]
    )

    g_keep, g_send, d_keys, d_values, small, small_probs = attend_back(
        core_flag, d_middle.astype(low), unit, unit_end, vo, keys, values, probs, queries, attended
    )
    mix_sum = plane.scatter(g_keep, g_send)
    small_far = swap_group(small)
    probs_far = swap_group(small_probs)
    grad_captions = captions_back(
        group_flag, ends, unit, scale, d_middle, d_keys, d_values, small, small_far, probs_far,
        kq, vo, kq_far, vo_far,
    ).reshape(rows_dev, length, width)

    grad_down = jnp.concatenate([part[:, :hidden] for part in lower_sum], 1)
    proj_own = jnp.concatenate([part[:, hidden:] for part in lower_sum], 1)
    proj_far = swap_group(proj_own)
    grad_proj = pick(
        group,
        jnp.concatenate([proj_own, proj_far], 1),
        jnp.concatenate([proj_far, proj_own], 1),
    )
    grad_out = mix_sum[1][:, COLS:]
    unit_mix = jnp.stack([mix_sum[0][:, COLS:], mix_sum[0][:, :COLS], mix_sum[1][:, :COLS]], 1)
    grad_qkv = unit_mix * ln1_gain[:, None, None]
    raised_sum = jnp.concatenate(raise_sum, 1)
    grad_up = raised_sum * ln2_gain[:, None]
    gains = jnp.stack(
        [
            jnp.sum(unit_mix * w_qkv.astype(full), (1, 2)),
            jnp.sum(raised_sum * w_up.astype(full), 1),
        ]
    )
    gains = gains + swap_group(gains)
    return (
        loss,
        grad_captions,
        grad_qkv,
        grad_out,
        grad_up,
        grad_down,
        grad_proj,
        gains[0],
        gains[1],
    )


def solution(mesh):
    return jax.shard_map(
        local,
        mesh=mesh,
        in_specs=(
            P("dp", None, None),
            P("dp", None),
            P("dp", None),
            P("dp", None),
            P(),
            P(),
            P("dp"),
            P("dp", None, "mp"),
            P("dp", "mp"),
            P("dp", "mp"),
            P("dp", "mp"),
            P("dp", None),
            P("dp"),
            P("dp"),
        ),
        out_specs=(
            P(),
            P("dp", None, None),
            P("dp", None, "mp"),
            P("dp", "mp"),
            P("dp", "mp"),
            P("dp", "mp"),
            P("dp", None),
            P("dp"),
            P("dp"),
        ),
        check_vma=False,
    )
```

profile of v0, /device:TPU:0, one launch (start us, length us, event | category | flops | bytes accessed | tf_op | source)
XLA Modules:
  0.0 300.4 jit_solution(15666963420147013703)
XLA Ops:
  5.9 7.5 %norm_first.1 = (bf16[2048,768]{1,0:T(8,128)(2,1)}, f32[2048,128]{1,0:T(8,128)}, bf16[128,768]{1,0:T(8,128)(2,1)}, bf16[128,768]{1,0:T(8,128)(2,1)}) custom-call(s32[1]{0:T(128)} %bitcast.1.group_ref, bf16[2048,768]{1,0:T(8,128)(2,1)} %bitcast.213, s32[128,1]{1,0:T(8,128)} %copy.44.ends_ref), custom_call_target="tpu_custom_call" | custom-call | tf_op jit(solution)/shard_map/norm_first/pallas_call | solution.py:226
  15.0 7.0 %all-to-all-start = ((bf16[16,8,768]{2,1,0:T(8,128)(2,1)}), bf16[16,8,768]{2,1,0:T(8,128)(2,1)S(1)}, u32[]{:S(2)}, u32[]{:S(2)}) async-start(bf16[16,8,768]{2,1,0:T(8,128)(2,1)} %fusion.4), calls=%async_computation | async-start | bytes 393216 | tf_op jit(solution)/shard_map/all_to_all | solution.py:547
  24.6 1.8 collective-permute-start.2
  27.9 2.4 collective-permute-start.5
  30.4 4.6 %collective-permute-done.3 = bf16[96,768]{1,0:T(8,128)(2,1)S(1)} collective-permute-done((bf16[96,768]{1,0:T(8,128)(2,1)S(1)}, bf16[96,768]{1,0:T(8,128)(2,1)S(1)}, u32[]{:S(2)}, u32[]{:S(2)}) %collective-permute-start.3) | collective-permute-done | bytes 147488 | tf_op jit(solution)/shard_map/ppermute | solution.py:59
  39.6 3.9 %collective-permute-start.17 = (bf16[96,1536]{1,0:T(8,128)(2,1)S(1)}, bf16[96,1536]{1,0:T(8,128)(2,1)S(1)}, u32[]{:S(2)}, u32[]{:S(2)}) collective-permute-start(bf16[96,1536]{1,0:T(8,128)(2,1)S(1)} %bitcast.223), channel_id=1, source_target_pairs={{0,24},{2,26},{4,28},{6,30},{8,0},{10,2},{12,4},{14,6},{16,8},{18,... | collective-permute-start | bytes 884744 | tf_op jit(solution)/shard_map/ppermute | solution.py:59
  46.4 3.6 %collective-permute-done.6 = bf16[96,768]{1,0:T(8,128)(2,1)S(1)} collective-permute-done((bf16[96,768]{1,0:T(8,128)(2,1)S(1)}, bf16[96,768]{1,0:T(8,128)(2,1)S(1)}, u32[]{:S(2)}, u32[]{:S(2)}) %collective-permute-start.6) | collective-permute-done | bytes 147488 | tf_op jit(solution)/shard_map/ppermute | solution.py:56
  50.1 6.9 %collective-permute-done.7 = bf16[96,768]{1,0:T(8,128)(2,1)S(1)} collective-permute-done((bf16[96,768]{1,0:T(8,128)(2,1)S(1)}, bf16[96,768]{1,0:T(8,128)(2,1)S(1)}, u32[]{:S(2)}, u32[]{:S(2)}) %collective-permute-start.7) | collective-permute-done | bytes 147488 | tf_op jit(solution)/shard_map/ppermute | solution.py:59
  62.0 3.0 collective-permute-done.8
  65.9 1.9 collective-permute-done.25
  69.6 6.5 %collective-permute-done.16 = bf16[96,1536]{1,0:T(8,128)(2,1)S(1)} collective-permute-done((bf16[96,1536]{1,0:T(8,128)(2,1)S(1)}, bf16[96,1536]{1,0:T(8,128)(2,1)S(1)}, u32[]{:S(2)}, u32[]{:S(2)}) %collective-permute-start.16) | collective-permute-done | bytes 294944 | tf_op jit(solution)/shard_map/ppermute | solution.py:56
  79.0 4.4 %collective-permute-done.18 = bf16[96,1536]{1,0:T(8,128)(2,1)S(1)} collective-permute-done((bf16[96,1536]{1,0:T(8,128)(2,1)S(1)}, bf16[96,1536]{1,0:T(8,128)(2,1)S(1)}, u32[]{:S(2)}, u32[]{:S(2)}) %collective-permute-start.18) | collective-permute-done | bytes 294944 | tf_op jit(solution)/shard_map/ppermute | solution.py:56
  87.0 3.7 %collective-permute-done.27 = bf16[96,896]{1,0:T(8,128)(2,1)S(1)} collective-permute-done((bf16[96,896]{1,0:T(8,128)(2,1)S(1)}, bf16[96,896]{1,0:T(8,128)(2,1)S(1)}, u32[]{:S(2)}, u32[]{:S(2)}) %collective-permute-start.27) | collective-permute-done | bytes 172064 | tf_op jit(solution)/shard_map/ppermute | solution.py:56
  94.4 6.8 %collective-permute-done.31 = bf16[96,896]{1,0:T(8,128)(2,1)S(1)} collective-permute-done((bf16[96,896]{1,0:T(8,128)(2,1)S(1)}, bf16[96,896]{1,0:T(8,128)(2,1)S(1)}, u32[]{:S(2)}, u32[]{:S(2)}) %collective-permute-start.31) | collective-permute-done | bytes 172064 | tf_op jit(solution)/shard_map/ppermute | solution.py:56
  101.3 1.6 broadcast_select_fusion.2
  102.9 11.6 %attend.1 = (bf16[2048,384]{1,0:T(8,128)(2,1)}, bf16[2048,384]{1,0:T(8,128)(2,1)}, f32[768,256]{1,0:T(8,128)}, bf16[128,384]{1,0:T(8,128)(2,1)}, bf16[128,384]{1,0:T(8,128)(2,1)}, /*index=5*/bf16[128,768]{1,0:T(8,128)(2,1)}) custom-call(bf16[2048,768]{1,0:T(8,128)(2,1)} %get-tuple-element.34.unit_ref, bf16[128,768]{1,0:T(8,128)(2,1)} %get-tuple-element.35.unit_end_ref, ...), custom_call_target="tpu_custom_call" | custom-call | tf_op jit(solution)/shard_map/attend/pallas_call | solution.py:307
  117.5 5.1 %collective-permute-done.11 = bf16[128,768]{1,0:T(8,128)(2,1)S(1)} collective-permute-done((bf16[128,768]{1,0:T(8,128)(2,1)}, bf16[128,768]{1,0:T(8,128)(2,1)S(1)}, u32[]{:S(2)}, u32[]{:S(2)}) %collective-permute-start.11) | collective-permute-done | bytes 196640 | tf_op jit(solution)/shard_map/ppermute | solution.py:129
  122.6 3.2 %collective-permute-done.12 = bf16[128,768]{1,0:T(8,128)(2,1)S(1)} collective-permute-done((bf16[128,768]{1,0:T(8,128)(2,1)}, bf16[128,768]{1,0:T(8,128)(2,1)S(1)}, u32[]{:S(2)}, u32[]{:S(2)}) %collective-permute-start.12) | collective-permute-done | bytes 196640 | tf_op jit(solution)/shard_map/ppermute | solution.py:129
  126.5 2.6 multiply_convert_fusion
  129.2 1.9 convolution_convert_fusion.3
  135.1 1.6 collective-permute-done.21
  141.9 2.0 fusion.41
  148.4 2.2 collective-permute-done.34
  151.7 2.9 collective-permute-start.37
  155.2 8.5 %collective-permute-done.48 = bf16[768,768]{1,0:T(8,128)(2,1)} collective-permute-done((bf16[768,768]{1,0:T(8,128)(2,1)S(1)}, bf16[768,768]{1,0:T(8,128)(2,1)}, u32[]{:S(2)}, u32[]{:S(2)}) %collective-permute-start.48) | collective-permute-done | bytes 1179680 | tf_op jit(solution)/shard_map/ppermute | solution.py:129
  170.7 1.7 multiply_reduce_fusion.4
  177.4 2.5 collective-permute-start.63
  180.5 2.1 fusion.1
  183.1 1.8 convolution_convert_fusion.2
  189.0 1.7 collective-permute-start.43
  193.2 1.7 copy.52
  195.8 2.2 collective-permute-done.43
  203.4 13.9 %attend_back.1 = (bf16[768,768]{1,0:T(8,128)(2,1)}, bf16[768,768]{1,0:T(8,128)(2,1)}, bf16[2048,384]{1,0:T(8,128)(2,1)}, bf16[2048,384]{1,0:T(8,128)(2,1)}, bf16...) custom-call(s32[1]{0:T(128)} %bitcast.4.core_ref, bf16[128,768]{1,0:T(8,128)(2,1)} %get-tuple-element.74.d_mid_ref, ...), custom_call_target="tpu_custom_call" | custom-call | tf_op jit(solution)/shard_map/attend_back/pallas_call | solution.py:387
  217.5 2.0 collective-permute-start.47
  221.2 10.0 %collective-permute-done.47.probs_far_ref = bf16[768,128]{1,0:T(8,128)(2,1)S(1)} collective-permute-done((bf16[768,128]{1,0:T(8,128)(2,1)}, bf16[768,128]{1,0:T(8,128)(2,1)S(1)}, u32[]{:S(2)}, u32[]{:S(2)}) %collective-permute-start.47) | collective-permute-done | bytes 196640 | tf_op jit(solution)/shard_map/ppermute | solution.py:129
  232.1 1.8 collective-permute-start.59
  234.0 3.2 %broadcast_select_fusion = (bf16[768,768]{1,0:T(8,128)(2,1)}, bf16[768,768]{1,0:T(8,128)(2,1)}) fusion(bf16[768,768]{1,0:T(8,128)(2,1)} %collective-permute-done.49, bf16[768,768]{1,0:T(8,128)(2,1)} %collective-permute-done.48, pred[]{:T(512)S(6)} %eq.103), kind=kLoop, calls=%fused_computation.18 | loop fusion | flops 1179648 | bytes 4718593 | tf_op jit(solution)/shard_map/jit(_where)/select_n | solution.py:40
  237.1 18.4 %captions_back.1 = f32[2048,768]{1,0:T(8,128)} custom-call(s32[1]{0:T(128)} %bitcast.1.group_ref, s32[128,1]{1,0:T(8,128)} %copy.44.ends_ref, bf16[2048,768]{1,0:T(8,128)(2,1)} %get-tuple-element.34.unit_ref, f32[2048,128]{1,0:T(8,128)} %get-tuple-element.45.scale_ref, f32[128,768]{1,0:T(8,128)} %get-tuple-element.75.d_mid_ref, ...), custom_call_target="tpu_custom_call" | custom-call | tf_op jit(solution)/shard_map/captions_back/pallas_call | solution.py:477
  257.9 1.7 collective-permute-start.66
  259.6 2.7 collective-permute-start.67
  265.3 1.8 collective-permute-done.65
  267.1 7.9 %collective-permute-done.66 = bf16[96,960]{1,0:T(8,128)(2,1)S(1)} collective-permute-done((bf16[96,960]{1,0:T(8,128)(2,1)S(1)}, bf16[96,960]{1,0:T(8,128)(2,1)S(1)}, u32[]{:S(2)}, u32[]{:S(2)}) %collective-permute-start.66) | collective-permute-done | bytes 184352 | tf_op jit(solution)/shard_map/ppermute | solution.py:59
  275.2 3.7 %collective-permute-done.51 = bf16[4,96,768]{2,1,0:T(8,128)(2,1)S(1)} collective-permute-done((bf16[4,96,768]{2,1,0:T(8,128)(2,1)S(1)}, bf16[4,96,768]{2,1,0:T(8,128)(2,1)S(1)}, u32[]{:S(2)}, u32[]{:S(2)}) %collective-permute-start.51) | collective-permute-done | bytes 589856 | tf_op jit(solution)/shard_map/ppermute | solution.py:56
  279.5 1.7 collective-permute-start.53
  281.2 1.8 collective-permute-start.54
  283.6 4.1 %collective-permute-done.52 = bf16[96,768]{1,0:T(8,128)(2,1)S(1)} collective-permute-done((bf16[96,768]{1,0:T(8,128)(2,1)S(1)}, bf16[96,768]{1,0:T(8,128)(2,1)S(1)}, u32[]{:S(2)}, u32[]{:S(2)}) %collective-permute-start.52) | collective-permute-done | bytes 147488 | tf_op jit(solution)/shard_map/ppermute | solution.py:59
  287.7 4.2 %collective-permute-done.53 = bf16[96,768]{1,0:T(8,128)(2,1)S(1)} collective-permute-done((bf16[96,768]{1,0:T(8,128)(2,1)S(1)}, bf16[96,768]{1,0:T(8,128)(2,1)S(1)}, u32[]{:S(2)}, u32[]{:S(2)}) %collective-permute-start.53) | collective-permute-done | bytes 147488 | tf_op jit(solution)/shard_map/ppermute | solution.py:59
  296.2 2.5 collective-permute-done.70
  (334 shorter events, 90.9 us)
Async XLA Ops:
  4.4 20.1 %collective-permute-start.1 = (bf16[48,768]{1,0:T(8,128)(2,1)S(1)}, bf16[48,768]{1,0:T(8,128)(2,1)S(1)}, u32[]{:S(2)}, u32[]{:S(2)}) collective-permute-start(bf16[48,768]{1,0:T(8,128)(2,1)S(1)} %get-tuple-element.60), channel_id=1, source_target_pairs={{0,2},{2,0},{4,6},{6,4},{8,10},{10,8},{12,14},{14,12},{16,18},{18,... | collective-permute-start | bytes 221192 | tf_op jit(solution)/shard_map/ppermute | solution.py:53
  13.3 112.5 %collective-permute-start = (bf16[128,768]{1,0:T(8,128)(2,1)}, bf16[128,768]{1,0:T(8,128)(2,1)S(1)}, u32[]{:S(2)}, u32[]{:S(2)}) collective-permute-start(bf16[128,768]{1,0:T(8,128)(2,1)} %get-tuple-element.33), channel_id=1, source_target_pairs={{0,2},{1,3},{2,0},{3,1},{4,6},{5,7},{6,4},{7,5},{8,10},{9,11},{10,... | collective-permute-start | bytes 589832 | tf_op jit(solution)/shard_map/ppermute | solution.py:129
  13.4 16.9 %collective-permute-start.13 = (bf16[48,1536]{1,0:T(8,128)(2,1)S(1)}, bf16[48,1536]{1,0:T(8,128)(2,1)S(1)}, u32[]{:S(2)}, u32[]{:S(2)}) collective-permute-start(bf16[48,1536]{1,0:T(8,128)(2,1)S(1)} %get-tuple-element.64), channel_id=1, source_target_pairs={{0,2},{2,0},{4,6},{6,4},{8,10},{10,8},{12,14},{14,12},{16,18},{18,... | collective-permute-start | bytes 442376 | tf_op jit(solution)/shard_map/ppermute | solution.py:53
  15.0 24.4 %all-to-all-start = ((bf16[16,8,768]{2,1,0:T(8,128)(2,1)}), bf16[16,8,768]{2,1,0:T(8,128)(2,1)S(1)}, u32[]{:S(2)}, u32[]{:S(2)}) async-start(bf16[16,8,768]{2,1,0:T(8,128)(2,1)} %fusion.4), calls=%async_computation | async-start | bytes 393216 | tf_op jit(solution)/shard_map/all_to_all | solution.py:547
  24.6 12.1 %collective-permute-start.2 = (bf16[96,768]{1,0:T(8,128)(2,1)S(1)}, bf16[96,768]{1,0:T(8,128)(2,1)S(1)}, u32[]{:S(2)}, u32[]{:S(2)}) collective-permute-start(bf16[96,768]{1,0:T(8,128)(2,1)S(1)} %bitcast.234), channel_id=1, source_target_pairs={{0,4},{2,6},{4,0},{6,2},{8,12},{10,14},{12,8},{14,10},{16,20},{18,... | collective-permute-start | bytes 442376 | tf_op jit(solution)/shard_map/ppermute | solution.py:56
  26.4 8.5 %collective-permute-start.3 = (bf16[96,768]{1,0:T(8,128)(2,1)S(1)}, bf16[96,768]{1,0:T(8,128)(2,1)S(1)}, u32[]{:S(2)}, u32[]{:S(2)}) collective-permute-start(bf16[96,768]{1,0:T(8,128)(2,1)S(1)} %bitcast.235), channel_id=1, source_target_pairs={{0,8},{2,10},{4,12},{6,14},{8,16},{10,18},{12,20},{14,22},{16,24},... | collective-permute-start | bytes 442376 | tf_op jit(solution)/shard_map/ppermute | solution.py:59
  27.9 11.8 %collective-permute-start.5 = (bf16[96,768]{1,0:T(8,128)(2,1)S(1)}, bf16[96,768]{1,0:T(8,128)(2,1)S(1)}, u32[]{:S(2)}, u32[]{:S(2)}) collective-permute-start(bf16[96,768]{1,0:T(8,128)(2,1)S(1)} %bitcast.236), channel_id=1, source_target_pairs={{0,24},{2,26},{4,28},{6,30},{8,0},{10,2},{12,4},{14,6},{16,8},{18,... | collective-permute-start | bytes 442376 | tf_op jit(solution)/shard_map/ppermute | solution.py:59
  35.0 25.4 %collective-permute-start.14 = (bf16[96,1536]{1,0:T(8,128)(2,1)S(1)}, bf16[96,1536]{1,0:T(8,128)(2,1)S(1)}, u32[]{:S(2)}, u32[]{:S(2)}) collective-permute-start(bf16[96,1536]{1,0:T(8,128)(2,1)S(1)} %bitcast.220), channel_id=1, source_target_pairs={{0,4},{2,6},{4,0},{6,2},{8,12},{10,14},{12,8},{14,10},{16,20},{18,... | collective-permute-start | bytes 884744 | tf_op jit(solution)/shard_map/ppermute | solution.py:56
  35.2 24.6 %collective-permute-start.15 = (bf16[96,1536]{1,0:T(8,128)(2,1)S(1)}, bf16[96,1536]{1,0:T(8,128)(2,1)S(1)}, u32[]{:S(2)}, u32[]{:S(2)}) collective-permute-start(bf16[96,1536]{1,0:T(8,128)(2,1)S(1)} %bitcast.221), channel_id=1, source_target_pairs={{0,8},{2,10},{4,12},{6,14},{8,16},{10,18},{12,20},{14,22},{16,24},... | collective-permute-start | bytes 884744 | tf_op jit(solution)/shard_map/ppermute | solution.py:59
  39.6 29.9 %collective-permute-start.17 = (bf16[96,1536]{1,0:T(8,128)(2,1)S(1)}, bf16[96,1536]{1,0:T(8,128)(2,1)S(1)}, u32[]{:S(2)}, u32[]{:S(2)}) collective-permute-start(bf16[96,1536]{1,0:T(8,128)(2,1)S(1)} %bitcast.223), channel_id=1, source_target_pairs={{0,24},{2,26},{4,28},{6,30},{8,0},{10,2},{12,4},{14,6},{16,8},{18,... | collective-permute-start | bytes 884744 | tf_op jit(solution)/shard_map/ppermute | solution.py:59
  60.4 9.0 %collective-permute-start.26 = (bf16[96,896]{1,0:T(8,128)(2,1)S(1)}, bf16[96,896]{1,0:T(8,128)(2,1)S(1)}, u32[]{:S(2)}, u32[]{:S(2)}) collective-permute-start(bf16[96,896]{1,0:T(8,128)(2,1)S(1)} %bitcast.231), channel_id=1, source_target_pairs={{0,8},{2,10},{4,12},{6,14},{8,16},{10,18},{12,20},{14,22},{16,24},... | collective-permute-start | bytes 516104 | tf_op jit(solution)/shard_map/ppermute | solution.py:59
  65.0 20.7 %collective-permute-start.28 = (bf16[96,896]{1,0:T(8,128)(2,1)S(1)}, bf16[96,896]{1,0:T(8,128)(2,1)S(1)}, u32[]{:S(2)}, u32[]{:S(2)}) collective-permute-start(bf16[96,896]{1,0:T(8,128)(2,1)S(1)} %bitcast.233), channel_id=1, source_target_pairs={{0,24},{2,26},{4,28},{6,30},{8,0},{10,2},{12,4},{14,6},{16,8},{18,... | collective-permute-start | bytes 516104 | tf_op jit(solution)/shard_map/ppermute | solution.py:59
  67.9 8.2 %collective-permute-start.16 = (bf16[96,1536]{1,0:T(8,128)(2,1)S(1)}, bf16[96,1536]{1,0:T(8,128)(2,1)S(1)}, u32[]{:S(2)}, u32[]{:S(2)}) collective-permute-start(bf16[96,1536]{1,0:T(8,128)(2,1)S(1)} %copy-done.18), channel_id=1, source_target_pairs={{0,4},{2,6},{4,0},{6,2},{8,12},{10,14},{12,8},{14,10},{16,20},{18,... | collective-permute-start | bytes 884744 | tf_op jit(solution)/shard_map/ppermute | solution.py:56
  69.4 31.8 %collective-permute-start.9 = (bf16[768,768]{1,0:T(8,128)(2,1)S(1)}, bf16[768,768]{1,0:T(8,128)(2,1)S(1)}, u32[]{:S(2)}, u32[]{:S(2)}) collective-permute-start(bf16[768,768]{1,0:T(8,128)(2,1)S(1)} %bitcast.209), channel_id=1, source_target_pairs={{0,2},{2,0},{4,6},{6,4},{8,10},{10,8},{12,14},{14,12},{16,18},{18,... | collective-permute-start | bytes 3538952 | tf_op jit(solution)/shard_map/ppermute | solution.py:53
  69.5 16.2 %collective-permute-start.19 = (bf16[96,1536]{1,0:T(8,128)(2,1)S(1)}, bf16[96,1536]{1,0:T(8,128)(2,1)S(1)}, u32[]{:S(2)}, u32[]{:S(2)}) collective-permute-start(bf16[96,1536]{1,0:T(8,128)(2,1)S(1)} %copy-done.18), channel_id=1, source_target_pairs={{0,8},{2,10},{4,12},{6,14},{8,16},{10,18},{12,20},{14,22},{16,24},... | collective-permute-start | bytes 884744 | tf_op jit(solution)/shard_map/ppermute | solution.py:59
  85.7 8.7 %collective-permute-start.29 = (bf16[96,896]{1,0:T(8,128)(2,1)S(1)}, bf16[96,896]{1,0:T(8,128)(2,1)S(1)}, u32[]{:S(2)}, u32[]{:S(2)}) collective-permute-start(bf16[96,896]{1,0:T(8,128)(2,1)S(1)} %collective-permute-done.28), channel_id=1, source_target_pairs={{0,4},{2,6},{4,0},{6,2},{8,12},{10,14},{12,8},{14,10},{16,20},{18,... | collective-permute-start | bytes 516104 | tf_op jit(solution)/shard_map/ppermute | solution.py:56
  90.7 25.5 %collective-permute-start.20 = (bf16[96,1536]{1,0:T(8,128)(2,1)S(1)}, bf16[96,1536]{1,0:T(8,128)(2,1)S(1)}, u32[]{:S(2)}, u32[]{:S(2)}) collective-permute-start(bf16[96,1536]{1,0:T(8,128)(2,1)S(1)} %collective-permute-done.19), channel_id=1, source_target_pairs={{0,4},{2,6},{4,0},{6,2},{8,12},{10,14},{12,8},{14,10},{16,20},{18,... | collective-permute-start | bytes 884744 | tf_op jit(solution)/shard_map/ppermute | solution.py:56
  92.9 8.3 %collective-permute-start.31 = (bf16[96,896]{1,0:T(8,128)(2,1)S(1)}, bf16[96,896]{1,0:T(8,128)(2,1)S(1)}, u32[]{:S(2)}, u32[]{:S(2)}) collective-permute-start(bf16[96,896]{1,0:T(8,128)(2,1)S(1)} %collective-permute-done.30), channel_id=1, source_target_pairs={{0,4},{2,6},{4,0},{6,2},{8,12},{10,14},{12,8},{14,10},{16,20},{18,... | collective-permute-start | bytes 516104 | tf_op jit(solution)/shard_map/ppermute | solution.py:56
  101.2 36.9 %collective-permute-start.32 = (bf16[768,896]{1,0:T(8,128)(2,1)S(1)}, bf16[768,896]{1,0:T(8,128)(2,1)}, u32[]{:S(2)}, u32[]{:S(2)}) collective-permute-start(bf16[768,896]{1,0:T(8,128)(2,1)S(1)} %bitcast.204), channel_id=1, source_target_pairs={{0,2},{2,0},{4,6},{6,4},{8,10},{10,8},{12,14},{14,12},{16,18},{18,... | collective-permute-start | bytes 4128776 | tf_op jit(solution)/shard_map/ppermute | solution.py:53
  116.9 9.0 %collective-permute-start.12 = (bf16[128,768]{1,0:T(8,128)(2,1)}, bf16[128,768]{1,0:T(8,128)(2,1)S(1)}, u32[]{:S(2)}, u32[]{:S(2)}) collective-permute-start(bf16[128,768]{1,0:T(8,128)(2,1)} %get-tuple-element.38), channel_id=1, source_target_pairs={{0,3},{1,2},{2,1},{3,0},{4,7},{5,6},{6,5},{7,4},{8,11},{9,10},{10,... | collective-permute-start | bytes 589832 | tf_op jit(solution)/shard_map/ppermute | solution.py:129
  117.2 8.7 %collective-permute-start.10 = (bf16[128,768]{1,0:T(8,128)(2,1)}, bf16[128,768]{1,0:T(8,128)(2,1)S(1)}, u32[]{:S(2)}, u32[]{:S(2)}) collective-permute-start(bf16[128,768]{1,0:T(8,128)(2,1)} %get-tuple-element.38), channel_id=1, source_target_pairs={{0,2},{1,3},{2,0},{3,1},{4,6},{5,7},{6,4},{7,5},{8,10},{9,11},{10,... | collective-permute-start | bytes 589832 | tf_op jit(solution)/shard_map/ppermute | solution.py:129
  133.4 30.4 %collective-permute-start.48 = (bf16[768,768]{1,0:T(8,128)(2,1)S(1)}, bf16[768,768]{1,0:T(8,128)(2,1)}, u32[]{:S(2)}, u32[]{:S(2)}) collective-permute-start(bf16[768,768]{1,0:T(8,128)(2,1)S(1)} %bitcast.210), channel_id=1, source_target_pairs={{0,1},{1,0},{2,3},{3,2},{4,5},{5,4},{6,7},{7,6},{8,9},{9,8},{10,11... | collective-permute-start | bytes 3538952 | tf_op jit(solution)/shard_map/ppermute | solution.py:129
  151.4 13.9 %collective-permute-start.36 = (f32[9,128]{1,0:T(8,128)S(1)}, f32[9,128]{1,0:T(8,128)}, u32[]{:S(2)}, u32[]{:S(2)}) collective-permute-start(f32[9,128]{1,0:T(8,128)S(1)} %add_add_fusion.2), channel_id=1, source_target_pairs={{0,8},{2,10},{4,12},{6,14},{8,16},{10,18},{12,20},{14,22},{16,24},... | collective-permute-start | bytes 13832 | tf_op jit(solution)/shard_map/ppermute | solution.py:59
  151.7 13.5 %collective-permute-start.37 = (f32[9,128]{1,0:T(8,128)S(1)}, f32[9,128]{1,0:T(8,128)}, u32[]{:S(2)}, u32[]{:S(2)}) collective-permute-start(f32[9,128]{1,0:T(8,128)S(1)} %add_add_fusion.2), channel_id=1, source_target_pairs={{0,16},{2,18},{4,20},{6,22},{8,24},{10,26},{12,28},{14,30},{16,0},... | collective-permute-start | bytes 13832 | tf_op jit(solution)/shard_map/ppermute | solution.py:59
  154.6 10.6 %collective-permute-start.38 = (f32[9,128]{1,0:T(8,128)S(1)}, f32[9,128]{1,0:T(8,128)}, u32[]{:S(2)}, u32[]{:S(2)}) collective-permute-start(f32[9,128]{1,0:T(8,128)S(1)} %add_add_fusion.2), channel_id=1, source_target_pairs={{0,24},{2,26},{4,28},{6,30},{8,0},{10,2},{12,4},{14,6},{16,8},{18,... | collective-permute-start | bytes 13832 | tf_op jit(solution)/shard_map/ppermute | solution.py:59
  163.7 57.1 %collective-permute-start.49 = (bf16[768,768]{1,0:T(8,128)(2,1)}, bf16[768,768]{1,0:T(8,128)(2,1)}, u32[]{:S(2)}, u32[]{:S(2)}) collective-permute-start(bf16[768,768]{1,0:T(8,128)(2,1)} %collective-permute-done.48), channel_id=1, source_target_pairs={{0,2},{2,0},{4,6},{6,4},{8,10},{10,8},{12,14},{14,12},{16,18},{18,... | collective-permute-start | bytes 3538952 | tf_op jit(solution)/shard_map/ppermute | solution.py:53
  163.7 23.9 %collective-permute-start.61 = (bf16[64,768]{1,0:T(8,128)(2,1)}, bf16[64,768]{1,0:T(8,128)(2,1)}, u32[]{:S(2)}, u32[]{:S(2)}) collective-permute-start(bf16[64,768]{1,0:T(8,128)(2,1)} %copy-done.24), channel_id=1, source_target_pairs={{0,1},{1,0},{2,3},{3,2},{4,5},{5,4},{6,7},{7,6},{8,9},{9,8},{10,11... | collective-permute-start | bytes 294920 | tf_op jit(solution)/shard_map/ppermute | solution.py:129
  177.4 10.3 %collective-permute-start.62 = (bf16[64,768]{1,0:T(8,128)(2,1)}, bf16[64,768]{1,0:T(8,128)(2,1)S(1)}, u32[]{:S(2)}, u32[]{:S(2)}) collective-permute-start(bf16[64,768]{1,0:T(8,128)(2,1)} %copy-done.24), channel_id=1, source_target_pairs={{0,2},{1,3},{2,0},{3,1},{4,6},{5,7},{6,4},{7,5},{8,10},{9,11},{10,... | collective-permute-start | bytes 294920 | tf_op jit(solution)/shard_map/ppermute | solution.py:129
  177.4 11.6 %collective-permute-start.63 = (bf16[64,768]{1,0:T(8,128)(2,1)}, bf16[64,768]{1,0:T(8,128)(2,1)S(1)}, u32[]{:S(2)}, u32[]{:S(2)}) collective-permute-start(bf16[64,768]{1,0:T(8,128)(2,1)} %copy-done.24), channel_id=1, source_target_pairs={{0,3},{1,2},{2,1},{3,0},{4,7},{5,6},{6,5},{7,4},{8,11},{9,10},{10,... | collective-permute-start | bytes 294920 | tf_op jit(solution)/shard_map/ppermute | solution.py:129
  186.3 14.0 %collective-permute-start.45 = (bf16[128,768]{1,0:T(8,128)(2,1)}, bf16[128,768]{1,0:T(8,128)(2,1)}, u32[]{:S(2)}, u32[]{:S(2)}) collective-permute-start(bf16[128,768]{1,0:T(8,128)(2,1)} %get-tuple-element.107), channel_id=1, source_target_pairs={{0,3},{1,2},{2,1},{3,0},{4,7},{5,6},{6,5},{7,4},{8,11},{9,10},{10,... | collective-permute-start | bytes 589832 | tf_op jit(solution)/shard_map/ppermute | solution.py:129
  187.6 13.6 %collective-permute-start.44 = (bf16[128,768]{1,0:T(8,128)(2,1)}, bf16[128,768]{1,0:T(8,128)(2,1)}, u32[]{:S(2)}, u32[]{:S(2)}) collective-permute-start(bf16[128,768]{1,0:T(8,128)(2,1)} %get-tuple-element.107), channel_id=1, source_target_pairs={{0,2},{1,3},{2,0},{3,1},{4,6},{5,7},{6,4},{7,5},{8,10},{9,11},{10,... | collective-permute-start | bytes 589832 | tf_op jit(solution)/shard_map/ppermute | solution.py:129
  187.6 29.9 %collective-permute-start.56 = (bf16[4,96,768]{2,1,0:T(8,128)(2,1)}, bf16[4,96,768]{2,1,0:T(8,128)(2,1)}, u32[]{:S(2)}, u32[]{:S(2)}) collective-permute-start(bf16[4,96,768]{2,1,0:T(8,128)(2,1)} %dynamic-slice_bitcast_fusion.1), channel_id=1, source_target_pairs={{0,4},{2,6},{4,0},{6,2},{8,12},{10,14},{12,8},{14,10},{16,20},{18,... | collective-permute-start | bytes 1769480 | tf_op jit(solution)/shard_map/ppermute | solution.py:56
  189.0 9.0 %collective-permute-start.43 = (bf16[128,768]{1,0:T(8,128)(2,1)}, bf16[128,768]{1,0:T(8,128)(2,1)}, u32[]{:S(2)}, u32[]{:S(2)}) collective-permute-start(bf16[128,768]{1,0:T(8,128)(2,1)} %get-tuple-element.106), channel_id=1, source_target_pairs={{0,1},{1,0},{2,3},{3,2},{4,5},{5,4},{6,7},{7,6},{8,9},{9,8},{10,11... | collective-permute-start | bytes 589832 | tf_op jit(solution)/shard_map/ppermute | solution.py:129
  198.0 57.8 %collective-permute-start.64 = (bf16[4,96,960]{2,1,0:T(8,128)(2,1)}, bf16[4,96,960]{2,1,0:T(8,128)(2,1)}, u32[]{:S(2)}, u32[]{:S(2)}) collective-permute-start(bf16[4,96,960]{2,1,0:T(8,128)(2,1)} %dynamic-slice_bitcast_fusion), channel_id=1, source_target_pairs={{0,4},{2,6},{4,0},{6,2},{8,12},{10,14},{12,8},{14,10},{16,20},{18,... | collective-permute-start | bytes 2211848 | tf_op jit(solution)/shard_map/ppermute | solution.py:56
  217.3 45.0 %collective-permute-start.50 = (bf16[768,768]{1,0:T(8,128)(2,1)}, bf16[768,768]{1,0:T(8,128)(2,1)}, u32[]{:S(2)}, u32[]{:S(2)}) collective-permute-start(bf16[768,768]{1,0:T(8,128)(2,1)} %get-tuple-element.56), channel_id=1, source_target_pairs={{0,2},{2,0},{4,6},{6,4},{8,10},{10,8},{12,14},{14,12},{16,18},{18,... | collective-permute-start | bytes 3538952 | tf_op jit(solution)/shard_map/ppermute | solution.py:53
  217.4 14.7 %collective-permute-start.46 = (bf16[128,1152]{1,0:T(8,128)(2,1)}, bf16[128,1152]{1,0:T(8,128)(2,1)}, u32[]{:S(2)}, u32[]{:S(2)}) collective-permute-start(bf16[128,1152]{1,0:T(8,128)(2,1)} %get-tuple-element.53.small_ref), channel_id=1, source_target_pairs={{0,1},{1,0},{2,3},{3,2},{4,5},{5,4},{6,7},{7,6},{8,9},{9,8},{10,11... | collective-permute-start | bytes 884744 | tf_op jit(solution)/shard_map/ppermute | solution.py:129
  217.5 13.7 %collective-permute-start.47 = (bf16[768,128]{1,0:T(8,128)(2,1)}, bf16[768,128]{1,0:T(8,128)(2,1)S(1)}, u32[]{:S(2)}, u32[]{:S(2)}) collective-permute-start(bf16[768,128]{1,0:T(8,128)(2,1)} %get-tuple-element.54), channel_id=1, source_target_pairs={{0,1},{1,0},{2,3},{3,2},{4,5},{5,4},{6,7},{7,6},{8,9},{9,8},{10,11... | collective-permute-start | bytes 589832 | tf_op jit(solution)/shard_map/ppermute | solution.py:129
  220.8 34.8 %collective-permute-start.57 = (bf16[96,768]{1,0:T(8,128)(2,1)S(1)}, bf16[96,768]{1,0:T(8,128)(2,1)S(1)}, u32[]{:S(2)}, u32[]{:S(2)}) collective-permute-start(bf16[96,768]{1,0:T(8,128)(2,1)S(1)} %get-tuple-element.96), channel_id=1, source_target_pairs={{0,8},{2,10},{4,12},{6,14},{8,16},{10,18},{12,20},{14,22},{16,24},... | collective-permute-start | bytes 442376 | tf_op jit(solution)/shard_map/ppermute | solution.py:59
  231.2 24.4 %collective-permute-start.58 = (bf16[96,768]{1,0:T(8,128)(2,1)S(1)}, bf16[96,768]{1,0:T(8,128)(2,1)S(1)}, u32[]{:S(2)}, u32[]{:S(2)}) collective-permute-start(bf16[96,768]{1,0:T(8,128)(2,1)S(1)} %get-tuple-element.98), channel_id=1, source_target_pairs={{0,16},{2,18},{4,20},{6,22},{8,24},{10,26},{12,28},{14,30},{16,0},... | collective-permute-start | bytes 442376 | tf_op jit(solution)/shard_map/ppermute | solution.py:59
  232.1 23.5 %collective-permute-start.59 = (bf16[96,768]{1,0:T(8,128)(2,1)S(1)}, bf16[96,768]{1,0:T(8,128)(2,1)S(1)}, u32[]{:S(2)}, u32[]{:S(2)}) collective-permute-start(bf16[96,768]{1,0:T(8,128)(2,1)S(1)} %get-tuple-element.97), channel_id=1, source_target_pairs={{0,24},{2,26},{4,28},{6,30},{8,0},{10,2},{12,4},{14,6},{16,8},{18,... | collective-permute-start | bytes 442376 | tf_op jit(solution)/shard_map/ppermute | solution.py:59
  257.3 9.8 %collective-permute-start.65 = (bf16[96,960]{1,0:T(8,128)(2,1)S(1)}, bf16[96,960]{1,0:T(8,128)(2,1)S(1)}, u32[]{:S(2)}, u32[]{:S(2)}) collective-permute-start(bf16[96,960]{1,0:T(8,128)(2,1)S(1)} %get-tuple-element.91), channel_id=1, source_target_pairs={{0,8},{2,10},{4,12},{6,14},{8,16},{10,18},{12,20},{14,22},{16,24},... | collective-permute-start | bytes 552968 | tf_op jit(solution)/shard_map/ppermute | solution.py:59
  257.9 17.1 %collective-permute-start.66 = (bf16[96,960]{1,0:T(8,128)(2,1)S(1)}, bf16[96,960]{1,0:T(8,128)(2,1)S(1)}, u32[]{:S(2)}, u32[]{:S(2)}) collective-permute-start(bf16[96,960]{1,0:T(8,128)(2,1)S(1)} %get-tuple-element.93), channel_id=1, source_target_pairs={{0,16},{2,18},{4,20},{6,22},{8,24},{10,26},{12,28},{14,30},{16,0},... | collective-permute-start | bytes 552968 | tf_op jit(solution)/shard_map/ppermute | solution.py:59
  259.6 15.4 %collective-permute-start.67 = (bf16[96,960]{1,0:T(8,128)(2,1)S(1)}, bf16[96,960]{1,0:T(8,128)(2,1)S(1)}, u32[]{:S(2)}, u32[]{:S(2)}) collective-permute-start(bf16[96,960]{1,0:T(8,128)(2,1)S(1)} %get-tuple-element.92), channel_id=1, source_target_pairs={{0,24},{2,26},{4,28},{6,30},{8,0},{10,2},{12,4},{14,6},{16,8},{18,... | collective-permute-start | bytes 552968 | tf_op jit(solution)/shard_map/ppermute | solution.py:59
  264.0 14.9 %collective-permute-start.51 = (bf16[4,96,768]{2,1,0:T(8,128)(2,1)S(1)}, bf16[4,96,768]{2,1,0:T(8,128)(2,1)S(1)}, u32[]{:S(2)}, u32[]{:S(2)}) collective-permute-start(bf16[4,96,768]{2,1,0:T(8,128)(2,1)S(1)} %dynamic-slice_bitcast_fusion.2), channel_id=1, source_target_pairs={{0,4},{2,6},{4,0},{6,2},{8,12},{10,14},{12,8},{14,10},{16,20},{18,... | collective-permute-start | bytes 1769480 | tf_op jit(solution)/shard_map/ppermute | solution.py:56
  279.1 8.6 %collective-permute-start.52 = (bf16[96,768]{1,0:T(8,128)(2,1)S(1)}, bf16[96,768]{1,0:T(8,128)(2,1)S(1)}, u32[]{:S(2)}, u32[]{:S(2)}) collective-permute-start(bf16[96,768]{1,0:T(8,128)(2,1)S(1)} %get-tuple-element.99), channel_id=1, source_target_pairs={{0,8},{2,10},{4,12},{6,14},{8,16},{10,18},{12,20},{14,22},{16,24},... | collective-permute-start | bytes 442376 | tf_op jit(solution)/shard_map/ppermute | solution.py:59
  279.5 12.4 %collective-permute-start.53 = (bf16[96,768]{1,0:T(8,128)(2,1)S(1)}, bf16[96,768]{1,0:T(8,128)(2,1)S(1)}, u32[]{:S(2)}, u32[]{:S(2)}) collective-permute-start(bf16[96,768]{1,0:T(8,128)(2,1)S(1)} %get-tuple-element.101), channel_id=1, source_target_pairs={{0,16},{2,18},{4,20},{6,22},{8,24},{10,26},{12,28},{14,30},{16,0},... | collective-permute-start | bytes 442376 | tf_op jit(solution)/shard_map/ppermute | solution.py:59
  281.2 10.7 %collective-permute-start.54 = (bf16[96,768]{1,0:T(8,128)(2,1)S(1)}, bf16[96,768]{1,0:T(8,128)(2,1)S(1)}, u32[]{:S(2)}, u32[]{:S(2)}) collective-permute-start(bf16[96,768]{1,0:T(8,128)(2,1)S(1)} %get-tuple-element.100), channel_id=1, source_target_pairs={{0,24},{2,26},{4,28},{6,30},{8,0},{10,2},{12,4},{14,6},{16,8},{18,... | collective-permute-start | bytes 442376 | tf_op jit(solution)/shard_map/ppermute | solution.py:59
  283.3 12.1 %collective-permute-start.69 = (f32[48,384]{1,0:T(8,128)S(1)}, f32[48,384]{1,0:T(8,128)S(1)}, u32[]{:S(2)}, u32[]{:S(2)}) collective-permute-start(f32[48,384]{1,0:T(8,128)S(1)} %pad_maximum_fusion.13), channel_id=1, source_target_pairs={{0,1},{1,0},{2,3},{3,2},{4,5},{5,4},{6,7},{7,6},{8,9},{9,8},{10,11... | collective-permute-start | bytes 221192 | tf_op jit(solution)/shard_map/ppermute | solution.py:129
  (64 other events, 402.9 us)
where the time goes:
time: 302 us; the launch traced here: 300 us
  waiting for transfers between devices  106 us (35%)
  starting transfers between devices  70.2 us (23%)
  Pallas kernels  51.4 us (17%)
  other arithmetic  24.5 us (8%)
  local copies, waits for them, and re-layouts  24.2 us (8%)
  matrix products  16.6 us (5%)
  between operations  7.1 us (2%)
    ppermute x16, waiting for transfers between devices, swap_side(): return lax.ppermute(x, 'dp', [(i, i ^ 2) for i in range(self.count)])  38 us
    ppermute x22, waiting for transfers between devices, swap_near(): return lax.ppermute(x, ('dp', 'mp'), [(i, i ^ flip) for i in range(size)])  35.3 us
    ppermute x21, waiting for transfers between devices, shift_depth(): lax.ppermute(x, 'dp', [(i, (i + 4 * step) % self.count) for i in range(se...  30.5 us
    ppermute x21, starting transfers between devices, shift_depth(): lax.ppermute(x, 'dp', [(i, (i + 4 * step) % self.count) for i in range(se...  26.1 us
    pallas_call x1, Pallas kernels, captions_back(): pl.pallas_call(captions_body, out_shape=jax.ShapeDtypeStruct(unit.shape,...  18.4 us
    ppermute x22, starting transfers between devices, swap_near(): return lax.ppermute(x, ('dp', 'mp'), [(i, i ^ flip) for i in range(size)])  17.7 us
    ppermute x16, starting transfers between devices, swap_side(): return lax.ppermute(x, 'dp', [(i, i ^ 2) for i in range(self.count)])  17.2 us
    pallas_call x1, Pallas kernels, attend_back(): pl.pallas_call(attend_back_body, grid=(steps,), out_shape=shapes(*[((WIDT...  13.9 us
  transfers between devices with their start and end apart: 72, of which 31 were waited for; matrix products, arithmetic and copies ran while one was open for 20% of the time, Pallas kernels for 17%

commit v1 on v0

--- a/solution.py
+++ b/solution.py
@@ -60,10 +60,11 @@
             x, "dp", [(i, (i + 4 * step) % self.count) for i in range(self.count)]
         )
 
-    def gather(self, mine, send, after=None):
+    def gather(self, mine, send, ring_after=(), last_after=None):
         if not self.fast:
             zero_all = lax.all_gather(pick(self.core, mine, send), "dp", axis=0, tiled=True)
             one_all = lax.all_gather(pick(self.core, send, mine), "dp", axis=0, tiled=True)
+            self.near = self.far = mine
             return pick(self.core, zero_all, one_all)
         rows, width = mine.shape
         arrived = self.swap_core(send)
@@ -71,12 +72,15 @@
         block = lax.dynamic_update_slice(block, mine[None], (self.core, 0, 0))
         block = lax.dynamic_update_slice(block, arrived[None], (1 - self.core, 0, 0))
         block = block.reshape(2 * rows, width)
-        if after is not None:
-            block, _ = lax.optimization_barrier((block, after))
+        if ring_after:
+            block = after(block, *ring_after)
         up = self.shift_depth(block, 1)
         down = self.shift_depth(block, -1)
         far = self.shift_depth(up, 1)
-        self.last = up
+        self.near = up
+        self.far = far
+        if last_after is not None:
+            far = after(far, last_after(self))
         whole = jnp.zeros((self.count // 2, 2 * rows, width), mine.dtype)
         for step, here in ((0, block), (1, up), (-1, down), (2, far)):
             place = ((self.depth - step) % 4) * 2
@@ -87,8 +91,23 @@
             )
         return whole.reshape(rows * self.count, width)
 
-    def scatter(self, keep, send=None):
+    def scatter_side(self, keep, send=None):
         if not self.fast:
+            return keep, send
+        rows = keep.shape[0] // self.count
+        width = keep.shape[1]
+        pair = keep
+        if send is not None:
+            pair = (keep.astype(full) + self.swap_core(send).astype(full)).astype(low)
+        self.pair = pair
+        pair = pair.reshape(4, 2, 2 * rows, width)
+        stay = lax.dynamic_index_in_dim(pair, self.side, 1, False)
+        leave = lax.dynamic_index_in_dim(pair, 1 - self.side, 1, False)
+        return (stay.astype(full) + self.swap_side(leave).astype(full)).astype(low)
+
+    def scatter_depth(self, quad_sum):
+        if not self.fast:
+            keep, send = quad_sum
             if send is None:
                 send = jnp.zeros_like(keep)
             halves = (pick(self.core, keep, send), pick(self.core, send, keep))
@@ -96,19 +115,16 @@
                 lax.psum_scatter(half, "dp", scatter_dimension=0, tiled=True).astype(full)
                 for half in halves
             ]
-        rows = keep.shape[0] // self.count
-        width = keep.shape[1]
-        pair = keep
-        if send is not None:
-            pair = (keep.astype(full) + self.swap_core(send).astype(full)).astype(low)
-        pair = pair.reshape(4, 2, 2 * rows, width)
-        stay = lax.dynamic_index_in_dim(pair, self.side, 1, False)
-        leave = lax.dynamic_index_in_dim(pair, 1 - self.side, 1, False)
-        quad_sum = (stay.astype(full) + self.swap_side(leave).astype(full)).astype(low)
         total = lax.dynamic_index_in_dim(quad_sum, self.depth, 0, False).astype(full)
         for step in range(1, 4):
             leave = lax.dynamic_index_in_dim(quad_sum, (self.depth + step) % 4, 0, False)
             total = total + self.shift_depth(leave, step).astype(full)
+        return total
+
+    def scatter_core(self, total):
+        if not self.fast:
+            return total
+        rows, width = total.shape[0] // 2, total.shape[1]
         total = total.reshape(2, rows, width)
         mine = lax.dynamic_index_in_dim(total, self.core, 0, False)
         arrived = self.swap_core(lax.dynamic_index_in_dim(total, 1 - self.core, 0, False))
@@ -133,6 +149,10 @@
     return swap_near(x, 1)
 
 
+def after(x, *others):
+    return lax.optimization_barrier((x, *others))[0]
+
+
 def roll_rows(x):
     half = x.shape[0] // 2
     return jnp.concatenate([x[half:], x[:half]], 0)
@@ -168,11 +188,15 @@
 
 def pack_body(core_ref, mix_ref, back_ref, raise_ref, lower_ref, embed_ref, g1_ref, g2_ref, *outs):
     first = core_ref[0] == 0
-    g1 = g1_ref[...]
-    g2 = g2_ref[...]
+    rows = back_ref.shape[0]
+    spot = lax.broadcasted_iota(jnp.int32, (rows, rows), 0)
+    diagonal = spot == lax.broadcasted_iota(jnp.int32, (rows, rows), 1)
+    g1, g2 = [
+        jnp.sum(jnp.where(diagonal, ref[...], 0.0), 1, keepdims=True) for ref in (g1_ref, g2_ref)
+    ]
 
     def part(index):
-        return (mix_ref[:, index, :].astype(full) * g1).astype(low)
+        return (mix_ref[index].astype(full) * g1).astype(low)
 
     def put(index, columns, zero, one):
         outs[index][:, columns] = jnp.where(first, zero, one)
@@ -332,17 +356,19 @@
     )(unit, unit_end, ends, kq, vo)
 
 
+def lane_group():
+    return lax.broadcasted_iota(jnp.int32, (BLOCK, 128), 1) // (2 * LENGTH)
+
+
 def attend_back_body(
-    core_ref, d_mid_ref, unit_ref, unit_end_ref, vo_ref, k_ref, v_ref, p_ref, q_ref, att_ref,
-    keep_ref, send_ref, dk_ref, dv_ref, small_ref, probs_ref,
-    sum_ref, d_att_ref, dq_ref,
+    core_ref, d_mid_ref, d_att_ref, unit_ref, unit_end_ref, k_ref, v_ref, p_ref, q_ref, att_ref,
+    keep_ref, send_ref, dk_ref, dv_ref, dq_ref, probs_ref, sum_ref,
 ):
     i = pl.program_id(0)
 
     @pl.when(i == 0)
     def _():
         sum_ref[...] = jnp.zeros_like(sum_ref)
-        d_att_ref[...] = mm(d_mid_ref[...], vo_ref[:, COLS:]).astype(low)
 
     values = v_ref[...]
     probs = p_ref[...]
@@ -358,19 +384,20 @@
     dk_ref[...] = d_keys
     dv_ref[...] = d_values
     spot = lax.broadcasted_iota(jnp.int32, (TOKENS, 128), 0) & (LENGTH - 1)
-    lane = lax.broadcasted_iota(jnp.int32, (TOKENS, 128), 1)
-    squeeze = (spot == lane).astype(low)
-    squeeze_far = (spot + LENGTH == lane).astype(low)
-    probs_ref[...] = (mm(probs_low, squeeze) + mm(d_scores, squeeze_far)).astype(low)
+    lane = lax.broadcasted_iota(jnp.int32, (TOKENS, 128), 1) & (2 * LENGTH - 1)
+    squeezed = mm(probs_low, (spot == lane).astype(low))
+    squeezed += mm(d_scores, (spot + LENGTH == lane).astype(low))
+    for first in (0, 4):
+        out = jnp.zeros((BLOCK, 128), full)
+        for h in range(first, min(first + 4, HEADS_HERE)):
+            out = jnp.where(lane_group() == h - first, squeezed[h * BLOCK : (h + 1) * BLOCK], out)
+        probs_ref[first * 4 : first * 4 + BLOCK] = out.astype(low)
     sum_ref[...] += mm_tn(unit_ref[...], jnp.concatenate([d_keys, d_values], 1))
 
     @pl.when(i == pl.num_programs(0) - 1)
     def _():
         first = core_ref[0] == 0
         d_queries = dq_ref[...]
-        small_ref[:, :COLS] = q_ref[...]
-        small_ref[:, COLS : 2 * COLS] = d_att_ref[...]
-        small_ref[:, 2 * COLS :] = d_queries
         g_key = sum_ref[:, :COLS].astype(low)
         g_value = sum_ref[:, COLS:].astype(low)
         g_query = mm_tn(unit_end_ref[...], d_queries).astype(low)
@@ -381,7 +408,7 @@
         send_ref[:, COLS:] = jnp.where(first, g_back, g_query)
 
 
-def attend_back(core, d_mid, unit, unit_end, vo, keys, values, probs, queries, attended):
+def attend_back(core, d_mid, d_att, unit, unit_end, keys, values, probs, queries, attended):
     count = d_mid.shape[0]
     steps = count // BLOCK
     return pl.pallas_call(
@@ -390,15 +417,15 @@
         out_shape=shapes(
             *[((WIDTH, 2 * COLS), low)] * 2,
             *[((count * LENGTH, COLS), low)] * 2,
-            ((count, 3 * COLS), low),
-            ((steps * STACK, 128), low),
+            ((count, COLS), low),
+            ((steps * 2 * BLOCK, 128), low),
         ),
         in_specs=[
             pl.BlockSpec(memory_space=pltpu.SMEM),
             whole_block((count, WIDTH)),
+            whole_block((count, COLS)),
             pl.BlockSpec((TOKENS, WIDTH), lambda i: (i, 0)),
             whole_block((count, WIDTH)),
-            whole_block(vo.shape),
             pl.BlockSpec((TOKENS, COLS), lambda i: (i, 0)),
             pl.BlockSpec((TOKENS, COLS), lambda i: (i, 0)),
             pl.BlockSpec((STACK, TOKENS), lambda i: (i, 0)),
@@ -410,16 +437,12 @@
             whole_block((WIDTH, 2 * COLS)),
             pl.BlockSpec((TOKENS, COLS), lambda i: (i, 0)),
             pl.BlockSpec((TOKENS, COLS), lambda i: (i, 0)),
-            whole_block((count, 3 * COLS)),
-            pl.BlockSpec((STACK, 128), lambda i: (i, 0)),
+            whole_block((count, COLS)),
+            pl.BlockSpec((2 * BLOCK, 128), lambda i: (i, 0)),
         ],
-        scratch_shapes=[
-            pltpu.VMEM((WIDTH, 2 * COLS), full),
-            pltpu.VMEM((count, COLS), low),
-            pltpu.VMEM((count, COLS), low),
-        ],
+        scratch_shapes=[pltpu.VMEM((WIDTH, 2 * COLS), full)],
         name="attend_back",
-    )(core, d_mid, unit, unit_end, vo, keys, values, probs, queries, attended)
+    )(core, d_mid, d_att, unit, unit_end, keys, values, probs, queries, attended)
 
 
 def place_rows(picks, rows):
@@ -429,33 +452,38 @@
 
 
 def captions_body(
-    group_ref, ends_ref, unit_ref, scale_ref, d_mid_ref, dk_ref, dv_ref, small_ref,
-    small_far_ref, probs_far_ref, kq_ref, vo_ref, kq_far_ref, vo_far_ref, out_ref, inner_end_ref,
+    group_ref, ends_ref, unit_ref, scale_ref, d_mid_ref, dk_ref, dv_ref, dq_ref,
+    q_far_ref, d_att_far_ref, dq_far_ref, probs_far_ref, kq_ref, vo_ref, kq_far_ref, vo_far_ref,
+    *refs,
 ):
+    out_ref, inner_end_ref = refs[-2:]
     i = pl.program_id(0)
-    count = small_ref.shape[0]
-    half = count // 2
 
     @pl.when(i == 0)
     def _():
-        far = mm_nt(small_far_ref[:, 2 * COLS :], kq_far_ref[:, COLS:])
-        own = mm_nt(small_ref[:, 2 * COLS :], kq_ref[:, COLS:])
-        inner_end_ref[:half] = own[:half] + far[half:]
-        inner_end_ref[half:] = own[half:] + far[:half]
-
-    steps = pl.num_programs(0)
-    far_rows = step_rows((i + steps // 2) % steps)
+        inner_end_ref[...] = mm_nt(dq_ref[...], kq_ref[:, COLS:]) + mm_nt(
+            dq_far_ref[...], kq_far_ref[:, COLS:]
+        )
+
     row, token = stack_grid()
     own_caption = token // LENGTH == row
-    lane = lax.broadcasted_iota(jnp.int32, (128, TOKENS), 0)
+    lane = lax.broadcasted_iota(jnp.int32, (128, TOKENS), 0) & (2 * LENGTH - 1)
     spot = lax.broadcasted_iota(jnp.int32, (128, TOKENS), 1) & (LENGTH - 1)
-    pair = probs_far_ref[...]
+    packed = probs_far_ref[...]
+    zero = jnp.zeros((BLOCK, 128), low)
+    pair = jnp.concatenate(
+        [
+            jnp.where(lane_group() == h % 4, packed[h // 4 * BLOCK : (h // 4 + 1) * BLOCK], zero)
+            for h in range(HEADS_HERE)
+        ],
+        0,
+    )
     probs = jnp.where(own_caption, mm(pair, (spot == lane).astype(low)), 0.0).astype(low)
     d_scores = jnp.where(
         own_caption, mm(pair, (spot + LENGTH == lane).astype(low)), 0.0
     ).astype(low)
-    d_keys = mm_tn(d_scores, head_stack(small_far_ref[far_rows, :COLS])).astype(low)
-    d_values = mm_tn(probs, head_stack(small_far_ref[far_rows, COLS : 2 * COLS])).astype(low)
+    d_keys = mm_tn(d_scores, head_stack(q_far_ref[step_rows(i), :])).astype(low)
+    d_values = mm_tn(probs, head_stack(d_att_far_ref[step_rows(i), :])).astype(low)
     inner = mm_nt(dk_ref[...], kq_ref[:, :COLS]) + mm_nt(dv_ref[...], vo_ref[:, :COLS])
     inner += mm_nt(d_keys, kq_far_ref[:, :COLS]) + mm_nt(d_values, vo_far_ref[:, :COLS])
     picks = end_picks(ends_ref[...], 2).astype(low)
@@ -469,39 +497,53 @@
 
 
 def captions_back(
-    group, ends, unit, scale, d_mid, d_keys, d_values, small, small_far, probs_far, kq, vo,
-    kq_far, vo_far,
+    part, group, ends, unit, scale, d_mid, d_keys, d_values, dq, q_far, d_att_far, dq_far,
+    probs_far, kq, vo, kq_far, vo_far, done=None,
 ):
     count = ends.shape[0]
     steps = count // BLOCK
+    half = steps // 2
+    start = part * half
+    far = (1 - part) * half
+    own_half = pl.BlockSpec((count // 2, COLS), lambda i, g: (part, 0))
+    far_half = pl.BlockSpec((count // 2, COLS), lambda i, g: (1 - part, 0))
+    operands = [
+        group, ends, unit, scale, d_mid, d_keys, d_values, dq, q_far, d_att_far, dq_far,
+        probs_far, kq, vo, kq_far, vo_far,
+    ]
+    in_specs = [
+        pl.BlockSpec((BLOCK, 1), lambda i, g: (i + start, 0)),
+        pl.BlockSpec((TOKENS, WIDTH), lambda i, g: (i + start, 0)),
+        pl.BlockSpec((TOKENS, 128), lambda i, g: (i + start, 0)),
+        pl.BlockSpec((BLOCK, WIDTH), lambda i, g: (i + start, 0)),
+        pl.BlockSpec((TOKENS, COLS), lambda i, g: (i + start, 0)),
+        pl.BlockSpec((TOKENS, COLS), lambda i, g: (i + start, 0)),
+        own_half,
+        far_half,
+        far_half,
+        far_half,
+        pl.BlockSpec((2 * BLOCK, 128), lambda i, g: (i + far, 0)),
+    ] + [whole_block(kq.shape)] * 4
+    aliases = {}
+    if done is not None:
+        aliases = {len(operands): 0}
+        operands.append(done)
+        in_specs.append(pl.BlockSpec(memory_space=pl.ANY))
     return pl.pallas_call(
         captions_body,
         out_shape=jax.ShapeDtypeStruct(unit.shape, full),
         grid_spec=pltpu.PrefetchScalarGridSpec(
             num_scalar_prefetch=1,
-            grid=(steps,),
-            in_specs=[
-                pl.BlockSpec((BLOCK, 1), lambda i, g: (i, 0)),
-                pl.BlockSpec((TOKENS, WIDTH), lambda i, g: (i, 0)),
-                pl.BlockSpec((TOKENS, 128), lambda i, g: (i, 0)),
-                pl.BlockSpec((BLOCK, WIDTH), lambda i, g: (i, 0)),
-                pl.BlockSpec((TOKENS, COLS), lambda i, g: (i, 0)),
-                pl.BlockSpec((TOKENS, COLS), lambda i, g: (i, 0)),
-                whole_block(small.shape),
-                whole_block(small.shape),
-                pl.BlockSpec((STACK, 128), lambda i, g: ((i + steps // 2) % steps, 0)),
-            ]
-            + [whole_block(kq.shape)] * 4,
+            grid=(half,),
+            in_specs=in_specs,
             out_specs=pl.BlockSpec(
-                (TOKENS, WIDTH), lambda i, g: ((i + g[0] * (steps // 2)) % steps, 0)
+                (TOKENS, WIDTH), lambda i, g: ((i + start + g[0] * half) % steps, 0)
             ),
-            scratch_shapes=[pltpu.VMEM((count, WIDTH), full)],
+            scratch_shapes=[pltpu.VMEM((count // 2, WIDTH), full)],
         ),
+        input_output_aliases=aliases,
         name="captions_back",
-    )(
-        group, ends, unit, scale, d_mid, d_keys, d_values, small, small_far, probs_far, kq, vo,
-        kq_far, vo_far,
-    )
+    )(*operands)
 
 
 def local(
@@ -533,17 +575,39 @@
     group_flag = group.reshape(1).astype(jnp.int32)
 
     packed = pack(
-        core_flag, w_qkv, w_out, w_up, w_down, w_proj, ln1_gain[:, None], ln2_gain[:, None]
+        core_flag,
+        w_qkv.transpose(1, 0, 2),
+        w_out,
+        w_up,
+        w_down,
+        w_proj,
+        ln1_gain[None],
+        ln2_gain[None],
     )
     mix_own = plane.gather(packed[0], packed[1])
+    mix_near, mix_last = plane.near, plane.far
     mix_other = plane.swap_core(mix_own)
-    feeds = plane.gather(packed[2], packed[3], plane.last if plane.fast else None)
+    kq = pick(core, mix_own, mix_other)
+    vo = pick(core, mix_other, mix_own)
+    far_own = swap_group(mix_own)
+    far_other = plane.swap_core(far_own)
+    kq_far = pick(core, far_own, far_other)
+    vo_far = pick(core, far_other, far_own)
+
+    flipped = jnp.concatenate([end_pos, end_pos], 0)
+    ends = lax.dynamic_slice_in_dim(flipped, group * CAP_DEV, rows_dev, 0)[:, None]
+    unit, scale, unit_end, stream_end = norm_first(
+        group_flag, after(captions, mix_near).reshape(rows_dev * length, width), ends
+    )
+    keys, values, probs, queries, attended, attention = attend(unit, unit_end, ends, kq, vo)
+    feeds = plane.gather(packed[2], packed[3], (mix_last,), lambda _: attention)
 
     cached = image_cache.astype(full)
     cached = (cached * lax.rsqrt(jnp.sum(cached * cached, -1, keepdims=True) + 1e-06)).astype(low)
     places = jnp.arange(rows_dev, dtype=jnp.int32)
     hand_out = (send_order[0][:, None] == places[None, :]).astype(low)
     outgoing = mm(hand_out, cached).astype(low).reshape(spread, per_peer, width)
+    outgoing = after(outgoing, mix_near)
     incoming = lax.all_to_all(outgoing, "dp", split_axis=0, concat_axis=0, tiled=True)
     own_arrive = lax.dynamic_slice_in_dim(arrive_order[0], group * CAP_DEV, CAP_DEV, 0)
     take_in = (own_arrive[:, None] == places[None, :]).astype(low)
@@ -560,7 +624,7 @@
             return jnp.concatenate([embed, half[:main], jnp.concatenate(parts, 0)], 1)
 
         third = plane.gather(
-            join(packed[4], picture_mine), join(packed[5], picture_send), plane.last
+            join(packed[4], picture_mine), join(packed[5], picture_send), (plane.far, attention)
         )
         third_other = plane.swap_core(third)
 
@@ -582,19 +646,6 @@
 
     pictures_all = sides(image_halves)
     w_embed = sides(embed_halves)
-    kq = pick(core, mix_own, mix_other)
-    vo = pick(core, mix_other, mix_own)
-    far_own = swap_group(mix_own)
-    far_other = plane.swap_core(far_own)
-    kq_far = pick(core, far_own, far_other)
-    vo_far = pick(core, far_other, far_own)
-
-    flipped = jnp.concatenate([end_pos, end_pos], 0)
-    ends = lax.dynamic_slice_in_dim(flipped, group * CAP_DEV, rows_dev, 0)[:, None]
-    unit, scale, unit_end, stream_end = norm_first(
-        group_flag, captions.reshape(rows_dev * length, width), ends
-    )
-    keys, values, probs, queries, attended, attention = attend(unit, unit_end, ends, kq, vo)
 
     stream_near = swap_near(stream_end, 2)
     from_group, from_core, from_both = [swap_near(attention, flip) for flip in (1, 2, 3)]
@@ -605,6 +656,8 @@
     middle = jnp.concatenate([stream_end, stream_near], 0).astype(full) + attention
     unit_second, scale_second = norm_rows(middle)
     second_low = unit_second.astype(low)
+    feeds = after(feeds, far_own)
+    queries_far = swap_group(queries)
     w_raise = feeds[:, :hidden]
     w_lower = feeds[:, hidden:]
     active, slope = gelu_parts(mm(second_low, w_raise))
@@ -671,8 +724,8 @@
     d_embed_half = pick(group, d_embed_all[:, :wide], d_embed_all[:, wide:])
     d_embed_here = pick(core, d_embed_half[:, :quarter], d_embed_half[:, quarter:])
     g_embed = mm_tn(pooled_all, d_embed_here).astype(low)
-    lower_sum = plane.scatter(jnp.concatenate([g_lower, g_embed], 1))
-    raise_sum = plane.scatter(g_raise)
+    lower_quad = plane.scatter_side(jnp.concatenate([g_lower, g_embed], 1))
+    raise_quad = plane.scatter_side(g_raise)
     inner = d_second[:rows_dev].astype(full)
     inner = inner + roll_rows(swap_near(d_second[:rows_dev], 1)).astype(full)
     inner = inner + swap_near(d_second[rows_dev:], 2).astype(full)
@@ -681,16 +734,30 @@
         inner, unit_second[:rows_dev], scale_second[:rows_dev]
     )
 
-    g_keep, g_send, d_keys, d_values, small, small_probs = attend_back(
-        core_flag, d_middle.astype(low), unit, unit_end, vo, keys, values, probs, queries, attended
-    )
-    mix_sum = plane.scatter(g_keep, g_send)
-    small_far = swap_group(small)
+    d_middle_low = d_middle.astype(low)
+    d_attended = mm(d_middle_low, vo[:, COLS:]).astype(low)
+    d_attended_far = swap_group(d_attended)
+    g_keep, g_send, d_keys, d_values, d_queries, small_probs = attend_back(
+        core_flag, d_middle_low, d_attended, unit, unit_end, keys, values, probs, queries, attended
+    )
+    d_queries_far = swap_group(d_queries)
     probs_far = swap_group(small_probs)
-    grad_captions = captions_back(
-        group_flag, ends, unit, scale, d_middle, d_keys, d_values, small, small_far, probs_far,
-        kq, vo, kq_far, vo_far,
-    ).reshape(rows_dev, length, width)
+    mix_quad = plane.scatter_side(g_keep, g_send)
+    lower_sum = plane.scatter_core(plane.scatter_depth(lower_quad))
+    raise_sum = plane.scatter_core(plane.scatter_depth(raise_quad))
+    operands = (
+        unit, scale, d_middle, d_keys, d_values, d_queries, queries_far, d_attended_far,
+        d_queries_far, probs_far, kq, vo, kq_far, vo_far,
+    )
+    first_ends = after(ends, lower_quad, plane.pair) if plane.fast else ends
+    first_half = captions_back(0, group_flag, first_ends, *operands)
+    second_ends = after(ends, mix_quad) if plane.fast else ends
+    grad_captions = captions_back(1, group_flag, second_ends, *operands, done=first_half)
+    mix_total = plane.scatter_depth(mix_quad)
+    if plane.fast:
+        mix_total, grad_captions = lax.optimization_barrier((mix_total, grad_captions))
+    mix_sum = plane.scatter_core(mix_total)
+    grad_captions = grad_captions.reshape(rows_dev, length, width)
 
     grad_down = jnp.concatenate([part[:, :hidden] for part in lower_sum], 1)
     proj_own = jnp.concatenate([part[:, hidden:] for part in lower_sum], 1)

time: 302 us -> 291 us (0.964)
  waiting for transfers between devices: 106 us -> 87.7 us
  starting transfers between devices: 70.2 us -> 75.5 us
  matrix products: 16.6 us -> 12.3 us
  Pallas kernels: 51.4 us -> 54.9 us
    ppermute x22 -> x24, waiting for transfers between devices: 35.3 us -> 18 us  [swap_near(): return lax.ppermute(x, ('dp', 'mp'), [(i, i ^ flip) for i in range(size)])]
    ppermute x16, waiting for transfers between devices: 38 us -> 32.2 us  [swap_side(): return lax.ppermute(x, 'dp', [(i, i ^ 2) for i in range(self.count)])]
    ppermute x21, waiting for transfers between devices: 30.5 us -> 36 us  [shift_depth(): lax.ppermute(x, 'dp', [(i, (i + 4 * step) % self.count) for i in range(se...]
    ppermute x21, starting transfers between devices: 26.1 us -> 30.9 us  [shift_depth(): lax.ppermute(x, 'dp', [(i, (i + 4 * step) % self.count) for i in range(se...]
    pallas_call x1 -> x2, Pallas kernels: 18.4 us -> 22.7 us  [captions_back(): pl.pallas_call(captions_body, out_shape=jax.ShapeDtypeStruct(unit.shape,...]
    all_to_all x1, starting transfers between devices: 7.01 us -> 3.52 us  [local(): lax.all_to_all(outgoing, 'dp', split_axis=0, concat_axis=0, tiled=True)]
    dot_general x6 -> x7, matrix products: 8.08 us -> 5.04 us  [mm(): lax.dot_general(a, b, (((1,), (0,)), ((), ())), preferred_element_type=full)]
    ppermute x22 -> x24, starting transfers between devices: 17.7 us -> 19.9 us  [swap_near(): return lax.ppermute(x, ('dp', 'mp'), [(i, i ^ flip) for i in range(size)])]
  transfers between devices with their start and end apart: 72 -> 74, of which waited for: 31 -> 33; matrix products, arithmetic and copies ran while one was open for 20% -> 21% of each run, Pallas kernels for 17% -> 19%
where the time goes in v1:
time: 291 us; the launch traced here: 289 us
  waiting for transfers between devices  87.7 us (30%)
  starting transfers between devices  75.5 us (26%)
  Pallas kernels  54.9 us (19%)
  other arithmetic  26.3 us (9%)
  local copies, waits for them, and re-layouts  25.7 us (9%)
  matrix products  12.3 us (4%)
  between operations  7.03 us (2%)
    ppermute x21, waiting for transfers between devices, shift_depth(): lax.ppermute(x, 'dp', [(i, (i + 4 * step) % self.count) for i in range(se...  36 us
    ppermute x16, waiting for transfers between devices, swap_side(): return lax.ppermute(x, 'dp', [(i, i ^ 2) for i in range(self.count)])  32.2 us
    ppermute x21, starting transfers between devices, shift_depth(): lax.ppermute(x, 'dp', [(i, (i + 4 * step) % self.count) for i in range(se...  30.9 us
    pallas_call x2, Pallas kernels, captions_back(): pl.pallas_call(captions_body, out_shape=jax.ShapeDtypeStruct(unit.shape,...  22.7 us
    ppermute x24, starting transfers between devices, swap_near(): return lax.ppermute(x, ('dp', 'mp'), [(i, i ^ flip) for i in range(size)])  19.9 us
    ppermute x16, starting transfers between devices, swap_side(): return lax.ppermute(x, 'dp', [(i, i ^ 2) for i in range(self.count)])  18.9 us
    ppermute x24, waiting for transfers between devices, swap_near(): return lax.ppermute(x, ('dp', 'mp'), [(i, i ^ flip) for i in range(size)])  18 us
    pallas_call x1, Pallas kernels, attend_back(): pl.pallas_call(attend_back_body, grid=(steps,), out_shape=shapes(*[((WIDT...  13.2 us
  transfers between devices with their start and end apart: 74, of which 33 were waited for; matrix products, arithmetic and copies ran while one was open for 21% of the time, Pallas kernels for 19%

profile of v1, /device:TPU:0, one launch (start us, length us, event | category | flops | bytes accessed | tf_op | source)
XLA Modules:
  0.0 289.4 jit_solution(16812591423876495497)
XLA Ops:
  7.1 5.1 %collective-permute-start.5 = (bf16[96,768]{1,0:T(8,128)(2,1)S(1)}, bf16[96,768]{1,0:T(8,128)(2,1)}, u32[]{:S(2)}, u32[]{:S(2)}) collective-permute-start(bf16[96,768]{1,0:T(8,128)(2,1)S(1)} %bitcast.238), channel_id=1, source_target_pairs={{0,24},{2,26},{4,28},{6,30},{8,0},{10,2},{12,4},{14,6},{16,8},{18,... | collective-permute-start | bytes 442376 | tf_op jit(solution)/shard_map/ppermute | solution.py:59
  15.6 5.2 %collective-permute-done.1 = bf16[96,768]{1,0:T(8,128)(2,1)S(1)} collective-permute-done((bf16[96,768]{1,0:T(8,128)(2,1)S(1)}, bf16[96,768]{1,0:T(8,128)(2,1)S(1)}, u32[]{:S(2)}, u32[]{:S(2)}) %collective-permute-start.1) | collective-permute-done | bytes 147488 | tf_op jit(solution)/shard_map/ppermute | solution.py:59
  20.7 3.5 %all-to-all-start = ((bf16[16,8,768]{2,1,0:T(8,128)(2,1)}), bf16[16,8,768]{2,1,0:T(8,128)(2,1)S(1)}, u32[]{:S(2)}, u32[]{:S(2)}) async-start(bf16[16,8,768]{2,1,0:T(8,128)(2,1)} %fusion.4), calls=%async_computation | async-start | bytes 393216 | tf_op jit(solution)/shard_map/all_to_all | solution.py:611
  24.3 7.4 %norm_first.1 = (bf16[2048,768]{1,0:T(8,128)(2,1)}, f32[2048,128]{1,0:T(8,128)}, bf16[128,768]{1,0:T(8,128)(2,1)}, bf16[128,768]{1,0:T(8,128)(2,1)}) custom-call(s32[1]{0:T(128)} %bitcast.1.group_ref, bf16[2048,768]{1,0:T(8,128)(2,1)} %bitcast.217, s32[128,1]{1,0:T(8,128)} %copy.41.ends_ref), custom_call_target="tpu_custom_call" | custom-call | tf_op jit(solution)/shard_map/norm_first/pallas_call | solution.py:250
  32.0 1.7 collective-permute-start.7
  37.1 2.9 collective-permute-done.7
  39.9 1.7 collective-permute-start.17
  42.2 1.7 collective-permute-start.14
  44.6 1.6 bitcast_dynamic-update-slice_fusion.21
  48.0 5.4 %collective-permute-done.8 = bf16[96,768]{1,0:T(8,128)(2,1)S(1)} collective-permute-done((bf16[96,768]{1,0:T(8,128)(2,1)S(1)}, bf16[96,768]{1,0:T(8,128)(2,1)S(1)}, u32[]{:S(2)}, u32[]{:S(2)}) %collective-permute-start.8) | collective-permute-done | bytes 147488 | tf_op jit(solution)/shard_map/ppermute | solution.py:56
  56.0 1.7 collective-permute-start.16
  59.5 6.1 %collective-permute-done.16 = bf16[96,1536]{1,0:T(8,128)(2,1)S(1)} collective-permute-done((bf16[96,1536]{1,0:T(8,128)(2,1)}, bf16[96,1536]{1,0:T(8,128)(2,1)S(1)}, u32[]{:S(2)}, u32[]{:S(2)}) %collective-permute-start.16) | collective-permute-done | bytes 294944 | tf_op jit(solution)/shard_map/ppermute | solution.py:56
  65.6 1.7 collective-permute-start.18
  68.3 6.1 %collective-permute-done.18 = bf16[96,1536]{1,0:T(8,128)(2,1)S(1)} collective-permute-done((bf16[96,1536]{1,0:T(8,128)(2,1)}, bf16[96,1536]{1,0:T(8,128)(2,1)S(1)}, u32[]{:S(2)}, u32[]{:S(2)}) %collective-permute-start.18) | collective-permute-done | bytes 294944 | tf_op jit(solution)/shard_map/ppermute | solution.py:56
  74.4 2.8 broadcast_select_fusion.2
  77.3 11.6 %attend.1 = (bf16[2048,384]{1,0:T(8,128)(2,1)}, bf16[2048,384]{1,0:T(8,128)(2,1)}, f32[768,256]{1,0:T(8,128)}, bf16[128,384]{1,0:T(8,128)(2,1)}, bf16[128,384]{1,0:T(8,128)(2,1)}, /*index=5*/bf16[128,768]{1,0:T(8,128)(2,1)}) custom-call(bf16[2048,768]{1,0:T(8,128)(2,1)} %get-tuple-element.45.unit_ref, bf16[128,768]{1,0:T(8,128)(2,1)} %get-tuple-element.46.unit_end_ref, ...), custom_call_target="tpu_custom_call" | custom-call | tf_op jit(solution)/shard_map/attend/pallas_call | solution.py:331
  88.9 3.6 %collective-permute-start.29 = (bf16[96,896]{1,0:T(8,128)(2,1)S(1)}, bf16[96,896]{1,0:T(8,128)(2,1)S(1)}, u32[]{:S(2)}, u32[]{:S(2)}) collective-permute-start(bf16[96,896]{1,0:T(8,128)(2,1)S(1)} %bitcast.234), channel_id=1, source_target_pairs={{0,24},{2,26},{4,28},{6,30},{8,0},{10,2},{12,4},{14,6},{16,8},{18,... | collective-permute-start | bytes 516104 | tf_op jit(solution)/shard_map/ppermute | solution.py:59
  94.1 3.8 %collective-permute-done.26 = bf16[96,896]{1,0:T(8,128)(2,1)S(1)} collective-permute-done((bf16[96,896]{1,0:T(8,128)(2,1)S(1)}, bf16[96,896]{1,0:T(8,128)(2,1)S(1)}, u32[]{:S(2)}, u32[]{:S(2)}) %collective-permute-start.26) | collective-permute-done | bytes 172064 | tf_op jit(solution)/shard_map/ppermute | solution.py:56
  97.9 1.8 collective-permute-done.27
  100.2 4.8 %collective-permute-done.12 = bf16[128,768]{1,0:T(8,128)(2,1)S(1)} collective-permute-done((bf16[128,768]{1,0:T(8,128)(2,1)S(1)}, bf16[128,768]{1,0:T(8,128)(2,1)S(1)}, u32[]{:S(2)}, u32[]{:S(2)}) %collective-permute-start.12) | collective-permute-done | bytes 196640 | tf_op jit(solution)/shard_map/ppermute | solution.py:145
  105.1 2.4 collective-permute-done.11
  113.7 4.1 %collective-permute-done.31 = bf16[96,896]{1,0:T(8,128)(2,1)S(1)} collective-permute-done((bf16[96,896]{1,0:T(8,128)(2,1)S(1)}, bf16[96,896]{1,0:T(8,128)(2,1)S(1)}, u32[]{:S(2)}, u32[]{:S(2)}) %collective-permute-start.31) | collective-permute-done | bytes 172064 | tf_op jit(solution)/shard_map/ppermute | solution.py:59
  118.4 2.7 collective-permute-done.28
  121.1 3.6 %collective-permute-done.30 = bf16[96,896]{1,0:T(8,128)(2,1)S(1)} collective-permute-done((bf16[96,896]{1,0:T(8,128)(2,1)S(1)}, bf16[96,896]{1,0:T(8,128)(2,1)S(1)}, u32[]{:S(2)}, u32[]{:S(2)}) %collective-permute-start.30) | collective-permute-done | bytes 172064 | tf_op jit(solution)/shard_map/ppermute | solution.py:56
  124.8 3.4 %collective-permute-done.32 = bf16[96,896]{1,0:T(8,128)(2,1)S(1)} collective-permute-done((bf16[96,896]{1,0:T(8,128)(2,1)S(1)}, bf16[96,896]{1,0:T(8,128)(2,1)S(1)}, u32[]{:S(2)}, u32[]{:S(2)}) %collective-permute-start.32) | collective-permute-done | bytes 172064 | tf_op jit(solution)/shard_map/ppermute | solution.py:56
  130.3 1.7 collective-permute-start.22
  132.8 3.2 %collective-permute-done.22 = bf16[64,768]{1,0:T(8,128)(2,1)S(1)} collective-permute-done((bf16[64,768]{1,0:T(8,128)(2,1)S(1)}, bf16[64,768]{1,0:T(8,128)(2,1)S(1)}, u32[]{:S(2)}, u32[]{:S(2)}) %collective-permute-start.22) | collective-permute-done | bytes 98336 | tf_op jit(solution)/shard_map/ppermute | solution.py:145
  139.2 2.0 fusion.42
  149.2 3.9 %collective-permute-start.39 = (f32[9,128]{1,0:T(8,128)S(1)}, f32[9,128]{1,0:T(8,128)S(1)}, u32[]{:S(2)}, u32[]{:S(2)}) collective-permute-start(f32[9,128]{1,0:T(8,128)S(1)} %add_add_fusion.2), channel_id=1, source_target_pairs={{0,24},{2,26},{4,28},{6,30},{8,0},{10,2},{12,4},{14,6},{16,8},{18,... | collective-permute-start | bytes 13832 | tf_op jit(solution)/shard_map/ppermute | solution.py:59
  153.7 3.2 %broadcast_select_fusion = (bf16[768,768]{1,0:T(8,128)(2,1)}, bf16[768,768]{1,0:T(8,128)(2,1)}) fusion(bf16[768,768]{1,0:T(8,128)(2,1)} %collective-permute-done.56, bf16[768,768]{1,0:T(8,128)(2,1)} %collective-permute-done.21, pred[]{:T(512)S(6)} %eq.103), kind=kLoop, calls=%fused_computation.18 | loop fusion | flops 1179648 | bytes 4718593 | tf_op jit(solution)/shard_map/jit(_where)/select_n | solution.py:40
  160.6 1.8 collective-permute-start.42
  168.1 1.9 fusion.14
  179.7 1.7 copy.45
  184.0 1.6 collective-permute-done.44
  191.4 13.2 %attend_back.1 = (bf16[768,768]{1,0:T(8,128)(2,1)}, bf16[768,768]{1,0:T(8,128)(2,1)}, bf16[2048,384]{1,0:T(8,128)(2,1)}, bf16[2048,384]{1,0:T(8,128)(2,1)}, bf16...) custom-call(s32[1]{0:T(128)} %bitcast.2.core_ref, bf16[128,768]{1,0:T(8,128)(2,1)} %copy-done.14, ...), custom_call_target="tpu_custom_call" | custom-call | tf_op jit(solution)/shard_map/attend_back/pallas_call | solution.py:414
  207.4 2.5 collective-permute-start.65
  211.8 2.9 collective-permute-done.63
  215.4 1.8 collective-permute-done.65
  217.2 5.4 %collective-permute-done.64 = bf16[96,768]{1,0:T(8,128)(2,1)S(1)} collective-permute-done((bf16[96,768]{1,0:T(8,128)(2,1)S(1)}, bf16[96,768]{1,0:T(8,128)(2,1)S(1)}, u32[]{:S(2)}, u32[]{:S(2)}) %collective-permute-start.64) | collective-permute-done | bytes 147488 | tf_op jit(solution)/shard_map/ppermute | solution.py:59
  224.4 3.8 %collective-permute-start.69 = (bf16[96,960]{1,0:T(8,128)(2,1)S(1)}, bf16[96,960]{1,0:T(8,128)(2,1)S(1)}, u32[]{:S(2)}, u32[]{:S(2)}) collective-permute-start(bf16[96,960]{1,0:T(8,128)(2,1)S(1)} %get-tuple-element.108), channel_id=1, source_target_pairs={{0,24},{2,26},{4,28},{6,30},{8,0},{10,2},{12,4},{14,6},{16,8},{18,... | collective-permute-start | bytes 552968 | tf_op jit(solution)/shard_map/ppermute | solution.py:59
  228.3 1.6 add_convert_fusion
  232.2 1.8 collective-permute-done.67
  235.5 2.4 collective-permute-done.69
  237.8 6.2 %collective-permute-done.68 = bf16[96,960]{1,0:T(8,128)(2,1)S(1)} collective-permute-done((bf16[96,960]{1,0:T(8,128)(2,1)S(1)}, bf16[96,960]{1,0:T(8,128)(2,1)S(1)}, u32[]{:S(2)}, u32[]{:S(2)}) %collective-permute-start.68) | collective-permute-done | bytes 184352 | tf_op jit(solution)/shard_map/ppermute | solution.py:59
  246.0 3.3 %collective-permute-start.51 = (bf16[96,768]{1,0:T(8,128)(2,1)S(1)}, bf16[96,768]{1,0:T(8,128)(2,1)S(1)}, u32[]{:S(2)}, u32[]{:S(2)}) collective-permute-start(bf16[96,768]{1,0:T(8,128)(2,1)S(1)} %get-tuple-element.116), channel_id=1, source_target_pairs={{0,24},{2,26},{4,28},{6,30},{8,0},{10,2},{12,4},{14,6},{16,8},{18,... | collective-permute-start | bytes 442376 | tf_op jit(solution)/shard_map/ppermute | solution.py:59
  253.2 1.7 collective-permute-done.53.d_att_far_ref
  257.4 11.3 %captions_back.2.refs_0_ = f32[2048,768]{1,0:T(8,128)} custom-call(s32[1]{0:T(128)} %bitcast.1.group_ref, s32[128,1]{1,0:T(8,128)} %copy.46.ends_ref, bf16[2048,768]{1,0:T(8,128)(2,1)} %get-tuple-element.45.unit_ref, f32[2048,128]{1,0:T(8,128)} %get-tuple-element.65.scale_ref, f32[128,768]{1,0:T(8,128)} %get-tuple-element.91.d_mid_ref, ...), custom_call_target="tpu_custom_call" | custom-call | tf_op jit(solution)/shard_map/captions_back/pallas_call | solution.py:532
  269.5 11.3 %captions_back.3 = f32[2048,768]{1,0:T(8,128)} custom-call(s32[1]{0:T(128)} %bitcast.1.group_ref, s32[128,1]{1,0:T(8,128)} %copy.47.ends_ref, bf16[2048,768]{1,0:T(8,128)(2,1)} %get-tuple-element.45.unit_ref, f32[2048,128]{1,0:T(8,128)} %get-tuple-element.65.scale_ref, f32[128,768]{1,0:T(8,128)} %get-tuple-element.91.d_mid_ref, ...), custom_call_target="tpu_custom_call", output_to_operand_aliasing={{}: (16, {})} | custom-call | tf_op jit(solution)/shard_map/captions_back/pallas_call | solution.py:532
  (361 shorter events, 95.6 us)
Async XLA Ops:
  2.7 12.9 %collective-permute-start.13 = (bf16[48,1536]{1,0:T(8,128)(2,1)S(1)}, bf16[48,1536]{1,0:T(8,128)(2,1)S(1)}, u32[]{:S(2)}, u32[]{:S(2)}) collective-permute-start(bf16[48,1536]{1,0:T(8,128)(2,1)S(1)} %get-tuple-element.80), channel_id=1, source_target_pairs={{0,2},{2,0},{4,6},{6,4},{8,10},{10,8},{12,14},{14,12},{16,18},{18,... | collective-permute-start | bytes 442376 | tf_op jit(solution)/shard_map/ppermute | solution.py:53
  7.1 28.1 %collective-permute-start.5 = (bf16[96,768]{1,0:T(8,128)(2,1)S(1)}, bf16[96,768]{1,0:T(8,128)(2,1)}, u32[]{:S(2)}, u32[]{:S(2)}) collective-permute-start(bf16[96,768]{1,0:T(8,128)(2,1)S(1)} %bitcast.238), channel_id=1, source_target_pairs={{0,24},{2,26},{4,28},{6,30},{8,0},{10,2},{12,4},{14,6},{16,8},{18,... | collective-permute-start | bytes 442376 | tf_op jit(solution)/shard_map/ppermute | solution.py:59
  12.2 23.5 %collective-permute-start.3 = (bf16[96,768]{1,0:T(8,128)(2,1)S(1)}, bf16[96,768]{1,0:T(8,128)(2,1)S(1)}, u32[]{:S(2)}, u32[]{:S(2)}) collective-permute-start(bf16[96,768]{1,0:T(8,128)(2,1)S(1)} %bitcast.239), channel_id=1, source_target_pairs={{0,4},{2,6},{4,0},{6,2},{8,12},{10,14},{12,8},{14,10},{16,20},{18,... | collective-permute-start | bytes 442376 | tf_op jit(solution)/shard_map/ppermute | solution.py:56
  20.7 34.8 %all-to-all-start = ((bf16[16,8,768]{2,1,0:T(8,128)(2,1)}), bf16[16,8,768]{2,1,0:T(8,128)(2,1)S(1)}, u32[]{:S(2)}, u32[]{:S(2)}) async-start(bf16[16,8,768]{2,1,0:T(8,128)(2,1)} %fusion.4), calls=%async_computation | async-start | bytes 393216 | tf_op jit(solution)/shard_map/all_to_all | solution.py:611
  31.7 77.3 %collective-permute-start.2 = (bf16[128,768]{1,0:T(8,128)(2,1)}, bf16[128,768]{1,0:T(8,128)(2,1)}, u32[]{:S(2)}, u32[]{:S(2)}) collective-permute-start(bf16[128,768]{1,0:T(8,128)(2,1)} %get-tuple-element.44), channel_id=1, source_target_pairs={{0,2},{1,3},{2,0},{3,1},{4,6},{5,7},{6,4},{7,5},{8,10},{9,11},{10,... | collective-permute-start | bytes 589832 | tf_op jit(solution)/shard_map/ppermute | solution.py:145
  32.0 7.9 %collective-permute-start.7 = (bf16[96,768]{1,0:T(8,128)(2,1)S(1)}, bf16[96,768]{1,0:T(8,128)(2,1)S(1)}, u32[]{:S(2)}, u32[]{:S(2)}) collective-permute-start(bf16[96,768]{1,0:T(8,128)(2,1)S(1)} %collective-permute-done.1), channel_id=1, source_target_pairs={{0,8},{2,10},{4,12},{6,14},{8,16},{10,18},{12,20},{14,22},{16,24},... | collective-permute-start | bytes 442376 | tf_op jit(solution)/shard_map/ppermute | solution.py:59
  33.7 8.5 %collective-permute-start.4 = (bf16[96,768]{1,0:T(8,128)(2,1)S(1)}, bf16[96,768]{1,0:T(8,128)(2,1)S(1)}, u32[]{:S(2)}, u32[]{:S(2)}) collective-permute-start(bf16[96,768]{1,0:T(8,128)(2,1)S(1)} %collective-permute-done.1), channel_id=1, source_target_pairs={{0,4},{2,6},{4,0},{6,2},{8,12},{10,14},{12,8},{14,10},{16,20},{18,... | collective-permute-start | bytes 442376 | tf_op jit(solution)/shard_map/ppermute | solution.py:56
  35.2 11.0 %collective-permute-start.6 = (bf16[96,768]{1,0:T(8,128)(2,1)}, bf16[96,768]{1,0:T(8,128)(2,1)S(1)}, u32[]{:S(2)}, u32[]{:S(2)}) collective-permute-start(bf16[96,768]{1,0:T(8,128)(2,1)} %collective-permute-done.5), channel_id=1, source_target_pairs={{0,4},{2,6},{4,0},{6,2},{8,12},{10,14},{12,8},{14,10},{16,20},{18,... | collective-permute-start | bytes 442376 | tf_op jit(solution)/shard_map/ppermute | solution.py:56
  39.9 19.0 %collective-permute-start.17 = (bf16[96,1536]{1,0:T(8,128)(2,1)S(1)}, bf16[96,1536]{1,0:T(8,128)(2,1)}, u32[]{:S(2)}, u32[]{:S(2)}) collective-permute-start(bf16[96,1536]{1,0:T(8,128)(2,1)S(1)} %bitcast.224), channel_id=1, source_target_pairs={{0,24},{2,26},{4,28},{6,30},{8,0},{10,2},{12,4},{14,6},{16,8},{18,... | collective-permute-start | bytes 884744 | tf_op jit(solution)/shard_map/ppermute | solution.py:59
  41.7 14.2 %collective-permute-start.15 = (bf16[96,1536]{1,0:T(8,128)(2,1)S(1)}, bf16[96,1536]{1,0:T(8,128)(2,1)}, u32[]{:S(2)}, u32[]{:S(2)}) collective-permute-start(bf16[96,1536]{1,0:T(8,128)(2,1)S(1)} %bitcast.225), channel_id=1, source_target_pairs={{0,8},{2,10},{4,12},{6,14},{8,16},{10,18},{12,20},{14,22},{16,24},... | collective-permute-start | bytes 884744 | tf_op jit(solution)/shard_map/ppermute | solution.py:59
  42.2 13.8 %collective-permute-start.14 = (bf16[96,1536]{1,0:T(8,128)(2,1)S(1)}, bf16[96,1536]{1,0:T(8,128)(2,1)S(1)}, u32[]{:S(2)}, u32[]{:S(2)}) collective-permute-start(bf16[96,1536]{1,0:T(8,128)(2,1)S(1)} %bitcast.227), channel_id=1, source_target_pairs={{0,4},{2,6},{4,0},{6,2},{8,12},{10,14},{12,8},{14,10},{16,20},{18,... | collective-permute-start | bytes 884744 | tf_op jit(solution)/shard_map/ppermute | solution.py:56
  54.0 74.3 %collective-permute-start.21 = (bf16[768,768]{1,0:T(8,128)(2,1)}, bf16[768,768]{1,0:T(8,128)(2,1)}, u32[]{:S(2)}, u32[]{:S(2)}) collective-permute-start(bf16[768,768]{1,0:T(8,128)(2,1)} %bitcast.19), channel_id=1, source_target_pairs={{0,1},{1,0},{2,3},{3,2},{4,5},{5,4},{6,7},{7,6},{8,9},{9,8},{10,11... | collective-permute-start | bytes 3538952 | tf_op jit(solution)/shard_map/ppermute | solution.py:145
  56.0 9.6 %collective-permute-start.16 = (bf16[96,1536]{1,0:T(8,128)(2,1)}, bf16[96,1536]{1,0:T(8,128)(2,1)S(1)}, u32[]{:S(2)}, u32[]{:S(2)}) collective-permute-start(bf16[96,1536]{1,0:T(8,128)(2,1)} %collective-permute-done.15), channel_id=1, source_target_pairs={{0,4},{2,6},{4,0},{6,2},{8,12},{10,14},{12,8},{14,10},{16,20},{18,... | collective-permute-start | bytes 884744 | tf_op jit(solution)/shard_map/ppermute | solution.py:56
  58.7 15.7 %collective-permute-start.9 = (bf16[768,768]{1,0:T(8,128)(2,1)}, bf16[768,768]{1,0:T(8,128)(2,1)S(1)}, u32[]{:S(2)}, u32[]{:S(2)}) collective-permute-start(bf16[768,768]{1,0:T(8,128)(2,1)} %bitcast.19), channel_id=1, source_target_pairs={{0,2},{2,0},{4,6},{6,4},{8,10},{10,8},{12,14},{14,12},{16,18},{18,... | collective-permute-start | bytes 3538952 | tf_op jit(solution)/shard_map/ppermute | solution.py:53
  59.0 29.9 %collective-permute-start.19 = (bf16[96,1536]{1,0:T(8,128)(2,1)}, bf16[96,1536]{1,0:T(8,128)(2,1)S(1)}, u32[]{:S(2)}, u32[]{:S(2)}) collective-permute-start(bf16[96,1536]{1,0:T(8,128)(2,1)} %collective-permute-done.15), channel_id=1, source_target_pairs={{0,8},{2,10},{4,12},{6,14},{8,16},{10,18},{12,20},{14,22},{16,24},... | collective-permute-start | bytes 884744 | tf_op jit(solution)/shard_map/ppermute | solution.py:59
  65.6 8.8 %collective-permute-start.18 = (bf16[96,1536]{1,0:T(8,128)(2,1)}, bf16[96,1536]{1,0:T(8,128)(2,1)S(1)}, u32[]{:S(2)}, u32[]{:S(2)}) collective-permute-start(bf16[96,1536]{1,0:T(8,128)(2,1)} %collective-permute-done.17), channel_id=1, source_target_pairs={{0,4},{2,6},{4,0},{6,2},{8,12},{10,14},{12,8},{14,10},{16,20},{18,... | collective-permute-start | bytes 884744 | tf_op jit(solution)/shard_map/ppermute | solution.py:56
  88.9 21.2 %collective-permute-start.29 = (bf16[96,896]{1,0:T(8,128)(2,1)S(1)}, bf16[96,896]{1,0:T(8,128)(2,1)S(1)}, u32[]{:S(2)}, u32[]{:S(2)}) collective-permute-start(bf16[96,896]{1,0:T(8,128)(2,1)S(1)} %bitcast.234), channel_id=1, source_target_pairs={{0,24},{2,26},{4,28},{6,30},{8,0},{10,2},{12,4},{14,6},{16,8},{18,... | collective-permute-start | bytes 516104 | tf_op jit(solution)/shard_map/ppermute | solution.py:59
  99.7 7.8 %collective-permute-start.11 = (bf16[128,768]{1,0:T(8,128)(2,1)S(1)}, bf16[128,768]{1,0:T(8,128)(2,1)S(1)}, u32[]{:S(2)}, u32[]{:S(2)}) collective-permute-start(bf16[128,768]{1,0:T(8,128)(2,1)S(1)} %copy-done.25), channel_id=1, source_target_pairs={{0,1},{1,0},{2,3},{3,2},{4,5},{5,4},{6,7},{7,6},{8,9},{9,8},{10,11... | collective-permute-start | bytes 589832 | tf_op jit(solution)/shard_map/ppermute | solution.py:145
  107.5 20.8 %collective-permute-start.20 = (bf16[96,1536]{1,0:T(8,128)(2,1)S(1)}, bf16[96,1536]{1,0:T(8,128)(2,1)S(1)}, u32[]{:S(2)}, u32[]{:S(2)}) collective-permute-start(bf16[96,1536]{1,0:T(8,128)(2,1)S(1)} %collective-permute-done.19), channel_id=1, source_target_pairs={{0,4},{2,6},{4,0},{6,2},{8,12},{10,14},{12,8},{14,10},{16,20},{18,... | collective-permute-start | bytes 884744 | tf_op jit(solution)/shard_map/ppermute | solution.py:56
  109.0 8.9 %collective-permute-start.31 = (bf16[96,896]{1,0:T(8,128)(2,1)S(1)}, bf16[96,896]{1,0:T(8,128)(2,1)S(1)}, u32[]{:S(2)}, u32[]{:S(2)}) collective-permute-start(bf16[96,896]{1,0:T(8,128)(2,1)S(1)} %collective-permute-done.27), channel_id=1, source_target_pairs={{0,8},{2,10},{4,12},{6,14},{8,16},{10,18},{12,20},{14,22},{16,24},... | collective-permute-start | bytes 516104 | tf_op jit(solution)/shard_map/ppermute | solution.py:59
  110.1 11.0 %collective-permute-start.28 = (bf16[96,896]{1,0:T(8,128)(2,1)S(1)}, bf16[96,896]{1,0:T(8,128)(2,1)S(1)}, u32[]{:S(2)}, u32[]{:S(2)}) collective-permute-start(bf16[96,896]{1,0:T(8,128)(2,1)S(1)} %collective-permute-done.27), channel_id=1, source_target_pairs={{0,4},{2,6},{4,0},{6,2},{8,12},{10,14},{12,8},{14,10},{16,20},{18,... | collective-permute-start | bytes 516104 | tf_op jit(solution)/shard_map/ppermute | solution.py:56
  110.6 14.1 %collective-permute-start.30 = (bf16[96,896]{1,0:T(8,128)(2,1)S(1)}, bf16[96,896]{1,0:T(8,128)(2,1)S(1)}, u32[]{:S(2)}, u32[]{:S(2)}) collective-permute-start(bf16[96,896]{1,0:T(8,128)(2,1)S(1)} %collective-permute-done.29), channel_id=1, source_target_pairs={{0,4},{2,6},{4,0},{6,2},{8,12},{10,14},{12,8},{14,10},{16,20},{18,... | collective-permute-start | bytes 516104 | tf_op jit(solution)/shard_map/ppermute | solution.py:56
  117.8 10.4 %collective-permute-start.32 = (bf16[96,896]{1,0:T(8,128)(2,1)S(1)}, bf16[96,896]{1,0:T(8,128)(2,1)S(1)}, u32[]{:S(2)}, u32[]{:S(2)}) collective-permute-start(bf16[96,896]{1,0:T(8,128)(2,1)S(1)} %collective-permute-done.31), channel_id=1, source_target_pairs={{0,4},{2,6},{4,0},{6,2},{8,12},{10,14},{12,8},{14,10},{16,20},{18,... | collective-permute-start | bytes 516104 | tf_op jit(solution)/shard_map/ppermute | solution.py:56
  128.2 9.2 %collective-permute-start.33 = (bf16[768,896]{1,0:T(8,128)(2,1)S(1)}, bf16[768,896]{1,0:T(8,128)(2,1)S(1)}, u32[]{:S(2)}, u32[]{:S(2)}) collective-permute-start(bf16[768,896]{1,0:T(8,128)(2,1)S(1)} %bitcast.206), channel_id=1, source_target_pairs={{0,2},{2,0},{4,6},{6,4},{8,10},{10,8},{12,14},{14,12},{16,18},{18,... | collective-permute-start | bytes 4128776 | tf_op jit(solution)/shard_map/ppermute | solution.py:53
  132.5 20.6 %collective-permute-start.56 = (bf16[768,768]{1,0:T(8,128)(2,1)}, bf16[768,768]{1,0:T(8,128)(2,1)}, u32[]{:S(2)}, u32[]{:S(2)}) collective-permute-start(bf16[768,768]{1,0:T(8,128)(2,1)} %collective-permute-done.21), channel_id=1, source_target_pairs={{0,2},{2,0},{4,6},{6,4},{8,10},{10,8},{12,14},{14,12},{16,18},{18,... | collective-permute-start | bytes 3538952 | tf_op jit(solution)/shard_map/ppermute | solution.py:53
  145.9 29.4 %collective-permute-start.59 = (bf16[64,768]{1,0:T(8,128)(2,1)}, bf16[64,768]{1,0:T(8,128)(2,1)}, u32[]{:S(2)}, u32[]{:S(2)}) collective-permute-start(bf16[64,768]{1,0:T(8,128)(2,1)} %copy-done.29), channel_id=1, source_target_pairs={{0,3},{1,2},{2,1},{3,0},{4,7},{5,6},{6,5},{7,4},{8,11},{9,10},{10,... | collective-permute-start | bytes 294920 | tf_op jit(solution)/shard_map/ppermute | solution.py:145
  147.5 28.3 %collective-permute-start.58 = (bf16[64,768]{1,0:T(8,128)(2,1)}, bf16[64,768]{1,0:T(8,128)(2,1)}, u32[]{:S(2)}, u32[]{:S(2)}) collective-permute-start(bf16[64,768]{1,0:T(8,128)(2,1)} %copy-done.29), channel_id=1, source_target_pairs={{0,2},{1,3},{2,0},{3,1},{4,6},{5,7},{6,4},{7,5},{8,10},{9,11},{10,... | collective-permute-start | bytes 294920 | tf_op jit(solution)/shard_map/ppermute | solution.py:145
  165.8 11.4 %collective-permute-start.57 = (bf16[64,768]{1,0:T(8,128)(2,1)}, bf16[64,768]{1,0:T(8,128)(2,1)S(1)}, u32[]{:S(2)}, u32[]{:S(2)}) collective-permute-start(bf16[64,768]{1,0:T(8,128)(2,1)} %copy-done.29), channel_id=1, source_target_pairs={{0,1},{1,0},{2,3},{3,2},{4,5},{5,4},{6,7},{7,6},{8,9},{9,8},{10,11... | collective-permute-start | bytes 294920 | tf_op jit(solution)/shard_map/ppermute | solution.py:145
  166.6 43.3 %collective-permute-start.40 = (f32[8,128]{1,0:T(8,128)S(1)}, f32[8,128]{1,0:T(8,128)S(1)}, u32[]{:S(2)}, u32[]{:S(2)}) collective-permute-start(f32[8,128]{1,0:T(8,128)S(1)} %broadcast_in_dim.195), channel_id=1, source_target_pairs={{0,1},{1,0},{2,3},{3,2},{4,5},{5,4},{6,7},{7,6},{8,9},{9,8},{10,11... | collective-permute-start | bytes 12296 | tf_op jit(solution)/shard_map/ppermute | solution.py:145
  173.9 13.4 %collective-permute-start.46 = (bf16[128,768]{1,0:T(8,128)(2,1)}, bf16[128,768]{1,0:T(8,128)(2,1)}, u32[]{:S(2)}, u32[]{:S(2)}) collective-permute-start(bf16[128,768]{1,0:T(8,128)(2,1)} %get-tuple-element.123), channel_id=1, source_target_pairs={{0,3},{1,2},{2,1},{3,0},{4,7},{5,6},{6,5},{7,4},{8,11},{9,10},{10,... | collective-permute-start | bytes 589832 | tf_op jit(solution)/shard_map/ppermute | solution.py:145
  175.3 13.0 %collective-permute-start.45 = (bf16[128,768]{1,0:T(8,128)(2,1)}, bf16[128,768]{1,0:T(8,128)(2,1)}, u32[]{:S(2)}, u32[]{:S(2)}) collective-permute-start(bf16[128,768]{1,0:T(8,128)(2,1)} %get-tuple-element.123), channel_id=1, source_target_pairs={{0,2},{1,3},{2,0},{3,1},{4,6},{5,7},{6,4},{7,5},{8,10},{9,11},{10,... | collective-permute-start | bytes 589832 | tf_op jit(solution)/shard_map/ppermute | solution.py:145
  175.8 9.8 %collective-permute-start.44 = (bf16[128,768]{1,0:T(8,128)(2,1)}, bf16[128,768]{1,0:T(8,128)(2,1)}, u32[]{:S(2)}, u32[]{:S(2)}) collective-permute-start(bf16[128,768]{1,0:T(8,128)(2,1)} %get-tuple-element.122), channel_id=1, source_target_pairs={{0,1},{1,0},{2,3},{3,2},{4,5},{5,4},{6,7},{7,6},{8,9},{9,8},{10,11... | collective-permute-start | bytes 589832 | tf_op jit(solution)/shard_map/ppermute | solution.py:145
  182.3 22.4 %collective-permute-start.62 = (bf16[4,96,768]{2,1,0:T(8,128)(2,1)}, bf16[4,96,768]{2,1,0:T(8,128)(2,1)}, u32[]{:S(2)}, u32[]{:S(2)}) collective-permute-start(bf16[4,96,768]{2,1,0:T(8,128)(2,1)} %dynamic-slice_bitcast_fusion.1), channel_id=1, source_target_pairs={{0,4},{2,6},{4,0},{6,2},{8,12},{10,14},{12,8},{14,10},{16,20},{18,... | collective-permute-start | bytes 1769480 | tf_op jit(solution)/shard_map/ppermute | solution.py:56
  185.6 37.2 %collective-permute-start.60 = (bf16[4,96,960]{2,1,0:T(8,128)(2,1)}, bf16[4,96,960]{2,1,0:T(8,128)(2,1)}, u32[]{:S(2)}, u32[]{:S(2)}) collective-permute-start(bf16[4,96,960]{2,1,0:T(8,128)(2,1)} %dynamic-slice_bitcast_fusion), channel_id=1, source_target_pairs={{0,4},{2,6},{4,0},{6,2},{8,12},{10,14},{12,8},{14,10},{16,20},{18,... | collective-permute-start | bytes 2211848 | tf_op jit(solution)/shard_map/ppermute | solution.py:56
  204.6 23.6 %collective-permute-start.47 = (bf16[768,768]{1,0:T(8,128)(2,1)}, bf16[768,768]{1,0:T(8,128)(2,1)}, u32[]{:S(2)}, u32[]{:S(2)}) collective-permute-start(bf16[768,768]{1,0:T(8,128)(2,1)} %get-tuple-element.63), channel_id=1, source_target_pairs={{0,2},{2,0},{4,6},{6,4},{8,10},{10,8},{12,14},{14,12},{16,18},{18,... | collective-permute-start | bytes 3538952 | tf_op jit(solution)/shard_map/ppermute | solution.py:53
  206.0 8.6 %collective-permute-start.63 = (bf16[96,768]{1,0:T(8,128)(2,1)S(1)}, bf16[96,768]{1,0:T(8,128)(2,1)S(1)}, u32[]{:S(2)}, u32[]{:S(2)}) collective-permute-start(bf16[96,768]{1,0:T(8,128)(2,1)S(1)} %get-tuple-element.112), channel_id=1, source_target_pairs={{0,8},{2,10},{4,12},{6,14},{8,16},{10,18},{12,20},{14,22},{16,24},... | collective-permute-start | bytes 442376 | tf_op jit(solution)/shard_map/ppermute | solution.py:59
  207.4 9.9 %collective-permute-start.65 = (bf16[96,768]{1,0:T(8,128)(2,1)S(1)}, bf16[96,768]{1,0:T(8,128)(2,1)S(1)}, u32[]{:S(2)}, u32[]{:S(2)}) collective-permute-start(bf16[96,768]{1,0:T(8,128)(2,1)S(1)} %get-tuple-element.113), channel_id=1, source_target_pairs={{0,24},{2,26},{4,28},{6,30},{8,0},{10,2},{12,4},{14,6},{16,8},{18,... | collective-permute-start | bytes 442376 | tf_op jit(solution)/shard_map/ppermute | solution.py:59
  209.9 12.7 %collective-permute-start.64 = (bf16[96,768]{1,0:T(8,128)(2,1)S(1)}, bf16[96,768]{1,0:T(8,128)(2,1)S(1)}, u32[]{:S(2)}, u32[]{:S(2)}) collective-permute-start(bf16[96,768]{1,0:T(8,128)(2,1)S(1)} %get-tuple-element.114), channel_id=1, source_target_pairs={{0,16},{2,18},{4,20},{6,22},{8,24},{10,26},{12,28},{14,30},{16,0},... | collective-permute-start | bytes 442376 | tf_op jit(solution)/shard_map/ppermute | solution.py:59
  214.6 35.6 %collective-permute-start.52 = (bf16[128,384]{1,0:T(8,128)(2,1)}, bf16[128,384]{1,0:T(8,128)(2,1)S(1)}, u32[]{:S(2)}, u32[]{:S(2)}) collective-permute-start(bf16[128,384]{1,0:T(8,128)(2,1)} %get-tuple-element.60.q_ref), channel_id=1, source_target_pairs={{0,1},{1,0},{2,3},{3,2},{4,5},{5,4},{6,7},{7,6},{8,9},{9,8},{10,11... | collective-permute-start | bytes 294920 | tf_op jit(solution)/shard_map/ppermute | solution.py:145
  224.3 9.7 %collective-permute-start.67 = (bf16[96,960]{1,0:T(8,128)(2,1)S(1)}, bf16[96,960]{1,0:T(8,128)(2,1)S(1)}, u32[]{:S(2)}, u32[]{:S(2)}) collective-permute-start(bf16[96,960]{1,0:T(8,128)(2,1)S(1)} %get-tuple-element.107), channel_id=1, source_target_pairs={{0,8},{2,10},{4,12},{6,14},{8,16},{10,18},{12,20},{14,22},{16,24},... | collective-permute-start | bytes 552968 | tf_op jit(solution)/shard_map/ppermute | solution.py:59
  224.4 13.4 %collective-permute-start.69 = (bf16[96,960]{1,0:T(8,128)(2,1)S(1)}, bf16[96,960]{1,0:T(8,128)(2,1)S(1)}, u32[]{:S(2)}, u32[]{:S(2)}) collective-permute-start(bf16[96,960]{1,0:T(8,128)(2,1)S(1)} %get-tuple-element.108), channel_id=1, source_target_pairs={{0,24},{2,26},{4,28},{6,30},{8,0},{10,2},{12,4},{14,6},{16,8},{18,... | collective-permute-start | bytes 552968 | tf_op jit(solution)/shard_map/ppermute | solution.py:59
  228.2 15.9 %collective-permute-start.68 = (bf16[96,960]{1,0:T(8,128)(2,1)S(1)}, bf16[96,960]{1,0:T(8,128)(2,1)S(1)}, u32[]{:S(2)}, u32[]{:S(2)}) collective-permute-start(bf16[96,960]{1,0:T(8,128)(2,1)S(1)} %get-tuple-element.109), channel_id=1, source_target_pairs={{0,16},{2,18},{4,20},{6,22},{8,24},{10,26},{12,28},{14,30},{16,0},... | collective-permute-start | bytes 552968 | tf_op jit(solution)/shard_map/ppermute | solution.py:59
  229.9 15.2 %collective-permute-start.48 = (bf16[4,96,768]{2,1,0:T(8,128)(2,1)S(1)}, bf16[4,96,768]{2,1,0:T(8,128)(2,1)S(1)}, u32[]{:S(2)}, u32[]{:S(2)}) collective-permute-start(bf16[4,96,768]{2,1,0:T(8,128)(2,1)S(1)} %dynamic-slice_bitcast_fusion.2), channel_id=1, source_target_pairs={{0,4},{2,6},{4,0},{6,2},{8,12},{10,14},{12,8},{14,10},{16,20},{18,... | collective-permute-start | bytes 1769480 | tf_op jit(solution)/shard_map/ppermute | solution.py:56
  234.0 17.8 %collective-permute-start.55 = (bf16[256,128]{1,0:T(8,128)(2,1)S(1)}, bf16[256,128]{1,0:T(8,128)(2,1)S(1)}, u32[]{:S(2)}, u32[]{:S(2)}) collective-permute-start(bf16[256,128]{1,0:T(8,128)(2,1)S(1)} %copy-done.45), channel_id=1, source_target_pairs={{0,1},{1,0},{2,3},{3,2},{4,5},{5,4},{6,7},{7,6},{8,9},{9,8},{10,11... | collective-permute-start | bytes 196616 | tf_op jit(solution)/shard_map/ppermute | solution.py:145
  245.4 35.5 %collective-permute-start.49 = (bf16[96,768]{1,0:T(8,128)(2,1)S(1)}, bf16[96,768]{1,0:T(8,128)(2,1)S(1)}, u32[]{:S(2)}, u32[]{:S(2)}) collective-permute-start(bf16[96,768]{1,0:T(8,128)(2,1)S(1)} %get-tuple-element.115), channel_id=1, source_target_pairs={{0,8},{2,10},{4,12},{6,14},{8,16},{10,18},{12,20},{14,22},{16,24},... | collective-permute-start | bytes 442376 | tf_op jit(solution)/shard_map/ppermute | solution.py:59
  246.0 34.9 %collective-permute-start.51 = (bf16[96,768]{1,0:T(8,128)(2,1)S(1)}, bf16[96,768]{1,0:T(8,128)(2,1)S(1)}, u32[]{:S(2)}, u32[]{:S(2)}) collective-permute-start(bf16[96,768]{1,0:T(8,128)(2,1)S(1)} %get-tuple-element.116), channel_id=1, source_target_pairs={{0,24},{2,26},{4,28},{6,30},{8,0},{10,2},{12,4},{14,6},{16,8},{18,... | collective-permute-start | bytes 442376 | tf_op jit(solution)/shard_map/ppermute | solution.py:59
  249.3 31.6 %collective-permute-start.50 = (bf16[96,768]{1,0:T(8,128)(2,1)S(1)}, bf16[96,768]{1,0:T(8,128)(2,1)S(1)}, u32[]{:S(2)}, u32[]{:S(2)}) collective-permute-start(bf16[96,768]{1,0:T(8,128)(2,1)S(1)} %get-tuple-element.117), channel_id=1, source_target_pairs={{0,16},{2,18},{4,20},{6,22},{8,24},{10,26},{12,28},{14,30},{16,0},... | collective-permute-start | bytes 442376 | tf_op jit(solution)/shard_map/ppermute | solution.py:59
  255.0 30.6 %collective-permute-start.71 = (f32[48,384]{1,0:T(8,128)S(1)}, f32[48,384]{1,0:T(8,128)S(1)}, u32[]{:S(2)}, u32[]{:S(2)}) collective-permute-start(f32[48,384]{1,0:T(8,128)S(1)} %pad_maximum_fusion.13), channel_id=1, source_target_pairs={{0,1},{1,0},{2,3},{3,2},{4,5},{5,4},{6,7},{7,6},{8,9},{9,8},{10,11... | collective-permute-start | bytes 221192 | tf_op jit(solution)/shard_map/ppermute | solution.py:145
  (77 other events, 399.1 us)

commit v2 on v1

--- a/solution.py
+++ b/solution.py
@@ -1,3 +1,4 @@
+import functools
 import math
 
 import jax
@@ -60,38 +61,36 @@
             x, "dp", [(i, (i + 4 * step) % self.count) for i in range(self.count)]
         )
 
-    def gather(self, mine, send, ring_after=(), last_after=None):
-        if not self.fast:
-            zero_all = lax.all_gather(pick(self.core, mine, send), "dp", axis=0, tiled=True)
-            one_all = lax.all_gather(pick(self.core, send, mine), "dp", axis=0, tiled=True)
-            self.near = self.far = mine
-            return pick(self.core, zero_all, one_all)
+    def join_cores(self, mine, send):
         rows, width = mine.shape
-        arrived = self.swap_core(send)
+        self.arrived = self.swap_core(send)
         block = jnp.zeros((2, rows, width), mine.dtype)
         block = lax.dynamic_update_slice(block, mine[None], (self.core, 0, 0))
-        block = lax.dynamic_update_slice(block, arrived[None], (1 - self.core, 0, 0))
-        block = block.reshape(2 * rows, width)
-        if ring_after:
-            block = after(block, *ring_after)
-        up = self.shift_depth(block, 1)
-        down = self.shift_depth(block, -1)
-        far = self.shift_depth(up, 1)
-        self.near = up
-        self.far = far
-        if last_after is not None:
-            far = after(far, last_after(self))
-        whole = jnp.zeros((self.count // 2, 2 * rows, width), mine.dtype)
-        for step, here in ((0, block), (1, up), (-1, down), (2, far)):
+        block = lax.dynamic_update_slice(block, self.arrived[None], (1 - self.core, 0, 0))
+        return block.reshape(2 * rows, width)
+
+    def spread_blocks(self, blocks, cuts):
+        rows = blocks[0][1].shape[0]
+        wholes = [
+            jnp.zeros((self.count // 2, rows, end - start), low)
+            for start, end in zip(cuts, cuts[1:])
+        ]
+        for step, here in blocks:
             place = ((self.depth - step) % 4) * 2
             across = self.swap_side(here)
-            whole = lax.dynamic_update_slice(whole, here[None], (place + self.side, 0, 0))
-            whole = lax.dynamic_update_slice(
-                whole, across[None], (place + 1 - self.side, 0, 0)
-            )
-        return whole.reshape(rows * self.count, width)
-
-    def scatter_side(self, keep, send=None):
+            for block, spot in ((here, place + self.side), (across, place + 1 - self.side)):
+                for i, (start, end) in enumerate(zip(cuts, cuts[1:])):
+                    wholes[i] = lax.dynamic_update_slice(
+                        wholes[i], block[None, :, start:end], (spot, 0, 0)
+                    )
+        return [whole.reshape(rows * self.count // 2, -1) for whole in wholes]
+
+    def gather_plain(self, mine, send):
+        zero_all = lax.all_gather(pick(self.core, mine, send), "dp", axis=0, tiled=True)
+        one_all = lax.all_gather(pick(self.core, send, mine), "dp", axis=0, tiled=True)
+        return pick(self.core, zero_all, one_all)
+
+    def scatter_side(self, keep, send=None, before=None):
         if not self.fast:
             return keep, send
         rows = keep.shape[0] // self.count
@@ -103,7 +102,10 @@
         pair = pair.reshape(4, 2, 2 * rows, width)
         stay = lax.dynamic_index_in_dim(pair, self.side, 1, False)
         leave = lax.dynamic_index_in_dim(pair, 1 - self.side, 1, False)
-        return (stay.astype(full) + self.swap_side(leave).astype(full)).astype(low)
+        arrived = self.swap_side(leave)
+        if before is not None:
+            arrived = after(arrived, before(self))
+        return (stay.astype(full) + arrived.astype(full)).astype(low)
 
     def scatter_depth(self, quad_sum):
         if not self.fast:
@@ -202,8 +204,8 @@
         outs[index][:, columns] = jnp.where(first, zero, one)
         outs[index + 1][:, columns] = jnp.where(first, one, zero)
 
-    put(0, slice(0, COLS), part(1), part(2))
-    put(0, slice(COLS, 2 * COLS), part(0), back_ref[...])
+    put(0, slice(0, COLS), part(1), part(0))
+    put(0, slice(COLS, 2 * COLS), part(2), back_ref[...])
     hidden = raise_ref.shape[1] // 2
     raised = (raise_ref[...].astype(full) * g2).astype(low)
     put(2, slice(0, hidden), raised[:, :hidden], raised[:, hidden:])
@@ -297,20 +299,17 @@
 
 
 def attend_body(
-    unit_ref, unit_end_ref, ends_ref, kq_ref, vo_ref, k_ref, v_ref, p_ref, q_ref, att_ref, out_ref
+    unit_ref, unit_end_ref, ends_ref, kv_ref, qo_ref, mixed_ref, p_ref, q_ref, att_ref, out_ref
 ):
     i = pl.program_id(0)
 
     @pl.when(i == 0)
     def _():
-        q_ref[...] = mm(unit_end_ref[...], kq_ref[:, COLS:]).astype(low)
-
-    unit = unit_ref[...]
-    keys = mm(unit, kq_ref[:, :COLS]).astype(low)
-    values = mm(unit, vo_ref[:, :COLS]).astype(low)
-    k_ref[...] = keys
-    v_ref[...] = values
-    scores = mm_nt(head_stack(q_ref[step_rows(i), :]), keys) * SCORE_SCALE
+        q_ref[...] = mm(unit_end_ref[...], qo_ref[:, :COLS]).astype(low)
+
+    mixed = mm(unit_ref[...], kv_ref[...]).astype(low)
+    mixed_ref[...] = mixed
+    scores = mm_nt(head_stack(q_ref[step_rows(i), :]), mixed[:, :COLS]) * SCORE_SCALE
     row, token = stack_grid()
     ends = jnp.concatenate([ends_ref[...]] * HEADS_HERE, 0)
     allowed = (token >= row * LENGTH) & (token <= row * LENGTH + ends)
@@ -318,21 +317,21 @@
     weight = jnp.exp(scores - jnp.max(scores, 1, keepdims=True))
     probs = weight / jnp.sum(weight, 1, keepdims=True)
     p_ref[...] = probs
-    att_ref[step_rows(i), :] = head_fold(mm(probs.astype(low), values)).astype(low)
+    att_ref[step_rows(i), :] = head_fold(mm(probs.astype(low), mixed[:, COLS:])).astype(low)
 
     @pl.when(i == pl.num_programs(0) - 1)
     def _():
-        out_ref[...] = mm_nt(att_ref[...], vo_ref[:, COLS:]).astype(low)
-
-
-def attend(unit, unit_end, ends, kq, vo):
+        out_ref[...] = mm_nt(att_ref[...], qo_ref[:, COLS:]).astype(low)
+
+
+def attend(unit, unit_end, ends, kv, qo):
     count = ends.shape[0]
     steps = count // BLOCK
     return pl.pallas_call(
         attend_body,
         grid=(steps,),
         out_shape=shapes(
-            *[((count * LENGTH, COLS), low)] * 2,
+            ((count * LENGTH, 2 * COLS), low),
             ((steps * STACK, TOKENS), full),
             *[((count, COLS), low)] * 2,
             ((count, WIDTH), low),
@@ -341,19 +340,18 @@
             pl.BlockSpec((TOKENS, WIDTH), lambda i: (i, 0)),
             whole_block((count, WIDTH)),
             pl.BlockSpec((BLOCK, 1), lambda i: (i, 0)),
-            whole_block(kq.shape),
-            whole_block(vo.shape),
+            whole_block(kv.shape),
+            whole_block(qo.shape),
         ],
         out_specs=[
-            pl.BlockSpec((TOKENS, COLS), lambda i: (i, 0)),
-            pl.BlockSpec((TOKENS, COLS), lambda i: (i, 0)),
+            pl.BlockSpec((TOKENS, 2 * COLS), lambda i: (i, 0)),
             pl.BlockSpec((STACK, TOKENS), lambda i: (i, 0)),
             whole_block((count, COLS)),
             whole_block((count, COLS)),
             whole_block((count, WIDTH)),
         ],
         name="attend",
-    )(unit, unit_end, ends, kq, vo)
+    )(unit, unit_end, ends, kv, qo)
 
 
 def lane_group():
@@ -361,28 +359,28 @@
 
 
 def attend_back_body(
-    core_ref, d_mid_ref, d_att_ref, unit_ref, unit_end_ref, k_ref, v_ref, p_ref, q_ref, att_ref,
-    keep_ref, send_ref, dk_ref, dv_ref, dq_ref, probs_ref, sum_ref,
+    core_ref, d_mid_ref, d_att_ref, unit_ref, unit_end_ref, mixed_ref, p_ref, q_ref, att_ref,
+    keep_ref, send_ref, d_mixed_ref, dq_ref, small_ref, sum_ref,
 ):
     i = pl.program_id(0)
+    count = dq_ref.shape[0]
 
     @pl.when(i == 0)
     def _():
         sum_ref[...] = jnp.zeros_like(sum_ref)
 
-    values = v_ref[...]
     probs = p_ref[...]
     probs_low = probs.astype(low)
     queries = head_stack(q_ref[step_rows(i), :])
     d_att = head_stack(d_att_ref[step_rows(i), :])
-    d_probs = mm_nt(d_att, values)
+    d_probs = mm_nt(d_att, mixed_ref[:, COLS:])
     d_scores = probs * (d_probs - jnp.sum(probs * d_probs, 1, keepdims=True))
     d_scores = (d_scores * SCORE_SCALE).astype(low)
-    dq_ref[step_rows(i), :] = head_fold(mm(d_scores, k_ref[...])).astype(low)
-    d_keys = mm_tn(d_scores, queries).astype(low)
-    d_values = mm_tn(probs_low, d_att).astype(low)
-    dk_ref[...] = d_keys
-    dv_ref[...] = d_values
+    dq_ref[step_rows(i), :] = head_fold(mm(d_scores, mixed_ref[:, :COLS])).astype(low)
+    d_mixed = jnp.concatenate(
+        [mm_tn(d_scores, queries).astype(low), mm_tn(probs_low, d_att).astype(low)], 1
+    )
+    d_mixed_ref[...] = d_mixed
     spot = lax.broadcasted_iota(jnp.int32, (TOKENS, 128), 0) & (LENGTH - 1)
     lane = lax.broadcasted_iota(jnp.int32, (TOKENS, 128), 1) & (2 * LENGTH - 1)
     squeezed = mm(probs_low, (spot == lane).astype(low))
@@ -391,24 +389,27 @@
         out = jnp.zeros((BLOCK, 128), full)
         for h in range(first, min(first + 4, HEADS_HERE)):
             out = jnp.where(lane_group() == h - first, squeezed[h * BLOCK : (h + 1) * BLOCK], out)
-        probs_ref[first * 4 : first * 4 + BLOCK] = out.astype(low)
-    sum_ref[...] += mm_tn(unit_ref[...], jnp.concatenate([d_keys, d_values], 1))
+        place = pl.multiple_of((2 * i + first // 4) * BLOCK, BLOCK)
+        small_ref[pl.ds(3 * count + place, BLOCK), :] = out.astype(low)
+    sum_ref[...] += mm_tn(unit_ref[...], d_mixed)
 
     @pl.when(i == pl.num_programs(0) - 1)
     def _():
         first = core_ref[0] == 0
         d_queries = dq_ref[...]
-        g_key = sum_ref[:, :COLS].astype(low)
-        g_value = sum_ref[:, COLS:].astype(low)
+        for piece in range(3):
+            small_ref[piece * count : (piece + 1) * count] = d_queries[
+                :, piece * 128 : (piece + 1) * 128
+            ]
+        g_mix = sum_ref[...].astype(low)
         g_query = mm_tn(unit_end_ref[...], d_queries).astype(low)
         g_back = mm_tn(d_mid_ref[...], att_ref[...]).astype(low)
-        keep_ref[:, :COLS] = jnp.where(first, g_key, g_value)
-        send_ref[:, :COLS] = jnp.where(first, g_value, g_key)
-        keep_ref[:, COLS:] = jnp.where(first, g_query, g_back)
-        send_ref[:, COLS:] = jnp.where(first, g_back, g_query)
-
-
-def attend_back(core, d_mid, d_att, unit, unit_end, keys, values, probs, queries, attended):
+        g_rest = jnp.concatenate([g_query, g_back], 1)
+        keep_ref[...] = jnp.where(first, g_mix, g_rest)
+        send_ref[...] = jnp.where(first, g_rest, g_mix)
+
+
+def attend_back(core, d_mid, d_att, unit, unit_end, mixed, probs, queries, attended):
     count = d_mid.shape[0]
     steps = count // BLOCK
     return pl.pallas_call(
@@ -416,9 +417,9 @@
         grid=(steps,),
         out_shape=shapes(
             *[((WIDTH, 2 * COLS), low)] * 2,
-            *[((count * LENGTH, COLS), low)] * 2,
+            ((count * LENGTH, 2 * COLS), low),
             ((count, COLS), low),
-            ((steps * 2 * BLOCK, 128), low),
+            ((3 * count + steps * 2 * BLOCK, 128), low),
         ),
         in_specs=[
             pl.BlockSpec(memory_space=pltpu.SMEM),
@@ -426,8 +427,7 @@
             whole_block((count, COLS)),
             pl.BlockSpec((TOKENS, WIDTH), lambda i: (i, 0)),
             whole_block((count, WIDTH)),
-            pl.BlockSpec((TOKENS, COLS), lambda i: (i, 0)),
-            pl.BlockSpec((TOKENS, COLS), lambda i: (i, 0)),
+            pl.BlockSpec((TOKENS, 2 * COLS), lambda i: (i, 0)),
             pl.BlockSpec((STACK, TOKENS), lambda i: (i, 0)),
             whole_block((count, COLS)),
             whole_block((count, COLS)),
@@ -435,14 +435,13 @@
         out_specs=[
             whole_block((WIDTH, 2 * COLS)),
             whole_block((WIDTH, 2 * COLS)),
-            pl.BlockSpec((TOKENS, COLS), lambda i: (i, 0)),
-            pl.BlockSpec((TOKENS, COLS), lambda i: (i, 0)),
+            pl.BlockSpec((TOKENS, 2 * COLS), lambda i: (i, 0)),
             whole_block((count, COLS)),
-            pl.BlockSpec((2 * BLOCK, 128), lambda i: (i, 0)),
+            whole_block((3 * count + steps * 2 * BLOCK, 128)),
         ],
         scratch_shapes=[pltpu.VMEM((WIDTH, 2 * COLS), full)],
         name="attend_back",
-    )(core, d_mid, d_att, unit, unit_end, keys, values, probs, queries, attended)
+    )(core, d_mid, d_att, unit, unit_end, mixed, probs, queries, attended)
 
 
 def place_rows(picks, rows):
@@ -452,25 +451,34 @@
 
 
 def captions_body(
-    group_ref, ends_ref, unit_ref, scale_ref, d_mid_ref, dk_ref, dv_ref, dq_ref,
-    q_far_ref, d_att_far_ref, dq_far_ref, probs_far_ref, kq_ref, vo_ref, kq_far_ref, vo_far_ref,
-    *refs,
+    part, group_ref, ends_ref, unit_ref, scale_ref, d_mid_ref, d_mixed_ref, dq_ref,
+    q_far_ref, d_att_far_ref, small_far_ref, kv_ref, qo_ref, kv_far_ref, qo_far_ref, *refs,
 ):
     out_ref, inner_end_ref = refs[-2:]
     i = pl.program_id(0)
+    half = dq_ref.shape[0]
+    far_start = (1 - part) * half
 
     @pl.when(i == 0)
     def _():
-        inner_end_ref[...] = mm_nt(dq_ref[...], kq_ref[:, COLS:]) + mm_nt(
-            dq_far_ref[...], kq_far_ref[:, COLS:]
+        dq_far = jnp.concatenate(
+            [
+                small_far_ref[piece * 2 * half + far_start : piece * 2 * half + far_start + half]
+                for piece in range(3)
+            ],
+            1,
+        )
+        inner_end_ref[...] = mm_nt(dq_ref[...], qo_ref[:, :COLS]) + mm_nt(
+            dq_far, qo_far_ref[:, :COLS]
         )
 
     row, token = stack_grid()
     own_caption = token // LENGTH == row
     lane = lax.broadcasted_iota(jnp.int32, (128, TOKENS), 0) & (2 * LENGTH - 1)
     spot = lax.broadcasted_iota(jnp.int32, (128, TOKENS), 1) & (LENGTH - 1)
-    packed = probs_far_ref[...]
     zero = jnp.zeros((BLOCK, 128), low)
+    place = pl.multiple_of(6 * half + 2 * far_start + 2 * BLOCK * i, 2 * BLOCK)
+    packed = small_far_ref[pl.ds(place, 2 * BLOCK), :]
     pair = jnp.concatenate(
         [
             jnp.where(lane_group() == h % 4, packed[h // 4 * BLOCK : (h // 4 + 1) * BLOCK], zero)
@@ -482,10 +490,14 @@
     d_scores = jnp.where(
         own_caption, mm(pair, (spot + LENGTH == lane).astype(low)), 0.0
     ).astype(low)
-    d_keys = mm_tn(d_scores, head_stack(q_far_ref[step_rows(i), :])).astype(low)
-    d_values = mm_tn(probs, head_stack(d_att_far_ref[step_rows(i), :])).astype(low)
-    inner = mm_nt(dk_ref[...], kq_ref[:, :COLS]) + mm_nt(dv_ref[...], vo_ref[:, :COLS])
-    inner += mm_nt(d_keys, kq_far_ref[:, :COLS]) + mm_nt(d_values, vo_far_ref[:, :COLS])
+    d_mixed = jnp.concatenate(
+        [
+            mm_tn(d_scores, head_stack(q_far_ref[step_rows(i), :])).astype(low),
+            mm_tn(probs, head_stack(d_att_far_ref[step_rows(i), :])).astype(low),
+        ],
+        1,
+    )
+    inner = mm_nt(d_mixed_ref[...], kv_ref[...]) + mm_nt(d_mixed, kv_far_ref[...])
     picks = end_picks(ends_ref[...], 2).astype(low)
     inner += place_rows(picks, inner_end_ref[step_rows(i), :])
     unit = unit_ref[...].astype(full)
@@ -497,40 +509,37 @@
 
 
 def captions_back(
-    part, group, ends, unit, scale, d_mid, d_keys, d_values, dq, q_far, d_att_far, dq_far,
-    probs_far, kq, vo, kq_far, vo_far, done=None,
+    part, group, ends, unit, scale, d_mid, d_mixed, dq, q_far, d_att_far, small_far, kv, qo,
+    kv_far, qo_far, done=None,
 ):
     count = ends.shape[0]
     steps = count // BLOCK
     half = steps // 2
     start = part * half
-    far = (1 - part) * half
     own_half = pl.BlockSpec((count // 2, COLS), lambda i, g: (part, 0))
     far_half = pl.BlockSpec((count // 2, COLS), lambda i, g: (1 - part, 0))
     operands = [
-        group, ends, unit, scale, d_mid, d_keys, d_values, dq, q_far, d_att_far, dq_far,
-        probs_far, kq, vo, kq_far, vo_far,
+        group, ends, unit, scale, d_mid, d_mixed, dq, q_far, d_att_far, small_far, kv, qo,
+        kv_far, qo_far,
     ]
     in_specs = [
         pl.BlockSpec((BLOCK, 1), lambda i, g: (i + start, 0)),
         pl.BlockSpec((TOKENS, WIDTH), lambda i, g: (i + start, 0)),
         pl.BlockSpec((TOKENS, 128), lambda i, g: (i + start, 0)),
         pl.BlockSpec((BLOCK, WIDTH), lambda i, g: (i + start, 0)),
-        pl.BlockSpec((TOKENS, COLS), lambda i, g: (i + start, 0)),
-        pl.BlockSpec((TOKENS, COLS), lambda i, g: (i + start, 0)),
+        pl.BlockSpec((TOKENS, 2 * COLS), lambda i, g: (i + start, 0)),
         own_half,
         far_half,
         far_half,
-        far_half,
-        pl.BlockSpec((2 * BLOCK, 128), lambda i, g: (i + far, 0)),
-    ] + [whole_block(kq.shape)] * 4
+        whole_block(small_far.shape),
+    ] + [whole_block(kv.shape)] * 4
     aliases = {}
     if done is not None:
         aliases = {len(operands): 0}
         operands.append(done)
         in_specs.append(pl.BlockSpec(memory_space=pl.ANY))
     return pl.pallas_call(
-        captions_body,
+        functools.partial(captions_body, part),
         out_shape=jax.ShapeDtypeStruct(unit.shape, full),
         grid_spec=pltpu.PrefetchScalarGridSpec(
             num_scalar_prefetch=1,
@@ -584,47 +593,67 @@
         ln1_gain[None],
         ln2_gain[None],
     )
-    mix_own = plane.gather(packed[0], packed[1])
-    mix_near, mix_last = plane.near, plane.far
-    mix_other = plane.swap_core(mix_own)
-    kq = pick(core, mix_own, mix_other)
-    vo = pick(core, mix_other, mix_own)
-    far_own = swap_group(mix_own)
-    far_other = plane.swap_core(far_own)
-    kq_far = pick(core, far_own, far_other)
-    vo_far = pick(core, far_other, far_own)
-
     flipped = jnp.concatenate([end_pos, end_pos], 0)
     ends = lax.dynamic_slice_in_dim(flipped, group * CAP_DEV, rows_dev, 0)[:, None]
-    unit, scale, unit_end, stream_end = norm_first(
-        group_flag, after(captions, mix_near).reshape(rows_dev * length, width), ends
-    )
-    keys, values, probs, queries, attended, attention = attend(unit, unit_end, ends, kq, vo)
-    feeds = plane.gather(packed[2], packed[3], (mix_last,), lambda _: attention)
+    wide = width // 2
+
+    def pictures_of_batch(outgoing):
+        incoming = lax.all_to_all(outgoing, "dp", split_axis=0, concat_axis=0, tiled=True)
+        own_arrive = lax.dynamic_slice_in_dim(arrive_order[0], group * CAP_DEV, CAP_DEV, 0)
+        take_in = (own_arrive[:, None] == places[None, :]).astype(low)
+        pictures = mm(take_in, incoming.reshape(rows_dev, width)).astype(low)
+        mine = pick(core, pictures[:, :wide], pictures[:, wide:])
+        send = pick(core, pictures[:, wide:], pictures[:, :wide])
+        return mine, send
 
     cached = image_cache.astype(full)
     cached = (cached * lax.rsqrt(jnp.sum(cached * cached, -1, keepdims=True) + 1e-06)).astype(low)
     places = jnp.arange(rows_dev, dtype=jnp.int32)
     hand_out = (send_order[0][:, None] == places[None, :]).astype(low)
     outgoing = mm(hand_out, cached).astype(low).reshape(spread, per_peer, width)
-    outgoing = after(outgoing, mix_near)
-    incoming = lax.all_to_all(outgoing, "dp", split_axis=0, concat_axis=0, tiled=True)
-    own_arrive = lax.dynamic_slice_in_dim(arrive_order[0], group * CAP_DEV, CAP_DEV, 0)
-    take_in = (own_arrive[:, None] == places[None, :]).astype(low)
-    pictures = mm(take_in, incoming.reshape(rows_dev, width)).astype(low)
-    wide = width // 2
-    picture_mine = pick(core, pictures[:, :wide], pictures[:, wide:])
-    picture_send = pick(core, pictures[:, wide:], pictures[:, :wide])
+
+    def first_parts(stream):
+        return norm_first(group_flag, stream.reshape(rows_dev * length, width), ends)
+
+    def attention_of(kv, qo, parts):
+        return attend(parts[0], parts[2], ends, kv, qo)
+
     main = rows if plane.fast else CAP_DEV
     spare = CAP_DEV - main
     if plane.fast:
 
-        def join(embed, half):
+        def join(feed, embed, half):
             parts = [half[main:, i * 128 : (i + 1) * 128] for i in range(wide // 128)]
-            return jnp.concatenate([embed, half[:main], jnp.concatenate(parts, 0)], 1)
-
-        third = plane.gather(
-            join(packed[4], picture_mine), join(packed[5], picture_send), (plane.far, attention)
+            return jnp.concatenate([feed, embed, half[:main], jnp.concatenate(parts, 0)], 1)
+
+        block = plane.join_cores(packed[0], packed[1])
+        pictures = pictures_of_batch(after(outgoing, plane.arrived))
+        up = plane.shift_depth(block, 1)
+        down = plane.shift_depth(block, -1)
+        up = after(up, pictures[0])
+        far = plane.shift_depth(up, 1)
+        parts = first_parts(after(captions, up))
+        far = after(far, parts[0])
+        (mix_own,) = plane.spread_blocks(
+            ((0, block), (1, up), (-1, down), (2, far)), (0, 2 * COLS)
+        )
+        mix_other = plane.swap_core(mix_own)
+        far_own = swap_group(mix_own)
+
+        block = plane.join_cores(
+            join(packed[2], packed[4], pictures[0]), join(packed[3], packed[5], pictures[1])
+        )
+        block = after(block, far)
+        one = plane.shift_depth(block, 1)
+        two = plane.shift_depth(one, 1)
+        kv = pick(core, mix_own, mix_other)
+        qo = pick(core, mix_other, mix_own)
+        attending = attention_of(kv, after(qo, one), parts)
+        two = after(two, attending[-1])
+        three = plane.shift_depth(two, 1)
+        cut = 2 * hidden
+        feeds, third = plane.spread_blocks(
+            ((0, block), (1, one), (2, two), (3, three)), (0, cut, cut + 2 * wide + 128)
         )
         third_other = plane.swap_core(third)
 
@@ -636,10 +665,24 @@
         image_halves = images(third), images(third_other)
         embed_halves = third[:, :wide], third_other[:, :wide]
     else:
-        image_half = plane.gather(picture_mine, picture_send)
+        pictures = pictures_of_batch(outgoing)
+        parts = first_parts(captions)
+        mix_own = plane.gather_plain(packed[0], packed[1])
+        mix_other = plane.swap_core(mix_own)
+        far_own = swap_group(mix_own)
+        kv = pick(core, mix_own, mix_other)
+        qo = pick(core, mix_other, mix_own)
+        attending = attention_of(kv, qo, parts)
+        feeds = plane.gather_plain(packed[2], packed[3])
+        image_half = plane.gather_plain(*pictures)
         image_halves = image_half, plane.swap_core(image_half)
-        embed_half = plane.gather(packed[4], packed[5])
+        embed_half = plane.gather_plain(packed[4], packed[5])
         embed_halves = embed_half, plane.swap_core(embed_half)
+    unit, scale, unit_end, stream_end = parts
+    mixed, probs, queries, attended, attention = attending
+    far_other = plane.swap_core(far_own)
+    kv_far = pick(core, far_own, far_other)
+    qo_far = pick(core, far_other, far_own)
 
     def sides(pair):
         return jnp.concatenate([pick(core, *pair), pick(core, pair[1], pair[0])], 1)
@@ -657,7 +700,6 @@
     unit_second, scale_second = norm_rows(middle)
     second_low = unit_second.astype(low)
     feeds = after(feeds, far_own)
-    queries_far = swap_group(queries)
     w_raise = feeds[:, :hidden]
     w_lower = feeds[:, hidden:]
     active, slope = gelu_parts(mm(second_low, w_raise))
@@ -726,6 +768,7 @@
     g_embed = mm_tn(pooled_all, d_embed_here).astype(low)
     lower_quad = plane.scatter_side(jnp.concatenate([g_lower, g_embed], 1))
     raise_quad = plane.scatter_side(g_raise)
+    queries_far = swap_group(queries)
     inner = d_second[:rows_dev].astype(full)
     inner = inner + roll_rows(swap_near(d_second[:rows_dev], 1)).astype(full)
     inner = inner + swap_near(d_second[rows_dev:], 2).astype(full)
@@ -735,24 +778,31 @@
     )
 
     d_middle_low = d_middle.astype(low)
-    d_attended = mm(d_middle_low, vo[:, COLS:]).astype(low)
+    d_attended = mm(d_middle_low, qo[:, COLS:]).astype(low)
     d_attended_far = swap_group(d_attended)
-    g_keep, g_send, d_keys, d_values, d_queries, small_probs = attend_back(
-        core_flag, d_middle_low, d_attended, unit, unit_end, keys, values, probs, queries, attended
-    )
-    d_queries_far = swap_group(d_queries)
-    probs_far = swap_group(small_probs)
-    mix_quad = plane.scatter_side(g_keep, g_send)
+    back_start = after(d_middle_low, lower_quad) if plane.fast else d_middle_low
+    g_keep, g_send, d_mixed, d_queries, small = attend_back(
+        core_flag, back_start, d_attended, unit, unit_end, mixed, probs, queries, attended
+    )
+    small_far = swap_group(small)
+    operands = (
+        unit, scale, d_middle, d_mixed, d_queries, queries_far, d_attended_far, small_far, kv, qo,
+        kv_far, qo_far,
+    )
+    halves = []
+
+    def first_half(plane):
+        first_ends = after(ends, raise_quad, plane.pair)
+        halves.append(captions_back(0, group_flag, first_ends, *operands))
+        return halves[0]
+
+    mix_quad = plane.scatter_side(g_keep, g_send, first_half)
+    if not plane.fast:
+        halves.append(captions_back(0, group_flag, ends, *operands))
     lower_sum = plane.scatter_core(plane.scatter_depth(lower_quad))
     raise_sum = plane.scatter_core(plane.scatter_depth(raise_quad))
-    operands = (
-        unit, scale, d_middle, d_keys, d_values, d_queries, queries_far, d_attended_far,
-        d_queries_far, probs_far, kq, vo, kq_far, vo_far,
-    )
-    first_ends = after(ends, lower_quad, plane.pair) if plane.fast else ends
-    first_half = captions_back(0, group_flag, first_ends, *operands)
     second_ends = after(ends, mix_quad) if plane.fast else ends
-    grad_captions = captions_back(1, group_flag, second_ends, *operands, done=first_half)
+    grad_captions = captions_back(1, group_flag, second_ends, *operands, done=halves[0])
     mix_total = plane.scatter_depth(mix_quad)
     if plane.fast:
         mix_total, grad_captions = lax.optimization_barrier((mix_total, grad_captions))
@@ -768,7 +818,7 @@
         jnp.concatenate([proj_far, proj_own], 1),
     )
     grad_out = mix_sum[1][:, COLS:]
-    unit_mix = jnp.stack([mix_sum[0][:, COLS:], mix_sum[0][:, :COLS], mix_sum[1][:, :COLS]], 1)
+    unit_mix = jnp.stack([mix_sum[1][:, :COLS], mix_sum[0][:, :COLS], mix_sum[0][:, COLS:]], 1)
     grad_qkv = unit_mix * ln1_gain[:, None, None]
     raised_sum = jnp.concatenate(raise_sum, 1)
     grad_up = raised_sum * ln2_gain[:, None]

time: 291 us -> 292 us (level)
  waiting for transfers between devices: 87.7 us -> 110 us
  starting transfers between devices: 75.5 us -> 61.3 us
  local copies, waits for them, and re-layouts: 25.7 us -> 20.7 us
  other arithmetic: 26.3 us -> 23 us
    ppermute x16 -> x12, waiting for transfers between devices: 32.2 us -> 46.5 us  [swap_side(): return lax.ppermute(x, 'dp', [(i, i ^ 2) for i in range(self.count)])]
    ppermute x21 -> x18, starting transfers between devices: 30.9 us -> 23.9 us  [shift_depth(): lax.ppermute(x, 'dp', [(i, (i + 4 * step) % self.count) for i in range(se...]
    ppermute x16 -> x12, starting transfers between devices: 18.9 us -> 13.2 us  [swap_side(): return lax.ppermute(x, 'dp', [(i, i ^ 2) for i in range(self.count)])]
    ppermute x21 -> x18, waiting for transfers between devices: 36 us -> 41.3 us  [shift_depth(): lax.ppermute(x, 'dp', [(i, (i + 4 * step) % self.count) for i in range(se...]
    all_to_all x1, waiting for transfers between devices: 0.01 us -> 4.37 us  [pictures_of_batch(): lax.all_to_all(outgoing, 'dp', split_axis=0, concat_axis=0, tiled=True)]
    dynamic_update_slice x28 -> x27, local copies, waits for them, and re-layouts: 8.7 us -> 4.96 us  [the longest x24 4.03 us: spread_blocks(): lax.dynamic_update_slice(wholes[i], block[None, :, start:end], (spot, 0, 0))]
    unnamed x105 -> x79, local copies, waits for them, and re-layouts: 2.58 us -> 5.52 us
    ppermute x24 -> x23, starting transfers between devices: 19.9 us -> 17.7 us  [swap_near(): return lax.ppermute(x, ('dp', 'mp'), [(i, i ^ flip) for i in range(size)])]
  transfers between devices with their start and end apart: 74 -> 65, of which waited for: 33 -> 28; matrix products, arithmetic and copies ran while one was open for 21% -> 18% of each run, Pallas kernels for 19% -> 18%
where the time goes in v2:
time: 292 us; the launch traced here: 291 us
  waiting for transfers between devices  110 us (38%)
  starting transfers between devices  61.3 us (21%)
  Pallas kernels  55.1 us (19%)
  other arithmetic  23 us (8%)
  local copies, waits for them, and re-layouts  20.7 us (7%)
  matrix products  13.1 us (4%)
  between operations  7.16 us (2%)
    ppermute x12, waiting for transfers between devices, swap_side(): return lax.ppermute(x, 'dp', [(i, i ^ 2) for i in range(self.count)])  46.5 us
    ppermute x18, waiting for transfers between devices, shift_depth(): lax.ppermute(x, 'dp', [(i, (i + 4 * step) % self.count) for i in range(se...  41.3 us
    ppermute x18, starting transfers between devices, shift_depth(): lax.ppermute(x, 'dp', [(i, (i + 4 * step) % self.count) for i in range(se...  23.9 us
    pallas_call x2, Pallas kernels, captions_back(): pl.pallas_call(functools.partial(captions_body, part), out_shape=jax.Shap...  21.3 us
    ppermute x23, starting transfers between devices, swap_near(): return lax.ppermute(x, ('dp', 'mp'), [(i, i ^ flip) for i in range(size)])  17.7 us
    ppermute x23, waiting for transfers between devices, swap_near(): return lax.ppermute(x, ('dp', 'mp'), [(i, i ^ flip) for i in range(size)])  17.4 us
    ppermute x12, starting transfers between devices, swap_side(): return lax.ppermute(x, 'dp', [(i, i ^ 2) for i in range(self.count)])  13.2 us
    pallas_call x1, Pallas kernels, attend_back(): pl.pallas_call(attend_back_body, grid=(steps,), out_shape=shapes(*[((WIDT...  13.1 us
  transfers between devices with their start and end apart: 65, of which 28 were waited for; matrix products, arithmetic and copies ran while one was open for 18% of the time, Pallas kernels for 18%

profile of v2, /device:TPU:0, one launch (start us, length us, event | category | flops | bytes accessed | tf_op | source)
XLA Modules:
  0.0 290.6 jit_solution(9575188255347707642)
XLA Ops:
  0.7 2.0 pack.1
  7.9 1.9 fusion.4
  10.8 4.6 %collective-permute-start.5 = (bf16[96,768]{1,0:T(8,128)(2,1)S(1)}, bf16[96,768]{1,0:T(8,128)(2,1)S(1)}, u32[]{:S(2)}, u32[]{:S(2)}) collective-permute-start(bf16[96,768]{1,0:T(8,128)(2,1)S(1)} %bitcast.255), channel_id=1, source_target_pairs={{0,24},{2,26},{4,28},{6,30},{8,0},{10,2},{12,4},{14,6},{16,8},{18,... | collective-permute-start | bytes 442376 | tf_op jit(solution)/shard_map/ppermute | solution.py:60
  15.5 1.5 collective-permute-start.3
  17.0 3.5 %all-to-all-start = ((bf16[16,8,768]{2,1,0:T(8,128)(2,1)}), bf16[16,8,768]{2,1,0:T(8,128)(2,1)S(1)}, u32[]{:S(2)}, u32[]{:S(2)}) async-start(bf16[16,8,768]{2,1,0:T(8,128)(2,1)} %fusion.4), calls=%async_computation | async-start | bytes 393216 | tf_op jit(solution)/shard_map/all_to_all | solution.py:601
  22.1 1.8 collective-permute-start.1
  24.1 1.5 collective-permute-start.6
  25.6 4.4 %all-to-all-done = bf16[16,8,768]{2,1,0:T(8,128)(2,1)S(1)} async-done(((bf16[16,8,768]{2,1,0:T(8,128)(2,1)}), bf16[16,8,768]{2,1,0:T(8,128)(2,1)S(1)}, u32[]{:S(2)}, u32[]{:S(2)}) %all-to-all-start) | async-done | bytes 196640 | tf_op jit(solution)/shard_map/all_to_all | solution.py:601
  33.6 7.4 %norm_first.1 = (bf16[2048,768]{1,0:T(8,128)(2,1)}, f32[2048,128]{1,0:T(8,128)}, bf16[128,768]{1,0:T(8,128)(2,1)}, bf16[128,768]{1,0:T(8,128)(2,1)}) custom-call(s32[1]{0:T(128)} %bitcast.1.group_ref, bf16[2048,768]{1,0:T(8,128)(2,1)} %bitcast.238, s32[128,1]{1,0:T(8,128)} %copy.41.ends_ref), custom_call_target="tpu_custom_call" | custom-call | tf_op jit(solution)/shard_map/norm_first/pallas_call | solution.py:252
  43.0 1.5 collective-permute-start.15
  46.2 2.2 collective-permute-done.8
  48.4 1.6 collective-permute-start.21
  50.0 8.8 %collective-permute-done.11 = bf16[96,2432]{1,0:T(8,128)(2,1)S(1)} collective-permute-done((bf16[96,2432]{1,0:T(8,128)(2,1)S(1)}, bf16[96,2432]{1,0:T(8,128)(2,1)S(1)}, u32[]{:S(2)}, u32[]{:S(2)}) %collective-permute-start.11) | collective-permute-done | bytes 466976 | tf_op jit(solution)/shard_map/ppermute | solution.py:60
  59.4 10.8 %collective-permute-done.16 = bf16[96,2432]{1,0:T(8,128)(2,1)S(1)} collective-permute-done((bf16[96,2432]{1,0:T(8,128)(2,1)S(1)}, bf16[96,2432]{1,0:T(8,128)(2,1)S(1)}, u32[]{:S(2)}, u32[]{:S(2)}) %collective-permute-start.16) | collective-permute-done | bytes 466976 | tf_op jit(solution)/shard_map/ppermute | solution.py:57
  71.7 1.7 broadcast_select_fusion.2
  73.4 11.3 %attend.1 = (bf16[2048,768]{1,0:T(8,128)(2,1)}, f32[768,256]{1,0:T(8,128)}, bf16[128,384]{1,0:T(8,128)(2,1)}, bf16[128,384]{1,0:T(8,128)(2,1)}, bf16[128,768]{1,0:T(8,128)(2,1)}) custom-call(bf16[2048,768]{1,0:T(8,128)(2,1)} %get-tuple-element.49.unit_ref, bf16[128,768]{1,0:T(8,128)(2,1)} %get-tuple-element.50.unit_end_ref, s32[128,1]{1,0:T(8,128)} %copy.41.ends_ref, ...), custom_call_target="tpu_custom_call" | custom-call | tf_op jit(solution)/shard_map/attend/pallas_call | solution.py:330
  84.9 1.6 collective-permute-start.13
  86.7 1.7 bitcast_dynamic-update-slice_fusion
  89.4 2.8 collective-permute-done.14
  92.5 4.0 %collective-permute-done.13 = bf16[128,768]{1,0:T(8,128)(2,1)S(1)} collective-permute-done((bf16[128,768]{1,0:T(8,128)(2,1)}, bf16[128,768]{1,0:T(8,128)(2,1)S(1)}, u32[]{:S(2)}, u32[]{:S(2)}) %collective-permute-start.13) | collective-permute-done | bytes 196640 | tf_op jit(solution)/shard_map/ppermute | solution.py:147
  97.7 9.2 %collective-permute-done.19 = bf16[96,2432]{1,0:T(8,128)(2,1)S(1)} collective-permute-done((bf16[96,2432]{1,0:T(8,128)(2,1)}, bf16[96,2432]{1,0:T(8,128)(2,1)S(1)}, u32[]{:S(2)}, u32[]{:S(2)}) %collective-permute-start.19) | collective-permute-done | bytes 466976 | tf_op jit(solution)/shard_map/ppermute | solution.py:60
  107.5 2.4 collective-permute-done.18
  110.0 9.3 %collective-permute-done.20 = bf16[96,2432]{1,0:T(8,128)(2,1)S(1)} collective-permute-done((bf16[96,2432]{1,0:T(8,128)(2,1)S(1)}, bf16[96,2432]{1,0:T(8,128)(2,1)S(1)}, u32[]{:S(2)}, u32[]{:S(2)}) %collective-permute-start.20) | collective-permute-done | bytes 466976 | tf_op jit(solution)/shard_map/ppermute | solution.py:57
  123.2 3.1 %collective-permute-done.22 = bf16[64,768]{1,0:T(8,128)(2,1)S(1)} collective-permute-done((bf16[64,768]{1,0:T(8,128)(2,1)S(1)}, bf16[64,768]{1,0:T(8,128)(2,1)S(1)}, u32[]{:S(2)}, u32[]{:S(2)}) %collective-permute-start.22) | collective-permute-done | bytes 98336 | tf_op jit(solution)/shard_map/ppermute | solution.py:147
  131.3 1.9 fusion.55
  137.4 1.6 collective-permute-done.27
  139.0 3.6 %collective-permute-start.31 = (f32[9,128]{1,0:T(8,128)S(1)}, f32[9,128]{1,0:T(8,128)S(1)}, u32[]{:S(2)}, u32[]{:S(2)}) collective-permute-start(f32[9,128]{1,0:T(8,128)S(1)} %add_add_fusion.2), channel_id=1, source_target_pairs={{0,24},{2,26},{4,28},{6,30},{8,0},{10,2},{12,4},{14,6},{16,8},{18,... | collective-permute-start | bytes 13832 | tf_op jit(solution)/shard_map/ppermute | solution.py:60
  144.1 3.0 %collective-permute-done.30 = f32[9,128]{1,0:T(8,128)S(1)} collective-permute-done((f32[9,128]{1,0:T(8,128)S(1)}, f32[9,128]{1,0:T(8,128)S(1)}, u32[]{:S(2)}, u32[]{:S(2)}) %collective-permute-start.30) | collective-permute-done | bytes 4640 | tf_op jit(solution)/shard_map/ppermute | solution.py:60
  148.0 1.8 multiply_reduce_fusion.4
  150.5 1.7 collective-permute-start.33
  152.1 3.2 %broadcast_select_fusion = (bf16[768,768]{1,0:T(8,128)(2,1)}, bf16[768,768]{1,0:T(8,128)(2,1)}) fusion(bf16[768,768]{1,0:T(8,128)(2,1)} %collective-permute-done.49, bf16[768,768]{1,0:T(8,128)(2,1)} %collective-permute-done.21, pred[]{:T(512)S(6)} %eq.99), kind=kLoop, calls=%fused_computation.18 | loop fusion | flops 1179648 | bytes 4718593 | tf_op jit(solution)/shard_map/jit(_where)/select_n | solution.py:41
  165.8 1.7 copy.45
  169.1 3.7 %collective-permute-done.36 = bf16[128,768]{1,0:T(8,128)(2,1)} collective-permute-done((bf16[128,768]{1,0:T(8,128)(2,1)}, bf16[128,768]{1,0:T(8,128)(2,1)}, u32[]{:S(2)}, u32[]{:S(2)}) %collective-permute-start.36) | collective-permute-done | bytes 196640 | tf_op jit(solution)/shard_map/ppermute | solution.py:147
  179.2 4.7 %collective-permute-done.45 = bf16[4,96,768]{2,1,0:T(8,128)(2,1)S(1)} collective-permute-done((bf16[4,96,768]{2,1,0:T(8,128)(2,1)S(1)}, bf16[4,96,768]{2,1,0:T(8,128)(2,1)S(1)}, u32[]{:S(2)}, u32[]{:S(2)}) %collective-permute-start.45) | collective-permute-done | bytes 589856 | tf_op jit(solution)/shard_map/ppermute | solution.py:57
  184.0 15.5 %collective-permute-done.42 = bf16[4,96,960]{2,1,0:T(8,128)(2,1)S(1)} collective-permute-done((bf16[4,96,960]{2,1,0:T(8,128)(2,1)S(1)}, bf16[4,96,960]{2,1,0:T(8,128)(2,1)S(1)}, u32[]{:S(2)}, u32[]{:S(2)}) %collective-permute-start.42) | collective-permute-done | bytes 737312 | tf_op jit(solution)/shard_map/ppermute | solution.py:57
  199.9 13.1 %attend_back.1 = (bf16[768,768]{1,0:T(8,128)(2,1)}, bf16[768,768]{1,0:T(8,128)(2,1)}, bf16[2048,768]{1,0:T(8,128)(2,1)}, bf16[128,384]{1,0:T(8,128)(2,1)}, bf16[640,128]{1,0:T(8,128)(2,1)}) custom-call(s32[1]{0:T(128)} %bitcast.2.core_ref, bf16[128,768]{1,0:T(8,128)(2,1)} %copy-done.13, bf16[128,384]{1,0:T(8,128)(2,1)} %convolution_convert_fusion.6.d_att_ref, ...), custom_call_target="tpu_custom_call" | custom-call | tf_op jit(solution)/shard_map/attend_back/pallas_call | solution.py:415
  214.0 3.0 %collective-permute-start.56 = (bf16[96,768]{1,0:T(8,128)(2,1)S(1)}, bf16[96,768]{1,0:T(8,128)(2,1)S(1)}, u32[]{:S(2)}, u32[]{:S(2)}) collective-permute-start(bf16[96,768]{1,0:T(8,128)(2,1)S(1)} %get-tuple-element.105), channel_id=1, source_target_pairs={{0,24},{2,26},{4,28},{6,30},{8,0},{10,2},{12,4},{14,6},{16,8},{18,... | collective-permute-start | bytes 442376 | tf_op jit(solution)/shard_map/ppermute | solution.py:60
  219.6 2.2 collective-permute-done.54
  223.6 6.2 %collective-permute-done.55 = bf16[96,768]{1,0:T(8,128)(2,1)S(1)} collective-permute-done((bf16[96,768]{1,0:T(8,128)(2,1)S(1)}, bf16[96,768]{1,0:T(8,128)(2,1)S(1)}, u32[]{:S(2)}, u32[]{:S(2)}) %collective-permute-start.55) | collective-permute-done | bytes 147488 | tf_op jit(solution)/shard_map/ppermute | solution.py:60
  232.0 3.8 %collective-permute-start.60 = (bf16[96,960]{1,0:T(8,128)(2,1)S(1)}, bf16[96,960]{1,0:T(8,128)(2,1)S(1)}, u32[]{:S(2)}, u32[]{:S(2)}) collective-permute-start(bf16[96,960]{1,0:T(8,128)(2,1)S(1)} %get-tuple-element.100), channel_id=1, source_target_pairs={{0,24},{2,26},{4,28},{6,30},{8,0},{10,2},{12,4},{14,6},{16,8},{18,... | collective-permute-start | bytes 552968 | tf_op jit(solution)/shard_map/ppermute | solution.py:60
  235.9 1.6 add_convert_fusion
  239.9 1.6 collective-permute-done.58
  243.0 2.5 collective-permute-done.60
  246.9 4.7 %collective-permute-done.59 = bf16[96,960]{1,0:T(8,128)(2,1)S(1)} collective-permute-done((bf16[96,960]{1,0:T(8,128)(2,1)S(1)}, bf16[96,960]{1,0:T(8,128)(2,1)S(1)}, u32[]{:S(2)}, u32[]{:S(2)}) %collective-permute-start.59) | collective-permute-done | bytes 184352 | tf_op jit(solution)/shard_map/ppermute | solution.py:60
  253.3 10.6 %captions_back.2.refs_0_ = f32[2048,768]{1,0:T(8,128)} custom-call(s32[1]{0:T(128)} %bitcast.1.group_ref, s32[128,1]{1,0:T(8,128)} %copy.46.ends_ref, bf16[2048,768]{1,0:T(8,128)(2,1)} %get-tuple-element.49.unit_ref, f32[2048,128]{1,0:T(8,128)} %get-tuple-element.69.scale_ref, f32[128,768]{1,0:T(8,128)} %get-tuple-element.83.d_mid_ref, ...), custom_call_target="tpu_custom_call" | custom-call | tf_op jit(solution)/shard_map/captions_back/pallas_call | solution.py:541
  265.3 3.8 %collective-permute-start.52 = (bf16[96,768]{1,0:T(8,128)(2,1)S(1)}, bf16[96,768]{1,0:T(8,128)(2,1)S(1)}, u32[]{:S(2)}, u32[]{:S(2)}) collective-permute-start(bf16[96,768]{1,0:T(8,128)(2,1)S(1)} %get-tuple-element.108), channel_id=1, source_target_pairs={{0,24},{2,26},{4,28},{6,30},{8,0},{10,2},{12,4},{14,6},{16,8},{18,... | collective-permute-start | bytes 442376 | tf_op jit(solution)/shard_map/ppermute | solution.py:60
  271.5 10.6 %captions_back.3 = f32[2048,768]{1,0:T(8,128)} custom-call(s32[1]{0:T(128)} %bitcast.1.group_ref, s32[128,1]{1,0:T(8,128)} %copy.47.ends_ref, bf16[2048,768]{1,0:T(8,128)(2,1)} %get-tuple-element.49.unit_ref, f32[2048,128]{1,0:T(8,128)} %get-tuple-element.69.scale_ref, f32[128,768]{1,0:T(8,128)} %get-tuple-element.83.d_mid_ref, ...), custom_call_target="tpu_custom_call", output_to_operand_aliasing={{}: (14, {})} | custom-call | tf_op jit(solution)/shard_map/captions_back/pallas_call | solution.py:541
  286.8 2.2 collective-permute-done.63
  (315 shorter events, 74.4 us)
Async XLA Ops:
  2.7 8.2 %collective-permute-start = (bf16[48,768]{1,0:T(8,128)(2,1)}, bf16[48,768]{1,0:T(8,128)(2,1)S(1)}, u32[]{:S(2)}, u32[]{:S(2)}) collective-permute-start(bf16[48,768]{1,0:T(8,128)(2,1)} %get-tuple-element.44), channel_id=1, source_target_pairs={{0,2},{2,0},{4,6},{6,4},{8,10},{10,8},{12,14},{14,12},{16,18},{18,... | collective-permute-start | bytes 221192 | tf_op jit(solution)/shard_map/ppermute | solution.py:54
  10.8 13.2 %collective-permute-start.5 = (bf16[96,768]{1,0:T(8,128)(2,1)S(1)}, bf16[96,768]{1,0:T(8,128)(2,1)S(1)}, u32[]{:S(2)}, u32[]{:S(2)}) collective-permute-start(bf16[96,768]{1,0:T(8,128)(2,1)S(1)} %bitcast.255), channel_id=1, source_target_pairs={{0,24},{2,26},{4,28},{6,30},{8,0},{10,2},{12,4},{14,6},{16,8},{18,... | collective-permute-start | bytes 442376 | tf_op jit(solution)/shard_map/ppermute | solution.py:60
  15.5 10.1 %collective-permute-start.3 = (bf16[96,768]{1,0:T(8,128)(2,1)S(1)}, bf16[96,768]{1,0:T(8,128)(2,1)S(1)}, u32[]{:S(2)}, u32[]{:S(2)}) collective-permute-start(bf16[96,768]{1,0:T(8,128)(2,1)S(1)} %bitcast.256), channel_id=1, source_target_pairs={{0,4},{2,6},{4,0},{6,2},{8,12},{10,14},{12,8},{14,10},{16,20},{18,... | collective-permute-start | bytes 442376 | tf_op jit(solution)/shard_map/ppermute | solution.py:57
  17.0 13.0 %all-to-all-start = ((bf16[16,8,768]{2,1,0:T(8,128)(2,1)}), bf16[16,8,768]{2,1,0:T(8,128)(2,1)S(1)}, u32[]{:S(2)}, u32[]{:S(2)}) async-start(bf16[16,8,768]{2,1,0:T(8,128)(2,1)} %fusion.4), calls=%async_computation | async-start | bytes 393216 | tf_op jit(solution)/shard_map/all_to_all | solution.py:601
  22.1 9.6 %collective-permute-start.1 = (bf16[96,768]{1,0:T(8,128)(2,1)S(1)}, bf16[96,768]{1,0:T(8,128)(2,1)S(1)}, u32[]{:S(2)}, u32[]{:S(2)}) collective-permute-start(bf16[96,768]{1,0:T(8,128)(2,1)S(1)} %bitcast.257), channel_id=1, source_target_pairs={{0,8},{2,10},{4,12},{6,14},{8,16},{10,18},{12,20},{14,22},{16,24},... | collective-permute-start | bytes 442376 | tf_op jit(solution)/shard_map/ppermute | solution.py:60
  24.1 18.0 %collective-permute-start.6 = (bf16[96,768]{1,0:T(8,128)(2,1)S(1)}, bf16[96,768]{1,0:T(8,128)(2,1)S(1)}, u32[]{:S(2)}, u32[]{:S(2)}) collective-permute-start(bf16[96,768]{1,0:T(8,128)(2,1)S(1)} %collective-permute-done.5), channel_id=1, source_target_pairs={{0,4},{2,6},{4,0},{6,2},{8,12},{10,14},{12,8},{14,10},{16,20},{18,... | collective-permute-start | bytes 442376 | tf_op jit(solution)/shard_map/ppermute | solution.py:57
  31.7 9.7 %collective-permute-start.7 = (bf16[96,768]{1,0:T(8,128)(2,1)S(1)}, bf16[96,768]{1,0:T(8,128)(2,1)}, u32[]{:S(2)}, u32[]{:S(2)}) collective-permute-start(bf16[96,768]{1,0:T(8,128)(2,1)S(1)} %collective-permute-done.1), channel_id=1, source_target_pairs={{0,8},{2,10},{4,12},{6,14},{8,16},{10,18},{12,20},{14,22},{16,24},... | collective-permute-start | bytes 442376 | tf_op jit(solution)/shard_map/ppermute | solution.py:60
  31.7 10.3 %collective-permute-start.4 = (bf16[96,768]{1,0:T(8,128)(2,1)S(1)}, bf16[96,768]{1,0:T(8,128)(2,1)S(1)}, u32[]{:S(2)}, u32[]{:S(2)}) collective-permute-start(bf16[96,768]{1,0:T(8,128)(2,1)S(1)} %collective-permute-done.1), channel_id=1, source_target_pairs={{0,4},{2,6},{4,0},{6,2},{8,12},{10,14},{12,8},{14,10},{16,20},{18,... | collective-permute-start | bytes 442376 | tf_op jit(solution)/shard_map/ppermute | solution.py:57
  33.2 9.8 %collective-permute-start.10 = (bf16[48,2432]{1,0:T(8,128)(2,1)S(1)}, bf16[48,2432]{1,0:T(8,128)(2,1)S(1)}, u32[]{:S(2)}, u32[]{:S(2)}) collective-permute-start(bf16[48,2432]{1,0:T(8,128)(2,1)S(1)} %maximum_maximum_fusion), channel_id=1, source_target_pairs={{0,2},{2,0},{4,6},{6,4},{8,10},{10,8},{12,14},{14,12},{16,18},{18,... | collective-permute-start | bytes 700424 | tf_op jit(solution)/shard_map/ppermute | solution.py:54
  41.0 56.1 %collective-permute-start.2 = (bf16[128,768]{1,0:T(8,128)(2,1)}, bf16[128,768]{1,0:T(8,128)(2,1)S(1)}, u32[]{:S(2)}, u32[]{:S(2)}) collective-permute-start(bf16[128,768]{1,0:T(8,128)(2,1)} %get-tuple-element.48), channel_id=1, source_target_pairs={{0,2},{1,3},{2,0},{3,1},{4,6},{5,7},{6,4},{7,5},{8,10},{9,11},{10,... | collective-permute-start | bytes 589832 | tf_op jit(solution)/shard_map/ppermute | solution.py:147
  43.0 15.7 %collective-permute-start.15 = (bf16[96,2432]{1,0:T(8,128)(2,1)S(1)}, bf16[96,2432]{1,0:T(8,128)(2,1)S(1)}, u32[]{:S(2)}, u32[]{:S(2)}) collective-permute-start(bf16[96,2432]{1,0:T(8,128)(2,1)S(1)} %bitcast.239), channel_id=1, source_target_pairs={{0,4},{2,6},{4,0},{6,2},{8,12},{10,14},{12,8},{14,10},{16,20},{18,... | collective-permute-start | bytes 1400840 | tf_op jit(solution)/shard_map/ppermute | solution.py:57
  44.6 14.2 %collective-permute-start.11 = (bf16[96,2432]{1,0:T(8,128)(2,1)S(1)}, bf16[96,2432]{1,0:T(8,128)(2,1)S(1)}, u32[]{:S(2)}, u32[]{:S(2)}) collective-permute-start(bf16[96,2432]{1,0:T(8,128)(2,1)S(1)} %bitcast.240), channel_id=1, source_target_pairs={{0,8},{2,10},{4,12},{6,14},{8,16},{10,18},{12,20},{14,22},{16,24},... | collective-permute-start | bytes 1400840 | tf_op jit(solution)/shard_map/ppermute | solution.py:60
  48.4 71.1 %collective-permute-start.21 = (bf16[768,768]{1,0:T(8,128)(2,1)S(1)}, bf16[768,768]{1,0:T(8,128)(2,1)}, u32[]{:S(2)}, u32[]{:S(2)}) collective-permute-start(bf16[768,768]{1,0:T(8,128)(2,1)S(1)} %bitcast.234), channel_id=1, source_target_pairs={{0,1},{1,0},{2,3},{3,2},{4,5},{5,4},{6,7},{7,6},{8,9},{9,8},{10,11... | collective-permute-start | bytes 3538952 | tf_op jit(solution)/shard_map/ppermute | solution.py:147
  50.0 21.8 %collective-permute-start.9 = (bf16[768,768]{1,0:T(8,128)(2,1)S(1)}, bf16[768,768]{1,0:T(8,128)(2,1)S(1)}, u32[]{:S(2)}, u32[]{:S(2)}) collective-permute-start(bf16[768,768]{1,0:T(8,128)(2,1)S(1)} %bitcast.235), channel_id=1, source_target_pairs={{0,2},{2,0},{4,6},{6,4},{8,10},{10,8},{12,14},{14,12},{16,18},{18,... | collective-permute-start | bytes 3538952 | tf_op jit(solution)/shard_map/ppermute | solution.py:54
  58.7 27.7 %collective-permute-start.17 = (bf16[96,2432]{1,0:T(8,128)(2,1)S(1)}, bf16[96,2432]{1,0:T(8,128)(2,1)}, u32[]{:S(2)}, u32[]{:S(2)}) collective-permute-start(bf16[96,2432]{1,0:T(8,128)(2,1)S(1)} %collective-permute-done.11), channel_id=1, source_target_pairs={{0,8},{2,10},{4,12},{6,14},{8,16},{10,18},{12,20},{14,22},{16,24},... | collective-permute-start | bytes 1400840 | tf_op jit(solution)/shard_map/ppermute | solution.py:60
  58.7 11.5 %collective-permute-start.16 = (bf16[96,2432]{1,0:T(8,128)(2,1)S(1)}, bf16[96,2432]{1,0:T(8,128)(2,1)S(1)}, u32[]{:S(2)}, u32[]{:S(2)}) collective-permute-start(bf16[96,2432]{1,0:T(8,128)(2,1)S(1)} %collective-permute-done.11), channel_id=1, source_target_pairs={{0,4},{2,6},{4,0},{6,2},{8,12},{10,14},{12,8},{14,10},{16,20},{18,... | collective-permute-start | bytes 1400840 | tf_op jit(solution)/shard_map/ppermute | solution.py:57
  84.8 7.4 %collective-permute-start.14 = (bf16[128,768]{1,0:T(8,128)(2,1)}, bf16[128,768]{1,0:T(8,128)(2,1)S(1)}, u32[]{:S(2)}, u32[]{:S(2)}) collective-permute-start(bf16[128,768]{1,0:T(8,128)(2,1)} %get-tuple-element.58), channel_id=1, source_target_pairs={{0,3},{1,2},{2,1},{3,0},{4,7},{5,6},{6,5},{7,4},{8,11},{9,10},{10,... | collective-permute-start | bytes 589832 | tf_op jit(solution)/shard_map/ppermute | solution.py:147
  84.9 11.6 %collective-permute-start.13 = (bf16[128,768]{1,0:T(8,128)(2,1)}, bf16[128,768]{1,0:T(8,128)(2,1)S(1)}, u32[]{:S(2)}, u32[]{:S(2)}) collective-permute-start(bf16[128,768]{1,0:T(8,128)(2,1)} %get-tuple-element.58), channel_id=1, source_target_pairs={{0,1},{1,0},{2,3},{3,2},{4,5},{5,4},{6,7},{7,6},{8,9},{9,8},{10,11... | collective-permute-start | bytes 589832 | tf_op jit(solution)/shard_map/ppermute | solution.py:147
  86.5 10.6 %collective-permute-start.12 = (bf16[128,768]{1,0:T(8,128)(2,1)}, bf16[128,768]{1,0:T(8,128)(2,1)S(1)}, u32[]{:S(2)}, u32[]{:S(2)}) collective-permute-start(bf16[128,768]{1,0:T(8,128)(2,1)} %get-tuple-element.58), channel_id=1, source_target_pairs={{0,2},{1,3},{2,0},{3,1},{4,6},{5,7},{6,4},{7,5},{8,10},{9,11},{10,... | collective-permute-start | bytes 589832 | tf_op jit(solution)/shard_map/ppermute | solution.py:147
  92.2 14.7 %collective-permute-start.19 = (bf16[96,2432]{1,0:T(8,128)(2,1)}, bf16[96,2432]{1,0:T(8,128)(2,1)S(1)}, u32[]{:S(2)}, u32[]{:S(2)}) collective-permute-start(bf16[96,2432]{1,0:T(8,128)(2,1)} %collective-permute-done.17), channel_id=1, source_target_pairs={{0,8},{2,10},{4,12},{6,14},{8,16},{10,18},{12,20},{14,22},{16,24},... | collective-permute-start | bytes 1400840 | tf_op jit(solution)/shard_map/ppermute | solution.py:60
  96.5 13.4 %collective-permute-start.18 = (bf16[96,2432]{1,0:T(8,128)(2,1)}, bf16[96,2432]{1,0:T(8,128)(2,1)S(1)}, u32[]{:S(2)}, u32[]{:S(2)}) collective-permute-start(bf16[96,2432]{1,0:T(8,128)(2,1)} %collective-permute-done.17), channel_id=1, source_target_pairs={{0,4},{2,6},{4,0},{6,2},{8,12},{10,14},{12,8},{14,10},{16,20},{18,... | collective-permute-start | bytes 1400840 | tf_op jit(solution)/shard_map/ppermute | solution.py:57
  106.9 12.4 %collective-permute-start.20 = (bf16[96,2432]{1,0:T(8,128)(2,1)S(1)}, bf16[96,2432]{1,0:T(8,128)(2,1)S(1)}, u32[]{:S(2)}, u32[]{:S(2)}) collective-permute-start(bf16[96,2432]{1,0:T(8,128)(2,1)S(1)} %collective-permute-done.19), channel_id=1, source_target_pairs={{0,4},{2,6},{4,0},{6,2},{8,12},{10,14},{12,8},{14,10},{16,20},{18,... | collective-permute-start | bytes 1400840 | tf_op jit(solution)/shard_map/ppermute | solution.py:57
  119.4 8.8 %collective-permute-start.25 = (bf16[768,896]{1,0:T(8,128)(2,1)S(1)}, bf16[768,896]{1,0:T(8,128)(2,1)S(1)}, u32[]{:S(2)}, u32[]{:S(2)}) collective-permute-start(bf16[768,896]{1,0:T(8,128)(2,1)S(1)} %bitcast.225), channel_id=1, source_target_pairs={{0,2},{2,0},{4,6},{6,4},{8,10},{10,8},{12,14},{14,12},{16,18},{18,... | collective-permute-start | bytes 4128776 | tf_op jit(solution)/shard_map/ppermute | solution.py:54
  122.8 27.7 %collective-permute-start.49 = (bf16[768,768]{1,0:T(8,128)(2,1)}, bf16[768,768]{1,0:T(8,128)(2,1)}, u32[]{:S(2)}, u32[]{:S(2)}) collective-permute-start(bf16[768,768]{1,0:T(8,128)(2,1)} %collective-permute-done.21), channel_id=1, source_target_pairs={{0,2},{2,0},{4,6},{6,4},{8,10},{10,8},{12,14},{14,12},{16,18},{18,... | collective-permute-start | bytes 3538952 | tf_op jit(solution)/shard_map/ppermute | solution.py:54
  143.2 109.4 %collective-permute-start.46 = (bf16[128,384]{1,0:T(8,128)(2,1)}, bf16[128,384]{1,0:T(8,128)(2,1)}, u32[]{:S(2)}, u32[]{:S(2)}) collective-permute-start(bf16[128,384]{1,0:T(8,128)(2,1)} %get-tuple-element.64.q_ref), channel_id=1, source_target_pairs={{0,1},{1,0},{2,3},{3,2},{4,5},{5,4},{6,7},{7,6},{8,9},{9,8},{10,11... | collective-permute-start | bytes 294920 | tf_op jit(solution)/shard_map/ppermute | solution.py:147
  143.9 18.2 %collective-permute-start.41 = (bf16[64,768]{1,0:T(8,128)(2,1)}, bf16[64,768]{1,0:T(8,128)(2,1)S(1)}, u32[]{:S(2)}, u32[]{:S(2)}) collective-permute-start(bf16[64,768]{1,0:T(8,128)(2,1)} %fusion.42), channel_id=1, source_target_pairs={{0,3},{1,2},{2,1},{3,0},{4,7},{5,6},{6,5},{7,4},{8,11},{9,10},{10,... | collective-permute-start | bytes 294920 | tf_op jit(solution)/shard_map/ppermute | solution.py:147
  155.3 7.4 %collective-permute-start.40 = (bf16[64,768]{1,0:T(8,128)(2,1)}, bf16[64,768]{1,0:T(8,128)(2,1)S(1)}, u32[]{:S(2)}, u32[]{:S(2)}) collective-permute-start(bf16[64,768]{1,0:T(8,128)(2,1)} %fusion.42), channel_id=1, source_target_pairs={{0,2},{1,3},{2,0},{3,1},{4,6},{5,7},{6,4},{7,5},{8,10},{9,11},{10,... | collective-permute-start | bytes 294920 | tf_op jit(solution)/shard_map/ppermute | solution.py:147
  155.3 8.0 %collective-permute-start.39 = (bf16[64,768]{1,0:T(8,128)(2,1)}, bf16[64,768]{1,0:T(8,128)(2,1)S(1)}, u32[]{:S(2)}, u32[]{:S(2)}) collective-permute-start(bf16[64,768]{1,0:T(8,128)(2,1)} %fusion.42), channel_id=1, source_target_pairs={{0,1},{1,0},{2,3},{3,2},{4,5},{5,4},{6,7},{7,6},{8,9},{9,8},{10,11... | collective-permute-start | bytes 294920 | tf_op jit(solution)/shard_map/ppermute | solution.py:147
  161.1 14.1 %collective-permute-start.38 = (bf16[128,768]{1,0:T(8,128)(2,1)}, bf16[128,768]{1,0:T(8,128)(2,1)}, u32[]{:S(2)}, u32[]{:S(2)}) collective-permute-start(bf16[128,768]{1,0:T(8,128)(2,1)} %get-tuple-element.115), channel_id=1, source_target_pairs={{0,3},{1,2},{2,1},{3,0},{4,7},{5,6},{6,5},{7,4},{8,11},{9,10},{10,... | collective-permute-start | bytes 589832 | tf_op jit(solution)/shard_map/ppermute | solution.py:147
  162.2 13.9 %collective-permute-start.37 = (bf16[128,768]{1,0:T(8,128)(2,1)}, bf16[128,768]{1,0:T(8,128)(2,1)}, u32[]{:S(2)}, u32[]{:S(2)}) collective-permute-start(bf16[128,768]{1,0:T(8,128)(2,1)} %get-tuple-element.115), channel_id=1, source_target_pairs={{0,2},{1,3},{2,0},{3,1},{4,6},{5,7},{6,4},{7,5},{8,10},{9,11},{10,... | collective-permute-start | bytes 589832 | tf_op jit(solution)/shard_map/ppermute | solution.py:147
  162.7 10.0 %collective-permute-start.36 = (bf16[128,768]{1,0:T(8,128)(2,1)}, bf16[128,768]{1,0:T(8,128)(2,1)}, u32[]{:S(2)}, u32[]{:S(2)}) collective-permute-start(bf16[128,768]{1,0:T(8,128)(2,1)} %get-tuple-element.114), channel_id=1, source_target_pairs={{0,1},{1,0},{2,3},{3,2},{4,5},{5,4},{6,7},{7,6},{8,9},{9,8},{10,11... | collective-permute-start | bytes 589832 | tf_op jit(solution)/shard_map/ppermute | solution.py:147
  167.6 16.3 %collective-permute-start.45 = (bf16[4,96,768]{2,1,0:T(8,128)(2,1)S(1)}, bf16[4,96,768]{2,1,0:T(8,128)(2,1)S(1)}, u32[]{:S(2)}, u32[]{:S(2)}) collective-permute-start(bf16[4,96,768]{2,1,0:T(8,128)(2,1)S(1)} %dynamic-slice_bitcast_fusion.1), channel_id=1, source_target_pairs={{0,4},{2,6},{4,0},{6,2},{8,12},{10,14},{12,8},{14,10},{16,20},{18,... | collective-permute-start | bytes 1769480 | tf_op jit(solution)/shard_map/ppermute | solution.py:57
  172.8 26.8 %collective-permute-start.42 = (bf16[4,96,960]{2,1,0:T(8,128)(2,1)S(1)}, bf16[4,96,960]{2,1,0:T(8,128)(2,1)S(1)}, u32[]{:S(2)}, u32[]{:S(2)}) collective-permute-start(bf16[4,96,960]{2,1,0:T(8,128)(2,1)S(1)} %dynamic-slice_bitcast_fusion), channel_id=1, source_target_pairs={{0,4},{2,6},{4,0},{6,2},{8,12},{10,14},{12,8},{14,10},{16,20},{18,... | collective-permute-start | bytes 2211848 | tf_op jit(solution)/shard_map/ppermute | solution.py:57
  213.0 22.8 %collective-permute-start.43 = (bf16[768,768]{1,0:T(8,128)(2,1)}, bf16[768,768]{1,0:T(8,128)(2,1)}, u32[]{:S(2)}, u32[]{:S(2)}) collective-permute-start(bf16[768,768]{1,0:T(8,128)(2,1)} %get-tuple-element.67), channel_id=1, source_target_pairs={{0,2},{2,0},{4,6},{6,4},{8,10},{10,8},{12,14},{14,12},{16,18},{18,... | collective-permute-start | bytes 3538952 | tf_op jit(solution)/shard_map/ppermute | solution.py:54
  213.2 8.6 %collective-permute-start.54 = (bf16[96,768]{1,0:T(8,128)(2,1)S(1)}, bf16[96,768]{1,0:T(8,128)(2,1)S(1)}, u32[]{:S(2)}, u32[]{:S(2)}) collective-permute-start(bf16[96,768]{1,0:T(8,128)(2,1)S(1)} %get-tuple-element.104), channel_id=1, source_target_pairs={{0,8},{2,10},{4,12},{6,14},{8,16},{10,18},{12,20},{14,22},{16,24},... | collective-permute-start | bytes 442376 | tf_op jit(solution)/shard_map/ppermute | solution.py:60
  214.0 9.6 %collective-permute-start.56 = (bf16[96,768]{1,0:T(8,128)(2,1)S(1)}, bf16[96,768]{1,0:T(8,128)(2,1)S(1)}, u32[]{:S(2)}, u32[]{:S(2)}) collective-permute-start(bf16[96,768]{1,0:T(8,128)(2,1)S(1)} %get-tuple-element.105), channel_id=1, source_target_pairs={{0,24},{2,26},{4,28},{6,30},{8,0},{10,2},{12,4},{14,6},{16,8},{18,... | collective-permute-start | bytes 442376 | tf_op jit(solution)/shard_map/ppermute | solution.py:60
  217.0 12.7 %collective-permute-start.55 = (bf16[96,768]{1,0:T(8,128)(2,1)S(1)}, bf16[96,768]{1,0:T(8,128)(2,1)S(1)}, u32[]{:S(2)}, u32[]{:S(2)}) collective-permute-start(bf16[96,768]{1,0:T(8,128)(2,1)S(1)} %get-tuple-element.106), channel_id=1, source_target_pairs={{0,16},{2,18},{4,20},{6,22},{8,24},{10,26},{12,28},{14,30},{16,0},... | collective-permute-start | bytes 442376 | tf_op jit(solution)/shard_map/ppermute | solution.py:60
  221.8 8.2 %collective-permute-start.32 = (f32[8,128]{1,0:T(8,128)S(1)}, f32[8,128]{1,0:T(8,128)S(1)}, u32[]{:S(2)}, u32[]{:S(2)}) collective-permute-start(f32[8,128]{1,0:T(8,128)S(1)} %broadcast_in_dim.183), channel_id=1, source_target_pairs={{0,1},{1,0},{2,3},{3,2},{4,5},{5,4},{6,7},{7,6},{8,9},{9,8},{10,11... | collective-permute-start | bytes 12296 | tf_op jit(solution)/shard_map/ppermute | solution.py:147
  231.9 9.7 %collective-permute-start.58 = (bf16[96,960]{1,0:T(8,128)(2,1)S(1)}, bf16[96,960]{1,0:T(8,128)(2,1)S(1)}, u32[]{:S(2)}, u32[]{:S(2)}) collective-permute-start(bf16[96,960]{1,0:T(8,128)(2,1)S(1)} %get-tuple-element.99), channel_id=1, source_target_pairs={{0,8},{2,10},{4,12},{6,14},{8,16},{10,18},{12,20},{14,22},{16,24},... | collective-permute-start | bytes 552968 | tf_op jit(solution)/shard_map/ppermute | solution.py:60
  232.0 13.5 %collective-permute-start.60 = (bf16[96,960]{1,0:T(8,128)(2,1)S(1)}, bf16[96,960]{1,0:T(8,128)(2,1)S(1)}, u32[]{:S(2)}, u32[]{:S(2)}) collective-permute-start(bf16[96,960]{1,0:T(8,128)(2,1)S(1)} %get-tuple-element.100), channel_id=1, source_target_pairs={{0,24},{2,26},{4,28},{6,30},{8,0},{10,2},{12,4},{14,6},{16,8},{18,... | collective-permute-start | bytes 552968 | tf_op jit(solution)/shard_map/ppermute | solution.py:60
  235.8 15.8 %collective-permute-start.59 = (bf16[96,960]{1,0:T(8,128)(2,1)S(1)}, bf16[96,960]{1,0:T(8,128)(2,1)S(1)}, u32[]{:S(2)}, u32[]{:S(2)}) collective-permute-start(bf16[96,960]{1,0:T(8,128)(2,1)S(1)} %get-tuple-element.101), channel_id=1, source_target_pairs={{0,16},{2,18},{4,20},{6,22},{8,24},{10,26},{12,28},{14,30},{16,0},... | collective-permute-start | bytes 552968 | tf_op jit(solution)/shard_map/ppermute | solution.py:60
  237.5 26.4 %collective-permute-start.44 = (bf16[4,96,768]{2,1,0:T(8,128)(2,1)S(1)}, bf16[4,96,768]{2,1,0:T(8,128)(2,1)}, u32[]{:S(2)}, u32[]{:S(2)}) collective-permute-start(bf16[4,96,768]{2,1,0:T(8,128)(2,1)S(1)} %dynamic-slice_bitcast_fusion.2), channel_id=1, source_target_pairs={{0,4},{2,6},{4,0},{6,2},{8,12},{10,14},{12,8},{14,10},{16,20},{18,... | collective-permute-start | bytes 1769480 | tf_op jit(solution)/shard_map/ppermute | solution.py:57
  241.6 11.0 %collective-permute-start.47 = (bf16[128,384]{1,0:T(8,128)(2,1)S(1)}, bf16[128,384]{1,0:T(8,128)(2,1)S(1)}, u32[]{:S(2)}, u32[]{:S(2)}) collective-permute-start(bf16[128,384]{1,0:T(8,128)(2,1)S(1)} %copy-done.26), channel_id=1, source_target_pairs={{0,1},{1,0},{2,3},{3,2},{4,5},{5,4},{6,7},{7,6},{8,9},{9,8},{10,11... | collective-permute-start | bytes 294920 | tf_op jit(solution)/shard_map/ppermute | solution.py:147
  251.7 17.3 %collective-permute-start.61 = (f32[48,960]{1,0:T(8,128)S(1)}, f32[48,960]{1,0:T(8,128)S(1)}, u32[]{:S(2)}, u32[]{:S(2)}) collective-permute-start(f32[48,960]{1,0:T(8,128)S(1)} %dynamic-slice_bitcast_fusion.3), channel_id=1, source_target_pairs={{0,2},{2,0},{4,6},{6,4},{8,10},{10,8},{12,14},{14,12},{16,18},{18,... | collective-permute-start | bytes 552968 | tf_op jit(solution)/shard_map/ppermute | solution.py:54
  265.2 16.9 %collective-permute-start.50 = (bf16[96,768]{1,0:T(8,128)(2,1)S(1)}, bf16[96,768]{1,0:T(8,128)(2,1)S(1)}, u32[]{:S(2)}, u32[]{:S(2)}) collective-permute-start(bf16[96,768]{1,0:T(8,128)(2,1)S(1)} %get-tuple-element.107), channel_id=1, source_target_pairs={{0,8},{2,10},{4,12},{6,14},{8,16},{10,18},{12,20},{14,22},{16,24},... | collective-permute-start | bytes 442376 | tf_op jit(solution)/shard_map/ppermute | solution.py:60
  265.3 16.9 %collective-permute-start.52 = (bf16[96,768]{1,0:T(8,128)(2,1)S(1)}, bf16[96,768]{1,0:T(8,128)(2,1)S(1)}, u32[]{:S(2)}, u32[]{:S(2)}) collective-permute-start(bf16[96,768]{1,0:T(8,128)(2,1)S(1)} %get-tuple-element.108), channel_id=1, source_target_pairs={{0,24},{2,26},{4,28},{6,30},{8,0},{10,2},{12,4},{14,6},{16,8},{18,... | collective-permute-start | bytes 442376 | tf_op jit(solution)/shard_map/ppermute | solution.py:60
  269.1 13.1 %collective-permute-start.51 = (bf16[96,768]{1,0:T(8,128)(2,1)S(1)}, bf16[96,768]{1,0:T(8,128)(2,1)S(1)}, u32[]{:S(2)}, u32[]{:S(2)}) collective-permute-start(bf16[96,768]{1,0:T(8,128)(2,1)S(1)} %get-tuple-element.109), channel_id=1, source_target_pairs={{0,16},{2,18},{4,20},{6,22},{8,24},{10,26},{12,28},{14,30},{16,0},... | collective-permute-start | bytes 442376 | tf_op jit(solution)/shard_map/ppermute | solution.py:60
  269.3 16.7 %collective-permute-start.62 = (f32[48,384]{1,0:T(8,128)S(1)}, f32[48,384]{1,0:T(8,128)S(1)}, u32[]{:S(2)}, u32[]{:S(2)}) collective-permute-start(f32[48,384]{1,0:T(8,128)S(1)} %pad_maximum_fusion.13), channel_id=1, source_target_pairs={{0,1},{1,0},{2,3},{3,2},{4,5},{5,4},{6,7},{7,6},{8,9},{9,8},{10,11... | collective-permute-start | bytes 221192 | tf_op jit(solution)/shard_map/ppermute | solution.py:147
  (55 other events, 371.4 us)

commit v3 on v2

--- a/solution.py
+++ b/solution.py
@@ -61,71 +61,49 @@
             x, "dp", [(i, (i + 4 * step) % self.count) for i in range(self.count)]
         )
 
-    def join_cores(self, mine, send):
+    def join_cores(self, mine, arrived):
         rows, width = mine.shape
-        self.arrived = self.swap_core(send)
         block = jnp.zeros((2, rows, width), mine.dtype)
         block = lax.dynamic_update_slice(block, mine[None], (self.core, 0, 0))
-        block = lax.dynamic_update_slice(block, self.arrived[None], (1 - self.core, 0, 0))
+        block = lax.dynamic_update_slice(block, arrived[None], (1 - self.core, 0, 0))
         return block.reshape(2 * rows, width)
 
-    def spread_blocks(self, blocks, cuts):
-        rows = blocks[0][1].shape[0]
-        wholes = [
+    def place(self, wholes, cuts, step, here, across):
+        spot = ((self.depth - step) % 4) * 2
+        for block, at in ((here, spot + self.side), (across, spot + 1 - self.side)):
+            wholes = [
+                lax.dynamic_update_slice(whole, block[None, :, start:end], (at, 0, 0))
+                for whole, start, end in zip(wholes, cuts, cuts[1:])
+            ]
+        return wholes
+
+    def empty(self, rows, cuts):
+        return [
             jnp.zeros((self.count // 2, rows, end - start), low)
             for start, end in zip(cuts, cuts[1:])
         ]
-        for step, here in blocks:
-            place = ((self.depth - step) % 4) * 2
-            across = self.swap_side(here)
-            for block, spot in ((here, place + self.side), (across, place + 1 - self.side)):
-                for i, (start, end) in enumerate(zip(cuts, cuts[1:])):
-                    wholes[i] = lax.dynamic_update_slice(
-                        wholes[i], block[None, :, start:end], (spot, 0, 0)
-                    )
-        return [whole.reshape(rows * self.count // 2, -1) for whole in wholes]
 
     def gather_plain(self, mine, send):
         zero_all = lax.all_gather(pick(self.core, mine, send), "dp", axis=0, tiled=True)
         one_all = lax.all_gather(pick(self.core, send, mine), "dp", axis=0, tiled=True)
         return pick(self.core, zero_all, one_all)
 
-    def scatter_side(self, keep, send=None, before=None):
-        if not self.fast:
-            return keep, send
-        rows = keep.shape[0] // self.count
-        width = keep.shape[1]
-        pair = keep
-        if send is not None:
-            pair = (keep.astype(full) + self.swap_core(send).astype(full)).astype(low)
-        self.pair = pair
-        pair = pair.reshape(4, 2, 2 * rows, width)
-        stay = lax.dynamic_index_in_dim(pair, self.side, 1, False)
-        leave = lax.dynamic_index_in_dim(pair, 1 - self.side, 1, False)
-        arrived = self.swap_side(leave)
-        if before is not None:
-            arrived = after(arrived, before(self))
-        return (stay.astype(full) + arrived.astype(full)).astype(low)
-
-    def scatter_depth(self, quad_sum):
-        if not self.fast:
-            keep, send = quad_sum
-            if send is None:
-                send = jnp.zeros_like(keep)
-            halves = (pick(self.core, keep, send), pick(self.core, send, keep))
-            return [
-                lax.psum_scatter(half, "dp", scatter_dimension=0, tiled=True).astype(full)
-                for half in halves
-            ]
-        total = lax.dynamic_index_in_dim(quad_sum, self.depth, 0, False).astype(full)
-        for step in range(1, 4):
-            leave = lax.dynamic_index_in_dim(quad_sum, (self.depth + step) % 4, 0, False)
-            total = total + self.shift_depth(leave, step).astype(full)
-        return total
+    def halve(self, x, axis, bit):
+        spot = (self.index // bit) % 2
+        stay = lax.dynamic_index_in_dim(x, spot, axis, False)
+        leave = lax.dynamic_index_in_dim(x, 1 - spot, axis, False)
+        return stay, lax.ppermute(leave, "dp", [(i, i ^ bit) for i in range(self.count)])
+
+    def scatter_plain(self, keep, send=None):
+        if send is None:
+            send = jnp.zeros_like(keep)
+        halves = (pick(self.core, keep, send), pick(self.core, send, keep))
+        return [
+            lax.psum_scatter(half, "dp", scatter_dimension=0, tiled=True).astype(full)
+            for half in halves
+        ]
 
     def scatter_core(self, total):
-        if not self.fast:
-            return total
         rows, width = total.shape[0] // 2, total.shape[1]
         total = total.reshape(2, rows, width)
         mine = lax.dynamic_index_in_dim(total, self.core, 0, False)
@@ -153,6 +131,14 @@
 
 def after(x, *others):
     return lax.optimization_barrier((x, *others))[0]
+
+
+def joint(*values):
+    return lax.optimization_barrier(values)
+
+
+def add_low(pair):
+    return (pair[0].astype(full) + pair[1].astype(full)).astype(low)
 
 
 def roll_rows(x):
@@ -442,6 +428,28 @@
         scratch_shapes=[pltpu.VMEM((WIDTH, 2 * COLS), full)],
         name="attend_back",
     )(core, d_mid, d_att, unit, unit_end, mixed, probs, queries, attended)
+
+
+def lower_back_body(flag_ref, d_out_ref, active_ref, both_ref, out_ref):
+    hidden = active_ref.shape[1]
+    quarter = WIDTH // 4
+    out_ref[:, :hidden] = mm_tn(d_out_ref[...], active_ref[...]).astype(low)
+    here = both_ref[:, :quarter]
+    for index in range(1, 4):
+        part = both_ref[:, index * quarter : (index + 1) * quarter]
+        here = jnp.where(flag_ref[0] == index, part, here)
+    out_ref[:, hidden:] = mm_tn(both_ref[:, WIDTH:], here).astype(low)
+
+
+def lower_back(flag, d_out, active, both):
+    vmem = pl.BlockSpec(memory_space=pltpu.VMEM)
+    return pl.pallas_call(
+        lower_back_body,
+        out_shape=jax.ShapeDtypeStruct((WIDTH, active.shape[1] + WIDTH // 4), low),
+        in_specs=[pl.BlockSpec(memory_space=pltpu.SMEM)] + [vmem] * 3,
+        out_specs=vmem,
+        name="lower_back",
+    )(flag, d_out, active, both)
 
 
 def place_rows(picks, rows):
@@ -579,7 +587,6 @@
     rows = w_out.shape[0]
     per_peer = rows_dev // spread
     hidden = w_up.shape[1] // 2
-    quarter = width // 4
     core_flag = core.reshape(1).astype(jnp.int32)
     group_flag = group.reshape(1).astype(jnp.int32)
 
@@ -597,8 +604,7 @@
     ends = lax.dynamic_slice_in_dim(flipped, group * CAP_DEV, rows_dev, 0)[:, None]
     wide = width // 2
 
-    def pictures_of_batch(outgoing):
-        incoming = lax.all_to_all(outgoing, "dp", split_axis=0, concat_axis=0, tiled=True)
+    def pictures_of_batch(incoming):
         own_arrive = lax.dynamic_slice_in_dim(arrive_order[0], group * CAP_DEV, CAP_DEV, 0)
         take_in = (own_arrive[:, None] == places[None, :]).astype(low)
         pictures = mm(take_in, incoming.reshape(rows_dev, width)).astype(low)
@@ -612,6 +618,9 @@
     hand_out = (send_order[0][:, None] == places[None, :]).astype(low)
     outgoing = mm(hand_out, cached).astype(low).reshape(spread, per_peer, width)
 
+    def deal(outgoing):
+        return lax.all_to_all(outgoing, "dp", split_axis=0, concat_axis=0, tiled=True)
+
     def first_parts(stream):
         return norm_first(group_flag, stream.reshape(rows_dev * length, width), ends)
 
@@ -626,35 +635,72 @@
             parts = [half[main:, i * 128 : (i + 1) * 128] for i in range(wide // 128)]
             return jnp.concatenate([feed, embed, half[:main], jnp.concatenate(parts, 0)], 1)
 
-        block = plane.join_cores(packed[0], packed[1])
-        pictures = pictures_of_batch(after(outgoing, plane.arrived))
+        mix_cuts = (0, 2 * COLS)
+        cuts = (0, 2 * hidden, 2 * hidden + 2 * wide + 128)
+        arrived = plane.swap_core(packed[1])
+        arrived, outgoing = joint(arrived, outgoing)
+        block = plane.join_cores(packed[0], arrived)
+        incoming = deal(outgoing)
         up = plane.shift_depth(block, 1)
         down = plane.shift_depth(block, -1)
-        up = after(up, pictures[0])
+        across = plane.swap_side(block)
+        up, down, across, block = joint(up, down, across, block)
+
+        mixes = plane.place(plane.empty(2 * rows, mix_cuts), mix_cuts, 0, block, across)
         far = plane.shift_depth(up, 1)
+        across_up = plane.swap_side(up)
+        across_down = plane.swap_side(down)
         parts = first_parts(after(captions, up))
-        far = after(far, parts[0])
-        (mix_own,) = plane.spread_blocks(
-            ((0, block), (1, up), (-1, down), (2, far)), (0, 2 * COLS)
+        far, across_up, across_down, incoming, *parts = joint(
+            far, across_up, across_down, incoming, *parts
         )
+
+        across = plane.swap_side(far)
+        pictures = pictures_of_batch(incoming)
+        mine = join(packed[2], packed[4], pictures[0])
+        arrived = plane.swap_core(join(packed[3], packed[5], pictures[1]))
+        stream_near = swap_near(parts[3], 2)
+        mixes = plane.place(mixes, mix_cuts, 1, up, across_up)
+        mixes = plane.place(mixes, mix_cuts, -1, down, across_down)
+        across, arrived, stream_near, mixes = joint(across, arrived, stream_near, mixes)
+
+        block = plane.join_cores(mine, arrived)
+        one = plane.shift_depth(block, 1)
+        across_block = plane.swap_side(block)
+        mixes = plane.place(mixes, mix_cuts, 2, far, across)
+        mix_own = mixes[0].reshape(width, 2 * COLS)
         mix_other = plane.swap_core(mix_own)
         far_own = swap_group(mix_own)
-
-        block = plane.join_cores(
-            join(packed[2], packed[4], pictures[0]), join(packed[3], packed[5], pictures[1])
-        )
-        block = after(block, far)
-        one = plane.shift_depth(block, 1)
-        two = plane.shift_depth(one, 1)
         kv = pick(core, mix_own, mix_other)
         qo = pick(core, mix_other, mix_own)
-        attending = attention_of(kv, after(qo, one), parts)
-        two = after(two, attending[-1])
+        one, kv, qo = joint(one, kv, qo)
+
+        two = plane.shift_depth(one, 1)
+        across_one = plane.swap_side(one)
+        attending = attention_of(kv, qo, parts)
+        two, across_block, across_one, *attending = joint(
+            two, across_block, across_one, *attending
+        )
+
         three = plane.shift_depth(two, 1)
-        cut = 2 * hidden
-        feeds, third = plane.spread_blocks(
-            ((0, block), (1, one), (2, two), (3, three)), (0, cut, cut + 2 * wide + 128)
+        across_two = plane.swap_side(two)
+        wholes = plane.place(plane.empty(2 * rows, cuts), cuts, 0, block, across_block)
+        wholes = plane.place(wholes, cuts, 1, one, across_one)
+        attention = after(attending[-1], far_own)
+        near = [swap_near(attention, flip) for flip in (1, 2, 3)]
+        three, across_two, *near = joint(three, across_two, *near)
+
+        across = plane.swap_side(three)
+        queries_far = swap_group(attending[2])
+        far_other = plane.swap_core(far_own)
+        kv_far = pick(core, far_own, far_other)
+        qo_far = pick(core, far_other, far_own)
+        wholes = plane.place(wholes, cuts, 2, two, across_two)
+        across, queries_far, kv_far, qo_far, wholes = joint(
+            across, queries_far, kv_far, qo_far, wholes
         )
+        wholes = plane.place(wholes, cuts, 3, three, across)
+        feeds, third = [whole.reshape(width, -1) for whole in wholes]
         third_other = plane.swap_core(third)
 
         def images(x):
@@ -665,7 +711,7 @@
         image_halves = images(third), images(third_other)
         embed_halves = third[:, :wide], third_other[:, :wide]
     else:
-        pictures = pictures_of_batch(outgoing)
+        pictures = pictures_of_batch(deal(outgoing))
         parts = first_parts(captions)
         mix_own = plane.gather_plain(packed[0], packed[1])
         mix_other = plane.swap_core(mix_own)
@@ -678,11 +724,15 @@
         image_halves = image_half, plane.swap_core(image_half)
         embed_half = plane.gather_plain(packed[4], packed[5])
         embed_halves = embed_half, plane.swap_core(embed_half)
+        far_other = plane.swap_core(far_own)
+        kv_far = pick(core, far_own, far_other)
+        qo_far = pick(core, far_other, far_own)
+        stream_near = swap_near(parts[3], 2)
+        attention = attending[-1]
+        near = [swap_near(attention, flip) for flip in (1, 2, 3)]
+        queries_far = swap_group(attending[2])
     unit, scale, unit_end, stream_end = parts
-    mixed, probs, queries, attended, attention = attending
-    far_other = plane.swap_core(far_own)
-    kv_far = pick(core, far_own, far_other)
-    qo_far = pick(core, far_other, far_own)
+    mixed, probs, queries, attended, _ = attending
 
     def sides(pair):
         return jnp.concatenate([pick(core, *pair), pick(core, pair[1], pair[0])], 1)
@@ -690,8 +740,7 @@
     pictures_all = sides(image_halves)
     w_embed = sides(embed_halves)
 
-    stream_near = swap_near(stream_end, 2)
-    from_group, from_core, from_both = [swap_near(attention, flip) for flip in (1, 2, 3)]
+    from_group, from_core, from_both = near
     attention = jnp.concatenate([attention, from_core], 0).astype(full)
     attention = attention + jnp.concatenate(
         [roll_rows(from_group), roll_rows(from_both)], 0
@@ -699,7 +748,6 @@
     middle = jnp.concatenate([stream_end, stream_near], 0).astype(full) + attention
     unit_second, scale_second = norm_rows(middle)
     second_low = unit_second.astype(low)
-    feeds = after(feeds, far_own)
     w_raise = feeds[:, :hidden]
     w_lower = feeds[:, hidden:]
     active, slope = gelu_parts(mm(second_low, w_raise))
@@ -745,8 +793,6 @@
     col_sum = totals[: spread * CAP_DEV]
     col_safe = jnp.where(batch_valid, col_sum, 1.0)
     objective = jnp.sum(totals[spread * CAP_DEV :]) + 0.5 * jnp.sum(jnp.log(col_safe))
-    objective = jnp.full((8, 128), objective)
-    loss = (objective + swap_group(objective))[0, 0] / total_valid
     d_sims = (
         weight * (0.5 / row_safe[:, None] + 0.5 / col_safe[None, :]) - target.astype(full)
     ).astype(low)
@@ -755,20 +801,19 @@
         (d_unit - unit_text * jnp.sum(unit_text * d_unit, -1, keepdims=True)) * inverse
     ).astype(low)
 
-    pooled_all = jnp.concatenate([pooled] + [swap_near(pooled, flip) for flip in (1, 2, 3)], 0)
-    d_embed_all = jnp.concatenate([d_embed] + [swap_near(d_embed, flip) for flip in (1, 2, 3)], 0)
+    both = jnp.concatenate([d_embed, pooled], 1)
+    both = jnp.concatenate([both] + [swap_near(both, flip) for flip in (1, 2, 3)], 0)
+    d_embed_all = both[:, :width]
     d_pooled = mm_nt(d_embed_all, w_embed)
     d_out_low = d_pooled.astype(low)
-    g_lower = mm_tn(d_out_low, active).astype(low)
     d_raised = (mm(d_out_low, w_lower) * slope).astype(low)
+    d_second = mm_nt(d_raised, w_raise).astype(low)
     g_raise = mm_tn(second_low, d_raised).astype(low)
-    d_second = mm_nt(d_raised, w_raise).astype(low)
-    d_embed_half = pick(group, d_embed_all[:, :wide], d_embed_all[:, wide:])
-    d_embed_here = pick(core, d_embed_half[:, :quarter], d_embed_half[:, quarter:])
-    g_embed = mm_tn(pooled_all, d_embed_here).astype(low)
-    lower_quad = plane.scatter_side(jnp.concatenate([g_lower, g_embed], 1))
-    raise_quad = plane.scatter_side(g_raise)
-    queries_far = swap_group(queries)
+    d_out_late = after(d_out_low, g_raise, d_second)
+    g_lower = lower_back(2 * group_flag + core_flag, d_out_late, active, both)
+    if plane.fast:
+        raise_stay, raise_in = plane.halve(g_raise.reshape(2, 2, 2, 2 * rows, -1), 1, 4)
+        lower_stay, lower_in = plane.halve(g_lower.reshape(2, 2, 2, 2 * rows, -1), 2, 2)
     inner = d_second[:rows_dev].astype(full)
     inner = inner + roll_rows(swap_near(d_second[:rows_dev], 1)).astype(full)
     inner = inner + swap_near(d_second[rows_dev:], 2).astype(full)
@@ -780,33 +825,49 @@
     d_middle_low = d_middle.astype(low)
     d_attended = mm(d_middle_low, qo[:, COLS:]).astype(low)
     d_attended_far = swap_group(d_attended)
-    back_start = after(d_middle_low, lower_quad) if plane.fast else d_middle_low
     g_keep, g_send, d_mixed, d_queries, small = attend_back(
-        core_flag, back_start, d_attended, unit, unit_end, mixed, probs, queries, attended
-    )
-    small_far = swap_group(small)
-    operands = (
-        unit, scale, d_middle, d_mixed, d_queries, queries_far, d_attended_far, small_far, kv, qo,
-        kv_far, qo_far,
-    )
-    halves = []
-
-    def first_half(plane):
-        first_ends = after(ends, raise_quad, plane.pair)
-        halves.append(captions_back(0, group_flag, first_ends, *operands))
-        return halves[0]
-
-    mix_quad = plane.scatter_side(g_keep, g_send, first_half)
-    if not plane.fast:
-        halves.append(captions_back(0, group_flag, ends, *operands))
-    lower_sum = plane.scatter_core(plane.scatter_depth(lower_quad))
-    raise_sum = plane.scatter_core(plane.scatter_depth(raise_quad))
-    second_ends = after(ends, mix_quad) if plane.fast else ends
-    grad_captions = captions_back(1, group_flag, second_ends, *operands, done=halves[0])
-    mix_total = plane.scatter_depth(mix_quad)
+        core_flag, d_middle_low, d_attended, unit, unit_end, mixed, probs, queries, attended
+    )
+
+    def captions_part(part, d_queries_here, done=None):
+        return captions_back(
+            part, group_flag, ends, unit, scale, d_middle, d_mixed, d_queries_here, queries_far,
+            d_attended_far, small_far, kv, qo, kv_far, qo_far, done=done,
+        )
+
     if plane.fast:
-        mix_total, grad_captions = lax.optimization_barrier((mix_total, grad_captions))
-    mix_sum = plane.scatter_core(mix_total)
+        raise_stay, raise_in, lower_stay, lower_in, small, d_queries, g_send = joint(
+            raise_stay, raise_in, lower_stay, lower_in, small, d_queries, g_send
+        )
+        small_far = swap_group(small)
+        mix_in = plane.swap_core(g_send)
+        raise_side = plane.halve(add_low((raise_stay, raise_in)), 1, 2)
+        lower_depth = plane.halve(add_low((lower_stay, lower_in)), 1, 4)
+        mix_pair = add_low((g_keep, mix_in)).reshape(2, 2, 2, 2 * rows, 2 * COLS)
+        mix_side = plane.halve(mix_pair, 2, 2)
+        first_half = captions_part(0, after(d_queries, mix_side[0]))
+        raise_side, lower_depth, mix_side, first_half = joint(
+            raise_side, lower_depth, mix_side, first_half
+        )
+        mix_depth = plane.halve(add_low(mix_side), 1, 4)
+        raise_last = plane.halve(add_low(raise_side), 0, 8)
+        lower_last = plane.halve(add_low(lower_depth), 0, 8)
+        starts = after(d_queries, mix_depth[0], raise_last[0], lower_last[0])
+        grad_captions = captions_part(1, starts, first_half)
+        mix_depth, raise_last, lower_last, grad_captions = joint(
+            mix_depth, raise_last, lower_last, grad_captions
+        )
+        mix_last = plane.halve(add_low(mix_depth), 0, 8)
+        raise_sum, lower_sum, mix_sum = [
+            plane.scatter_core(pair[0].astype(full) + pair[1].astype(full))
+            for pair in (raise_last, lower_last, mix_last)
+        ]
+    else:
+        small_far = swap_group(small)
+        grad_captions = captions_part(1, d_queries, captions_part(0, d_queries))
+        raise_sum = plane.scatter_plain(g_raise)
+        lower_sum = plane.scatter_plain(g_lower)
+        mix_sum = plane.scatter_plain(g_keep, g_send)
     grad_captions = grad_captions.reshape(rows_dev, length, width)
 
     grad_down = jnp.concatenate([part[:, :hidden] for part in lower_sum], 1)
@@ -826,9 +887,11 @@
         [
             jnp.sum(unit_mix * w_qkv.astype(full), (1, 2)),
             jnp.sum(raised_sum * w_up.astype(full), 1),
+            jnp.broadcast_to(objective, (rows,)),
         ]
     )
     gains = gains + swap_group(gains)
+    loss = gains[2, 0] / total_valid
     return (
         loss,
         grad_captions,

time: 292 us -> 251 us (0.86)
  waiting for transfers between devices: 110 us -> 58.2 us
  local copies, waits for them, and re-layouts: 20.7 us -> 29.6 us
  starting transfers between devices: 61.3 us -> 55.7 us
  matrix products: 13.1 us -> 17.6 us
  Pallas kernels: 55.1 us -> 58.3 us
    ppermute x12 -> x9, waiting for transfers between devices: 46.5 us -> 11.5 us  [swap_side(): return lax.ppermute(x, 'dp', [(i, i ^ 2) for i in range(self.count)])]
    ppermute x18 -> x9, waiting for transfers between devices: 41.3 us -> 17.3 us  [shift_depth(): lax.ppermute(x, 'dp', [(i, (i + 4 * step) % self.count) for i in range(se...]
    ppermute x18 -> x9, starting transfers between devices: 23.9 us -> 12.4 us  [shift_depth(): lax.ppermute(x, 'dp', [(i, (i + 4 * step) % self.count) for i in range(se...]
    dynamic_update_slice x26, local copies, waits for them, and re-layouts: 4.06 us -> 13.9 us  [the longest x24 13.9 us: place(): lax.dynamic_update_slice(whole, block[None, :, start:end], (at, 0, 0))]
    ppermute x0 -> x9, starting transfers between devices: none -> 8.88 us  [halve(): lax.ppermute(leave, 'dp', [(i, i ^ bit) for i in range(self.count)])]
    ppermute x0 -> x9, waiting for transfers between devices: none -> 6.49 us  [halve(): lax.ppermute(leave, 'dp', [(i, i ^ bit) for i in range(self.count)])]
    ppermute x23 -> x19, waiting for transfers between devices: 17.4 us -> 22.5 us  [swap_near(): return lax.ppermute(x, ('dp', 'mp'), [(i, i ^ flip) for i in range(size)])]
    dot_general x4, matrix products: 3.48 us -> 8.44 us  [mm_nt(): lax.dot_general(a, b, (((1,), (1,)), ((), ())), preferred_element_type=full)]
  transfers between devices with their start and end apart: 65 -> 58, of which waited for: 28 -> 18; matrix products, arithmetic and copies ran while one was open for 18% -> 21% of each run, Pallas kernels for 18% -> 23%
where the time goes in v3:
time: 251 us; the launch traced here: 250 us
  Pallas kernels  58.3 us (23%)
  waiting for transfers between devices  58.2 us (23%)
  starting transfers between devices  55.7 us (22%)
  local copies, waits for them, and re-layouts  29.6 us (12%)
  other arithmetic  22.9 us (9%)
  matrix products  17.6 us (7%)
  between operations  7.16 us (3%)
    ppermute x19, waiting for transfers between devices, swap_near(): return lax.ppermute(x, ('dp', 'mp'), [(i, i ^ flip) for i in range(size)])  22.5 us
    pallas_call x2, Pallas kernels, captions_back(): pl.pallas_call(functools.partial(captions_body, part), out_shape=jax.Shap...  21.3 us
    ppermute x9, waiting for transfers between devices, shift_depth(): lax.ppermute(x, 'dp', [(i, (i + 4 * step) % self.count) for i in range(se...  17.3 us
    ppermute x19, starting transfers between devices, swap_near(): return lax.ppermute(x, ('dp', 'mp'), [(i, i ^ flip) for i in range(size)])  15.1 us
    dynamic_update_slice x24, local copies, waits for them, and re-layouts, place(): lax.dynamic_update_slice(whole, block[None, :, start:end], (at, 0, 0))  13.9 us
    pallas_call x1, Pallas kernels, attend_back(): pl.pallas_call(attend_back_body, grid=(steps,), out_shape=shapes(*[((WIDT...  13 us
    ppermute x9, starting transfers between devices, shift_depth(): lax.ppermute(x, 'dp', [(i, (i + 4 * step) % self.count) for i in range(se...  12.4 us
    ppermute x9, waiting for transfers between devices, swap_side(): return lax.ppermute(x, 'dp', [(i, i ^ 2) for i in range(self.count)])  11.5 us
  transfers between devices with their start and end apart: 58, of which 18 were waited for; matrix products, arithmetic and copies ran while one was open for 21% of the time, Pallas kernels for 23%

profile of v3, /device:TPU:0, one launch (start us, length us, event | category | flops | bytes accessed | tf_op | source)
XLA Modules:
  0.0 249.6 jit_solution(3556785874339886133)
XLA Ops:
  0.7 2.0 pack.1
  7.4 1.9 fusion.1
  10.8 2.5 %collective-permute-start.3 = (bf16[96,768]{1,0:T(8,128)(2,1)S(1)}, bf16[96,768]{1,0:T(8,128)(2,1)S(1)}, u32[]{:S(2)}, u32[]{:S(2)}) collective-permute-start(bf16[96,768]{1,0:T(8,128)(2,1)S(1)} %bitcast.223), channel_id=1, source_target_pairs={{0,4},{2,6},{4,0},{6,2},{8,12},{10,14},{12,8},{14,10},{16,20},{18,... | collective-permute-start | bytes 442376 | tf_op jit(solution)/shard_map/ppermute | solution.py:57
  13.4 3.6 %collective-permute-start.2 = (bf16[96,768]{1,0:T(8,128)(2,1)S(1)}, bf16[96,768]{1,0:T(8,128)(2,1)S(1)}, u32[]{:S(2)}, u32[]{:S(2)}) collective-permute-start(bf16[96,768]{1,0:T(8,128)(2,1)S(1)} %bitcast.224), channel_id=1, source_target_pairs={{0,24},{2,26},{4,28},{6,30},{8,0},{10,2},{12,4},{14,6},{16,8},{18,... | collective-permute-start | bytes 442376 | tf_op jit(solution)/shard_map/ppermute | solution.py:60
  18.6 5.1 %all-to-all-start = ((bf16[16,8,768]{2,1,0:T(8,128)(2,1)}), bf16[16,8,768]{2,1,0:T(8,128)(2,1)S(1)}, u32[]{:S(2)}, u32[]{:S(2)}) async-start(bf16[16,8,768]{2,1,0:T(8,128)(2,1)} %fusion.1), calls=%async_computation | async-start | bytes 393216 | tf_op jit(solution)/shard_map/all_to_all | solution.py:622
  28.3 7.4 %norm_first.1 = (bf16[2048,768]{1,0:T(8,128)(2,1)}, f32[2048,128]{1,0:T(8,128)}, bf16[128,768]{1,0:T(8,128)(2,1)}, bf16[128,768]{1,0:T(8,128)(2,1)}) custom-call(s32[1]{0:T(128)} %bitcast.9.group_ref, bf16[2048,768]{1,0:T(8,128)(2,1)} %bitcast.206, s32[128,1]{1,0:T(8,128)} %copy.37.ends_ref), custom_call_target="tpu_custom_call" | custom-call | tf_op jit(solution)/shard_map/norm_first/pallas_call | solution.py:238
  37.9 3.4 %collective-permute-done.7 = bf16[96,768]{1,0:T(8,128)(2,1)S(1)} collective-permute-done((bf16[96,768]{1,0:T(8,128)(2,1)S(1)}, bf16[96,768]{1,0:T(8,128)(2,1)S(1)}, u32[]{:S(2)}, u32[]{:S(2)}) %collective-permute-start.7) | collective-permute-done | bytes 147488 | tf_op jit(solution)/shard_map/ppermute | solution.py:57
  41.6 1.6 collective-permute-start.15
  44.3 1.5 collective-permute-start.10
  45.9 1.7 broadcast_select_fusion.2
  47.6 11.1 %collective-permute-done.10 = bf16[96,2432]{1,0:T(8,128)(2,1)} collective-permute-done((bf16[96,2432]{1,0:T(8,128)(2,1)S(1)}, bf16[96,2432]{1,0:T(8,128)(2,1)}, u32[]{:S(2)}, u32[]{:S(2)}) %collective-permute-start.10) | collective-permute-done | bytes 466976 | tf_op jit(solution)/shard_map/ppermute | solution.py:60
  59.7 1.7 broadcast_in_dim.163
  62.1 11.3 %attend.1 = (bf16[2048,768]{1,0:T(8,128)(2,1)}, f32[768,256]{1,0:T(8,128)}, bf16[128,384]{1,0:T(8,128)(2,1)}, bf16[128,384]{1,0:T(8,128)(2,1)}, bf16[128,768]{1,0:T(8,128)(2,1)}) custom-call(bf16[2048,768]{1,0:T(8,128)(2,1)} %get-tuple-element.122.unit_ref, bf16[128,768]{1,0:T(8,128)(2,1)} %get-tuple-element.123.unit_end_ref, s32[128,1]{1,0:T(8,128)} %copy.37.ends_ref, ...), custom_call_target="tpu_custom_call" | custom-call | tf_op jit(solution)/shard_map/attend/pallas_call | solution.py:316
  74.1 1.5 collective-permute-start.18
  78.8 1.7 bitcast_dynamic-update-slice_fusion.6
  80.5 1.7 bitcast_dynamic-update-slice_fusion.5
  82.2 1.8 bitcast_dynamic-update-slice_fusion.4
  84.0 1.7 bitcast_dynamic-update-slice_fusion.3
  89.2 1.9 collective-permute-done.16
  93.6 2.8 %broadcast_select_fusion = (bf16[768,768]{1,0:T(8,128)(2,1)}, bf16[768,768]{1,0:T(8,128)(2,1)}) fusion(bf16[768,768]{1,0:T(8,128)(2,1)S(1)} %collective-permute-done.23, bf16[768,768]{1,0:T(8,128)(2,1)} %collective-permute-done.15, pred[]{:T(512)S(6)} %eq.94), kind=kLoop, calls=%fused_computation.12 | loop fusion | flops 1179648 | bytes 4718593 | tf_op jit(solution)/shard_map/jit(_where)/select_n | solution.py:41
  96.4 6.5 %collective-permute-done.21 = bf16[96,2432]{1,0:T(8,128)(2,1)S(1)} collective-permute-done((bf16[96,2432]{1,0:T(8,128)(2,1)S(1)}, bf16[96,2432]{1,0:T(8,128)(2,1)S(1)}, u32[]{:S(2)}, u32[]{:S(2)}) %collective-permute-start.21) | collective-permute-done | bytes 466976 | tf_op jit(solution)/shard_map/ppermute | solution.py:57
  104.5 1.8 multiply_convert_fusion
  106.3 1.9 convolution_convert_fusion.2
  110.7 3.3 %collective-permute-done.24 = bf16[64,768]{1,0:T(8,128)(2,1)S(1)} collective-permute-done((bf16[64,768]{1,0:T(8,128)(2,1)S(1)}, bf16[64,768]{1,0:T(8,128)(2,1)S(1)}, u32[]{:S(2)}, u32[]{:S(2)}) %collective-permute-start.24) | collective-permute-done | bytes 98336 | tf_op jit(solution)/shard_map/ppermute | solution.py:125
  116.8 2.0 fusion.29
  123.1 1.5 collective-permute-done.29
  125.1 2.1 collective-permute-start.33
  127.9 1.9 collective-permute-start.31
  129.8 1.9 collective-permute-done.32
  131.8 1.5 collective-permute-done.31
  133.3 1.6 multiply_reduce_fusion.4
  135.2 1.6 collective-permute-start.35
  137.3 5.0 %collective-permute-done.36 = bf16[64,1536]{1,0:T(8,128)(2,1)S(1)} collective-permute-done((bf16[64,1536]{1,0:T(8,128)(2,1)S(1)}, bf16[64,1536]{1,0:T(8,128)(2,1)S(1)}, u32[]{:S(2)}, u32[]{:S(2)}) %collective-permute-start.36) | collective-permute-done | bytes 196640 | tf_op jit(solution)/shard_map/ppermute | solution.py:125
  142.3 4.4 %collective-permute-done.34 = bf16[64,1536]{1,0:T(8,128)(2,1)} collective-permute-done((bf16[64,1536]{1,0:T(8,128)(2,1)S(1)}, bf16[64,1536]{1,0:T(8,128)(2,1)}, u32[]{:S(2)}, u32[]{:S(2)}) %collective-permute-start.34) | collective-permute-done | bytes 196640 | tf_op jit(solution)/shard_map/ppermute | solution.py:125
  147.8 2.7 %fusion.62 = (bf16[256,768]{1,0:T(8,128)(2,1)S(1)}, f32[256,768]{1,0:T(8,128)}) fusion(bf16[768,384]{1,0:T(8,128)(2,1)} %copy-done.12, bf16[768,384]{1,0:T(8,128)(2,1)S(1)} %copy-done.11, bf16[256,1536]{1,0:T(8,128)(2,1)S(1)} %pad_maximum_fusion.6.both_ref), kind=kOutput, calls=%fused_computation.213 | convolution fusion | flops 304545792 | bytes 2752512 | tf_op jit(solution)/shard_map/dot_general | solution.py:33
  151.3 1.8 fusion
  153.1 1.8 convolution_convert_fusion.1
  156.3 2.2 collective-permute-start.39
  158.5 3.3 %lower_back.1 = bf16[768,960]{1,0:T(8,128)(2,1)} custom-call(s32[1]{0:T(128)S(6)} %add.437.flag_ref, bf16[256,768]{1,0:T(8,128)(2,1)} %copy-done.17, bf16[256,768]{1,0:T(8,128)(2,1)} %copy-done.4, bf16[256,1536]{1,0:T(8,128)(2,1)} %copy-done.3), custom_call_target="tpu_custom_call" | custom-call | tf_op jit(solution)/shard_map/lower_back/pallas_call | solution.py:446
  161.8 2.4 dynamic-slice_bitcast_fusion
  171.6 13.0 %attend_back.1 = (bf16[768,768]{1,0:T(8,128)(2,1)}, bf16[768,768]{1,0:T(8,128)(2,1)}, bf16[2048,768]{1,0:T(8,128)(2,1)}, bf16[128,384]{1,0:T(8,128)(2,1)}, bf16[640,128]{1,0:T(8,128)(2,1)}) custom-call(s32[1]{0:T(128)} %bitcast.core_ref, bf16[128,768]{1,0:T(8,128)(2,1)} %copy-done.8, bf16[128,384]{1,0:T(8,128)(2,1)} %convolution_convert_fusion.4.d_att_ref, ...), custom_call_target="tpu_custom_call" | custom-call | tf_op jit(solution)/shard_map/attend_back/pallas_call | solution.py:401
  191.6 2.0 collective-permute-start.46
  193.6 6.1 %collective-permute-done.46.d_att_far_ref = bf16[128,384]{1,0:T(8,128)(2,1)S(1)} collective-permute-done((bf16[128,384]{1,0:T(8,128)(2,1)S(1)}, bf16[128,384]{1,0:T(8,128)(2,1)S(1)}, u32[]{:S(2)}, u32[]{:S(2)}) %collective-permute-start.46) | collective-permute-done | bytes 98336 | tf_op jit(solution)/shard_map/ppermute | solution.py:125
  200.5 10.6 %captions_back.2.refs_0_ = f32[2048,768]{1,0:T(8,128)} custom-call(s32[1]{0:T(128)} %bitcast.9.group_ref, s32[128,1]{1,0:T(8,128)} %copy.37.ends_ref, bf16[2048,768]{1,0:T(8,128)(2,1)} %get-tuple-element.122.unit_ref, f32[2048,128]{1,0:T(8,128)} %get-tuple-element.158.scale_ref, f32[128,768]{1,0:T(8,128)} %get-tuple-element.189.d_mid_ref, ...), custom_call_target="tpu_custom_call" | custom-call | tf_op jit(solution)/shard_map/captions_back/pallas_call | solution.py:549
  214.4 2.5 %collective-permute-start.50 = (bf16[96,960]{1,0:T(8,128)(2,1)S(1)}, bf16[96,960]{1,0:T(8,128)(2,1)S(1)}, u32[]{:S(2)}, u32[]{:S(2)}) collective-permute-start(bf16[96,960]{1,0:T(8,128)(2,1)S(1)} %get-tuple-element.221), channel_id=1, source_target_pairs={{0,16},{2,18},{4,20},{6,22},{8,24},{10,26},{12,28},{14,30},{16,0},... | collective-permute-start | bytes 552968 | tf_op jit(solution)/shard_map/ppermute | solution.py:95
  219.5 10.6 %captions_back.3 = f32[2048,768]{1,0:T(8,128)} custom-call(s32[1]{0:T(128)} %bitcast.9.group_ref, s32[128,1]{1,0:T(8,128)} %copy.37.ends_ref, bf16[2048,768]{1,0:T(8,128)(2,1)} %get-tuple-element.122.unit_ref, f32[2048,128]{1,0:T(8,128)} %get-tuple-element.158.scale_ref, f32[128,768]{1,0:T(8,128)} %get-tuple-element.189.d_mid_ref, ...), custom_call_target="tpu_custom_call", output_to_operand_aliasing={{}: (14, {})} | custom-call | tf_op jit(solution)/shard_map/captions_back/pallas_call | solution.py:549
  231.6 6.5 %collective-permute-done.51 = bf16[96,768]{1,0:T(8,128)(2,1)S(1)} collective-permute-done((bf16[96,768]{1,0:T(8,128)(2,1)S(1)}, bf16[96,768]{1,0:T(8,128)(2,1)S(1)}, u32[]{:S(2)}, u32[]{:S(2)}) %collective-permute-start.51) | collective-permute-done | bytes 147488 | tf_op jit(solution)/shard_map/ppermute | solution.py:95
  242.4 1.5 collective-permute-start.54
  (295 shorter events, 70.1 us)
Async XLA Ops:
  2.7 8.2 %collective-permute-start = (bf16[48,768]{1,0:T(8,128)(2,1)}, bf16[48,768]{1,0:T(8,128)(2,1)S(1)}, u32[]{:S(2)}, u32[]{:S(2)}) collective-permute-start(bf16[48,768]{1,0:T(8,128)(2,1)} %get-tuple-element.96), channel_id=1, source_target_pairs={{0,2},{2,0},{4,6},{6,4},{8,10},{10,8},{12,14},{14,12},{16,18},{18,... | collective-permute-start | bytes 221192 | tf_op jit(solution)/shard_map/ppermute | solution.py:54
  10.8 12.9 %collective-permute-start.3 = (bf16[96,768]{1,0:T(8,128)(2,1)S(1)}, bf16[96,768]{1,0:T(8,128)(2,1)S(1)}, u32[]{:S(2)}, u32[]{:S(2)}) collective-permute-start(bf16[96,768]{1,0:T(8,128)(2,1)S(1)} %bitcast.223), channel_id=1, source_target_pairs={{0,4},{2,6},{4,0},{6,2},{8,12},{10,14},{12,8},{14,10},{16,20},{18,... | collective-permute-start | bytes 442376 | tf_op jit(solution)/shard_map/ppermute | solution.py:57
  13.4 10.3 %collective-permute-start.2 = (bf16[96,768]{1,0:T(8,128)(2,1)S(1)}, bf16[96,768]{1,0:T(8,128)(2,1)S(1)}, u32[]{:S(2)}, u32[]{:S(2)}) collective-permute-start(bf16[96,768]{1,0:T(8,128)(2,1)S(1)} %bitcast.224), channel_id=1, source_target_pairs={{0,24},{2,26},{4,28},{6,30},{8,0},{10,2},{12,4},{14,6},{16,8},{18,... | collective-permute-start | bytes 442376 | tf_op jit(solution)/shard_map/ppermute | solution.py:60
  17.0 7.6 %collective-permute-start.1 = (bf16[96,768]{1,0:T(8,128)(2,1)S(1)}, bf16[96,768]{1,0:T(8,128)(2,1)S(1)}, u32[]{:S(2)}, u32[]{:S(2)}) collective-permute-start(bf16[96,768]{1,0:T(8,128)(2,1)S(1)} %bitcast.225), channel_id=1, source_target_pairs={{0,8},{2,10},{4,12},{6,14},{8,16},{10,18},{12,20},{14,22},{16,24},... | collective-permute-start | bytes 442376 | tf_op jit(solution)/shard_map/ppermute | solution.py:60
  18.6 17.2 %all-to-all-start = ((bf16[16,8,768]{2,1,0:T(8,128)(2,1)}), bf16[16,8,768]{2,1,0:T(8,128)(2,1)S(1)}, u32[]{:S(2)}, u32[]{:S(2)}) async-start(bf16[16,8,768]{2,1,0:T(8,128)(2,1)} %fusion.1), calls=%async_computation | async-start | bytes 393216 | tf_op jit(solution)/shard_map/all_to_all | solution.py:622
  24.5 11.2 %collective-permute-start.5 = (bf16[96,768]{1,0:T(8,128)(2,1)S(1)}, bf16[96,768]{1,0:T(8,128)(2,1)S(1)}, u32[]{:S(2)}, u32[]{:S(2)}) collective-permute-start(bf16[96,768]{1,0:T(8,128)(2,1)S(1)} %collective-permute-done.1), channel_id=1, source_target_pairs={{0,4},{2,6},{4,0},{6,2},{8,12},{10,14},{12,8},{14,10},{16,20},{18,... | collective-permute-start | bytes 442376 | tf_op jit(solution)/shard_map/ppermute | solution.py:57
  25.7 10.1 %collective-permute-start.4 = (bf16[96,768]{1,0:T(8,128)(2,1)S(1)}, bf16[96,768]{1,0:T(8,128)(2,1)S(1)}, u32[]{:S(2)}, u32[]{:S(2)}) collective-permute-start(bf16[96,768]{1,0:T(8,128)(2,1)S(1)} %collective-permute-done.1), channel_id=1, source_target_pairs={{0,8},{2,10},{4,12},{6,14},{8,16},{10,18},{12,20},{14,22},{16,24},... | collective-permute-start | bytes 442376 | tf_op jit(solution)/shard_map/ppermute | solution.py:60
  27.2 8.6 %collective-permute-start.6 = (bf16[96,768]{1,0:T(8,128)(2,1)S(1)}, bf16[96,768]{1,0:T(8,128)(2,1)S(1)}, u32[]{:S(2)}, u32[]{:S(2)}) collective-permute-start(bf16[96,768]{1,0:T(8,128)(2,1)S(1)} %collective-permute-done.2), channel_id=1, source_target_pairs={{0,4},{2,6},{4,0},{6,2},{8,12},{10,14},{12,8},{14,10},{16,20},{18,... | collective-permute-start | bytes 442376 | tf_op jit(solution)/shard_map/ppermute | solution.py:57
  36.1 5.2 %collective-permute-start.7 = (bf16[96,768]{1,0:T(8,128)(2,1)S(1)}, bf16[96,768]{1,0:T(8,128)(2,1)S(1)}, u32[]{:S(2)}, u32[]{:S(2)}) collective-permute-start(bf16[96,768]{1,0:T(8,128)(2,1)S(1)} %collective-permute-done.4), channel_id=1, source_target_pairs={{0,4},{2,6},{4,0},{6,2},{8,12},{10,14},{12,8},{14,10},{16,20},{18,... | collective-permute-start | bytes 442376 | tf_op jit(solution)/shard_map/ppermute | solution.py:57
  41.6 31.9 %collective-permute-start.15 = (bf16[768,768]{1,0:T(8,128)(2,1)S(1)}, bf16[768,768]{1,0:T(8,128)(2,1)}, u32[]{:S(2)}, u32[]{:S(2)}) collective-permute-start(bf16[768,768]{1,0:T(8,128)(2,1)S(1)} %bitcast.204), channel_id=1, source_target_pairs={{0,1},{1,0},{2,3},{3,2},{4,5},{5,4},{6,7},{7,6},{8,9},{9,8},{10,11... | collective-permute-start | bytes 3538952 | tf_op jit(solution)/shard_map/ppermute | solution.py:125
  43.2 30.3 %collective-permute-start.13 = (bf16[96,2432]{1,0:T(8,128)(2,1)S(1)}, bf16[96,2432]{1,0:T(8,128)(2,1)}, u32[]{:S(2)}, u32[]{:S(2)}) collective-permute-start(bf16[96,2432]{1,0:T(8,128)(2,1)S(1)} %bitcast.207), channel_id=1, source_target_pairs={{0,4},{2,6},{4,0},{6,2},{8,12},{10,14},{12,8},{14,10},{16,20},{18,... | collective-permute-start | bytes 1400840 | tf_op jit(solution)/shard_map/ppermute | solution.py:57
  44.3 14.4 %collective-permute-start.10 = (bf16[96,2432]{1,0:T(8,128)(2,1)S(1)}, bf16[96,2432]{1,0:T(8,128)(2,1)}, u32[]{:S(2)}, u32[]{:S(2)}) collective-permute-start(bf16[96,2432]{1,0:T(8,128)(2,1)S(1)} %bitcast.208), channel_id=1, source_target_pairs={{0,8},{2,10},{4,12},{6,14},{8,16},{10,18},{12,20},{14,22},{16,24},... | collective-permute-start | bytes 1400840 | tf_op jit(solution)/shard_map/ppermute | solution.py:60
  58.7 14.7 %collective-permute-start.14 = (bf16[96,2432]{1,0:T(8,128)(2,1)}, bf16[96,2432]{1,0:T(8,128)(2,1)}, u32[]{:S(2)}, u32[]{:S(2)}) collective-permute-start(bf16[96,2432]{1,0:T(8,128)(2,1)} %collective-permute-done.10), channel_id=1, source_target_pairs={{0,4},{2,6},{4,0},{6,2},{8,12},{10,14},{12,8},{14,10},{16,20},{18,... | collective-permute-start | bytes 1400840 | tf_op jit(solution)/shard_map/ppermute | solution.py:57
  59.7 13.8 %collective-permute-start.12 = (bf16[96,2432]{1,0:T(8,128)(2,1)}, bf16[96,2432]{1,0:T(8,128)(2,1)}, u32[]{:S(2)}, u32[]{:S(2)}) collective-permute-start(bf16[96,2432]{1,0:T(8,128)(2,1)} %collective-permute-done.10), channel_id=1, source_target_pairs={{0,8},{2,10},{4,12},{6,14},{8,16},{10,18},{12,20},{14,22},{16,24},... | collective-permute-start | bytes 1400840 | tf_op jit(solution)/shard_map/ppermute | solution.py:60
  73.5 15.1 %collective-permute-start.20 = (bf16[128,768]{1,0:T(8,128)(2,1)}, bf16[128,768]{1,0:T(8,128)(2,1)S(1)}, u32[]{:S(2)}, u32[]{:S(2)}) collective-permute-start(bf16[128,768]{1,0:T(8,128)(2,1)} %get-tuple-element.132), channel_id=1, source_target_pairs={{0,3},{1,2},{2,1},{3,0},{4,7},{5,6},{6,5},{7,4},{8,11},{9,10},{10,... | collective-permute-start | bytes 589832 | tf_op jit(solution)/shard_map/ppermute | solution.py:125
  73.5 15.1 %collective-permute-start.19 = (bf16[128,768]{1,0:T(8,128)(2,1)}, bf16[128,768]{1,0:T(8,128)(2,1)S(1)}, u32[]{:S(2)}, u32[]{:S(2)}) collective-permute-start(bf16[128,768]{1,0:T(8,128)(2,1)} %get-tuple-element.132), channel_id=1, source_target_pairs={{0,2},{1,3},{2,0},{3,1},{4,6},{5,7},{6,4},{7,5},{8,10},{9,11},{10,... | collective-permute-start | bytes 589832 | tf_op jit(solution)/shard_map/ppermute | solution.py:125
  74.1 15.1 %collective-permute-start.18 = (bf16[128,768]{1,0:T(8,128)(2,1)}, bf16[128,768]{1,0:T(8,128)(2,1)S(1)}, u32[]{:S(2)}, u32[]{:S(2)}) collective-permute-start(bf16[128,768]{1,0:T(8,128)(2,1)} %get-tuple-element.132), channel_id=1, source_target_pairs={{0,1},{1,0},{2,3},{3,2},{4,5},{5,4},{6,7},{7,6},{8,9},{9,8},{10,11... | collective-permute-start | bytes 589832 | tf_op jit(solution)/shard_map/ppermute | solution.py:125
  75.7 13.5 %collective-permute-start.17 = (bf16[96,2432]{1,0:T(8,128)(2,1)}, bf16[96,2432]{1,0:T(8,128)(2,1)S(1)}, u32[]{:S(2)}, u32[]{:S(2)}) collective-permute-start(bf16[96,2432]{1,0:T(8,128)(2,1)} %collective-permute-done.12), channel_id=1, source_target_pairs={{0,4},{2,6},{4,0},{6,2},{8,12},{10,14},{12,8},{14,10},{16,20},{18,... | collective-permute-start | bytes 1400840 | tf_op jit(solution)/shard_map/ppermute | solution.py:57
  76.7 14.4 %collective-permute-start.16 = (bf16[96,2432]{1,0:T(8,128)(2,1)}, bf16[96,2432]{1,0:T(8,128)(2,1)S(1)}, u32[]{:S(2)}, u32[]{:S(2)}) collective-permute-start(bf16[96,2432]{1,0:T(8,128)(2,1)} %collective-permute-done.12), channel_id=1, source_target_pairs={{0,8},{2,10},{4,12},{6,14},{8,16},{10,18},{12,20},{14,22},{16,24},... | collective-permute-start | bytes 1400840 | tf_op jit(solution)/shard_map/ppermute | solution.py:60
  88.5 5.0 %collective-permute-start.23 = (bf16[768,768]{1,0:T(8,128)(2,1)}, bf16[768,768]{1,0:T(8,128)(2,1)S(1)}, u32[]{:S(2)}, u32[]{:S(2)}) collective-permute-start(bf16[768,768]{1,0:T(8,128)(2,1)} %collective-permute-done.15), channel_id=1, source_target_pairs={{0,2},{2,0},{4,6},{6,4},{8,10},{10,8},{12,14},{14,12},{16,18},{18,... | collective-permute-start | bytes 3538952 | tf_op jit(solution)/shard_map/ppermute | solution.py:54
  88.6 7.8 %collective-permute-start.22 = (bf16[128,384]{1,0:T(8,128)(2,1)S(1)}, bf16[128,384]{1,0:T(8,128)(2,1)S(1)}, u32[]{:S(2)}, u32[]{:S(2)}) collective-permute-start(bf16[128,384]{1,0:T(8,128)(2,1)S(1)} %copy-done.25), channel_id=1, source_target_pairs={{0,1},{1,0},{2,3},{3,2},{4,5},{5,4},{6,7},{7,6},{8,9},{9,8},{10,11... | collective-permute-start | bytes 294920 | tf_op jit(solution)/shard_map/ppermute | solution.py:125
  91.4 11.5 %collective-permute-start.21 = (bf16[96,2432]{1,0:T(8,128)(2,1)S(1)}, bf16[96,2432]{1,0:T(8,128)(2,1)S(1)}, u32[]{:S(2)}, u32[]{:S(2)}) collective-permute-start(bf16[96,2432]{1,0:T(8,128)(2,1)S(1)} %collective-permute-done.16), channel_id=1, source_target_pairs={{0,4},{2,6},{4,0},{6,2},{8,12},{10,14},{12,8},{14,10},{16,20},{18,... | collective-permute-start | bytes 1400840 | tf_op jit(solution)/shard_map/ppermute | solution.py:57
  103.7 11.6 %collective-permute-start.27 = (bf16[768,896]{1,0:T(8,128)(2,1)S(1)}, bf16[768,896]{1,0:T(8,128)(2,1)S(1)}, u32[]{:S(2)}, u32[]{:S(2)}) collective-permute-start(bf16[768,896]{1,0:T(8,128)(2,1)S(1)} %bitcast.199), channel_id=1, source_target_pairs={{0,2},{2,0},{4,6},{6,4},{8,10},{10,8},{12,14},{14,12},{16,18},{18,... | collective-permute-start | bytes 4128776 | tf_op jit(solution)/shard_map/ppermute | solution.py:54
  108.3 5.7 %collective-permute-start.24 = (bf16[64,768]{1,0:T(8,128)(2,1)S(1)}, bf16[64,768]{1,0:T(8,128)(2,1)S(1)}, u32[]{:S(2)}, u32[]{:S(2)}) collective-permute-start(bf16[64,768]{1,0:T(8,128)(2,1)S(1)} %get-tuple-element.225), channel_id=1, source_target_pairs={{0,1},{1,0},{2,3},{3,2},{4,5},{5,4},{6,7},{7,6},{8,9},{9,8},{10,11... | collective-permute-start | bytes 294920 | tf_op jit(solution)/shard_map/ppermute | solution.py:125
  109.3 5.9 %collective-permute-start.26 = (bf16[64,768]{1,0:T(8,128)(2,1)S(1)}, bf16[64,768]{1,0:T(8,128)(2,1)S(1)}, u32[]{:S(2)}, u32[]{:S(2)}) collective-permute-start(bf16[64,768]{1,0:T(8,128)(2,1)S(1)} %get-tuple-element.226), channel_id=1, source_target_pairs={{0,3},{1,2},{2,1},{3,0},{4,7},{5,6},{6,5},{7,4},{8,11},{9,10},{10,... | collective-permute-start | bytes 294920 | tf_op jit(solution)/shard_map/ppermute | solution.py:125
  110.2 5.0 %collective-permute-start.25 = (bf16[64,768]{1,0:T(8,128)(2,1)S(1)}, bf16[64,768]{1,0:T(8,128)(2,1)S(1)}, u32[]{:S(2)}, u32[]{:S(2)}) collective-permute-start(bf16[64,768]{1,0:T(8,128)(2,1)S(1)} %get-tuple-element.227), channel_id=1, source_target_pairs={{0,2},{1,3},{2,0},{3,1},{4,6},{5,7},{6,4},{7,5},{8,10},{9,11},{10,... | collective-permute-start | bytes 294920 | tf_op jit(solution)/shard_map/ppermute | solution.py:125
  125.1 4.8 %collective-permute-start.33 = (f32[9,128]{1,0:T(8,128)S(1)}, f32[9,128]{1,0:T(8,128)S(1)}, u32[]{:S(2)}, u32[]{:S(2)}) collective-permute-start(f32[9,128]{1,0:T(8,128)S(1)} %add_add_fusion.2), channel_id=1, source_target_pairs={{0,24},{2,26},{4,28},{6,30},{8,0},{10,2},{12,4},{14,6},{16,8},{18,... | collective-permute-start | bytes 13832 | tf_op jit(solution)/shard_map/ppermute | solution.py:60
  127.9 5.4 %collective-permute-start.31 = (f32[9,128]{1,0:T(8,128)S(1)}, f32[9,128]{1,0:T(8,128)S(1)}, u32[]{:S(2)}, u32[]{:S(2)}) collective-permute-start(f32[9,128]{1,0:T(8,128)S(1)} %add_add_fusion.2), channel_id=1, source_target_pairs={{0,8},{2,10},{4,12},{6,14},{8,16},{10,18},{12,20},{14,22},{16,24},... | collective-permute-start | bytes 13832 | tf_op jit(solution)/shard_map/ppermute | solution.py:60
  135.1 7.2 %collective-permute-start.36 = (bf16[64,1536]{1,0:T(8,128)(2,1)S(1)}, bf16[64,1536]{1,0:T(8,128)(2,1)S(1)}, u32[]{:S(2)}, u32[]{:S(2)}) collective-permute-start(bf16[64,1536]{1,0:T(8,128)(2,1)S(1)} %pad_maximum_fusion.12), channel_id=1, source_target_pairs={{0,3},{1,2},{2,1},{3,0},{4,7},{5,6},{6,5},{7,4},{8,11},{9,10},{10,... | collective-permute-start | bytes 589832 | tf_op jit(solution)/shard_map/ppermute | solution.py:125
  135.2 7.1 %collective-permute-start.35 = (bf16[64,1536]{1,0:T(8,128)(2,1)S(1)}, bf16[64,1536]{1,0:T(8,128)(2,1)}, u32[]{:S(2)}, u32[]{:S(2)}) collective-permute-start(bf16[64,1536]{1,0:T(8,128)(2,1)S(1)} %pad_maximum_fusion.12), channel_id=1, source_target_pairs={{0,2},{1,3},{2,0},{3,1},{4,6},{5,7},{6,4},{7,5},{8,10},{9,11},{10,... | collective-permute-start | bytes 589832 | tf_op jit(solution)/shard_map/ppermute | solution.py:125
  136.8 9.9 %collective-permute-start.34 = (bf16[64,1536]{1,0:T(8,128)(2,1)S(1)}, bf16[64,1536]{1,0:T(8,128)(2,1)}, u32[]{:S(2)}, u32[]{:S(2)}) collective-permute-start(bf16[64,1536]{1,0:T(8,128)(2,1)S(1)} %pad_maximum_fusion.12), channel_id=1, source_target_pairs={{0,1},{1,0},{2,3},{3,2},{4,5},{5,4},{6,7},{7,6},{8,9},{9,8},{10,11... | collective-permute-start | bytes 589832 | tf_op jit(solution)/shard_map/ppermute | solution.py:125
  155.8 12.7 %collective-permute-start.41 = (bf16[128,768]{1,0:T(8,128)(2,1)}, bf16[128,768]{1,0:T(8,128)(2,1)S(1)}, u32[]{:S(2)}, u32[]{:S(2)}) collective-permute-start(bf16[128,768]{1,0:T(8,128)(2,1)} %get-tuple-element.224), channel_id=1, source_target_pairs={{0,3},{1,2},{2,1},{3,0},{4,7},{5,6},{6,5},{7,4},{8,11},{9,10},{10,... | collective-permute-start | bytes 589832 | tf_op jit(solution)/shard_map/ppermute | solution.py:125
  155.8 12.7 %collective-permute-start.40 = (bf16[128,768]{1,0:T(8,128)(2,1)}, bf16[128,768]{1,0:T(8,128)(2,1)}, u32[]{:S(2)}, u32[]{:S(2)}) collective-permute-start(bf16[128,768]{1,0:T(8,128)(2,1)} %get-tuple-element.224), channel_id=1, source_target_pairs={{0,2},{1,3},{2,0},{3,1},{4,6},{5,7},{6,4},{7,5},{8,10},{9,11},{10,... | collective-permute-start | bytes 589832 | tf_op jit(solution)/shard_map/ppermute | solution.py:125
  156.3 11.2 %collective-permute-start.39 = (bf16[128,768]{1,0:T(8,128)(2,1)}, bf16[128,768]{1,0:T(8,128)(2,1)}, u32[]{:S(2)}, u32[]{:S(2)}) collective-permute-start(bf16[128,768]{1,0:T(8,128)(2,1)} %get-tuple-element.223), channel_id=1, source_target_pairs={{0,1},{1,0},{2,3},{3,2},{4,5},{5,4},{6,7},{7,6},{8,9},{9,8},{10,11... | collective-permute-start | bytes 589832 | tf_op jit(solution)/shard_map/ppermute | solution.py:125
  164.3 20.3 %collective-permute-start.38 = (bf16[2,2,96,960]{3,2,1,0:T(8,128)(2,1)}, bf16[2,2,96,960]{3,2,1,0:T(8,128)(2,1)}, u32[]{:S(2)}, u32[]{:S(2)}) collective-permute-start(bf16[2,2,96,960]{3,2,1,0:T(8,128)(2,1)} %get-tuple-element.199), channel_id=1, source_target_pairs={{0,4},{2,6},{4,0},{6,2},{8,12},{10,14},{12,8},{14,10},{16,20},{18,... | collective-permute-start | bytes 2211848 | tf_op jit(solution)/shard_map/ppermute | solution.py:95
  166.2 18.4 %collective-permute-start.37 = (bf16[2,2,96,768]{3,2,1,0:T(8,128)(2,1)}, bf16[2,2,96,768]{3,2,1,0:T(8,128)(2,1)}, u32[]{:S(2)}, u32[]{:S(2)}) collective-permute-start(bf16[2,2,96,768]{3,2,1,0:T(8,128)(2,1)} %get-tuple-element.207), channel_id=1, source_target_pairs={{0,8},{2,10},{4,12},{6,14},{8,0},{10,2},{12,4},{14,6},{16,24},{18,... | collective-permute-start | bytes 1769480 | tf_op jit(solution)/shard_map/ppermute | solution.py:95
  187.0 24.1 %collective-permute-start.43 = (bf16[2,96,960]{2,1,0:T(8,128)(2,1)}, bf16[2,96,960]{2,1,0:T(8,128)(2,1)}, u32[]{:S(2)}, u32[]{:S(2)}) collective-permute-start(bf16[2,96,960]{2,1,0:T(8,128)(2,1)} %get-tuple-element.209), channel_id=1, source_target_pairs={{0,8},{2,10},{4,12},{6,14},{8,0},{10,2},{12,4},{14,6},{16,24},{18,... | collective-permute-start | bytes 1105928 | tf_op jit(solution)/shard_map/ppermute | solution.py:95
  188.2 22.9 %collective-permute-start.45 = (bf16[2,2,96,768]{3,2,1,0:T(8,128)(2,1)S(1)}, bf16[2,2,96,768]{3,2,1,0:T(8,128)(2,1)S(1)}, u32[]{:S(2)}, u32[]{:S(2)}) collective-permute-start(bf16[2,2,96,768]{3,2,1,0:T(8,128)(2,1)S(1)} %get-tuple-element.205), channel_id=1, source_target_pairs={{0,4},{2,6},{4,0},{6,2},{8,12},{10,14},{12,8},{14,10},{16,20},{18,... | collective-permute-start | bytes 1769480 | tf_op jit(solution)/shard_map/ppermute | solution.py:95
  190.5 20.6 %collective-permute-start.42 = (bf16[2,96,768]{2,1,0:T(8,128)(2,1)S(1)}, bf16[2,96,768]{2,1,0:T(8,128)(2,1)S(1)}, u32[]{:S(2)}, u32[]{:S(2)}) collective-permute-start(bf16[2,96,768]{2,1,0:T(8,128)(2,1)S(1)} %get-tuple-element.215), channel_id=1, source_target_pairs={{0,4},{2,6},{4,0},{6,2},{8,12},{10,14},{12,8},{14,10},{16,20},{18,... | collective-permute-start | bytes 884744 | tf_op jit(solution)/shard_map/ppermute | solution.py:95
  191.6 8.2 %collective-permute-start.47 = (bf16[640,128]{1,0:T(8,128)(2,1)}, bf16[640,128]{1,0:T(8,128)(2,1)S(1)}, u32[]{:S(2)}, u32[]{:S(2)}) collective-permute-start(bf16[640,128]{1,0:T(8,128)(2,1)} %get-tuple-element.163), channel_id=1, source_target_pairs={{0,1},{1,0},{2,3},{3,2},{4,5},{5,4},{6,7},{7,6},{8,9},{9,8},{10,11... | collective-permute-start | bytes 491528 | tf_op jit(solution)/shard_map/ppermute | solution.py:125
  191.6 8.1 %collective-permute-start.46 = (bf16[128,384]{1,0:T(8,128)(2,1)S(1)}, bf16[128,384]{1,0:T(8,128)(2,1)S(1)}, u32[]{:S(2)}, u32[]{:S(2)}) collective-permute-start(bf16[128,384]{1,0:T(8,128)(2,1)S(1)} %copy-done.26), channel_id=1, source_target_pairs={{0,1},{1,0},{2,3},{3,2},{4,5},{5,4},{6,7},{7,6},{8,9},{9,8},{10,11... | collective-permute-start | bytes 294920 | tf_op jit(solution)/shard_map/ppermute | solution.py:125
  211.4 18.7 %collective-permute-start.49 = (bf16[96,768]{1,0:T(8,128)(2,1)S(1)}, bf16[96,768]{1,0:T(8,128)(2,1)S(1)}, u32[]{:S(2)}, u32[]{:S(2)}) collective-permute-start(bf16[96,768]{1,0:T(8,128)(2,1)S(1)} %get-tuple-element.230), channel_id=1, source_target_pairs={{0,16},{2,18},{4,20},{6,22},{8,24},{10,26},{12,28},{14,30},{16,0},... | collective-permute-start | bytes 442376 | tf_op jit(solution)/shard_map/ppermute | solution.py:95
  212.0 18.1 %collective-permute-start.48 = (bf16[2,96,768]{2,1,0:T(8,128)(2,1)S(1)}, bf16[2,96,768]{2,1,0:T(8,128)(2,1)S(1)}, u32[]{:S(2)}, u32[]{:S(2)}) collective-permute-start(bf16[2,96,768]{2,1,0:T(8,128)(2,1)S(1)} %get-tuple-element.213), channel_id=1, source_target_pairs={{0,8},{2,10},{4,12},{6,14},{8,0},{10,2},{12,4},{14,6},{16,24},{18,... | collective-permute-start | bytes 884744 | tf_op jit(solution)/shard_map/ppermute | solution.py:95
  214.4 15.7 %collective-permute-start.50 = (bf16[96,960]{1,0:T(8,128)(2,1)S(1)}, bf16[96,960]{1,0:T(8,128)(2,1)S(1)}, u32[]{:S(2)}, u32[]{:S(2)}) collective-permute-start(bf16[96,960]{1,0:T(8,128)(2,1)S(1)} %get-tuple-element.221), channel_id=1, source_target_pairs={{0,16},{2,18},{4,20},{6,22},{8,24},{10,26},{12,28},{14,30},{16,0},... | collective-permute-start | bytes 552968 | tf_op jit(solution)/shard_map/ppermute | solution.py:95
  230.2 7.8 %collective-permute-start.51 = (bf16[96,768]{1,0:T(8,128)(2,1)S(1)}, bf16[96,768]{1,0:T(8,128)(2,1)S(1)}, u32[]{:S(2)}, u32[]{:S(2)}) collective-permute-start(bf16[96,768]{1,0:T(8,128)(2,1)S(1)} %dynamic-slice_bitcast_fusion.17), channel_id=1, source_target_pairs={{0,16},{2,18},{4,20},{6,22},{8,24},{10,26},{12,28},{14,30},{16,0},... | collective-permute-start | bytes 442376 | tf_op jit(solution)/shard_map/ppermute | solution.py:95
  230.9 7.3 %collective-permute-start.53 = (f32[48,768]{1,0:T(8,128)S(1)}, f32[48,768]{1,0:T(8,128)S(1)}, u32[]{:S(2)}, u32[]{:S(2)}) collective-permute-start(f32[48,768]{1,0:T(8,128)S(1)} %dynamic-slice_bitcast_fusion.15), channel_id=1, source_target_pairs={{0,2},{2,0},{4,6},{6,4},{8,10},{10,8},{12,14},{14,12},{16,18},{18,... | collective-permute-start | bytes 442376 | tf_op jit(solution)/shard_map/ppermute | solution.py:54
  231.0 8.2 %collective-permute-start.55 = (f32[48,960]{1,0:T(8,128)S(1)}, f32[48,960]{1,0:T(8,128)S(1)}, u32[]{:S(2)}, u32[]{:S(2)}) collective-permute-start(f32[48,960]{1,0:T(8,128)S(1)} %dynamic-slice_bitcast_fusion.12), channel_id=1, source_target_pairs={{0,2},{2,0},{4,6},{6,4},{8,10},{10,8},{12,14},{14,12},{16,18},{18,... | collective-permute-start | bytes 552968 | tf_op jit(solution)/shard_map/ppermute | solution.py:54
  239.4 4.7 %collective-permute-start.56 = (f32[48,384]{1,0:T(8,128)S(1)}, f32[48,384]{1,0:T(8,128)S(1)}, u32[]{:S(2)}, u32[]{:S(2)}) collective-permute-start(f32[48,384]{1,0:T(8,128)S(1)} %pad_maximum_fusion.13), channel_id=1, source_target_pairs={{0,1},{1,0},{2,3},{3,2},{4,5},{5,4},{6,7},{7,6},{8,9},{9,8},{10,11... | collective-permute-start | bytes 221192 | tf_op jit(solution)/shard_map/ppermute | solution.py:125
  (45 other events, 238.4 us)

commit v4 on v3

--- a/solution.py
+++ b/solution.py
@@ -17,7 +17,7 @@
 WIDTH = 768
 HEADS_HERE = 6
 COLS = HEADS_HERE * HEAD
-BLOCK = 16
+BLOCK = 32
 TOKENS = BLOCK * LENGTH
 STACK = HEADS_HERE * BLOCK
 
@@ -77,9 +77,10 @@
             ]
         return wholes
 
-    def empty(self, rows, cuts):
+    def empty(self, rows, cuts, start_of):
+        zero = after(jnp.zeros((), low), start_of)
         return [
-            jnp.zeros((self.count // 2, rows, end - start), low)
+            jnp.broadcast_to(zero, (self.count // 2, rows, end - start))
             for start, end in zip(cuts, cuts[1:])
         ]
 
@@ -110,14 +111,8 @@
         arrived = self.swap_core(lax.dynamic_index_in_dim(total, 1 - self.core, 0, False))
         return pick(self.core, mine, arrived), pick(self.core, arrived, mine)
 
-    def total(self, x):
-        if not self.fast:
-            return lax.psum(x, "dp")
-        x = (x + self.swap_core(x)) + (self.swap_side(x) + self.swap_both(x))
-        return x + sum(self.shift_depth(x, step) for step in range(1, 4))
-
-    def swap_both(self, x):
-        return lax.ppermute(x, "dp", [(i, i ^ 3) for i in range(self.count)])
+    def flip(self, x, bits):
+        return lax.ppermute(x, "dp", [(i, i ^ bits) for i in range(self.count)])
 
 
 def swap_near(x, flip):
@@ -164,6 +159,9 @@
     cumulative = 0.5 * (1.0 + lax.erf(raised * 0.7071067811865476))
     slope = cumulative + raised * jnp.exp(-0.5 * raised * raised) * 0.3989422804014327
     return raised * cumulative, slope
+
+
+LIMIT = pltpu.CompilerParams(vmem_limit_bytes=18 * 1024 * 1024)
 
 
 def whole_block(shape):
@@ -427,29 +425,31 @@
         ],
         scratch_shapes=[pltpu.VMEM((WIDTH, 2 * COLS), full)],
         name="attend_back",
+        compiler_params=LIMIT,
     )(core, d_mid, d_att, unit, unit_end, mixed, probs, queries, attended)
 
 
-def lower_back_body(flag_ref, d_out_ref, active_ref, both_ref, out_ref):
+def lower_back_body(flag_ref, d_out_ref, active_ref, pooled_ref, d_embed_ref, out_ref):
     hidden = active_ref.shape[1]
     quarter = WIDTH // 4
     out_ref[:, :hidden] = mm_tn(d_out_ref[...], active_ref[...]).astype(low)
-    here = both_ref[:, :quarter]
+    here = d_embed_ref[:, :quarter]
     for index in range(1, 4):
-        part = both_ref[:, index * quarter : (index + 1) * quarter]
+        part = d_embed_ref[:, index * quarter : (index + 1) * quarter]
         here = jnp.where(flag_ref[0] == index, part, here)
-    out_ref[:, hidden:] = mm_tn(both_ref[:, WIDTH:], here).astype(low)
-
-
-def lower_back(flag, d_out, active, both):
+    out_ref[:, hidden:] = mm_tn(pooled_ref[...], here).astype(low)
+
+
+def lower_back(flag, d_out, active, pooled, d_embed):
     vmem = pl.BlockSpec(memory_space=pltpu.VMEM)
     return pl.pallas_call(
         lower_back_body,
         out_shape=jax.ShapeDtypeStruct((WIDTH, active.shape[1] + WIDTH // 4), low),
-        in_specs=[pl.BlockSpec(memory_space=pltpu.SMEM)] + [vmem] * 3,
+        in_specs=[pl.BlockSpec(memory_space=pltpu.SMEM)] + [vmem] * 4,
         out_specs=vmem,
         name="lower_back",
-    )(flag, d_out, active, both)
+        compiler_params=LIMIT,
+    )(flag, d_out, active, pooled, d_embed)
 
 
 def place_rows(picks, rows):
@@ -600,8 +600,10 @@
         ln1_gain[None],
         ln2_gain[None],
     )
-    flipped = jnp.concatenate([end_pos, end_pos], 0)
-    ends = lax.dynamic_slice_in_dim(flipped, group * CAP_DEV, rows_dev, 0)[:, None]
+    def order_ends(end_pos):
+        flipped = jnp.concatenate([end_pos, end_pos], 0)
+        return lax.dynamic_slice_in_dim(flipped, group * CAP_DEV, rows_dev, 0)[:, None]
+
     wide = width // 2
 
     def pictures_of_batch(incoming):
@@ -612,19 +614,22 @@
         send = pick(core, pictures[:, wide:], pictures[:, :wide])
         return mine, send
 
-    cached = image_cache.astype(full)
-    cached = (cached * lax.rsqrt(jnp.sum(cached * cached, -1, keepdims=True) + 1e-06)).astype(low)
+    def prepare(image_cache):
+        cached = image_cache.astype(full)
+        norms = jnp.sum(cached * cached, -1, keepdims=True)
+        cached = (cached * lax.rsqrt(norms + 1e-06)).astype(low)
+        hand_out = (send_order[0][:, None] == places[None, :]).astype(low)
+        return mm(hand_out, cached).astype(low).reshape(spread, per_peer, width)
+
     places = jnp.arange(rows_dev, dtype=jnp.int32)
-    hand_out = (send_order[0][:, None] == places[None, :]).astype(low)
-    outgoing = mm(hand_out, cached).astype(low).reshape(spread, per_peer, width)
 
     def deal(outgoing):
         return lax.all_to_all(outgoing, "dp", split_axis=0, concat_axis=0, tiled=True)
 
-    def first_parts(stream):
+    def first_parts(stream, ends):
         return norm_first(group_flag, stream.reshape(rows_dev * length, width), ends)
 
-    def attention_of(kv, qo, parts):
+    def attention_of(kv, qo, parts, ends):
         return attend(parts[0], parts[2], ends, kv, qo)
 
     main = rows if plane.fast else CAP_DEV
@@ -638,31 +643,30 @@
         mix_cuts = (0, 2 * COLS)
         cuts = (0, 2 * hidden, 2 * hidden + 2 * wide + 128)
         arrived = plane.swap_core(packed[1])
-        arrived, outgoing = joint(arrived, outgoing)
+        arrived, cache = joint(arrived, image_cache)
         block = plane.join_cores(packed[0], arrived)
-        incoming = deal(outgoing)
+        outgoing = prepare(cache)
         up = plane.shift_depth(block, 1)
         down = plane.shift_depth(block, -1)
         across = plane.swap_side(block)
-        up, down, across, block = joint(up, down, across, block)
-
-        mixes = plane.place(plane.empty(2 * rows, mix_cuts), mix_cuts, 0, block, across)
+        up, down, across, block, outgoing = joint(up, down, across, block, outgoing)
+
+        incoming = deal(outgoing)
+        mixes = plane.place(plane.empty(2 * rows, mix_cuts, block), mix_cuts, 0, block, across)
         far = plane.shift_depth(up, 1)
         across_up = plane.swap_side(up)
         across_down = plane.swap_side(down)
-        parts = first_parts(after(captions, up))
-        far, across_up, across_down, incoming, *parts = joint(
-            far, across_up, across_down, incoming, *parts
-        )
+        far, across_up, across_down = joint(far, across_up, across_down)
 
         across = plane.swap_side(far)
         pictures = pictures_of_batch(incoming)
         mine = join(packed[2], packed[4], pictures[0])
         arrived = plane.swap_core(join(packed[3], packed[5], pictures[1]))
-        stream_near = swap_near(parts[3], 2)
         mixes = plane.place(mixes, mix_cuts, 1, up, across_up)
         mixes = plane.place(mixes, mix_cuts, -1, down, across_down)
-        across, arrived, stream_near, mixes = joint(across, arrived, stream_near, mixes)
+        across, arrived, mixes, counts, keep_mask, end_pos = joint(
+            across, arrived, mixes, counts, keep_mask, end_pos
+        )
 
         block = plane.join_cores(mine, arrived)
         one = plane.shift_depth(block, 1)
@@ -673,18 +677,21 @@
         far_own = swap_group(mix_own)
         kv = pick(core, mix_own, mix_other)
         qo = pick(core, mix_other, mix_own)
-        one, kv, qo = joint(one, kv, qo)
+        ends = order_ends(end_pos)
+        parts = first_parts(after(captions, block), ends)
+        one, kv, qo, *parts = joint(one, kv, qo, *parts)
 
         two = plane.shift_depth(one, 1)
         across_one = plane.swap_side(one)
-        attending = attention_of(kv, qo, parts)
-        two, across_block, across_one, *attending = joint(
-            two, across_block, across_one, *attending
+        stream_near = swap_near(parts[3], 2)
+        attending = attention_of(kv, qo, parts, ends)
+        two, across_block, across_one, stream_near, *attending = joint(
+            two, across_block, across_one, stream_near, *attending
         )
 
         three = plane.shift_depth(two, 1)
         across_two = plane.swap_side(two)
-        wholes = plane.place(plane.empty(2 * rows, cuts), cuts, 0, block, across_block)
+        wholes = plane.place(plane.empty(2 * rows, cuts, attending[-1]), cuts, 0, block, across_block)
         wholes = plane.place(wholes, cuts, 1, one, across_one)
         attention = after(attending[-1], far_own)
         near = [swap_near(attention, flip) for flip in (1, 2, 3)]
@@ -711,14 +718,15 @@
         image_halves = images(third), images(third_other)
         embed_halves = third[:, :wide], third_other[:, :wide]
     else:
-        pictures = pictures_of_batch(deal(outgoing))
-        parts = first_parts(captions)
+        pictures = pictures_of_batch(deal(prepare(image_cache)))
+        ends = order_ends(end_pos)
+        parts = first_parts(captions, ends)
         mix_own = plane.gather_plain(packed[0], packed[1])
         mix_other = plane.swap_core(mix_own)
         far_own = swap_group(mix_own)
         kv = pick(core, mix_own, mix_other)
         qo = pick(core, mix_other, mix_own)
-        attending = attention_of(kv, qo, parts)
+        attending = attention_of(kv, qo, parts, ends)
         feeds = plane.gather_plain(packed[2], packed[3])
         image_half = plane.gather_plain(*pictures)
         image_halves = image_half, plane.swap_core(image_half)
@@ -789,7 +797,20 @@
     row_part = 0.5 * jnp.sum(jnp.log(row_safe)) - jnp.sum(jnp.where(target, sims, 0.0))
     col_part = jnp.sum(weight, 0)
     totals = jnp.concatenate([col_part, jnp.full((128,), 1.0 / 128, full) * row_part])
-    totals = plane.total(totals.reshape(-1, 128)).reshape(-1)
+    totals = totals.reshape(-1, 128)
+    if plane.fast:
+        pooled_group = swap_near(pooled, 1)
+        for bits in ((1, 4), (2, 8)):
+            sent = [plane.flip(totals, bits[0]), plane.flip(totals, bits[1])]
+            sent.append(plane.flip(totals, sum(bits)))
+            if bits[0] == 1:
+                sent.append(pooled_group)
+            sent = joint(*sent)
+            totals = (totals + sent[0]) + (sent[1] + sent[2])
+            pooled_group = sent[3] if bits[0] == 1 else pooled_group
+    else:
+        totals = lax.psum(totals, "dp")
+    totals = totals.reshape(-1)
     col_sum = totals[: spread * CAP_DEV]
     col_safe = jnp.where(batch_valid, col_sum, 1.0)
     objective = jnp.sum(totals[spread * CAP_DEV :]) + 0.5 * jnp.sum(jnp.log(col_safe))
@@ -801,16 +822,23 @@
         (d_unit - unit_text * jnp.sum(unit_text * d_unit, -1, keepdims=True)) * inverse
     ).astype(low)
 
-    both = jnp.concatenate([d_embed, pooled], 1)
-    both = jnp.concatenate([both] + [swap_near(both, flip) for flip in (1, 2, 3)], 0)
-    d_embed_all = both[:, :width]
+    d_embed_near = [swap_near(d_embed, flip) for flip in (1, 2, 3)]
+    if plane.fast:
+        pooled_pair = jnp.concatenate([pooled, pooled_group], 0)
+        *d_embed_near, objective, pooled_near = joint(
+            *d_embed_near, objective, plane.swap_core(pooled_pair)
+        )
+        pooled_all = jnp.concatenate([pooled_pair, pooled_near], 0)
+    else:
+        pooled_all = jnp.concatenate([pooled] + [swap_near(pooled, flip) for flip in (1, 2, 3)], 0)
+    d_embed_all = jnp.concatenate([d_embed, *d_embed_near], 0)
     d_pooled = mm_nt(d_embed_all, w_embed)
     d_out_low = d_pooled.astype(low)
     d_raised = (mm(d_out_low, w_lower) * slope).astype(low)
     d_second = mm_nt(d_raised, w_raise).astype(low)
     g_raise = mm_tn(second_low, d_raised).astype(low)
     d_out_late = after(d_out_low, g_raise, d_second)
-    g_lower = lower_back(2 * group_flag + core_flag, d_out_late, active, both)
+    g_lower = lower_back(2 * group_flag + core_flag, d_out_late, active, pooled_all, d_embed_all)
     if plane.fast:
         raise_stay, raise_in = plane.halve(g_raise.reshape(2, 2, 2, 2 * rows, -1), 1, 4)
         lower_stay, lower_in = plane.halve(g_lower.reshape(2, 2, 2, 2 * rows, -1), 2, 2)
@@ -829,10 +857,10 @@
         core_flag, d_middle_low, d_attended, unit, unit_end, mixed, probs, queries, attended
     )
 
-    def captions_part(part, d_queries_here, done=None):
+    def captions_part(part, d_queries_here, far_parts, done=None):
         return captions_back(
             part, group_flag, ends, unit, scale, d_middle, d_mixed, d_queries_here, queries_far,
-            d_attended_far, small_far, kv, qo, kv_far, qo_far, done=done,
+            *far_parts, kv, qo, kv_far, qo_far, done=done,
         )
 
     if plane.fast:
@@ -841,30 +869,35 @@
         )
         small_far = swap_group(small)
         mix_in = plane.swap_core(g_send)
-        raise_side = plane.halve(add_low((raise_stay, raise_in)), 1, 2)
-        lower_depth = plane.halve(add_low((lower_stay, lower_in)), 1, 4)
+        raise_pair = add_low((raise_stay, raise_in))
+        lower_pair = add_low((lower_stay, lower_in))
+        raise_side = plane.halve(raise_pair, 1, 2)
+        small_far, mix_in, d_attended_far, *raise_side, lower_pair = joint(
+            small_far, mix_in, d_attended_far, *raise_side, lower_pair
+        )
+        raise_last = plane.halve(add_low(raise_side), 0, 8)
+        lower_depth = plane.halve(lower_pair, 1, 4)
         mix_pair = add_low((g_keep, mix_in)).reshape(2, 2, 2, 2 * rows, 2 * COLS)
         mix_side = plane.halve(mix_pair, 2, 2)
-        first_half = captions_part(0, after(d_queries, mix_side[0]))
-        raise_side, lower_depth, mix_side, first_half = joint(
-            raise_side, lower_depth, mix_side, first_half
+        first_half = captions_part(0, after(d_queries, mix_side[0]), (d_attended_far, small_far))
+        raise_last, lower_depth, mix_side, first_half = joint(
+            raise_last, lower_depth, mix_side, first_half
         )
         mix_depth = plane.halve(add_low(mix_side), 1, 4)
-        raise_last = plane.halve(add_low(raise_side), 0, 8)
         lower_last = plane.halve(add_low(lower_depth), 0, 8)
-        starts = after(d_queries, mix_depth[0], raise_last[0], lower_last[0])
-        grad_captions = captions_part(1, starts, first_half)
-        mix_depth, raise_last, lower_last, grad_captions = joint(
-            mix_depth, raise_last, lower_last, grad_captions
-        )
+        starts = after(d_queries, mix_depth[0], lower_last[0])
+        grad_captions = captions_part(1, starts, (d_attended_far, small_far), first_half)
+        mix_depth, lower_last, grad_captions = joint(mix_depth, lower_last, grad_captions)
         mix_last = plane.halve(add_low(mix_depth), 0, 8)
-        raise_sum, lower_sum, mix_sum = [
+        raise_sum, lower_sum = [
             plane.scatter_core(pair[0].astype(full) + pair[1].astype(full))
-            for pair in (raise_last, lower_last, mix_last)
+            for pair in (raise_last, lower_last)
         ]
+        mix_last, raise_sum, lower_sum = joint(mix_last, raise_sum, lower_sum)
+        mix_sum = plane.scatter_core(mix_last[0].astype(full) + mix_last[1].astype(full))
     else:
-        small_far = swap_group(small)
-        grad_captions = captions_part(1, d_queries, captions_part(0, d_queries))
+        far_parts = d_attended_far, swap_group(small)
+        grad_captions = captions_part(1, d_queries, far_parts, captions_part(0, d_queries, far_parts))
         raise_sum = plane.scatter_plain(g_raise)
         lower_sum = plane.scatter_plain(g_lower)
         mix_sum = plane.scatter_plain(g_keep, g_send)

time: 251 us -> 226 us (0.900)
  local copies, waits for them, and re-layouts: 29.6 us -> 17.7 us
  Pallas kernels: 58.3 us -> 47.7 us
  matrix products: 17.6 us -> 10.8 us
  waiting for transfers between devices: 58.2 us -> 62 us
    dynamic_update_slice x24, local copies, waits for them, and re-layouts: 13.9 us -> 6.25 us  [place(): lax.dynamic_update_slice(whole, block[None, :, start:end], (at, 0, 0))]
    ppermute x9 -> x6, waiting for transfers between devices: 17.3 us -> 10.3 us  [shift_depth(): lax.ppermute(x, 'dp', [(i, (i + 4 * step) % self.count) for i in range(se...]
    ppermute x1 -> x6, starting transfers between devices: 0.67 us -> 6.31 us  [flip(): return lax.ppermute(x, 'dp', [(i, i ^ bits) for i in range(self.count)])]
    ppermute x1 -> x6, waiting for transfers between devices: 0.42 us -> 5.76 us  [flip(): return lax.ppermute(x, 'dp', [(i, i ^ bits) for i in range(self.count)])]
    pallas_call x1, Pallas kernels: 13 us -> 8.22 us  [attend_back(): pl.pallas_call(attend_back_body, grid=(steps,), out_shape=shapes(*[((WIDT...]
    ppermute x9 -> x8, waiting for transfers between devices: 11.5 us -> 16.1 us  [swap_side(): return lax.ppermute(x, 'dp', [(i, i ^ 2) for i in range(self.count)])]
    ppermute x9 -> x6, starting transfers between devices: 12.4 us -> 8.1 us  [shift_depth(): lax.ppermute(x, 'dp', [(i, (i + 4 * step) % self.count) for i in range(se...]
    dot_general x4, matrix products: 8.44 us -> 4.59 us  [mm_nt(): lax.dot_general(a, b, (((1,), (1,)), ((), ())), preferred_element_type=full)]
  transfers between devices with their start and end apart: 58 -> 60, of which waited for: 18 -> 24; matrix products, arithmetic and copies ran while one was open for 21% -> 18% of each run, Pallas kernels for 23% -> 20%
where the time goes in v4:
time: 226 us; the launch traced here: 225 us
  waiting for transfers between devices  62 us (27%)
  starting transfers between devices  57 us (25%)
  Pallas kernels  47.7 us (21%)
  other arithmetic  22.9 us (10%)
  local copies, waits for them, and re-layouts  17.7 us (8%)
  matrix products  10.8 us (5%)
  between operations  7 us (3%)
    pallas_call x2, Pallas kernels, captions_back(): pl.pallas_call(functools.partial(captions_body, part), out_shape=jax.Shap...  21.2 us
    ppermute x20, waiting for transfers between devices, swap_near(): return lax.ppermute(x, ('dp', 'mp'), [(i, i ^ flip) for i in range(size)])  19.4 us
    ppermute x20, starting transfers between devices, swap_near(): return lax.ppermute(x, ('dp', 'mp'), [(i, i ^ flip) for i in range(size)])  17.2 us
    ppermute x8, waiting for transfers between devices, swap_side(): return lax.ppermute(x, 'dp', [(i, i ^ 2) for i in range(self.count)])  16.1 us
    ppermute x6, waiting for transfers between devices, shift_depth(): lax.ppermute(x, 'dp', [(i, (i + 4 * step) % self.count) for i in range(se...  10.3 us
    ppermute x8, starting transfers between devices, swap_side(): return lax.ppermute(x, 'dp', [(i, i ^ 2) for i in range(self.count)])  10.3 us
    pallas_call x1, Pallas kernels, attend(): pl.pallas_call(attend_body, grid=(steps,), out_shape=shapes(((count * LEN...  9.92 us
    ppermute x9, starting transfers between devices, halve(): lax.ppermute(leave, 'dp', [(i, i ^ bit) for i in range(self.count)])  9.69 us
  transfers between devices with their start and end apart: 60, of which 24 were waited for; matrix products, arithmetic and copies ran while one was open for 18% of the time, Pallas kernels for 20%

profile of v4, /device:TPU:0, one launch (start us, length us, event | category | flops | bytes accessed | tf_op | source)
XLA Modules:
  0.0 225.0 jit_solution(1836291838956057164)
XLA Ops:
  0.7 2.1 pack.1
  4.8 2.8 %collective-permute-start.1 = (bf16[96,768]{1,0:T(8,128)(2,1)S(1)}, bf16[96,768]{1,0:T(8,128)(2,1)S(1)}, u32[]{:S(2)}, u32[]{:S(2)}) collective-permute-start(bf16[96,768]{1,0:T(8,128)(2,1)S(1)} %bitcast.226), channel_id=1, source_target_pairs={{0,8},{2,10},{4,12},{6,14},{8,16},{10,18},{12,20},{14,22},{16,24},... | collective-permute-start | bytes 442376 | tf_op jit(solution)/shard_map/ppermute | solution.py:60
  7.6 2.1 collective-permute-start.2
  9.7 1.6 collective-permute-start.3
  12.4 1.9 collective-permute-done.1
  14.4 2.2 collective-permute-done.2
  17.7 1.5 collective-permute-start.5
  19.2 4.1 %all-to-all-start = ((bf16[16,8,768]{2,1,0:T(8,128)(2,1)}), bf16[16,8,768]{2,1,0:T(8,128)(2,1)S(1)}, u32[]{:S(2)}, u32[]{:S(2)}) async-start(bf16[16,8,768]{2,1,0:T(8,128)(2,1)} %fusion.1), calls=%async_computation | async-start | bytes 393216 | tf_op jit(solution)/shard_map/all_to_all | solution.py:627
  23.3 2.0 collective-permute-start.6
  25.5 5.8 %collective-permute-done.6 = bf16[96,768]{1,0:T(8,128)(2,1)S(1)} collective-permute-done((bf16[96,768]{1,0:T(8,128)(2,1)S(1)}, bf16[96,768]{1,0:T(8,128)(2,1)S(1)}, u32[]{:S(2)}, u32[]{:S(2)}) %collective-permute-start.6) | collective-permute-done | bytes 147488 | tf_op jit(solution)/shard_map/ppermute | solution.py:57
  31.2 1.5 collective-permute-start.7
  33.2 3.1 %collective-permute-done.7 = bf16[96,768]{1,0:T(8,128)(2,1)S(1)} collective-permute-done((bf16[96,768]{1,0:T(8,128)(2,1)S(1)}, bf16[96,768]{1,0:T(8,128)(2,1)S(1)}, u32[]{:S(2)}, u32[]{:S(2)}) %collective-permute-start.7) | collective-permute-done | bytes 147488 | tf_op jit(solution)/shard_map/ppermute | solution.py:57
  36.6 1.9 collective-permute-start.9
  39.4 1.5 collective-permute-start.15
  42.0 5.5 %norm_first.1 = (bf16[2048,768]{1,0:T(8,128)(2,1)}, f32[2048,128]{1,0:T(8,128)}, bf16[128,768]{1,0:T(8,128)(2,1)}, bf16[128,768]{1,0:T(8,128)(2,1)}) custom-call(s32[1]{0:T(128)} %bitcast.23.group_ref, bf16[2048,768]{1,0:T(8,128)(2,1)} %bitcast.209, s32[128,1]{1,0:T(8,128)} %copy.37.ends_ref), custom_call_target="tpu_custom_call" | custom-call | tf_op jit(solution)/shard_map/norm_first/pallas_call | solution.py:236
  47.5 2.9 %broadcast_select_fusion.2 = (bf16[768,768]{1,0:T(8,128)(2,1)}, bf16[768,768]{1,0:T(8,128)(2,1)}) fusion(bf16[768,768]{1,0:T(8,128)(2,1)} %collective-permute-done.10, pred[]{:T(512)S(6)} %eq.94, bf16[8,96,768]{2,1,0:T(8,128)(2,1)S(1)} %bitcast_dynamic-update-slice_fusion.15), kind=kLoop, calls=%fused_computation.14 | loop fusion | flops 1179648 | bytes 4718593 | tf_op jit(solution)/shard_map/jit(_where)/select_n | solution.py:41
  50.4 1.7 collective-permute-done.9
  54.9 9.9 %attend.1 = (bf16[2048,768]{1,0:T(8,128)(2,1)}, f32[768,512]{1,0:T(8,128)}, bf16[128,384]{1,0:T(8,128)(2,1)}, bf16[128,384]{1,0:T(8,128)(2,1)}, bf16[128,768]{1,0:T(8,128)(2,1)}) custom-call(bf16[2048,768]{1,0:T(8,128)(2,1)} %get-tuple-element.150.unit_ref, bf16[128,768]{1,0:T(8,128)(2,1)} %get-tuple-element.151.unit_end_ref, s32[128,1]{1,0:T(8,128)} %copy.37.ends_ref, ...), custom_call_target="tpu_custom_call" | custom-call | tf_op jit(solution)/shard_map/attend/pallas_call | solution.py:314
  64.8 1.7 collective-permute-done.11
  75.9 1.5 collective-permute-start.22
  77.5 2.8 %collective-permute-done.16 = bf16[96,2432]{1,0:T(8,128)(2,1)S(1)} collective-permute-done((bf16[96,2432]{1,0:T(8,128)(2,1)}, bf16[96,2432]{1,0:T(8,128)(2,1)S(1)}, u32[]{:S(2)}, u32[]{:S(2)}) %collective-permute-start.16) | collective-permute-done | bytes 466976 | tf_op jit(solution)/shard_map/ppermute | solution.py:60
  83.0 1.6 broadcast_select_fusion
  84.6 7.1 %collective-permute-done.21 = bf16[96,2432]{1,0:T(8,128)(2,1)S(1)} collective-permute-done((bf16[96,2432]{1,0:T(8,128)(2,1)S(1)}, bf16[96,2432]{1,0:T(8,128)(2,1)S(1)}, u32[]{:S(2)}, u32[]{:S(2)}) %collective-permute-start.21) | collective-permute-done | bytes 466976 | tf_op jit(solution)/shard_map/ppermute | solution.py:57
  91.9 1.6 multiply_convert_fusion
  96.5 2.1 collective-permute-done.26
  98.6 2.8 %collective-permute-done.24 = bf16[64,768]{1,0:T(8,128)(2,1)S(1)} collective-permute-done((bf16[64,768]{1,0:T(8,128)(2,1)S(1)}, bf16[64,768]{1,0:T(8,128)(2,1)S(1)}, u32[]{:S(2)}, u32[]{:S(2)}) %collective-permute-start.24) | collective-permute-done | bytes 98336 | tf_op jit(solution)/shard_map/ppermute | solution.py:120
  104.1 2.0 fusion.27
  108.6 1.7 collective-permute-start.29
  110.5 2.0 collective-permute-done.29
  115.3 2.2 collective-permute-start.33
  118.6 1.6 pad_maximum_fusion.12
  120.2 2.7 %collective-permute-done.34 = f32[9,128]{1,0:T(8,128)S(1)} collective-permute-done((f32[9,128]{1,0:T(8,128)S(1)}, f32[9,128]{1,0:T(8,128)S(1)}, u32[]{:S(2)}, u32[]{:S(2)}) %collective-permute-start.34) | collective-permute-done | bytes 4640 | tf_op jit(solution)/shard_map/ppermute | solution.py:115
  123.6 1.6 multiply_reduce_fusion.4
  126.0 1.6 collective-permute-start.37
  131.1 1.6 fusion.60
  142.3 5.3 %collective-permute-done.41 = bf16[128,768]{1,0:T(8,128)(2,1)S(1)} collective-permute-done((bf16[128,768]{1,0:T(8,128)(2,1)S(1)}, bf16[128,768]{1,0:T(8,128)(2,1)S(1)}, u32[]{:S(2)}, u32[]{:S(2)}) %collective-permute-start.41) | collective-permute-done | bytes 196640 | tf_op jit(solution)/shard_map/ppermute | solution.py:120
  149.7 8.2 %attend_back.1 = (bf16[768,768]{1,0:T(8,128)(2,1)S(1)}, bf16[768,768]{1,0:T(8,128)(2,1)}, bf16[2048,768]{1,0:T(8,128)(2,1)S(1)}, bf16[128,384]{1,0:T(8,128)(2,1)S(1)}, bf16[640,128]{1,0:T(8,128)(2,1)S(1)}) custom-call(s32[1]{0:T(128)} %bitcast.core_ref, bf16[128,768]{1,0:T(8,128)(2,1)S(1)} %get-tuple-element.242.d_mid_ref, ...), custom_call_target="tpu_custom_call" | custom-call | tf_op jit(solution)/shard_map/attend_back/pallas_call | solution.py:399
  157.9 1.6 copy-done.3
  161.8 1.5 collective-permute-start.46
  164.1 3.3 %collective-permute-done.46.d_att_far_ref = bf16[128,384]{1,0:T(8,128)(2,1)S(1)} collective-permute-done((bf16[128,384]{1,0:T(8,128)(2,1)S(1)}, bf16[128,384]{1,0:T(8,128)(2,1)S(1)}, u32[]{:S(2)}, u32[]{:S(2)}) %collective-permute-start.46) | collective-permute-done | bytes 98336 | tf_op jit(solution)/shard_map/ppermute | solution.py:120
  167.5 2.6 %collective-permute-done.44.small_far_ref = bf16[640,128]{1,0:T(8,128)(2,1)S(1)} collective-permute-done((bf16[640,128]{1,0:T(8,128)(2,1)S(1)}, bf16[640,128]{1,0:T(8,128)(2,1)S(1)}, u32[]{:S(2)}, u32[]{:S(2)}) %collective-permute-start.44) | collective-permute-done | bytes 163872 | tf_op jit(solution)/shard_map/ppermute | solution.py:120
  170.3 1.6 add_convert_fusion
  176.7 10.6 %captions_back.2.refs_0_ = f32[2048,768]{1,0:T(8,128)} custom-call(s32[1]{0:T(128)} %bitcast.23.group_ref, s32[128,1]{1,0:T(8,128)} %copy.37.ends_ref, bf16[2048,768]{1,0:T(8,128)(2,1)} %get-tuple-element.150.unit_ref, f32[2048,128]{1,0:T(8,128)} %get-tuple-element.206.scale_ref, f32[128,768]{1,0:T(8,128)} %get-tuple-element.243.d_mid_ref, ...), custom_call_target="tpu_custom_call" | custom-call | tf_op jit(solution)/shard_map/captions_back/pallas_call | solution.py:549
  188.8 2.7 %collective-permute-start.52 = (bf16[96,960]{1,0:T(8,128)(2,1)S(1)}, bf16[96,960]{1,0:T(8,128)(2,1)S(1)}, u32[]{:S(2)}, u32[]{:S(2)}) collective-permute-start(bf16[96,960]{1,0:T(8,128)(2,1)S(1)} %get-tuple-element.275), channel_id=1, source_target_pairs={{0,16},{2,18},{4,20},{6,22},{8,24},{10,26},{12,28},{14,30},{16,0},... | collective-permute-start | bytes 552968 | tf_op jit(solution)/shard_map/ppermute | solution.py:96
  191.5 10.6 %captions_back.3 = f32[2048,768]{1,0:T(8,128)} custom-call(s32[1]{0:T(128)} %bitcast.23.group_ref, s32[128,1]{1,0:T(8,128)} %copy.37.ends_ref, bf16[2048,768]{1,0:T(8,128)(2,1)} %get-tuple-element.150.unit_ref, f32[2048,128]{1,0:T(8,128)} %get-tuple-element.206.scale_ref, f32[128,768]{1,0:T(8,128)} %get-tuple-element.243.d_mid_ref, ...), custom_call_target="tpu_custom_call", output_to_operand_aliasing={{}: (14, {})} | custom-call | tf_op jit(solution)/shard_map/captions_back/pallas_call | solution.py:549
  203.8 9.0 %collective-permute-done.53 = bf16[96,768]{1,0:T(8,128)(2,1)S(1)} collective-permute-done((bf16[96,768]{1,0:T(8,128)(2,1)S(1)}, bf16[96,768]{1,0:T(8,128)(2,1)S(1)}, u32[]{:S(2)}, u32[]{:S(2)}) %collective-permute-start.53) | collective-permute-done | bytes 147488 | tf_op jit(solution)/shard_map/ppermute | solution.py:96
  214.1 1.5 collective-permute-start.58
  219.5 2.0 collective-permute-done.57
  (330 shorter events, 65.2 us)
Async XLA Ops:
  4.8 9.6 %collective-permute-start.1 = (bf16[96,768]{1,0:T(8,128)(2,1)S(1)}, bf16[96,768]{1,0:T(8,128)(2,1)S(1)}, u32[]{:S(2)}, u32[]{:S(2)}) collective-permute-start(bf16[96,768]{1,0:T(8,128)(2,1)S(1)} %bitcast.226), channel_id=1, source_target_pairs={{0,8},{2,10},{4,12},{6,14},{8,16},{10,18},{12,20},{14,22},{16,24},... | collective-permute-start | bytes 442376 | tf_op jit(solution)/shard_map/ppermute | solution.py:60
  7.6 8.9 %collective-permute-start.2 = (bf16[96,768]{1,0:T(8,128)(2,1)S(1)}, bf16[96,768]{1,0:T(8,128)(2,1)S(1)}, u32[]{:S(2)}, u32[]{:S(2)}) collective-permute-start(bf16[96,768]{1,0:T(8,128)(2,1)S(1)} %bitcast.227), channel_id=1, source_target_pairs={{0,24},{2,26},{4,28},{6,30},{8,0},{10,2},{12,4},{14,6},{16,8},{18,... | collective-permute-start | bytes 442376 | tf_op jit(solution)/shard_map/ppermute | solution.py:60
  9.7 6.9 %collective-permute-start.3 = (bf16[96,768]{1,0:T(8,128)(2,1)S(1)}, bf16[96,768]{1,0:T(8,128)(2,1)S(1)}, u32[]{:S(2)}, u32[]{:S(2)}) collective-permute-start(bf16[96,768]{1,0:T(8,128)(2,1)S(1)} %bitcast.228), channel_id=1, source_target_pairs={{0,4},{2,6},{4,0},{6,2},{8,12},{10,14},{12,8},{14,10},{16,20},{18,... | collective-permute-start | bytes 442376 | tf_op jit(solution)/shard_map/ppermute | solution.py:57
  16.6 8.9 %collective-permute-start.4 = (bf16[96,768]{1,0:T(8,128)(2,1)S(1)}, bf16[96,768]{1,0:T(8,128)(2,1)S(1)}, u32[]{:S(2)}, u32[]{:S(2)}) collective-permute-start(bf16[96,768]{1,0:T(8,128)(2,1)S(1)} %collective-permute-done.1), channel_id=1, source_target_pairs={{0,8},{2,10},{4,12},{6,14},{8,16},{10,18},{12,20},{14,22},{16,24},... | collective-permute-start | bytes 442376 | tf_op jit(solution)/shard_map/ppermute | solution.py:60
  17.7 7.8 %collective-permute-start.5 = (bf16[96,768]{1,0:T(8,128)(2,1)S(1)}, bf16[96,768]{1,0:T(8,128)(2,1)S(1)}, u32[]{:S(2)}, u32[]{:S(2)}) collective-permute-start(bf16[96,768]{1,0:T(8,128)(2,1)S(1)} %collective-permute-done.1), channel_id=1, source_target_pairs={{0,4},{2,6},{4,0},{6,2},{8,12},{10,14},{12,8},{14,10},{16,20},{18,... | collective-permute-start | bytes 442376 | tf_op jit(solution)/shard_map/ppermute | solution.py:57
  19.2 13.6 %all-to-all-start = ((bf16[16,8,768]{2,1,0:T(8,128)(2,1)}), bf16[16,8,768]{2,1,0:T(8,128)(2,1)S(1)}, u32[]{:S(2)}, u32[]{:S(2)}) async-start(bf16[16,8,768]{2,1,0:T(8,128)(2,1)} %fusion.1), calls=%async_computation | async-start | bytes 393216 | tf_op jit(solution)/shard_map/all_to_all | solution.py:627
  23.3 7.9 %collective-permute-start.6 = (bf16[96,768]{1,0:T(8,128)(2,1)S(1)}, bf16[96,768]{1,0:T(8,128)(2,1)S(1)}, u32[]{:S(2)}, u32[]{:S(2)}) collective-permute-start(bf16[96,768]{1,0:T(8,128)(2,1)S(1)} %collective-permute-done.2), channel_id=1, source_target_pairs={{0,4},{2,6},{4,0},{6,2},{8,12},{10,14},{12,8},{14,10},{16,20},{18,... | collective-permute-start | bytes 442376 | tf_op jit(solution)/shard_map/ppermute | solution.py:57
  31.2 5.2 %collective-permute-start.7 = (bf16[96,768]{1,0:T(8,128)(2,1)S(1)}, bf16[96,768]{1,0:T(8,128)(2,1)S(1)}, u32[]{:S(2)}, u32[]{:S(2)}) collective-permute-start(bf16[96,768]{1,0:T(8,128)(2,1)S(1)} %collective-permute-done.4), channel_id=1, source_target_pairs={{0,4},{2,6},{4,0},{6,2},{8,12},{10,14},{12,8},{14,10},{16,20},{18,... | collective-permute-start | bytes 442376 | tf_op jit(solution)/shard_map/ppermute | solution.py:57
  36.4 11.1 %collective-permute-start.10 = (bf16[768,768]{1,0:T(8,128)(2,1)S(1)}, bf16[768,768]{1,0:T(8,128)(2,1)}, u32[]{:S(2)}, u32[]{:S(2)}) collective-permute-start(bf16[768,768]{1,0:T(8,128)(2,1)S(1)} %bitcast.206), channel_id=1, source_target_pairs={{0,2},{2,0},{4,6},{6,4},{8,10},{10,8},{12,14},{14,12},{16,18},{18,... | collective-permute-start | bytes 3538952 | tf_op jit(solution)/shard_map/ppermute | solution.py:54
  36.6 15.5 %collective-permute-start.9 = (bf16[96,2432]{1,0:T(8,128)(2,1)S(1)}, bf16[96,2432]{1,0:T(8,128)(2,1)S(1)}, u32[]{:S(2)}, u32[]{:S(2)}) collective-permute-start(bf16[96,2432]{1,0:T(8,128)(2,1)S(1)} %bitcast.210), channel_id=1, source_target_pairs={{0,8},{2,10},{4,12},{6,14},{8,16},{10,18},{12,20},{14,22},{16,24},... | collective-permute-start | bytes 1400840 | tf_op jit(solution)/shard_map/ppermute | solution.py:60
  38.6 26.3 %collective-permute-start.12 = (bf16[96,2432]{1,0:T(8,128)(2,1)S(1)}, bf16[96,2432]{1,0:T(8,128)(2,1)}, u32[]{:S(2)}, u32[]{:S(2)}) collective-permute-start(bf16[96,2432]{1,0:T(8,128)(2,1)S(1)} %bitcast.211), channel_id=1, source_target_pairs={{0,4},{2,6},{4,0},{6,2},{8,12},{10,14},{12,8},{14,10},{16,20},{18,... | collective-permute-start | bytes 1400840 | tf_op jit(solution)/shard_map/ppermute | solution.py:57
  39.4 27.9 %collective-permute-start.15 = (bf16[768,768]{1,0:T(8,128)(2,1)S(1)}, bf16[768,768]{1,0:T(8,128)(2,1)S(1)}, u32[]{:S(2)}, u32[]{:S(2)}) collective-permute-start(bf16[768,768]{1,0:T(8,128)(2,1)S(1)} %bitcast.207), channel_id=1, source_target_pairs={{0,1},{1,0},{2,3},{3,2},{4,5},{5,4},{6,7},{7,6},{8,9},{9,8},{10,11... | collective-permute-start | bytes 3538952 | tf_op jit(solution)/shard_map/ppermute | solution.py:120
  52.2 14.4 %collective-permute-start.11 = (bf16[96,2432]{1,0:T(8,128)(2,1)S(1)}, bf16[96,2432]{1,0:T(8,128)(2,1)}, u32[]{:S(2)}, u32[]{:S(2)}) collective-permute-start(bf16[96,2432]{1,0:T(8,128)(2,1)S(1)} %collective-permute-done.9), channel_id=1, source_target_pairs={{0,8},{2,10},{4,12},{6,14},{8,16},{10,18},{12,20},{14,22},{16,24},... | collective-permute-start | bytes 1400840 | tf_op jit(solution)/shard_map/ppermute | solution.py:60
  52.2 14.4 %collective-permute-start.13 = (bf16[96,2432]{1,0:T(8,128)(2,1)S(1)}, bf16[96,2432]{1,0:T(8,128)(2,1)}, u32[]{:S(2)}, u32[]{:S(2)}) collective-permute-start(bf16[96,2432]{1,0:T(8,128)(2,1)S(1)} %collective-permute-done.9), channel_id=1, source_target_pairs={{0,4},{2,6},{4,0},{6,2},{8,12},{10,14},{12,8},{14,10},{16,20},{18,... | collective-permute-start | bytes 1400840 | tf_op jit(solution)/shard_map/ppermute | solution.py:57
  54.0 10.8 %collective-permute-start.14 = (bf16[128,768]{1,0:T(8,128)(2,1)S(1)}, bf16[128,768]{1,0:T(8,128)(2,1)}, u32[]{:S(2)}, u32[]{:S(2)}) collective-permute-start(bf16[128,768]{1,0:T(8,128)(2,1)S(1)} %copy-done.26), channel_id=1, source_target_pairs={{0,2},{1,3},{2,0},{3,1},{4,6},{5,7},{6,4},{7,5},{8,10},{9,11},{10,... | collective-permute-start | bytes 589832 | tf_op jit(solution)/shard_map/ppermute | solution.py:120
  66.6 13.7 %collective-permute-start.16 = (bf16[96,2432]{1,0:T(8,128)(2,1)}, bf16[96,2432]{1,0:T(8,128)(2,1)S(1)}, u32[]{:S(2)}, u32[]{:S(2)}) collective-permute-start(bf16[96,2432]{1,0:T(8,128)(2,1)} %collective-permute-done.11), channel_id=1, source_target_pairs={{0,8},{2,10},{4,12},{6,14},{8,16},{10,18},{12,20},{14,22},{16,24},... | collective-permute-start | bytes 1400840 | tf_op jit(solution)/shard_map/ppermute | solution.py:60
  66.7 13.5 %collective-permute-start.17 = (bf16[96,2432]{1,0:T(8,128)(2,1)}, bf16[96,2432]{1,0:T(8,128)(2,1)S(1)}, u32[]{:S(2)}, u32[]{:S(2)}) collective-permute-start(bf16[96,2432]{1,0:T(8,128)(2,1)} %collective-permute-done.11), channel_id=1, source_target_pairs={{0,4},{2,6},{4,0},{6,2},{8,12},{10,14},{12,8},{14,10},{16,20},{18,... | collective-permute-start | bytes 1400840 | tf_op jit(solution)/shard_map/ppermute | solution.py:57
  67.3 8.5 %collective-permute-start.18 = (bf16[128,768]{1,0:T(8,128)(2,1)}, bf16[128,768]{1,0:T(8,128)(2,1)S(1)}, u32[]{:S(2)}, u32[]{:S(2)}) collective-permute-start(bf16[128,768]{1,0:T(8,128)(2,1)} %get-tuple-element.161), channel_id=1, source_target_pairs={{0,1},{1,0},{2,3},{3,2},{4,5},{5,4},{6,7},{7,6},{8,9},{9,8},{10,11... | collective-permute-start | bytes 589832 | tf_op jit(solution)/shard_map/ppermute | solution.py:120
  68.7 7.2 %collective-permute-start.19 = (bf16[128,768]{1,0:T(8,128)(2,1)}, bf16[128,768]{1,0:T(8,128)(2,1)S(1)}, u32[]{:S(2)}, u32[]{:S(2)}) collective-permute-start(bf16[128,768]{1,0:T(8,128)(2,1)} %get-tuple-element.161), channel_id=1, source_target_pairs={{0,2},{1,3},{2,0},{3,1},{4,6},{5,7},{6,4},{7,5},{8,10},{9,11},{10,... | collective-permute-start | bytes 589832 | tf_op jit(solution)/shard_map/ppermute | solution.py:120
  68.7 8.7 %collective-permute-start.20 = (bf16[128,768]{1,0:T(8,128)(2,1)}, bf16[128,768]{1,0:T(8,128)(2,1)S(1)}, u32[]{:S(2)}, u32[]{:S(2)}) collective-permute-start(bf16[128,768]{1,0:T(8,128)(2,1)} %get-tuple-element.161), channel_id=1, source_target_pairs={{0,3},{1,2},{2,1},{3,0},{4,7},{5,6},{6,5},{7,4},{8,11},{9,10},{10,... | collective-permute-start | bytes 589832 | tf_op jit(solution)/shard_map/ppermute | solution.py:120
  75.8 7.2 %collective-permute-start.23 = (bf16[768,768]{1,0:T(8,128)(2,1)S(1)}, bf16[768,768]{1,0:T(8,128)(2,1)S(1)}, u32[]{:S(2)}, u32[]{:S(2)}) collective-permute-start(bf16[768,768]{1,0:T(8,128)(2,1)S(1)} %collective-permute-done.15), channel_id=1, source_target_pairs={{0,2},{2,0},{4,6},{6,4},{8,10},{10,8},{12,14},{14,12},{16,18},{18,... | collective-permute-start | bytes 3538952 | tf_op jit(solution)/shard_map/ppermute | solution.py:54
  75.9 8.6 %collective-permute-start.22 = (bf16[128,384]{1,0:T(8,128)(2,1)S(1)}, bf16[128,384]{1,0:T(8,128)(2,1)S(1)}, u32[]{:S(2)}, u32[]{:S(2)}) collective-permute-start(bf16[128,384]{1,0:T(8,128)(2,1)S(1)} %copy-done.10), channel_id=1, source_target_pairs={{0,1},{1,0},{2,3},{3,2},{4,5},{5,4},{6,7},{7,6},{8,9},{9,8},{10,11... | collective-permute-start | bytes 294920 | tf_op jit(solution)/shard_map/ppermute | solution.py:120
  80.2 11.5 %collective-permute-start.21 = (bf16[96,2432]{1,0:T(8,128)(2,1)S(1)}, bf16[96,2432]{1,0:T(8,128)(2,1)S(1)}, u32[]{:S(2)}, u32[]{:S(2)}) collective-permute-start(bf16[96,2432]{1,0:T(8,128)(2,1)S(1)} %collective-permute-done.16), channel_id=1, source_target_pairs={{0,4},{2,6},{4,0},{6,2},{8,12},{10,14},{12,8},{14,10},{16,20},{18,... | collective-permute-start | bytes 1400840 | tf_op jit(solution)/shard_map/ppermute | solution.py:57
  91.8 10.6 %collective-permute-start.27 = (bf16[768,896]{1,0:T(8,128)(2,1)S(1)}, bf16[768,896]{1,0:T(8,128)(2,1)S(1)}, u32[]{:S(2)}, u32[]{:S(2)}) collective-permute-start(bf16[768,896]{1,0:T(8,128)(2,1)S(1)} %bitcast.198), channel_id=1, source_target_pairs={{0,2},{2,0},{4,6},{6,4},{8,10},{10,8},{12,14},{14,12},{16,18},{18,... | collective-permute-start | bytes 4128776 | tf_op jit(solution)/shard_map/ppermute | solution.py:54
  95.1 6.2 %collective-permute-start.24 = (bf16[64,768]{1,0:T(8,128)(2,1)S(1)}, bf16[64,768]{1,0:T(8,128)(2,1)S(1)}, u32[]{:S(2)}, u32[]{:S(2)}) collective-permute-start(bf16[64,768]{1,0:T(8,128)(2,1)S(1)} %get-tuple-element.279), channel_id=1, source_target_pairs={{0,1},{1,0},{2,3},{3,2},{4,5},{5,4},{6,7},{7,6},{8,9},{9,8},{10,11... | collective-permute-start | bytes 294920 | tf_op jit(solution)/shard_map/ppermute | solution.py:120
  101.4 9.0 %collective-permute-start.31 = (bf16[64,768]{1,0:T(8,128)(2,1)S(1)}, bf16[64,768]{1,0:T(8,128)(2,1)}, u32[]{:S(2)}, u32[]{:S(2)}) collective-permute-start(bf16[64,768]{1,0:T(8,128)(2,1)S(1)} %fusion.20), channel_id=1, source_target_pairs={{0,1},{1,0},{2,3},{3,2},{4,5},{5,4},{6,7},{7,6},{8,9},{9,8},{10,11... | collective-permute-start | bytes 294920 | tf_op jit(solution)/shard_map/ppermute | solution.py:120
  114.2 6.0 %collective-permute-start.32 = (f32[9,128]{1,0:T(8,128)S(1)}, f32[9,128]{1,0:T(8,128)S(1)}, u32[]{:S(2)}, u32[]{:S(2)}) collective-permute-start(f32[9,128]{1,0:T(8,128)S(1)} %add_add_fusion.2), channel_id=1, source_target_pairs={{0,4},{2,6},{4,0},{6,2},{8,12},{10,14},{12,8},{14,10},{16,20},{18,... | collective-permute-start | bytes 13832 | tf_op jit(solution)/shard_map/ppermute | solution.py:115
  117.5 5.4 %collective-permute-start.34 = (f32[9,128]{1,0:T(8,128)S(1)}, f32[9,128]{1,0:T(8,128)S(1)}, u32[]{:S(2)}, u32[]{:S(2)}) collective-permute-start(f32[9,128]{1,0:T(8,128)S(1)} %add_add_fusion.2), channel_id=1, source_target_pairs={{0,20},{2,22},{4,16},{6,18},{8,28},{10,30},{12,24},{14,26},{16,4},... | collective-permute-start | bytes 13832 | tf_op jit(solution)/shard_map/ppermute | solution.py:115
  120.2 10.9 %collective-permute-start.38 = (bf16[128,768]{1,0:T(8,128)(2,1)}, bf16[128,768]{1,0:T(8,128)(2,1)}, u32[]{:S(2)}, u32[]{:S(2)}) collective-permute-start(bf16[128,768]{1,0:T(8,128)(2,1)} %pad_maximum_fusion.12), channel_id=1, source_target_pairs={{0,2},{2,0},{4,6},{6,4},{8,10},{10,8},{12,14},{14,12},{16,18},{18,... | collective-permute-start | bytes 589832 | tf_op jit(solution)/shard_map/ppermute | solution.py:54
  125.4 5.7 %collective-permute-start.35 = (bf16[64,768]{1,0:T(8,128)(2,1)S(1)}, bf16[64,768]{1,0:T(8,128)(2,1)S(1)}, u32[]{:S(2)}, u32[]{:S(2)}) collective-permute-start(bf16[64,768]{1,0:T(8,128)(2,1)S(1)} %multiply_convert_fusion.1), channel_id=1, source_target_pairs={{0,1},{1,0},{2,3},{3,2},{4,5},{5,4},{6,7},{7,6},{8,9},{9,8},{10,11... | collective-permute-start | bytes 294920 | tf_op jit(solution)/shard_map/ppermute | solution.py:120
  126.0 5.1 %collective-permute-start.36 = (bf16[64,768]{1,0:T(8,128)(2,1)S(1)}, bf16[64,768]{1,0:T(8,128)(2,1)S(1)}, u32[]{:S(2)}, u32[]{:S(2)}) collective-permute-start(bf16[64,768]{1,0:T(8,128)(2,1)S(1)} %multiply_convert_fusion.1), channel_id=1, source_target_pairs={{0,2},{1,3},{2,0},{3,1},{4,6},{5,7},{6,4},{7,5},{8,10},{9,11},{10,... | collective-permute-start | bytes 294920 | tf_op jit(solution)/shard_map/ppermute | solution.py:120
  126.0 5.1 %collective-permute-start.37 = (bf16[64,768]{1,0:T(8,128)(2,1)S(1)}, bf16[64,768]{1,0:T(8,128)(2,1)S(1)}, u32[]{:S(2)}, u32[]{:S(2)}) collective-permute-start(bf16[64,768]{1,0:T(8,128)(2,1)S(1)} %multiply_convert_fusion.1), channel_id=1, source_target_pairs={{0,3},{1,2},{2,1},{3,0},{4,7},{5,6},{6,5},{7,4},{8,11},{9,10},{10,... | collective-permute-start | bytes 294920 | tf_op jit(solution)/shard_map/ppermute | solution.py:120
  134.4 7.9 %collective-permute-start.43 = (bf16[128,768]{1,0:T(8,128)(2,1)S(1)}, bf16[128,768]{1,0:T(8,128)(2,1)S(1)}, u32[]{:S(2)}, u32[]{:S(2)}) collective-permute-start(bf16[128,768]{1,0:T(8,128)(2,1)S(1)} %get-tuple-element.278), channel_id=1, source_target_pairs={{0,3},{1,2},{2,1},{3,0},{4,7},{5,6},{6,5},{7,4},{8,11},{9,10},{10,... | collective-permute-start | bytes 589832 | tf_op jit(solution)/shard_map/ppermute | solution.py:120
  135.5 12.1 %collective-permute-start.42 = (bf16[128,768]{1,0:T(8,128)(2,1)S(1)}, bf16[128,768]{1,0:T(8,128)(2,1)S(1)}, u32[]{:S(2)}, u32[]{:S(2)}) collective-permute-start(bf16[128,768]{1,0:T(8,128)(2,1)S(1)} %get-tuple-element.278), channel_id=1, source_target_pairs={{0,2},{1,3},{2,0},{3,1},{4,6},{5,7},{6,4},{7,5},{8,10},{9,11},{10,... | collective-permute-start | bytes 589832 | tf_op jit(solution)/shard_map/ppermute | solution.py:120
  135.7 23.9 %collective-permute-start.39 = (bf16[2,2,96,768]{3,2,1,0:T(8,128)(2,1)S(1)}, bf16[2,2,96,768]{3,2,1,0:T(8,128)(2,1)S(1)}, u32[]{:S(2)}, u32[]{:S(2)}) collective-permute-start(bf16[2,2,96,768]{3,2,1,0:T(8,128)(2,1)S(1)} %get-tuple-element.261), channel_id=1, source_target_pairs={{0,8},{2,10},{4,12},{6,14},{8,0},{10,2},{12,4},{14,6},{16,24},{18,... | collective-permute-start | bytes 1769480 | tf_op jit(solution)/shard_map/ppermute | solution.py:96
  140.0 19.6 %collective-permute-start.40 = (bf16[2,2,96,960]{3,2,1,0:T(8,128)(2,1)S(1)}, bf16[2,2,96,960]{3,2,1,0:T(8,128)(2,1)S(1)}, u32[]{:S(2)}, u32[]{:S(2)}) collective-permute-start(bf16[2,2,96,960]{3,2,1,0:T(8,128)(2,1)S(1)} %get-tuple-element.253), channel_id=1, source_target_pairs={{0,4},{2,6},{4,0},{6,2},{8,12},{10,14},{12,8},{14,10},{16,20},{18,... | collective-permute-start | bytes 2211848 | tf_op jit(solution)/shard_map/ppermute | solution.py:96
  140.9 6.7 %collective-permute-start.41 = (bf16[128,768]{1,0:T(8,128)(2,1)S(1)}, bf16[128,768]{1,0:T(8,128)(2,1)S(1)}, u32[]{:S(2)}, u32[]{:S(2)}) collective-permute-start(bf16[128,768]{1,0:T(8,128)(2,1)S(1)} %get-tuple-element.277), channel_id=1, source_target_pairs={{0,1},{1,0},{2,3},{3,2},{4,5},{5,4},{6,7},{7,6},{8,9},{9,8},{10,11... | collective-permute-start | bytes 589832 | tf_op jit(solution)/shard_map/ppermute | solution.py:120
  159.6 10.7 %collective-permute-start.45 = (bf16[768,768]{1,0:T(8,128)(2,1)}, bf16[768,768]{1,0:T(8,128)(2,1)}, u32[]{:S(2)}, u32[]{:S(2)}) collective-permute-start(bf16[768,768]{1,0:T(8,128)(2,1)} %get-tuple-element.196), channel_id=1, source_target_pairs={{0,2},{2,0},{4,6},{6,4},{8,10},{10,8},{12,14},{14,12},{16,18},{18,... | collective-permute-start | bytes 3538952 | tf_op jit(solution)/shard_map/ppermute | solution.py:54
  160.7 9.6 %collective-permute-start.47 = (bf16[2,96,768]{2,1,0:T(8,128)(2,1)}, bf16[2,96,768]{2,1,0:T(8,128)(2,1)}, u32[]{:S(2)}, u32[]{:S(2)}) collective-permute-start(bf16[2,96,768]{2,1,0:T(8,128)(2,1)} %get-tuple-element.269), channel_id=1, source_target_pairs={{0,4},{2,6},{4,0},{6,2},{8,12},{10,14},{12,8},{14,10},{16,20},{18,... | collective-permute-start | bytes 884744 | tf_op jit(solution)/shard_map/ppermute | solution.py:96
  161.8 5.7 %collective-permute-start.46 = (bf16[128,384]{1,0:T(8,128)(2,1)S(1)}, bf16[128,384]{1,0:T(8,128)(2,1)S(1)}, u32[]{:S(2)}, u32[]{:S(2)}) collective-permute-start(bf16[128,384]{1,0:T(8,128)(2,1)S(1)} %convolution_convert_fusion.4.d_att_ref), channel_id=1, source_target_pairs={{0,1},{1,0},{2,3},{3,2},{4,5},{5,4},{6,7},{7,6},{8,9},{9,8},{10,11... | collective-permute-start | bytes 294920 | tf_op jit(solution)/shard_map/ppermute | solution.py:120
  163.2 6.9 %collective-permute-start.44 = (bf16[640,128]{1,0:T(8,128)(2,1)S(1)}, bf16[640,128]{1,0:T(8,128)(2,1)S(1)}, u32[]{:S(2)}, u32[]{:S(2)}) collective-permute-start(bf16[640,128]{1,0:T(8,128)(2,1)S(1)} %get-tuple-element.195), channel_id=1, source_target_pairs={{0,1},{1,0},{2,3},{3,2},{4,5},{5,4},{6,7},{7,6},{8,9},{9,8},{10,11... | collective-permute-start | bytes 491528 | tf_op jit(solution)/shard_map/ppermute | solution.py:120
  172.0 15.6 %collective-permute-start.50 = (bf16[2,2,96,768]{3,2,1,0:T(8,128)(2,1)S(1)}, bf16[2,2,96,768]{3,2,1,0:T(8,128)(2,1)S(1)}, u32[]{:S(2)}, u32[]{:S(2)}) collective-permute-start(bf16[2,2,96,768]{3,2,1,0:T(8,128)(2,1)S(1)} %get-tuple-element.259), channel_id=1, source_target_pairs={{0,4},{2,6},{4,0},{6,2},{8,12},{10,14},{12,8},{14,10},{16,20},{18,... | collective-permute-start | bytes 1769480 | tf_op jit(solution)/shard_map/ppermute | solution.py:96
  174.0 13.6 %collective-permute-start.49 = (bf16[2,96,960]{2,1,0:T(8,128)(2,1)}, bf16[2,96,960]{2,1,0:T(8,128)(2,1)S(1)}, u32[]{:S(2)}, u32[]{:S(2)}) collective-permute-start(bf16[2,96,960]{2,1,0:T(8,128)(2,1)} %get-tuple-element.263), channel_id=1, source_target_pairs={{0,8},{2,10},{4,12},{6,14},{8,0},{10,2},{12,4},{14,6},{16,24},{18,... | collective-permute-start | bytes 1105928 | tf_op jit(solution)/shard_map/ppermute | solution.py:96
  175.8 11.4 %collective-permute-start.48 = (bf16[96,768]{1,0:T(8,128)(2,1)S(1)}, bf16[96,768]{1,0:T(8,128)(2,1)S(1)}, u32[]{:S(2)}, u32[]{:S(2)}) collective-permute-start(bf16[96,768]{1,0:T(8,128)(2,1)S(1)} %get-tuple-element.286), channel_id=1, source_target_pairs={{0,16},{2,18},{4,20},{6,22},{8,24},{10,26},{12,28},{14,30},{16,0},... | collective-permute-start | bytes 442376 | tf_op jit(solution)/shard_map/ppermute | solution.py:96
  187.9 14.3 %collective-permute-start.51 = (bf16[2,96,768]{2,1,0:T(8,128)(2,1)S(1)}, bf16[2,96,768]{2,1,0:T(8,128)(2,1)S(1)}, u32[]{:S(2)}, u32[]{:S(2)}) collective-permute-start(bf16[2,96,768]{2,1,0:T(8,128)(2,1)S(1)} %get-tuple-element.267), channel_id=1, source_target_pairs={{0,8},{2,10},{4,12},{6,14},{8,0},{10,2},{12,4},{14,6},{16,24},{18,... | collective-permute-start | bytes 884744 | tf_op jit(solution)/shard_map/ppermute | solution.py:96
  188.5 13.6 %collective-permute-start.54 = (f32[48,768]{1,0:T(8,128)S(1)}, f32[48,768]{1,0:T(8,128)S(1)}, u32[]{:S(2)}, u32[]{:S(2)}) collective-permute-start(f32[48,768]{1,0:T(8,128)S(1)} %dynamic-slice_bitcast_fusion.16), channel_id=1, source_target_pairs={{0,2},{2,0},{4,6},{6,4},{8,10},{10,8},{12,14},{14,12},{16,18},{18,... | collective-permute-start | bytes 442376 | tf_op jit(solution)/shard_map/ppermute | solution.py:54
  188.8 13.3 %collective-permute-start.52 = (bf16[96,960]{1,0:T(8,128)(2,1)S(1)}, bf16[96,960]{1,0:T(8,128)(2,1)S(1)}, u32[]{:S(2)}, u32[]{:S(2)}) collective-permute-start(bf16[96,960]{1,0:T(8,128)(2,1)S(1)} %get-tuple-element.275), channel_id=1, source_target_pairs={{0,16},{2,18},{4,20},{6,22},{8,24},{10,26},{12,28},{14,30},{16,0},... | collective-permute-start | bytes 552968 | tf_op jit(solution)/shard_map/ppermute | solution.py:96
  202.6 10.2 %collective-permute-start.53 = (bf16[96,768]{1,0:T(8,128)(2,1)S(1)}, bf16[96,768]{1,0:T(8,128)(2,1)S(1)}, u32[]{:S(2)}, u32[]{:S(2)}) collective-permute-start(bf16[96,768]{1,0:T(8,128)(2,1)S(1)} %get-tuple-element.284), channel_id=1, source_target_pairs={{0,16},{2,18},{4,20},{6,22},{8,24},{10,26},{12,28},{14,30},{16,0},... | collective-permute-start | bytes 442376 | tf_op jit(solution)/shard_map/ppermute | solution.py:96
  (61 other events, 367.0 us)

commit v5 on v4

--- a/solution.py
+++ b/solution.py
@@ -459,33 +459,35 @@
 
 
 def captions_body(
-    part, group_ref, ends_ref, unit_ref, scale_ref, d_mid_ref, d_mixed_ref, dq_ref,
+    start, blocks, group_ref, ends_ref, unit_ref, scale_ref, d_mid_ref, d_mixed_ref, dq_ref,
     q_far_ref, d_att_far_ref, small_far_ref, kv_ref, qo_ref, kv_far_ref, qo_far_ref, *refs,
 ):
     out_ref, inner_end_ref = refs[-2:]
     i = pl.program_id(0)
-    half = dq_ref.shape[0]
-    far_start = (1 - part) * half
+    count = dq_ref.shape[0]
+    steps = count // BLOCK
+    far = (start + steps // 2) % steps
+    rows = blocks * BLOCK
 
     @pl.when(i == 0)
     def _():
         dq_far = jnp.concatenate(
             [
-                small_far_ref[piece * 2 * half + far_start : piece * 2 * half + far_start + half]
+                small_far_ref[piece * count + far * BLOCK : piece * count + far * BLOCK + rows]
                 for piece in range(3)
             ],
             1,
         )
-        inner_end_ref[...] = mm_nt(dq_ref[...], qo_ref[:, :COLS]) + mm_nt(
-            dq_far, qo_far_ref[:, :COLS]
-        )
+        inner_end_ref[...] = mm_nt(
+            dq_ref[start * BLOCK : start * BLOCK + rows], qo_ref[:, :COLS]
+        ) + mm_nt(dq_far, qo_far_ref[:, :COLS])
 
     row, token = stack_grid()
     own_caption = token // LENGTH == row
     lane = lax.broadcasted_iota(jnp.int32, (128, TOKENS), 0) & (2 * LENGTH - 1)
     spot = lax.broadcasted_iota(jnp.int32, (128, TOKENS), 1) & (LENGTH - 1)
     zero = jnp.zeros((BLOCK, 128), low)
-    place = pl.multiple_of(6 * half + 2 * far_start + 2 * BLOCK * i, 2 * BLOCK)
+    place = pl.multiple_of(3 * count + 2 * BLOCK * (far + i), 2 * BLOCK)
     packed = small_far_ref[pl.ds(place, 2 * BLOCK), :]
     pair = jnp.concatenate(
         [
@@ -500,8 +502,8 @@
     ).astype(low)
     d_mixed = jnp.concatenate(
         [
-            mm_tn(d_scores, head_stack(q_far_ref[step_rows(i), :])).astype(low),
-            mm_tn(probs, head_stack(d_att_far_ref[step_rows(i), :])).astype(low),
+            mm_tn(d_scores, head_stack(q_far_ref[step_rows(far + i), :])).astype(low),
+            mm_tn(probs, head_stack(d_att_far_ref[step_rows(far + i), :])).astype(low),
         ],
         1,
     )
@@ -517,15 +519,12 @@
 
 
 def captions_back(
-    part, group, ends, unit, scale, d_mid, d_mixed, dq, q_far, d_att_far, small_far, kv, qo,
+    start, blocks, group, ends, unit, scale, d_mid, d_mixed, dq, q_far, d_att_far, small_far, kv, qo,
     kv_far, qo_far, done=None,
 ):
     count = ends.shape[0]
     steps = count // BLOCK
     half = steps // 2
-    start = part * half
-    own_half = pl.BlockSpec((count // 2, COLS), lambda i, g: (part, 0))
-    far_half = pl.BlockSpec((count // 2, COLS), lambda i, g: (1 - part, 0))
     operands = [
         group, ends, unit, scale, d_mid, d_mixed, dq, q_far, d_att_far, small_far, kv, qo,
         kv_far, qo_far,
@@ -536,9 +535,7 @@
         pl.BlockSpec((TOKENS, 128), lambda i, g: (i + start, 0)),
         pl.BlockSpec((BLOCK, WIDTH), lambda i, g: (i + start, 0)),
         pl.BlockSpec((TOKENS, 2 * COLS), lambda i, g: (i + start, 0)),
-        own_half,
-        far_half,
-        far_half,
+        *[whole_block((count, COLS))] * 3,
         whole_block(small_far.shape),
     ] + [whole_block(kv.shape)] * 4
     aliases = {}
@@ -547,16 +544,16 @@
         operands.append(done)
         in_specs.append(pl.BlockSpec(memory_space=pl.ANY))
     return pl.pallas_call(
-        functools.partial(captions_body, part),
+        functools.partial(captions_body, start, blocks),
         out_shape=jax.ShapeDtypeStruct(unit.shape, full),
         grid_spec=pltpu.PrefetchScalarGridSpec(
             num_scalar_prefetch=1,
-            grid=(half,),
+            grid=(blocks,),
             in_specs=in_specs,
             out_specs=pl.BlockSpec(
                 (TOKENS, WIDTH), lambda i, g: ((i + start + g[0] * half) % steps, 0)
             ),
-            scratch_shapes=[pltpu.VMEM((count // 2, WIDTH), full)],
+            scratch_shapes=[pltpu.VMEM((blocks * BLOCK, WIDTH), full)],
         ),
         input_output_aliases=aliases,
         name="captions_back",
@@ -645,18 +642,17 @@
         arrived = plane.swap_core(packed[1])
         arrived, cache = joint(arrived, image_cache)
         block = plane.join_cores(packed[0], arrived)
-        outgoing = prepare(cache)
+        incoming = deal(prepare(cache))
         up = plane.shift_depth(block, 1)
         down = plane.shift_depth(block, -1)
         across = plane.swap_side(block)
-        up, down, across, block, outgoing = joint(up, down, across, block, outgoing)
-
-        incoming = deal(outgoing)
+        up, down, across, block = joint(up, down, across, block)
+
         mixes = plane.place(plane.empty(2 * rows, mix_cuts, block), mix_cuts, 0, block, across)
         far = plane.shift_depth(up, 1)
         across_up = plane.swap_side(up)
         across_down = plane.swap_side(down)
-        far, across_up, across_down = joint(far, across_up, across_down)
+        far, across_up, across_down, incoming = joint(far, across_up, across_down, incoming)
 
         across = plane.swap_side(far)
         pictures = pictures_of_batch(incoming)
@@ -842,10 +838,8 @@
     if plane.fast:
         raise_stay, raise_in = plane.halve(g_raise.reshape(2, 2, 2, 2 * rows, -1), 1, 4)
         lower_stay, lower_in = plane.halve(g_lower.reshape(2, 2, 2, 2 * rows, -1), 2, 2)
-    inner = d_second[:rows_dev].astype(full)
-    inner = inner + roll_rows(swap_near(d_second[:rows_dev], 1)).astype(full)
-    inner = inner + swap_near(d_second[rows_dev:], 2).astype(full)
-    inner = inner + roll_rows(swap_near(d_second[rows_dev:], 3)).astype(full)
+    d_second = add_low((d_second[:rows_dev], swap_near(d_second[rows_dev:], 2)))
+    inner = d_second.astype(full) + roll_rows(swap_near(d_second, 1)).astype(full)
     d_middle = d_pooled[:rows_dev] + norm_back(
         inner, unit_second[:rows_dev], scale_second[:rows_dev]
     )
@@ -857,55 +851,70 @@
         core_flag, d_middle_low, d_attended, unit, unit_end, mixed, probs, queries, attended
     )
 
-    def captions_part(part, d_queries_here, far_parts, done=None):
+    def early_parts(raise_sum, lower_sum):
+        grad_down = jnp.concatenate([part[:, :hidden] for part in lower_sum], 1)
+        proj_own = jnp.concatenate([part[:, hidden:] for part in lower_sum], 1)
+        raised_sum = jnp.concatenate(raise_sum, 1)
+        gain_second = jnp.sum(raised_sum * w_up.astype(full), 1)
+        early = jnp.stack([gain_second, jnp.broadcast_to(objective, (rows,))])
+        return proj_own, grad_down, raised_sum, early
+
+    def captions_part(start, blocks, d_queries_here, far_parts, done=None):
         return captions_back(
-            part, group_flag, ends, unit, scale, d_middle, d_mixed, d_queries_here, queries_far,
+            start, blocks, group_flag, ends, unit, scale, d_middle, d_mixed, d_queries_here, queries_far,
             *far_parts, kv, qo, kv_far, qo_far, done=done,
         )
 
     if plane.fast:
-        raise_stay, raise_in, lower_stay, lower_in, small, d_queries, g_send = joint(
-            raise_stay, raise_in, lower_stay, lower_in, small, d_queries, g_send
+        raise_stay, raise_in, lower_stay, lower_in, small, d_queries, g_send, d_attended_far = joint(
+            raise_stay, raise_in, lower_stay, lower_in, small, d_queries, g_send, d_attended_far
         )
         small_far = swap_group(small)
         mix_in = plane.swap_core(g_send)
         raise_pair = add_low((raise_stay, raise_in))
         lower_pair = add_low((lower_stay, lower_in))
         raise_side = plane.halve(raise_pair, 1, 2)
-        small_far, mix_in, d_attended_far, *raise_side, lower_pair = joint(
-            small_far, mix_in, d_attended_far, *raise_side, lower_pair
+        small_far, mix_in, *raise_side, lower_pair = joint(
+            small_far, mix_in, *raise_side, lower_pair
         )
         raise_last = plane.halve(add_low(raise_side), 0, 8)
         lower_depth = plane.halve(lower_pair, 1, 4)
         mix_pair = add_low((g_keep, mix_in)).reshape(2, 2, 2, 2 * rows, 2 * COLS)
         mix_side = plane.halve(mix_pair, 2, 2)
-        first_half = captions_part(0, after(d_queries, mix_side[0]), (d_attended_far, small_far))
+        far_parts = d_attended_far, small_far
+        half = rows_dev // BLOCK // 2
+        first_half = captions_part(0, half, after(d_queries, mix_side[0]), far_parts)
         raise_last, lower_depth, mix_side, first_half = joint(
             raise_last, lower_depth, mix_side, first_half
         )
         mix_depth = plane.halve(add_low(mix_side), 1, 4)
         lower_last = plane.halve(add_low(lower_depth), 0, 8)
         starts = after(d_queries, mix_depth[0], lower_last[0])
-        grad_captions = captions_part(1, starts, (d_attended_far, small_far), first_half)
-        mix_depth, lower_last, grad_captions = joint(mix_depth, lower_last, grad_captions)
+        third_part = captions_part(half, half // 2, starts, far_parts, first_half)
+        mix_depth, lower_last, third_part = joint(mix_depth, lower_last, third_part)
         mix_last = plane.halve(add_low(mix_depth), 0, 8)
+        starts = after(d_queries, mix_last[0])
+        grad_captions = captions_part(half + half // 2, half - half // 2, starts, far_parts, third_part)
         raise_sum, lower_sum = [
             plane.scatter_core(pair[0].astype(full) + pair[1].astype(full))
             for pair in (raise_last, lower_last)
         ]
-        mix_last, raise_sum, lower_sum = joint(mix_last, raise_sum, lower_sum)
+        proj_own, grad_down, raised_sum, early = early_parts(raise_sum, lower_sum)
+        proj_far, early_far = swap_group(proj_own), swap_group(early)
+        mix_last, proj_far, early_far, grad_down, raised_sum, grad_captions = joint(
+            mix_last, proj_far, early_far, grad_down, raised_sum, grad_captions
+        )
         mix_sum = plane.scatter_core(mix_last[0].astype(full) + mix_last[1].astype(full))
     else:
         far_parts = d_attended_far, swap_group(small)
-        grad_captions = captions_part(1, d_queries, far_parts, captions_part(0, d_queries, far_parts))
+        grad_captions = captions_part(0, rows_dev // BLOCK, d_queries, far_parts)
         raise_sum = plane.scatter_plain(g_raise)
         lower_sum = plane.scatter_plain(g_lower)
+        proj_own, grad_down, raised_sum, early = early_parts(raise_sum, lower_sum)
+        proj_far, early_far = swap_group(proj_own), swap_group(early)
         mix_sum = plane.scatter_plain(g_keep, g_send)
     grad_captions = grad_captions.reshape(rows_dev, length, width)
 
-    grad_down = jnp.concatenate([part[:, :hidden] for part in lower_sum], 1)
-    proj_own = jnp.concatenate([part[:, hidden:] for part in lower_sum], 1)
-    proj_far = swap_group(proj_own)
     grad_proj = pick(
         group,
         jnp.concatenate([proj_own, proj_far], 1),
@@ -914,17 +923,11 @@
     grad_out = mix_sum[1][:, COLS:]
     unit_mix = jnp.stack([mix_sum[1][:, :COLS], mix_sum[0][:, :COLS], mix_sum[0][:, COLS:]], 1)
     grad_qkv = unit_mix * ln1_gain[:, None, None]
-    raised_sum = jnp.concatenate(raise_sum, 1)
     grad_up = raised_sum * ln2_gain[:, None]
-    gains = jnp.stack(
-        [
-            jnp.sum(unit_mix * w_qkv.astype(full), (1, 2)),
-            jnp.sum(raised_sum * w_up.astype(full), 1),
-            jnp.broadcast_to(objective, (rows,)),
-        ]
-    )
-    gains = gains + swap_group(gains)
-    loss = gains[2, 0] / total_valid
+    early = early + early_far
+    loss = early[1, 0] / total_valid
+    gain_first = jnp.sum(unit_mix * w_qkv.astype(full), (1, 2))[None]
+    gain_first = gain_first + swap_group(gain_first)
     return (
         loss,
         grad_captions,
@@ -933,8 +936,8 @@
         grad_up,
         grad_down,
         grad_proj,
-        gains[0],
-        gains[1],
+        gain_first[0],
+        early[0],
     )
 
 

time: 226 us -> 221 us (0.978)
  waiting for transfers between devices: 62 us -> 52.6 us
  Pallas kernels: 47.7 us -> 51.9 us
    ppermute x8, waiting for transfers between devices: 16.1 us -> 11.6 us  [swap_side(): return lax.ppermute(x, 'dp', [(i, i ^ 2) for i in range(self.count)])]
    pallas_call x2 -> x3, Pallas kernels: 21.2 us -> 25.1 us  [captions_back(): pl.pallas_call(functools.partial(captions_body, start, blocks), out_shape...]
    ppermute x20, waiting for transfers between devices: 19.4 us -> 15.8 us  [swap_near(): return lax.ppermute(x, ('dp', 'mp'), [(i, i ^ flip) for i in range(size)])]
    ppermute x9, waiting for transfers between devices: 9.66 us -> 6.54 us  [halve(): lax.ppermute(leave, 'dp', [(i, i ^ bit) for i in range(self.count)])]
    ppermute x6, waiting for transfers between devices: 10.3 us -> 13.2 us  [shift_depth(): lax.ppermute(x, 'dp', [(i, (i + 4 * step) % self.count) for i in range(se...]
  transfers between devices with their start and end apart: 60 -> 60, of which waited for: 24 -> 22; matrix products, arithmetic and copies ran while one was open for 18% -> 18% of each run, Pallas kernels for 20% -> 23%
where the time goes in v5:
time: 221 us; the launch traced here: 220 us
  starting transfers between devices  57.4 us (26%)
  waiting for transfers between devices  52.6 us (24%)
  Pallas kernels  51.9 us (23%)
  other arithmetic  23.3 us (11%)
  local copies, waits for them, and re-layouts  17 us (8%)
  matrix products  10.7 us (5%)
  between operations  6.87 us (3%)
    pallas_call x3, Pallas kernels, captions_back(): pl.pallas_call(functools.partial(captions_body, start, blocks), out_shape...  25.1 us
    ppermute x20, starting transfers between devices, swap_near(): return lax.ppermute(x, ('dp', 'mp'), [(i, i ^ flip) for i in range(size)])  19.4 us
    ppermute x20, waiting for transfers between devices, swap_near(): return lax.ppermute(x, ('dp', 'mp'), [(i, i ^ flip) for i in range(size)])  15.8 us
    ppermute x6, waiting for transfers between devices, shift_depth(): lax.ppermute(x, 'dp', [(i, (i + 4 * step) % self.count) for i in range(se...  13.2 us
    ppermute x8, waiting for transfers between devices, swap_side(): return lax.ppermute(x, 'dp', [(i, i ^ 2) for i in range(self.count)])  11.6 us
    ppermute x9, starting transfers between devices, halve(): lax.ppermute(leave, 'dp', [(i, i ^ bit) for i in range(self.count)])  10.5 us
    pallas_call x1, Pallas kernels, attend(): pl.pallas_call(attend_body, grid=(steps,), out_shape=shapes(((count * LEN...  9.92 us
    ppermute x8, starting transfers between devices, swap_side(): return lax.ppermute(x, 'dp', [(i, i ^ 2) for i in range(self.count)])  8.75 us
  transfers between devices with their start and end apart: 60, of which 22 were waited for; matrix products, arithmetic and copies ran while one was open for 18% of the time, Pallas kernels for 23%

profile of v5, /device:TPU:0, one launch (start us, length us, event | category | flops | bytes accessed | tf_op | source)
XLA Modules:
  0.0 219.8 jit_solution(2593819086615950731)
XLA Ops:
  0.7 2.1 pack.1
  4.8 2.8 %collective-permute-start.1 = (bf16[96,768]{1,0:T(8,128)(2,1)S(1)}, bf16[96,768]{1,0:T(8,128)(2,1)S(1)}, u32[]{:S(2)}, u32[]{:S(2)}) collective-permute-start(bf16[96,768]{1,0:T(8,128)(2,1)S(1)} %bitcast.226), channel_id=1, source_target_pairs={{0,8},{2,10},{4,12},{6,14},{8,16},{10,18},{12,20},{14,22},{16,24},... | collective-permute-start | bytes 442376 | tf_op jit(solution)/shard_map/ppermute | solution.py:60
  7.6 2.1 collective-permute-start.2
  9.7 1.6 collective-permute-start.3
  12.4 3.5 %all-to-all-start = ((bf16[16,8,768]{2,1,0:T(8,128)(2,1)}), bf16[16,8,768]{2,1,0:T(8,128)(2,1)S(1)}, u32[]{:S(2)}, u32[]{:S(2)}) async-start(bf16[16,8,768]{2,1,0:T(8,128)(2,1)} %fusion.1), calls=%async_computation | async-start | bytes 393216 | tf_op jit(solution)/shard_map/all_to_all | solution.py:624
  17.9 1.5 collective-permute-start.5
  20.1 7.1 %collective-permute-done.4 = bf16[96,768]{1,0:T(8,128)(2,1)S(1)} collective-permute-done((bf16[96,768]{1,0:T(8,128)(2,1)S(1)}, bf16[96,768]{1,0:T(8,128)(2,1)S(1)}, u32[]{:S(2)}, u32[]{:S(2)}) %collective-permute-start.4) | collective-permute-done | bytes 147488 | tf_op jit(solution)/shard_map/ppermute | solution.py:60
  29.6 4.0 %collective-permute-done.7 = bf16[96,768]{1,0:T(8,128)(2,1)S(1)} collective-permute-done((bf16[96,768]{1,0:T(8,128)(2,1)S(1)}, bf16[96,768]{1,0:T(8,128)(2,1)S(1)}, u32[]{:S(2)}, u32[]{:S(2)}) %collective-permute-start.7) | collective-permute-done | bytes 147488 | tf_op jit(solution)/shard_map/ppermute | solution.py:57
  33.8 1.5 collective-permute-start.9
  36.3 1.5 collective-permute-start.15
  39.0 5.5 %norm_first.1 = (bf16[2048,768]{1,0:T(8,128)(2,1)}, f32[2048,128]{1,0:T(8,128)}, bf16[128,768]{1,0:T(8,128)(2,1)}, bf16[128,768]{1,0:T(8,128)(2,1)}) custom-call(s32[1]{0:T(128)} %bitcast.23.group_ref, bf16[2048,768]{1,0:T(8,128)(2,1)} %bitcast.209, s32[128,1]{1,0:T(8,128)} %copy.40.ends_ref), custom_call_target="tpu_custom_call" | custom-call | tf_op jit(solution)/shard_map/norm_first/pallas_call | solution.py:236
  44.5 2.9 %broadcast_select_fusion.2 = (bf16[768,768]{1,0:T(8,128)(2,1)}, bf16[768,768]{1,0:T(8,128)(2,1)}) fusion(bf16[768,768]{1,0:T(8,128)(2,1)} %collective-permute-done.10, pred[]{:T(512)S(6)} %eq.94, bf16[8,96,768]{2,1,0:T(8,128)(2,1)S(1)} %bitcast_dynamic-update-slice_fusion.15), kind=kLoop, calls=%fused_computation.14 | loop fusion | flops 1179648 | bytes 4718593 | tf_op jit(solution)/shard_map/jit(_where)/select_n | solution.py:41
  51.3 9.9 %attend.1 = (bf16[2048,768]{1,0:T(8,128)(2,1)}, f32[768,512]{1,0:T(8,128)}, bf16[128,384]{1,0:T(8,128)(2,1)}, bf16[128,384]{1,0:T(8,128)(2,1)}, bf16[128,768]{1,0:T(8,128)(2,1)}) custom-call(bf16[2048,768]{1,0:T(8,128)(2,1)} %get-tuple-element.152.unit_ref, bf16[128,768]{1,0:T(8,128)(2,1)} %get-tuple-element.153.unit_end_ref, s32[128,1]{1,0:T(8,128)} %copy.40.ends_ref, ...), custom_call_target="tpu_custom_call" | custom-call | tf_op jit(solution)/shard_map/attend/pallas_call | solution.py:314
  61.3 1.6 collective-permute-done.11
  64.1 1.5 collective-permute-start.18
  72.7 1.6 collective-permute-start.22
  74.3 2.6 %collective-permute-done.16 = bf16[96,2432]{1,0:T(8,128)(2,1)S(1)} collective-permute-done((bf16[96,2432]{1,0:T(8,128)(2,1)}, bf16[96,2432]{1,0:T(8,128)(2,1)S(1)}, u32[]{:S(2)}, u32[]{:S(2)}) %collective-permute-start.16) | collective-permute-done | bytes 466976 | tf_op jit(solution)/shard_map/ppermute | solution.py:60
  79.7 1.6 broadcast_select_fusion
  81.2 6.8 %collective-permute-done.21 = bf16[96,2432]{1,0:T(8,128)(2,1)S(1)} collective-permute-done((bf16[96,2432]{1,0:T(8,128)(2,1)S(1)}, bf16[96,2432]{1,0:T(8,128)(2,1)S(1)}, u32[]{:S(2)}, u32[]{:S(2)}) %collective-permute-start.21) | collective-permute-done | bytes 466976 | tf_op jit(solution)/shard_map/ppermute | solution.py:57
  88.3 1.6 multiply_convert_fusion
  90.4 1.7 collective-permute-start.26
  92.8 2.5 %collective-permute-done.26 = bf16[64,768]{1,0:T(8,128)(2,1)S(1)} collective-permute-done((bf16[64,768]{1,0:T(8,128)(2,1)S(1)}, bf16[64,768]{1,0:T(8,128)(2,1)S(1)}, u32[]{:S(2)}, u32[]{:S(2)}) %collective-permute-start.26) | collective-permute-done | bytes 98336 | tf_op jit(solution)/shard_map/ppermute | solution.py:120
  95.3 2.4 %collective-permute-done.24 = bf16[64,768]{1,0:T(8,128)(2,1)S(1)} collective-permute-done((bf16[64,768]{1,0:T(8,128)(2,1)S(1)}, bf16[64,768]{1,0:T(8,128)(2,1)S(1)}, u32[]{:S(2)}, u32[]{:S(2)}) %collective-permute-start.24) | collective-permute-done | bytes 98336 | tf_op jit(solution)/shard_map/ppermute | solution.py:120
  97.8 1.6 collective-permute-start.31
  101.1 1.9 fusion.28
  107.3 2.0 collective-permute-done.29
  111.3 2.7 %collective-permute-start.33 = (f32[9,128]{1,0:T(8,128)S(1)}, f32[9,128]{1,0:T(8,128)S(1)}, u32[]{:S(2)}, u32[]{:S(2)}) collective-permute-start(f32[9,128]{1,0:T(8,128)S(1)} %add_add_fusion.2), channel_id=1, source_target_pairs={{0,16},{2,18},{4,20},{6,22},{8,24},{10,26},{12,28},{14,30},{16,0},... | collective-permute-start | bytes 13832 | tf_op jit(solution)/shard_map/ppermute | solution.py:115
  114.6 1.6 pad_maximum_fusion.13
  116.2 3.2 %collective-permute-done.34 = f32[9,128]{1,0:T(8,128)S(1)} collective-permute-done((f32[9,128]{1,0:T(8,128)S(1)}, f32[9,128]{1,0:T(8,128)S(1)}, u32[]{:S(2)}, u32[]{:S(2)}) %collective-permute-start.34) | collective-permute-done | bytes 4640 | tf_op jit(solution)/shard_map/ppermute | solution.py:115
  120.1 1.6 multiply_reduce_fusion.4
  122.5 1.6 collective-permute-start.37
  127.6 1.6 fusion.57
  137.9 2.2 collective-permute-done.42
  142.2 8.5 %attend_back.1 = (bf16[768,768]{1,0:T(8,128)(2,1)S(1)}, bf16[768,768]{1,0:T(8,128)(2,1)}, bf16[2048,768]{1,0:T(8,128)(2,1)S(1)}, bf16[128,384]{1,0:T(8,128)(2,1)S(1)}, bf16[640,128]{1,0:T(8,128)(2,1)S(1)}) custom-call(s32[1]{0:T(128)} %bitcast.core_ref, bf16[128,768]{1,0:T(8,128)(2,1)S(1)} %get-tuple-element.246.d_mid_ref, ...), custom_call_target="tpu_custom_call" | custom-call | tf_op jit(solution)/shard_map/attend_back/pallas_call | solution.py:399
  150.7 1.6 copy-done.3
  152.3 3.7 %collective-permute-done.40 = bf16[2,2,96,960]{3,2,1,0:T(8,128)(2,1)S(1)} collective-permute-done((bf16[2,2,96,960]{3,2,1,0:T(8,128)(2,1)S(1)}, bf16[2,2,96,960]{3,2,1,0:T(8,128)(2,1)S(1)}, u32[]{:S(2)}, u32[]{:S(2)}) %collective-permute-start.40) | collective-permute-done | bytes 737312 | tf_op jit(solution)/shard_map/ppermute | solution.py:96
  158.0 1.5 collective-permute-start.44
  159.8 4.6 %collective-permute-done.44.small_far_ref = bf16[640,128]{1,0:T(8,128)(2,1)S(1)} collective-permute-done((bf16[640,128]{1,0:T(8,128)(2,1)S(1)}, bf16[640,128]{1,0:T(8,128)(2,1)S(1)}, u32[]{:S(2)}, u32[]{:S(2)}) %collective-permute-start.44) | collective-permute-done | bytes 163872 | tf_op jit(solution)/shard_map/ppermute | solution.py:120
  164.3 2.4 %collective-permute-done.46 = bf16[2,96,768]{2,1,0:T(8,128)(2,1)} collective-permute-done((bf16[2,96,768]{2,1,0:T(8,128)(2,1)}, bf16[2,96,768]{2,1,0:T(8,128)(2,1)}, u32[]{:S(2)}, u32[]{:S(2)}) %collective-permute-start.46) | collective-permute-done | bytes 294944 | tf_op jit(solution)/shard_map/ppermute | solution.py:96
  166.7 1.6 add_convert_fusion
  173.0 10.6 %captions_back.3.refs_0_ = f32[2048,768]{1,0:T(8,128)} custom-call(s32[1]{0:T(128)} %bitcast.23.group_ref, s32[128,1]{1,0:T(8,128)} %copy.40.ends_ref, bf16[2048,768]{1,0:T(8,128)(2,1)} %get-tuple-element.152.unit_ref, f32[2048,128]{1,0:T(8,128)} %get-tuple-element.208.scale_ref, f32[128,768]{1,0:T(8,128)} %get-tuple-element.247.d_mid_ref, ...), custom_call_target="tpu_custom_call" | custom-call | tf_op jit(solution)/shard_map/captions_back/pallas_call | solution.py:546
  185.3 2.4 %collective-permute-start.52 = (bf16[96,960]{1,0:T(8,128)(2,1)S(1)}, bf16[96,960]{1,0:T(8,128)(2,1)S(1)}, u32[]{:S(2)}, u32[]{:S(2)}) collective-permute-start(bf16[96,960]{1,0:T(8,128)(2,1)S(1)} %get-tuple-element.278), channel_id=1, source_target_pairs={{0,16},{2,18},{4,20},{6,22},{8,24},{10,26},{12,28},{14,30},{16,0},... | collective-permute-start | bytes 552968 | tf_op jit(solution)/shard_map/ppermute | solution.py:96
  187.7 7.3 %captions_back.4.refs_0_ = f32[2048,768]{1,0:T(8,128)} custom-call(s32[1]{0:T(128)} %bitcast.23.group_ref, s32[128,1]{1,0:T(8,128)} %copy.40.ends_ref, bf16[2048,768]{1,0:T(8,128)(2,1)} %get-tuple-element.152.unit_ref, f32[2048,128]{1,0:T(8,128)} %get-tuple-element.208.scale_ref, ...), custom_call_target="tpu_custom_call", output_to_operand_aliasing={{}: (14, {})} | custom-call | tf_op jit(solution)/shard_map/captions_back/pallas_call | solution.py:546
  195.2 1.5 collective-permute-start.56
  198.3 7.2 %captions_back.5 = f32[2048,768]{1,0:T(8,128)} custom-call(s32[1]{0:T(128)} %bitcast.23.group_ref, s32[128,1]{1,0:T(8,128)} %copy.40.ends_ref, bf16[2048,768]{1,0:T(8,128)(2,1)} %get-tuple-element.152.unit_ref, f32[2048,128]{1,0:T(8,128)} %get-tuple-element.208.scale_ref, f32[128,768]{1,0:T(8,128)} %get-tuple-element.247.d_mid_ref, ...), custom_call_target="tpu_custom_call", output_to_operand_aliasing={{}: (14, {})} | custom-call | tf_op jit(solution)/shard_map/captions_back/pallas_call | solution.py:546
  205.7 1.5 collective-permute-start.55
  207.9 2.2 collective-permute-done.55
  214.5 1.5 collective-permute-start.58
  (330 shorter events, 65.1 us)
Async XLA Ops:
  4.8 11.2 %collective-permute-start.1 = (bf16[96,768]{1,0:T(8,128)(2,1)S(1)}, bf16[96,768]{1,0:T(8,128)(2,1)S(1)}, u32[]{:S(2)}, u32[]{:S(2)}) collective-permute-start(bf16[96,768]{1,0:T(8,128)(2,1)S(1)} %bitcast.226), channel_id=1, source_target_pairs={{0,8},{2,10},{4,12},{6,14},{8,16},{10,18},{12,20},{14,22},{16,24},... | collective-permute-start | bytes 442376 | tf_op jit(solution)/shard_map/ppermute | solution.py:60
  7.6 8.9 %collective-permute-start.2 = (bf16[96,768]{1,0:T(8,128)(2,1)S(1)}, bf16[96,768]{1,0:T(8,128)(2,1)S(1)}, u32[]{:S(2)}, u32[]{:S(2)}) collective-permute-start(bf16[96,768]{1,0:T(8,128)(2,1)S(1)} %bitcast.227), channel_id=1, source_target_pairs={{0,24},{2,26},{4,28},{6,30},{8,0},{10,2},{12,4},{14,6},{16,8},{18,... | collective-permute-start | bytes 442376 | tf_op jit(solution)/shard_map/ppermute | solution.py:60
  9.7 6.9 %collective-permute-start.3 = (bf16[96,768]{1,0:T(8,128)(2,1)S(1)}, bf16[96,768]{1,0:T(8,128)(2,1)S(1)}, u32[]{:S(2)}, u32[]{:S(2)}) collective-permute-start(bf16[96,768]{1,0:T(8,128)(2,1)S(1)} %bitcast.228), channel_id=1, source_target_pairs={{0,4},{2,6},{4,0},{6,2},{8,12},{10,14},{12,8},{14,10},{16,20},{18,... | collective-permute-start | bytes 442376 | tf_op jit(solution)/shard_map/ppermute | solution.py:57
  12.4 15.5 %all-to-all-start = ((bf16[16,8,768]{2,1,0:T(8,128)(2,1)}), bf16[16,8,768]{2,1,0:T(8,128)(2,1)S(1)}, u32[]{:S(2)}, u32[]{:S(2)}) async-start(bf16[16,8,768]{2,1,0:T(8,128)(2,1)} %fusion.1), calls=%async_computation | async-start | bytes 393216 | tf_op jit(solution)/shard_map/all_to_all | solution.py:624
  16.5 10.6 %collective-permute-start.4 = (bf16[96,768]{1,0:T(8,128)(2,1)S(1)}, bf16[96,768]{1,0:T(8,128)(2,1)S(1)}, u32[]{:S(2)}, u32[]{:S(2)}) collective-permute-start(bf16[96,768]{1,0:T(8,128)(2,1)S(1)} %collective-permute-done.1), channel_id=1, source_target_pairs={{0,8},{2,10},{4,12},{6,14},{8,16},{10,18},{12,20},{14,22},{16,24},... | collective-permute-start | bytes 442376 | tf_op jit(solution)/shard_map/ppermute | solution.py:60
  17.9 9.2 %collective-permute-start.5 = (bf16[96,768]{1,0:T(8,128)(2,1)S(1)}, bf16[96,768]{1,0:T(8,128)(2,1)S(1)}, u32[]{:S(2)}, u32[]{:S(2)}) collective-permute-start(bf16[96,768]{1,0:T(8,128)(2,1)S(1)} %collective-permute-done.1), channel_id=1, source_target_pairs={{0,4},{2,6},{4,0},{6,2},{8,12},{10,14},{12,8},{14,10},{16,20},{18,... | collective-permute-start | bytes 442376 | tf_op jit(solution)/shard_map/ppermute | solution.py:57
  19.3 8.6 %collective-permute-start.6 = (bf16[96,768]{1,0:T(8,128)(2,1)S(1)}, bf16[96,768]{1,0:T(8,128)(2,1)S(1)}, u32[]{:S(2)}, u32[]{:S(2)}) collective-permute-start(bf16[96,768]{1,0:T(8,128)(2,1)S(1)} %collective-permute-done.2), channel_id=1, source_target_pairs={{0,4},{2,6},{4,0},{6,2},{8,12},{10,14},{12,8},{14,10},{16,20},{18,... | collective-permute-start | bytes 442376 | tf_op jit(solution)/shard_map/ppermute | solution.py:57
  28.2 5.3 %collective-permute-start.7 = (bf16[96,768]{1,0:T(8,128)(2,1)S(1)}, bf16[96,768]{1,0:T(8,128)(2,1)S(1)}, u32[]{:S(2)}, u32[]{:S(2)}) collective-permute-start(bf16[96,768]{1,0:T(8,128)(2,1)S(1)} %collective-permute-done.4), channel_id=1, source_target_pairs={{0,4},{2,6},{4,0},{6,2},{8,12},{10,14},{12,8},{14,10},{16,20},{18,... | collective-permute-start | bytes 442376 | tf_op jit(solution)/shard_map/ppermute | solution.py:57
  33.6 10.9 %collective-permute-start.10 = (bf16[768,768]{1,0:T(8,128)(2,1)S(1)}, bf16[768,768]{1,0:T(8,128)(2,1)}, u32[]{:S(2)}, u32[]{:S(2)}) collective-permute-start(bf16[768,768]{1,0:T(8,128)(2,1)S(1)} %bitcast.206), channel_id=1, source_target_pairs={{0,2},{2,0},{4,6},{6,4},{8,10},{10,8},{12,14},{14,12},{16,18},{18,... | collective-permute-start | bytes 3538952 | tf_op jit(solution)/shard_map/ppermute | solution.py:54
  33.8 14.9 %collective-permute-start.9 = (bf16[96,2432]{1,0:T(8,128)(2,1)S(1)}, bf16[96,2432]{1,0:T(8,128)(2,1)S(1)}, u32[]{:S(2)}, u32[]{:S(2)}) collective-permute-start(bf16[96,2432]{1,0:T(8,128)(2,1)S(1)} %bitcast.210), channel_id=1, source_target_pairs={{0,8},{2,10},{4,12},{6,14},{8,16},{10,18},{12,20},{14,22},{16,24},... | collective-permute-start | bytes 1400840 | tf_op jit(solution)/shard_map/ppermute | solution.py:60
  35.3 25.9 %collective-permute-start.12 = (bf16[96,2432]{1,0:T(8,128)(2,1)S(1)}, bf16[96,2432]{1,0:T(8,128)(2,1)}, u32[]{:S(2)}, u32[]{:S(2)}) collective-permute-start(bf16[96,2432]{1,0:T(8,128)(2,1)S(1)} %bitcast.211), channel_id=1, source_target_pairs={{0,4},{2,6},{4,0},{6,2},{8,12},{10,14},{12,8},{14,10},{16,20},{18,... | collective-permute-start | bytes 1400840 | tf_op jit(solution)/shard_map/ppermute | solution.py:57
  36.3 27.8 %collective-permute-start.15 = (bf16[768,768]{1,0:T(8,128)(2,1)S(1)}, bf16[768,768]{1,0:T(8,128)(2,1)S(1)}, u32[]{:S(2)}, u32[]{:S(2)}) collective-permute-start(bf16[768,768]{1,0:T(8,128)(2,1)S(1)} %bitcast.207), channel_id=1, source_target_pairs={{0,1},{1,0},{2,3},{3,2},{4,5},{5,4},{6,7},{7,6},{8,9},{9,8},{10,11... | collective-permute-start | bytes 3538952 | tf_op jit(solution)/shard_map/ppermute | solution.py:120
  48.8 14.1 %collective-permute-start.11 = (bf16[96,2432]{1,0:T(8,128)(2,1)S(1)}, bf16[96,2432]{1,0:T(8,128)(2,1)}, u32[]{:S(2)}, u32[]{:S(2)}) collective-permute-start(bf16[96,2432]{1,0:T(8,128)(2,1)S(1)} %collective-permute-done.9), channel_id=1, source_target_pairs={{0,8},{2,10},{4,12},{6,14},{8,16},{10,18},{12,20},{14,22},{16,24},... | collective-permute-start | bytes 1400840 | tf_op jit(solution)/shard_map/ppermute | solution.py:60
  48.8 14.1 %collective-permute-start.13 = (bf16[96,2432]{1,0:T(8,128)(2,1)S(1)}, bf16[96,2432]{1,0:T(8,128)(2,1)}, u32[]{:S(2)}, u32[]{:S(2)}) collective-permute-start(bf16[96,2432]{1,0:T(8,128)(2,1)S(1)} %collective-permute-done.9), channel_id=1, source_target_pairs={{0,4},{2,6},{4,0},{6,2},{8,12},{10,14},{12,8},{14,10},{16,20},{18,... | collective-permute-start | bytes 1400840 | tf_op jit(solution)/shard_map/ppermute | solution.py:57
  50.5 10.8 %collective-permute-start.14 = (bf16[128,768]{1,0:T(8,128)(2,1)S(1)}, bf16[128,768]{1,0:T(8,128)(2,1)}, u32[]{:S(2)}, u32[]{:S(2)}) collective-permute-start(bf16[128,768]{1,0:T(8,128)(2,1)S(1)} %copy-done.26), channel_id=1, source_target_pairs={{0,2},{1,3},{2,0},{3,1},{4,6},{5,7},{6,4},{7,5},{8,10},{9,11},{10,... | collective-permute-start | bytes 589832 | tf_op jit(solution)/shard_map/ppermute | solution.py:120
  62.9 14.0 %collective-permute-start.16 = (bf16[96,2432]{1,0:T(8,128)(2,1)}, bf16[96,2432]{1,0:T(8,128)(2,1)S(1)}, u32[]{:S(2)}, u32[]{:S(2)}) collective-permute-start(bf16[96,2432]{1,0:T(8,128)(2,1)} %collective-permute-done.11), channel_id=1, source_target_pairs={{0,8},{2,10},{4,12},{6,14},{8,16},{10,18},{12,20},{14,22},{16,24},... | collective-permute-start | bytes 1400840 | tf_op jit(solution)/shard_map/ppermute | solution.py:60
  62.9 14.0 %collective-permute-start.17 = (bf16[96,2432]{1,0:T(8,128)(2,1)}, bf16[96,2432]{1,0:T(8,128)(2,1)S(1)}, u32[]{:S(2)}, u32[]{:S(2)}) collective-permute-start(bf16[96,2432]{1,0:T(8,128)(2,1)} %collective-permute-done.11), channel_id=1, source_target_pairs={{0,4},{2,6},{4,0},{6,2},{8,12},{10,14},{12,8},{14,10},{16,20},{18,... | collective-permute-start | bytes 1400840 | tf_op jit(solution)/shard_map/ppermute | solution.py:57
  64.1 8.5 %collective-permute-start.18 = (bf16[128,768]{1,0:T(8,128)(2,1)}, bf16[128,768]{1,0:T(8,128)(2,1)S(1)}, u32[]{:S(2)}, u32[]{:S(2)}) collective-permute-start(bf16[128,768]{1,0:T(8,128)(2,1)} %get-tuple-element.163), channel_id=1, source_target_pairs={{0,1},{1,0},{2,3},{3,2},{4,5},{5,4},{6,7},{7,6},{8,9},{9,8},{10,11... | collective-permute-start | bytes 589832 | tf_op jit(solution)/shard_map/ppermute | solution.py:120
  65.7 7.1 %collective-permute-start.19 = (bf16[128,768]{1,0:T(8,128)(2,1)}, bf16[128,768]{1,0:T(8,128)(2,1)S(1)}, u32[]{:S(2)}, u32[]{:S(2)}) collective-permute-start(bf16[128,768]{1,0:T(8,128)(2,1)} %get-tuple-element.163), channel_id=1, source_target_pairs={{0,2},{1,3},{2,0},{3,1},{4,6},{5,7},{6,4},{7,5},{8,10},{9,11},{10,... | collective-permute-start | bytes 589832 | tf_op jit(solution)/shard_map/ppermute | solution.py:120
  65.7 8.7 %collective-permute-start.20 = (bf16[128,768]{1,0:T(8,128)(2,1)}, bf16[128,768]{1,0:T(8,128)(2,1)S(1)}, u32[]{:S(2)}, u32[]{:S(2)}) collective-permute-start(bf16[128,768]{1,0:T(8,128)(2,1)} %get-tuple-element.163), channel_id=1, source_target_pairs={{0,3},{1,2},{2,1},{3,0},{4,7},{5,6},{6,5},{7,4},{8,11},{9,10},{10,... | collective-permute-start | bytes 589832 | tf_op jit(solution)/shard_map/ppermute | solution.py:120
  72.6 7.0 %collective-permute-start.23 = (bf16[768,768]{1,0:T(8,128)(2,1)S(1)}, bf16[768,768]{1,0:T(8,128)(2,1)S(1)}, u32[]{:S(2)}, u32[]{:S(2)}) collective-permute-start(bf16[768,768]{1,0:T(8,128)(2,1)S(1)} %collective-permute-done.15), channel_id=1, source_target_pairs={{0,2},{2,0},{4,6},{6,4},{8,10},{10,8},{12,14},{14,12},{16,18},{18,... | collective-permute-start | bytes 3538952 | tf_op jit(solution)/shard_map/ppermute | solution.py:54
  72.7 8.5 %collective-permute-start.22 = (bf16[128,384]{1,0:T(8,128)(2,1)S(1)}, bf16[128,384]{1,0:T(8,128)(2,1)S(1)}, u32[]{:S(2)}, u32[]{:S(2)}) collective-permute-start(bf16[128,384]{1,0:T(8,128)(2,1)S(1)} %copy-done.10), channel_id=1, source_target_pairs={{0,1},{1,0},{2,3},{3,2},{4,5},{5,4},{6,7},{7,6},{8,9},{9,8},{10,11... | collective-permute-start | bytes 294920 | tf_op jit(solution)/shard_map/ppermute | solution.py:120
  76.9 11.1 %collective-permute-start.21 = (bf16[96,2432]{1,0:T(8,128)(2,1)S(1)}, bf16[96,2432]{1,0:T(8,128)(2,1)S(1)}, u32[]{:S(2)}, u32[]{:S(2)}) collective-permute-start(bf16[96,2432]{1,0:T(8,128)(2,1)S(1)} %collective-permute-done.16), channel_id=1, source_target_pairs={{0,4},{2,6},{4,0},{6,2},{8,12},{10,14},{12,8},{14,10},{16,20},{18,... | collective-permute-start | bytes 1400840 | tf_op jit(solution)/shard_map/ppermute | solution.py:57
  88.1 11.2 %collective-permute-start.27 = (bf16[768,896]{1,0:T(8,128)(2,1)S(1)}, bf16[768,896]{1,0:T(8,128)(2,1)S(1)}, u32[]{:S(2)}, u32[]{:S(2)}) collective-permute-start(bf16[768,896]{1,0:T(8,128)(2,1)S(1)} %bitcast.198), channel_id=1, source_target_pairs={{0,2},{2,0},{4,6},{6,4},{8,10},{10,8},{12,14},{14,12},{16,18},{18,... | collective-permute-start | bytes 4128776 | tf_op jit(solution)/shard_map/ppermute | solution.py:54
  92.1 5.6 %collective-permute-start.24 = (bf16[64,768]{1,0:T(8,128)(2,1)S(1)}, bf16[64,768]{1,0:T(8,128)(2,1)S(1)}, u32[]{:S(2)}, u32[]{:S(2)}) collective-permute-start(bf16[64,768]{1,0:T(8,128)(2,1)S(1)} %get-tuple-element.280), channel_id=1, source_target_pairs={{0,1},{1,0},{2,3},{3,2},{4,5},{5,4},{6,7},{7,6},{8,9},{9,8},{10,11... | collective-permute-start | bytes 294920 | tf_op jit(solution)/shard_map/ppermute | solution.py:120
  97.8 9.5 %collective-permute-start.31 = (bf16[64,768]{1,0:T(8,128)(2,1)S(1)}, bf16[64,768]{1,0:T(8,128)(2,1)}, u32[]{:S(2)}, u32[]{:S(2)}) collective-permute-start(bf16[64,768]{1,0:T(8,128)(2,1)S(1)} %fusion.21), channel_id=1, source_target_pairs={{0,1},{1,0},{2,3},{3,2},{4,5},{5,4},{6,7},{7,6},{8,9},{9,8},{10,11... | collective-permute-start | bytes 294920 | tf_op jit(solution)/shard_map/ppermute | solution.py:120
  110.2 6.0 %collective-permute-start.32 = (f32[9,128]{1,0:T(8,128)S(1)}, f32[9,128]{1,0:T(8,128)S(1)}, u32[]{:S(2)}, u32[]{:S(2)}) collective-permute-start(f32[9,128]{1,0:T(8,128)S(1)} %add_add_fusion.2), channel_id=1, source_target_pairs={{0,4},{2,6},{4,0},{6,2},{8,12},{10,14},{12,8},{14,10},{16,20},{18,... | collective-permute-start | bytes 13832 | tf_op jit(solution)/shard_map/ppermute | solution.py:115
  114.0 5.4 %collective-permute-start.34 = (f32[9,128]{1,0:T(8,128)S(1)}, f32[9,128]{1,0:T(8,128)S(1)}, u32[]{:S(2)}, u32[]{:S(2)}) collective-permute-start(f32[9,128]{1,0:T(8,128)S(1)} %add_add_fusion.2), channel_id=1, source_target_pairs={{0,20},{2,22},{4,16},{6,18},{8,28},{10,30},{12,24},{14,26},{16,4},... | collective-permute-start | bytes 13832 | tf_op jit(solution)/shard_map/ppermute | solution.py:115
  116.2 11.4 %collective-permute-start.38 = (bf16[128,768]{1,0:T(8,128)(2,1)}, bf16[128,768]{1,0:T(8,128)(2,1)}, u32[]{:S(2)}, u32[]{:S(2)}) collective-permute-start(bf16[128,768]{1,0:T(8,128)(2,1)} %pad_maximum_fusion.13), channel_id=1, source_target_pairs={{0,2},{2,0},{4,6},{6,4},{8,10},{10,8},{12,14},{14,12},{16,18},{18,... | collective-permute-start | bytes 589832 | tf_op jit(solution)/shard_map/ppermute | solution.py:54
  121.9 5.7 %collective-permute-start.35 = (bf16[64,768]{1,0:T(8,128)(2,1)S(1)}, bf16[64,768]{1,0:T(8,128)(2,1)S(1)}, u32[]{:S(2)}, u32[]{:S(2)}) collective-permute-start(bf16[64,768]{1,0:T(8,128)(2,1)S(1)} %multiply_convert_fusion.1), channel_id=1, source_target_pairs={{0,1},{1,0},{2,3},{3,2},{4,5},{5,4},{6,7},{7,6},{8,9},{9,8},{10,11... | collective-permute-start | bytes 294920 | tf_op jit(solution)/shard_map/ppermute | solution.py:120
  122.5 5.1 %collective-permute-start.36 = (bf16[64,768]{1,0:T(8,128)(2,1)S(1)}, bf16[64,768]{1,0:T(8,128)(2,1)S(1)}, u32[]{:S(2)}, u32[]{:S(2)}) collective-permute-start(bf16[64,768]{1,0:T(8,128)(2,1)S(1)} %multiply_convert_fusion.1), channel_id=1, source_target_pairs={{0,2},{1,3},{2,0},{3,1},{4,6},{5,7},{6,4},{7,5},{8,10},{9,11},{10,... | collective-permute-start | bytes 294920 | tf_op jit(solution)/shard_map/ppermute | solution.py:120
  122.5 5.1 %collective-permute-start.37 = (bf16[64,768]{1,0:T(8,128)(2,1)S(1)}, bf16[64,768]{1,0:T(8,128)(2,1)S(1)}, u32[]{:S(2)}, u32[]{:S(2)}) collective-permute-start(bf16[64,768]{1,0:T(8,128)(2,1)S(1)} %multiply_convert_fusion.1), channel_id=1, source_target_pairs={{0,3},{1,2},{2,1},{3,0},{4,7},{5,6},{6,5},{7,4},{8,11},{9,10},{10,... | collective-permute-start | bytes 294920 | tf_op jit(solution)/shard_map/ppermute | solution.py:120
  131.8 20.5 %collective-permute-start.39 = (bf16[2,2,96,768]{3,2,1,0:T(8,128)(2,1)S(1)}, bf16[2,2,96,768]{3,2,1,0:T(8,128)(2,1)S(1)}, u32[]{:S(2)}, u32[]{:S(2)}) collective-permute-start(bf16[2,2,96,768]{3,2,1,0:T(8,128)(2,1)S(1)} %get-tuple-element.264), channel_id=1, source_target_pairs={{0,8},{2,10},{4,12},{6,14},{8,0},{10,2},{12,4},{14,6},{16,24},{18,... | collective-permute-start | bytes 1769480 | tf_op jit(solution)/shard_map/ppermute | solution.py:96
  133.4 6.7 %collective-permute-start.42 = (bf16[128,768]{1,0:T(8,128)(2,1)S(1)}, bf16[128,768]{1,0:T(8,128)(2,1)S(1)}, u32[]{:S(2)}, u32[]{:S(2)}) collective-permute-start(bf16[128,768]{1,0:T(8,128)(2,1)S(1)} %add_convert_fusion.7), channel_id=1, source_target_pairs={{0,1},{1,0},{2,3},{3,2},{4,5},{5,4},{6,7},{7,6},{8,9},{9,8},{10,11... | collective-permute-start | bytes 589832 | tf_op jit(solution)/shard_map/ppermute | solution.py:120
  137.0 19.0 %collective-permute-start.40 = (bf16[2,2,96,960]{3,2,1,0:T(8,128)(2,1)S(1)}, bf16[2,2,96,960]{3,2,1,0:T(8,128)(2,1)S(1)}, u32[]{:S(2)}, u32[]{:S(2)}) collective-permute-start(bf16[2,2,96,960]{3,2,1,0:T(8,128)(2,1)S(1)} %get-tuple-element.256), channel_id=1, source_target_pairs={{0,4},{2,6},{4,0},{6,2},{8,12},{10,14},{12,8},{14,10},{16,20},{18,... | collective-permute-start | bytes 2211848 | tf_op jit(solution)/shard_map/ppermute | solution.py:96
  141.5 10.8 %collective-permute-start.43 = (bf16[128,384]{1,0:T(8,128)(2,1)S(1)}, bf16[128,384]{1,0:T(8,128)(2,1)S(1)}, u32[]{:S(2)}, u32[]{:S(2)}) collective-permute-start(bf16[128,384]{1,0:T(8,128)(2,1)S(1)} %convolution_convert_fusion.4.d_att_ref), channel_id=1, source_target_pairs={{0,1},{1,0},{2,3},{3,2},{4,5},{5,4},{6,7},{7,6},{8,9},{9,8},{10,11... | collective-permute-start | bytes 294920 | tf_op jit(solution)/shard_map/ppermute | solution.py:120
  156.0 10.7 %collective-permute-start.45 = (bf16[768,768]{1,0:T(8,128)(2,1)}, bf16[768,768]{1,0:T(8,128)(2,1)}, u32[]{:S(2)}, u32[]{:S(2)}) collective-permute-start(bf16[768,768]{1,0:T(8,128)(2,1)} %get-tuple-element.198), channel_id=1, source_target_pairs={{0,2},{2,0},{4,6},{6,4},{8,10},{10,8},{12,14},{14,12},{16,18},{18,... | collective-permute-start | bytes 3538952 | tf_op jit(solution)/shard_map/ppermute | solution.py:54
  156.9 9.8 %collective-permute-start.46 = (bf16[2,96,768]{2,1,0:T(8,128)(2,1)}, bf16[2,96,768]{2,1,0:T(8,128)(2,1)}, u32[]{:S(2)}, u32[]{:S(2)}) collective-permute-start(bf16[2,96,768]{2,1,0:T(8,128)(2,1)} %get-tuple-element.272), channel_id=1, source_target_pairs={{0,4},{2,6},{4,0},{6,2},{8,12},{10,14},{12,8},{14,10},{16,20},{18,... | collective-permute-start | bytes 884744 | tf_op jit(solution)/shard_map/ppermute | solution.py:96
  158.0 6.3 %collective-permute-start.44 = (bf16[640,128]{1,0:T(8,128)(2,1)S(1)}, bf16[640,128]{1,0:T(8,128)(2,1)S(1)}, u32[]{:S(2)}, u32[]{:S(2)}) collective-permute-start(bf16[640,128]{1,0:T(8,128)(2,1)S(1)} %get-tuple-element.197), channel_id=1, source_target_pairs={{0,1},{1,0},{2,3},{3,2},{4,5},{5,4},{6,7},{7,6},{8,9},{9,8},{10,11... | collective-permute-start | bytes 491528 | tf_op jit(solution)/shard_map/ppermute | solution.py:120
  168.4 15.6 %collective-permute-start.49 = (bf16[2,2,96,768]{3,2,1,0:T(8,128)(2,1)S(1)}, bf16[2,2,96,768]{3,2,1,0:T(8,128)(2,1)S(1)}, u32[]{:S(2)}, u32[]{:S(2)}) collective-permute-start(bf16[2,2,96,768]{3,2,1,0:T(8,128)(2,1)S(1)} %get-tuple-element.262), channel_id=1, source_target_pairs={{0,4},{2,6},{4,0},{6,2},{8,12},{10,14},{12,8},{14,10},{16,20},{18,... | collective-permute-start | bytes 1769480 | tf_op jit(solution)/shard_map/ppermute | solution.py:96
  170.3 13.8 %collective-permute-start.48 = (bf16[2,96,960]{2,1,0:T(8,128)(2,1)}, bf16[2,96,960]{2,1,0:T(8,128)(2,1)S(1)}, u32[]{:S(2)}, u32[]{:S(2)}) collective-permute-start(bf16[2,96,960]{2,1,0:T(8,128)(2,1)} %get-tuple-element.266), channel_id=1, source_target_pairs={{0,8},{2,10},{4,12},{6,14},{8,0},{10,2},{12,4},{14,6},{16,24},{18,... | collective-permute-start | bytes 1105928 | tf_op jit(solution)/shard_map/ppermute | solution.py:96
  172.8 10.9 %collective-permute-start.47 = (bf16[96,768]{1,0:T(8,128)(2,1)S(1)}, bf16[96,768]{1,0:T(8,128)(2,1)S(1)}, u32[]{:S(2)}, u32[]{:S(2)}) collective-permute-start(bf16[96,768]{1,0:T(8,128)(2,1)S(1)} %get-tuple-element.287), channel_id=1, source_target_pairs={{0,16},{2,18},{4,20},{6,22},{8,24},{10,26},{12,28},{14,30},{16,0},... | collective-permute-start | bytes 442376 | tf_op jit(solution)/shard_map/ppermute | solution.py:96
  184.3 12.4 %collective-permute-start.51 = (bf16[2,96,768]{2,1,0:T(8,128)(2,1)S(1)}, bf16[2,96,768]{2,1,0:T(8,128)(2,1)S(1)}, u32[]{:S(2)}, u32[]{:S(2)}) collective-permute-start(bf16[2,96,768]{2,1,0:T(8,128)(2,1)S(1)} %get-tuple-element.270), channel_id=1, source_target_pairs={{0,8},{2,10},{4,12},{6,14},{8,0},{10,2},{12,4},{14,6},{16,24},{18,... | collective-permute-start | bytes 884744 | tf_op jit(solution)/shard_map/ppermute | solution.py:96
  185.1 9.9 %collective-permute-start.50 = (f32[48,768]{1,0:T(8,128)S(1)}, f32[48,768]{1,0:T(8,128)S(1)}, u32[]{:S(2)}, u32[]{:S(2)}) collective-permute-start(f32[48,768]{1,0:T(8,128)S(1)} %dynamic-slice_bitcast_fusion.18), channel_id=1, source_target_pairs={{0,2},{2,0},{4,6},{6,4},{8,10},{10,8},{12,14},{14,12},{16,18},{18,... | collective-permute-start | bytes 442376 | tf_op jit(solution)/shard_map/ppermute | solution.py:54
  185.3 11.3 %collective-permute-start.52 = (bf16[96,960]{1,0:T(8,128)(2,1)S(1)}, bf16[96,960]{1,0:T(8,128)(2,1)S(1)}, u32[]{:S(2)}, u32[]{:S(2)}) collective-permute-start(bf16[96,960]{1,0:T(8,128)(2,1)S(1)} %get-tuple-element.278), channel_id=1, source_target_pairs={{0,16},{2,18},{4,20},{6,22},{8,24},{10,26},{12,28},{14,30},{16,0},... | collective-permute-start | bytes 552968 | tf_op jit(solution)/shard_map/ppermute | solution.py:96
  195.2 12.7 %collective-permute-start.56 = (f32[2,48]{1,0:T(2,128)S(1)}, f32[2,48]{1,0:T(2,128)S(1)}, u32[]{:S(2)}, u32[]{:S(2)}) collective-permute-start(f32[2,48]{1,0:T(2,128)S(1)} %stack.19), channel_id=1, source_target_pairs={{0,1},{1,0},{2,3},{3,2},{4,5},{5,4},{6,7},{7,6},{8,9},{9,8},{10,11... | collective-permute-start | bytes 1160 | tf_op jit(solution)/shard_map/ppermute | solution.py:120
  196.8 8.7 %collective-permute-start.54 = (f32[48,960]{1,0:T(8,128)S(1)}, f32[48,960]{1,0:T(8,128)S(1)}, u32[]{:S(2)}, u32[]{:S(2)}) collective-permute-start(f32[48,960]{1,0:T(8,128)S(1)} %dynamic-slice_bitcast_fusion.12), channel_id=1, source_target_pairs={{0,2},{2,0},{4,6},{6,4},{8,10},{10,8},{12,14},{14,12},{16,18},{18,... | collective-permute-start | bytes 552968 | tf_op jit(solution)/shard_map/ppermute | solution.py:54
  197.0 11.0 %collective-permute-start.53 = (bf16[96,768]{1,0:T(8,128)(2,1)S(1)}, bf16[96,768]{1,0:T(8,128)(2,1)S(1)}, u32[]{:S(2)}, u32[]{:S(2)}) collective-permute-start(bf16[96,768]{1,0:T(8,128)(2,1)S(1)} %get-tuple-element.285), channel_id=1, source_target_pairs={{0,16},{2,18},{4,20},{6,22},{8,24},{10,26},{12,28},{14,30},{16,0},... | collective-permute-start | bytes 442376 | tf_op jit(solution)/shard_map/ppermute | solution.py:96
  (61 other events, 361.5 us)

commit v6 on v5

--- a/solution.py
+++ b/solution.py
@@ -450,6 +450,104 @@
         name="lower_back",
         compiler_params=LIMIT,
     )(flag, d_out, active, pooled, d_embed)
+
+
+def own_slots(index_ref, valid, main):
+    count = valid.shape[1]
+    row = lax.broadcasted_iota(jnp.int32, (CAP_DEV, count), 0)
+    spare = CAP_DEV - main
+    first = index_ref[0] * main + row
+    second = count // CAP_DEV * main + index_ref[0] * spare + row - main
+    slot = jnp.where(row < main, first, second)
+    spot = lax.broadcasted_iota(jnp.int32, (CAP_DEV, count), 1) == slot
+    own = jnp.sum(jnp.where(spot, valid, 0.0), 1, keepdims=True)
+    return jnp.where(spot, valid, 0.0), own
+
+
+def loss_front_body(
+    main, index_ref, middle_ref, *refs
+):
+    feeds = refs[:4]
+    valid_ref, embed_ref, picture_ref = refs[4:7]
+    pooled_ref, text_ref, inverse_ref, weight_ref, row_ref, total_ref = refs[7:]
+    total = middle_ref[...]
+    for ref in feeds:
+        total = total + ref[...].astype(full)
+    pooled = total.astype(low)
+    pooled_ref[...] = pooled
+    embedding = mm(pooled, embed_ref[...])
+    inverse = lax.rsqrt(jnp.sum(embedding * embedding, -1, keepdims=True) + 1e-06)
+    text = embedding * inverse
+    text_ref[...] = text
+    inverse_ref[...] = jnp.broadcast_to(inverse, inverse_ref.shape)
+    sims = LOGIT_SCALE * mm_nt(text.astype(low), picture_ref[...])
+    valid = valid_ref[...]
+    target, own = own_slots(index_ref, valid, main)
+    weight = jnp.where((own > 0.5) & (valid > 0.5), jnp.exp(sims), 0.0)
+    weight_ref[...] = weight
+    row_safe = jnp.where(own > 0.5, jnp.sum(weight, 1, keepdims=True), 1.0)
+    row_ref[...] = jnp.broadcast_to(0.5 / row_safe, row_ref.shape)
+    part = 0.5 * jnp.log(row_safe) - jnp.sum(target * sims, 1, keepdims=True)
+    part = jnp.sum(part, 0, keepdims=True)
+    columns = jnp.sum(weight, 0, keepdims=True)
+    blocks = columns.shape[1] // 128
+    for block in range(blocks):
+        total_ref[block : block + 1] = columns[:, block * 128 : (block + 1) * 128]
+    total_ref[blocks:] = jnp.broadcast_to(part * (1.0 / 128), (1, 128))
+
+
+def loss_front(main, index, middle, feeds, valid, w_embed, pictures):
+    vmem = pl.BlockSpec(memory_space=pltpu.VMEM)
+    count = pictures.shape[0]
+    return pl.pallas_call(
+        functools.partial(loss_front_body, main),
+        out_shape=shapes(
+            ((CAP_DEV, WIDTH), low),
+            ((CAP_DEV, WIDTH), full),
+            ((CAP_DEV, 128), full),
+            ((CAP_DEV, count), full),
+            ((CAP_DEV, 128), full),
+            ((count // 128 + 1, 128), full),
+        ),
+        in_specs=[pl.BlockSpec(memory_space=pltpu.SMEM)] + [vmem] * 8,
+        out_specs=[vmem] * 6,
+        name="loss_front",
+        compiler_params=LIMIT,
+    )(index, middle, *feeds, valid, w_embed, pictures)
+
+
+def loss_back_body(main, parts, index_ref, *refs):
+    totals = refs[:parts]
+    valid_ref, text_ref, inverse_ref, weight_ref, row_ref, picture_ref = refs[parts:-2]
+    d_embed_ref, objective_ref = refs[-2:]
+    total = totals[0][...]
+    for ref in totals[1:]:
+        total = total + ref[...]
+    valid = valid_ref[...]
+    blocks = valid.shape[1] // 128
+    columns = jnp.concatenate([total[block : block + 1] for block in range(blocks)], 1)
+    col_safe = jnp.where(valid > 0.5, columns, 1.0)
+    logs = 0.5 * jnp.sum(jnp.log(col_safe), 1, keepdims=True)
+    rows_part = jnp.sum(total[blocks:], 1, keepdims=True)
+    objective_ref[...] = jnp.broadcast_to(logs + rows_part, objective_ref.shape)
+    target, _ = own_slots(index_ref, valid, main)
+    d_sims = weight_ref[...] * (row_ref[:, :1] + 0.5 / col_safe) - target
+    d_unit = LOGIT_SCALE * mm(d_sims.astype(low), picture_ref[...])
+    text = text_ref[...]
+    along = jnp.sum(text * d_unit, -1, keepdims=True)
+    d_embed_ref[...] = ((d_unit - text * along) * inverse_ref[:, :1]).astype(low)
+
+
+def loss_back(main, index, totals, valid, text, inverse, weight, row, pictures):
+    vmem = pl.BlockSpec(memory_space=pltpu.VMEM)
+    return pl.pallas_call(
+        functools.partial(loss_back_body, main, len(totals)),
+        out_shape=shapes(((CAP_DEV, WIDTH), low), ((1, 128), full)),
+        in_specs=[pl.BlockSpec(memory_space=pltpu.SMEM)] + [vmem] * (6 + len(totals)),
+        out_specs=[vmem] * 2,
+        name="loss_back",
+        compiler_params=LIMIT,
+    )(index, *totals, valid, text, inverse, weight, row, pictures)
 
 
 def place_rows(picks, rows):
@@ -757,66 +855,35 @@
     active, slope = gelu_parts(mm(second_low, w_raise))
     active = active.astype(low)
     lowered = mm_nt(active, w_lower).astype(low)
-    feed = lowered[:CAP_DEV].astype(full)
-    for flip in (1, 2, 3):
-        part = swap_near(lowered[flip * CAP_DEV : (flip + 1) * CAP_DEV], flip)
-        feed = feed + part.astype(full)
-    pooled = (middle[:CAP_DEV] + feed).astype(low)
-    embedding = mm(pooled, w_embed)
-    inverse = lax.rsqrt(jnp.sum(embedding * embedding, -1, keepdims=True) + 1e-06)
-    unit_text = embedding * inverse
-    text_low = unit_text.astype(low)
+    feed_parts = [lowered[:CAP_DEV]] + [
+        swap_near(lowered[flip * CAP_DEV : (flip + 1) * CAP_DEV], flip) for flip in (1, 2, 3)
+    ]
 
     keep_rows = keep_mask.reshape(spread, MICRO, CAP_DEV) == 1
     filled = jnp.arange(CAP_DEV, dtype=jnp.int32)[None, None, :] < counts[:, :, None]
-    valid = keep_rows & filled
-    total_valid = jnp.sum(valid.astype(full))
+    valid = (keep_rows & filled).astype(full)
+    total_valid = jnp.sum(valid)
     batch_valid = lax.dynamic_index_in_dim(valid, group, 1, False)
-    own_valid = lax.dynamic_index_in_dim(batch_valid, plane.index, 0, False)
     batch_valid = jnp.concatenate(
         [batch_valid[:, :main].reshape(-1), batch_valid[:, main:].reshape(-1)]
-    )
-    sims = LOGIT_SCALE * mm_nt(text_low, pictures_all)
-    allowed = own_valid[:, None] & batch_valid[None, :]
-    weight = jnp.where(allowed, jnp.exp(sims), 0.0)
-    row_sum = jnp.sum(weight, 1)
-    place = jnp.arange(CAP_DEV, dtype=jnp.int32)
-    slot = jnp.where(
-        place < main,
-        plane.index * main + place,
-        spread * main + plane.index * spare + place - main,
-    )
-    target = (
-        jnp.arange(spread * CAP_DEV, dtype=jnp.int32)[None, :] == slot[:, None]
-    ) & own_valid[:, None]
-    row_safe = jnp.where(own_valid, row_sum, 1.0)
-    row_part = 0.5 * jnp.sum(jnp.log(row_safe)) - jnp.sum(jnp.where(target, sims, 0.0))
-    col_part = jnp.sum(weight, 0)
-    totals = jnp.concatenate([col_part, jnp.full((128,), 1.0 / 128, full) * row_part])
-    totals = totals.reshape(-1, 128)
+    )[None]
+    if plane.fast:
+        batch_valid = after(batch_valid, near[0])
+    place_flag = plane.index.reshape(1).astype(jnp.int32)
+    pooled, unit_text, inverse, weight, row_half, totals = loss_front(
+        main, place_flag, middle[:CAP_DEV], feed_parts, batch_valid, w_embed, pictures_all
+    )
     if plane.fast:
         pooled_group = swap_near(pooled, 1)
-        for bits in ((1, 4), (2, 8)):
-            sent = [plane.flip(totals, bits[0]), plane.flip(totals, bits[1])]
-            sent.append(plane.flip(totals, sum(bits)))
-            if bits[0] == 1:
-                sent.append(pooled_group)
-            sent = joint(*sent)
-            totals = (totals + sent[0]) + (sent[1] + sent[2])
-            pooled_group = sent[3] if bits[0] == 1 else pooled_group
+        sent = [plane.flip(totals, bits) for bits in (1, 4, 5)]
+        *sent, pooled_group = joint(*sent, pooled_group)
+        totals = (totals + sent[0]) + (sent[1] + sent[2])
+        totals = totals, *joint(*[plane.flip(totals, bits) for bits in (2, 8, 10)])
     else:
-        totals = lax.psum(totals, "dp")
-    totals = totals.reshape(-1)
-    col_sum = totals[: spread * CAP_DEV]
-    col_safe = jnp.where(batch_valid, col_sum, 1.0)
-    objective = jnp.sum(totals[spread * CAP_DEV :]) + 0.5 * jnp.sum(jnp.log(col_safe))
-    d_sims = (
-        weight * (0.5 / row_safe[:, None] + 0.5 / col_safe[None, :]) - target.astype(full)
-    ).astype(low)
-    d_unit = LOGIT_SCALE * mm(d_sims, pictures_all)
-    d_embed = (
-        (d_unit - unit_text * jnp.sum(unit_text * d_unit, -1, keepdims=True)) * inverse
-    ).astype(low)
+        totals = (lax.psum(totals, "dp"),)
+    d_embed, objective = loss_back(
+        main, place_flag, totals, batch_valid, unit_text, inverse, weight, row_half, pictures_all
+    )
 
     d_embed_near = [swap_near(d_embed, flip) for flip in (1, 2, 3)]
     if plane.fast:
@@ -856,7 +923,7 @@
         proj_own = jnp.concatenate([part[:, hidden:] for part in lower_sum], 1)
         raised_sum = jnp.concatenate(raise_sum, 1)
         gain_second = jnp.sum(raised_sum * w_up.astype(full), 1)
-        early = jnp.stack([gain_second, jnp.broadcast_to(objective, (rows,))])
+        early = jnp.stack([gain_second, jnp.broadcast_to(objective[0, 0], (rows,))])
         return proj_own, grad_down, raised_sum, early
 
     def captions_part(start, blocks, d_queries_here, far_parts, done=None):

time: 221 us -> 213 us (0.964)
  waiting for transfers between devices: 52.6 us -> 62.2 us
  other arithmetic: 23.3 us -> 15.5 us
  matrix products: 10.7 us -> 5.62 us
  starting transfers between devices: 57.4 us -> 53.5 us
  between operations: 6.87 us -> 4.4 us
    ppermute x9, waiting for transfers between devices: 6.54 us -> 10 us  [halve(): lax.ppermute(leave, 'dp', [(i, i ^ bit) for i in range(self.count)])]
    ppermute x20, waiting for transfers between devices: 15.8 us -> 19.2 us  [swap_near(): return lax.ppermute(x, ('dp', 'mp'), [(i, i ^ flip) for i in range(size)])]
    dot_general x4 -> x3, matrix products: 4.5 us -> 1.51 us  [mm_nt(): lax.dot_general(a, b, (((1,), (1,)), ((), ())), preferred_element_type=full)]
    ppermute x9, starting transfers between devices: 10.5 us -> 7.92 us  [halve(): lax.ppermute(leave, 'dp', [(i, i ^ bit) for i in range(self.count)])]
    dot_general x7 -> x5, matrix products: 5.71 us -> 3.6 us  [mm(): lax.dot_general(a, b, (((1,), (0,)), ((), ())), preferred_element_type=full)]
  transfers between devices with their start and end apart: 60 -> 60, of which waited for: 22 -> 29; matrix products, arithmetic and copies ran while one was open for 18% -> 14% of each run, Pallas kernels for 23% -> 24%
where the time goes in v6:
time: 213 us; the launch traced here: 212 us
  waiting for transfers between devices  62.2 us (29%)
  Pallas kernels  53.5 us (25%)
  starting transfers between devices  53.5 us (25%)
  local copies, waits for them, and re-layouts  17.6 us (8%)
  other arithmetic  15.5 us (7%)
  matrix products  5.62 us (3%)
  between operations  4.4 us (2%)
    pallas_call x3, Pallas kernels, captions_back(): pl.pallas_call(functools.partial(captions_body, start, blocks), out_shape...  25.1 us
    ppermute x20, waiting for transfers between devices, swap_near(): return lax.ppermute(x, ('dp', 'mp'), [(i, i ^ flip) for i in range(size)])  19.2 us
    ppermute x20, starting transfers between devices, swap_near(): return lax.ppermute(x, ('dp', 'mp'), [(i, i ^ flip) for i in range(size)])  17.6 us
    ppermute x6, waiting for transfers between devices, shift_depth(): lax.ppermute(x, 'dp', [(i, (i + 4 * step) % self.count) for i in range(se...  13.3 us
    ppermute x8, waiting for transfers between devices, swap_side(): return lax.ppermute(x, 'dp', [(i, i ^ 2) for i in range(self.count)])  12.4 us
    ppermute x9, waiting for transfers between devices, halve(): lax.ppermute(leave, 'dp', [(i, i ^ bit) for i in range(self.count)])  10 us
    pallas_call x1, Pallas kernels, attend(): pl.pallas_call(attend_body, grid=(steps,), out_shape=shapes(((count * LEN...  9.93 us
    ppermute x8, starting transfers between devices, swap_side(): return lax.ppermute(x, 'dp', [(i, i ^ 2) for i in range(self.count)])  8.91 us
  transfers between devices with their start and end apart: 60, of which 29 were waited for; matrix products, arithmetic and copies ran while one was open for 14% of the time, Pallas kernels for 24%

profile of v6, /device:TPU:0, one launch (start us, length us, event | category | flops | bytes accessed | tf_op | source)
XLA Modules:
  0.0 212.4 jit_solution(5997266716921953)
XLA Ops:
  0.7 2.1 pack.1
  4.4 3.0 %collective-permute-start.1 = (bf16[96,768]{1,0:T(8,128)(2,1)S(1)}, bf16[96,768]{1,0:T(8,128)(2,1)S(1)}, u32[]{:S(2)}, u32[]{:S(2)}) collective-permute-start(bf16[96,768]{1,0:T(8,128)(2,1)S(1)} %bitcast.217), channel_id=1, source_target_pairs={{0,8},{2,10},{4,12},{6,14},{8,16},{10,18},{12,20},{14,22},{16,24},... | collective-permute-start | bytes 442376 | tf_op jit(solution)/shard_map/ppermute | solution.py:60
  7.4 2.1 collective-permute-start.2
  9.5 1.6 collective-permute-start.3
  12.2 3.5 %all-to-all-start = ((bf16[16,8,768]{2,1,0:T(8,128)(2,1)}), bf16[16,8,768]{2,1,0:T(8,128)(2,1)S(1)}, u32[]{:S(2)}, u32[]{:S(2)}) async-start(bf16[16,8,768]{2,1,0:T(8,128)(2,1)} %fusion.1), calls=%async_computation | async-start | bytes 393216 | tf_op jit(solution)/shard_map/all_to_all | solution.py:722
  16.2 1.5 collective-permute-start.4
  17.7 1.5 collective-permute-start.5
  19.8 7.1 %collective-permute-done.4 = bf16[96,768]{1,0:T(8,128)(2,1)S(1)} collective-permute-done((bf16[96,768]{1,0:T(8,128)(2,1)S(1)}, bf16[96,768]{1,0:T(8,128)(2,1)S(1)}, u32[]{:S(2)}, u32[]{:S(2)}) %collective-permute-start.4) | collective-permute-done | bytes 147488 | tf_op jit(solution)/shard_map/ppermute | solution.py:60
  29.4 4.0 %collective-permute-done.7 = bf16[96,768]{1,0:T(8,128)(2,1)S(1)} collective-permute-done((bf16[96,768]{1,0:T(8,128)(2,1)S(1)}, bf16[96,768]{1,0:T(8,128)(2,1)S(1)}, u32[]{:S(2)}, u32[]{:S(2)}) %collective-permute-start.7) | collective-permute-done | bytes 147488 | tf_op jit(solution)/shard_map/ppermute | solution.py:57
  33.6 1.5 collective-permute-start.9
  36.1 1.5 collective-permute-start.15
  38.6 5.5 %norm_first.1 = (bf16[2048,768]{1,0:T(8,128)(2,1)}, f32[2048,128]{1,0:T(8,128)}, bf16[128,768]{1,0:T(8,128)(2,1)}, bf16[128,768]{1,0:T(8,128)(2,1)}) custom-call(s32[1]{0:T(128)} %bitcast.23.group_ref, bf16[2048,768]{1,0:T(8,128)(2,1)} %bitcast.200, s32[128,1]{1,0:T(8,128)} %copy.33.ends_ref), custom_call_target="tpu_custom_call" | custom-call | tf_op jit(solution)/shard_map/norm_first/pallas_call | solution.py:236
  44.1 2.9 %broadcast_select_fusion.2 = (bf16[768,768]{1,0:T(8,128)(2,1)}, bf16[768,768]{1,0:T(8,128)(2,1)}) fusion(bf16[768,768]{1,0:T(8,128)(2,1)} %collective-permute-done.10, pred[]{:T(512)S(6)} %eq.81, bf16[8,96,768]{2,1,0:T(8,128)(2,1)S(1)} %bitcast_dynamic-update-slice_fusion.15), kind=kLoop, calls=%fused_computation.14 | loop fusion | flops 1179648 | bytes 4718593 | tf_op jit(solution)/shard_map/jit(_where)/select_n | solution.py:41
  46.9 1.7 collective-permute-done.9
  50.8 9.9 %attend.1 = (bf16[2048,768]{1,0:T(8,128)(2,1)}, f32[768,512]{1,0:T(8,128)}, bf16[128,384]{1,0:T(8,128)(2,1)}, bf16[128,384]{1,0:T(8,128)(2,1)}, bf16[128,768]{1,0:T(8,128)(2,1)}) custom-call(bf16[2048,768]{1,0:T(8,128)(2,1)} %get-tuple-element.161.unit_ref, bf16[128,768]{1,0:T(8,128)(2,1)} %get-tuple-element.162.unit_end_ref, s32[128,1]{1,0:T(8,128)} %copy.33.ends_ref, ...), custom_call_target="tpu_custom_call" | custom-call | tf_op jit(solution)/shard_map/attend/pallas_call | solution.py:314
  60.7 2.0 collective-permute-done.11
  63.9 1.5 collective-permute-start.18
  72.6 1.6 collective-permute-start.22
  74.2 2.2 %collective-permute-done.16 = bf16[96,2432]{1,0:T(8,128)(2,1)S(1)} collective-permute-done((bf16[96,2432]{1,0:T(8,128)(2,1)}, bf16[96,2432]{1,0:T(8,128)(2,1)S(1)}, u32[]{:S(2)}, u32[]{:S(2)}) %collective-permute-start.16) | collective-permute-done | bytes 466976 | tf_op jit(solution)/shard_map/ppermute | solution.py:60
  79.2 1.6 broadcast_select_fusion
  80.8 7.6 %collective-permute-done.21 = bf16[96,2432]{1,0:T(8,128)(2,1)S(1)} collective-permute-done((bf16[96,2432]{1,0:T(8,128)(2,1)S(1)}, bf16[96,2432]{1,0:T(8,128)(2,1)S(1)}, u32[]{:S(2)}, u32[]{:S(2)}) %collective-permute-start.21) | collective-permute-done | bytes 466976 | tf_op jit(solution)/shard_map/ppermute | solution.py:57
  88.7 1.6 multiply_convert_fusion
  90.9 1.6 collective-permute-start.24
  94.8 1.8 collective-permute-done.24.refs_1_
  98.8 1.6 collective-permute-start.31
  102.3 1.8 collective-permute-done.29
  106.1 2.5 %collective-permute-start.33 = (f32[9,128]{1,0:T(8,128)S(1)}, f32[9,128]{1,0:T(8,128)S(1)}, u32[]{:S(2)}, u32[]{:S(2)}) collective-permute-start(f32[9,128]{1,0:T(8,128)S(1)} %add_add_fusion.1.refs_0_), channel_id=1, source_target_pairs={{0,16},{2,18},{4,20},{6,22},{8,24},{10,26},{12,28},{14,30},{16,0},... | collective-permute-start | bytes 13832 | tf_op jit(solution)/shard_map/ppermute | solution.py:115
  110.7 3.4 %collective-permute-done.34.refs_3_ = f32[9,128]{1,0:T(8,128)S(1)} collective-permute-done((f32[9,128]{1,0:T(8,128)S(1)}, f32[9,128]{1,0:T(8,128)S(1)}, u32[]{:S(2)}, u32[]{:S(2)}) %collective-permute-start.34) | collective-permute-done | bytes 4640 | tf_op jit(solution)/shard_map/ppermute | solution.py:115
  114.6 1.3 collective-permute-start.35
  116.8 2.9 %collective-permute-done.35 = bf16[64,768]{1,0:T(8,128)(2,1)S(1)} collective-permute-done((bf16[64,768]{1,0:T(8,128)(2,1)S(1)}, bf16[64,768]{1,0:T(8,128)(2,1)S(1)}, u32[]{:S(2)}, u32[]{:S(2)}) %collective-permute-start.35) | collective-permute-done | bytes 98336 | tf_op jit(solution)/shard_map/ppermute | solution.py:120
  119.7 1.3 collective-permute-done.37
  130.2 3.4 %collective-permute-done.42 = bf16[128,768]{1,0:T(8,128)(2,1)S(1)} collective-permute-done((bf16[128,768]{1,0:T(8,128)(2,1)S(1)}, bf16[128,768]{1,0:T(8,128)(2,1)S(1)}, u32[]{:S(2)}, u32[]{:S(2)}) %collective-permute-start.42) | collective-permute-done | bytes 196640 | tf_op jit(solution)/shard_map/ppermute | solution.py:120
  135.7 8.5 %attend_back.1 = (bf16[768,768]{1,0:T(8,128)(2,1)S(1)}, bf16[768,768]{1,0:T(8,128)(2,1)}, bf16[2048,768]{1,0:T(8,128)(2,1)S(1)}, bf16[128,384]{1,0:T(8,128)(2,1)S(1)}, bf16[640,128]{1,0:T(8,128)(2,1)S(1)}) custom-call(s32[1]{0:T(128)} %bitcast.core_ref, bf16[128,768]{1,0:T(8,128)(2,1)S(1)} %get-tuple-element.261.d_mid_ref, ...), custom_call_target="tpu_custom_call" | custom-call | tf_op jit(solution)/shard_map/attend_back/pallas_call | solution.py:399
  144.2 1.6 copy-done.3
  145.8 2.7 %collective-permute-done.40 = bf16[2,2,96,960]{3,2,1,0:T(8,128)(2,1)S(1)} collective-permute-done((bf16[2,2,96,960]{3,2,1,0:T(8,128)(2,1)S(1)}, bf16[2,2,96,960]{3,2,1,0:T(8,128)(2,1)S(1)}, u32[]{:S(2)}, u32[]{:S(2)}) %collective-permute-start.40) | collective-permute-done | bytes 737312 | tf_op jit(solution)/shard_map/ppermute | solution.py:96
  150.6 1.4 collective-permute-start.44
  152.4 4.6 %collective-permute-done.44.small_far_ref = bf16[640,128]{1,0:T(8,128)(2,1)S(1)} collective-permute-done((bf16[640,128]{1,0:T(8,128)(2,1)S(1)}, bf16[640,128]{1,0:T(8,128)(2,1)S(1)}, u32[]{:S(2)}, u32[]{:S(2)}) %collective-permute-start.44) | collective-permute-done | bytes 163872 | tf_op jit(solution)/shard_map/ppermute | solution.py:120
  156.9 2.3 %collective-permute-done.46 = bf16[2,96,768]{2,1,0:T(8,128)(2,1)S(1)} collective-permute-done((bf16[2,96,768]{2,1,0:T(8,128)(2,1)}, bf16[2,96,768]{2,1,0:T(8,128)(2,1)S(1)}, u32[]{:S(2)}, u32[]{:S(2)}) %collective-permute-start.46) | collective-permute-done | bytes 294944 | tf_op jit(solution)/shard_map/ppermute | solution.py:96
  159.3 1.6 add_convert_fusion
  162.1 1.3 collective-permute-start.48
  163.6 10.7 %captions_back.3.refs_0_ = f32[2048,768]{1,0:T(8,128)} custom-call(s32[1]{0:T(128)} %bitcast.23.group_ref, s32[128,1]{1,0:T(8,128)} %copy.33.ends_ref, bf16[2048,768]{1,0:T(8,128)(2,1)} %get-tuple-element.161.unit_ref, f32[2048,128]{1,0:T(8,128)} %get-tuple-element.226.scale_ref, f32[128,768]{1,0:T(8,128)} %get-tuple-element.262.d_mid_ref, ...), custom_call_target="tpu_custom_call" | custom-call | tf_op jit(solution)/shard_map/captions_back/pallas_call | solution.py:644
  176.1 1.3 collective-permute-start.51
  178.6 7.2 %captions_back.4.refs_0_ = f32[2048,768]{1,0:T(8,128)} custom-call(s32[1]{0:T(128)} %bitcast.23.group_ref, s32[128,1]{1,0:T(8,128)} %copy.33.ends_ref, bf16[2048,768]{1,0:T(8,128)(2,1)} %get-tuple-element.161.unit_ref, f32[2048,128]{1,0:T(8,128)} %get-tuple-element.226.scale_ref, ...), custom_call_target="tpu_custom_call", output_to_operand_aliasing={{}: (14, {})} | custom-call | tf_op jit(solution)/shard_map/captions_back/pallas_call | solution.py:644
  186.0 1.5 collective-permute-start.56
  187.6 2.7 %collective-permute-done.52 = bf16[96,960]{1,0:T(8,128)(2,1)S(1)} collective-permute-done((bf16[96,960]{1,0:T(8,128)(2,1)S(1)}, bf16[96,960]{1,0:T(8,128)(2,1)S(1)}, u32[]{:S(2)}, u32[]{:S(2)}) %collective-permute-start.52) | collective-permute-done | bytes 184352 | tf_op jit(solution)/shard_map/ppermute | solution.py:96
  190.7 7.2 %captions_back.5 = f32[2048,768]{1,0:T(8,128)} custom-call(s32[1]{0:T(128)} %bitcast.23.group_ref, s32[128,1]{1,0:T(8,128)} %copy.33.ends_ref, bf16[2048,768]{1,0:T(8,128)(2,1)} %get-tuple-element.161.unit_ref, f32[2048,128]{1,0:T(8,128)} %get-tuple-element.226.scale_ref, f32[128,768]{1,0:T(8,128)} %get-tuple-element.262.d_mid_ref, ...), custom_call_target="tpu_custom_call", output_to_operand_aliasing={{}: (14, {})} | custom-call | tf_op jit(solution)/shard_map/captions_back/pallas_call | solution.py:644
  200.4 2.3 %collective-permute-done.55 = f32[48,384]{1,0:T(8,128)S(1)} collective-permute-done((f32[48,384]{1,0:T(8,128)S(1)}, f32[48,384]{1,0:T(8,128)S(1)}, u32[]{:S(2)}, u32[]{:S(2)}) %collective-permute-start.55) | collective-permute-done | bytes 73760 | tf_op jit(solution)/shard_map/ppermute | solution.py:120
  209.3 1.4 collective-permute-done.58
  (310 shorter events, 60.7 us)
Async XLA Ops:
  4.4 11.4 %collective-permute-start.1 = (bf16[96,768]{1,0:T(8,128)(2,1)S(1)}, bf16[96,768]{1,0:T(8,128)(2,1)S(1)}, u32[]{:S(2)}, u32[]{:S(2)}) collective-permute-start(bf16[96,768]{1,0:T(8,128)(2,1)S(1)} %bitcast.217), channel_id=1, source_target_pairs={{0,8},{2,10},{4,12},{6,14},{8,16},{10,18},{12,20},{14,22},{16,24},... | collective-permute-start | bytes 442376 | tf_op jit(solution)/shard_map/ppermute | solution.py:60
  7.4 8.8 %collective-permute-start.2 = (bf16[96,768]{1,0:T(8,128)(2,1)S(1)}, bf16[96,768]{1,0:T(8,128)(2,1)S(1)}, u32[]{:S(2)}, u32[]{:S(2)}) collective-permute-start(bf16[96,768]{1,0:T(8,128)(2,1)S(1)} %bitcast.218), channel_id=1, source_target_pairs={{0,24},{2,26},{4,28},{6,30},{8,0},{10,2},{12,4},{14,6},{16,8},{18,... | collective-permute-start | bytes 442376 | tf_op jit(solution)/shard_map/ppermute | solution.py:60
  9.5 6.7 %collective-permute-start.3 = (bf16[96,768]{1,0:T(8,128)(2,1)S(1)}, bf16[96,768]{1,0:T(8,128)(2,1)S(1)}, u32[]{:S(2)}, u32[]{:S(2)}) collective-permute-start(bf16[96,768]{1,0:T(8,128)(2,1)S(1)} %bitcast.219), channel_id=1, source_target_pairs={{0,4},{2,6},{4,0},{6,2},{8,12},{10,14},{12,8},{14,10},{16,20},{18,... | collective-permute-start | bytes 442376 | tf_op jit(solution)/shard_map/ppermute | solution.py:57
  12.2 15.5 %all-to-all-start = ((bf16[16,8,768]{2,1,0:T(8,128)(2,1)}), bf16[16,8,768]{2,1,0:T(8,128)(2,1)S(1)}, u32[]{:S(2)}, u32[]{:S(2)}) async-start(bf16[16,8,768]{2,1,0:T(8,128)(2,1)} %fusion.1), calls=%async_computation | async-start | bytes 393216 | tf_op jit(solution)/shard_map/all_to_all | solution.py:722
  16.2 10.7 %collective-permute-start.4 = (bf16[96,768]{1,0:T(8,128)(2,1)S(1)}, bf16[96,768]{1,0:T(8,128)(2,1)S(1)}, u32[]{:S(2)}, u32[]{:S(2)}) collective-permute-start(bf16[96,768]{1,0:T(8,128)(2,1)S(1)} %collective-permute-done.1), channel_id=1, source_target_pairs={{0,8},{2,10},{4,12},{6,14},{8,16},{10,18},{12,20},{14,22},{16,24},... | collective-permute-start | bytes 442376 | tf_op jit(solution)/shard_map/ppermute | solution.py:60
  17.7 9.2 %collective-permute-start.5 = (bf16[96,768]{1,0:T(8,128)(2,1)S(1)}, bf16[96,768]{1,0:T(8,128)(2,1)S(1)}, u32[]{:S(2)}, u32[]{:S(2)}) collective-permute-start(bf16[96,768]{1,0:T(8,128)(2,1)S(1)} %collective-permute-done.1), channel_id=1, source_target_pairs={{0,4},{2,6},{4,0},{6,2},{8,12},{10,14},{12,8},{14,10},{16,20},{18,... | collective-permute-start | bytes 442376 | tf_op jit(solution)/shard_map/ppermute | solution.py:57
  19.1 8.6 %collective-permute-start.6 = (bf16[96,768]{1,0:T(8,128)(2,1)S(1)}, bf16[96,768]{1,0:T(8,128)(2,1)S(1)}, u32[]{:S(2)}, u32[]{:S(2)}) collective-permute-start(bf16[96,768]{1,0:T(8,128)(2,1)S(1)} %collective-permute-done.2), channel_id=1, source_target_pairs={{0,4},{2,6},{4,0},{6,2},{8,12},{10,14},{12,8},{14,10},{16,20},{18,... | collective-permute-start | bytes 442376 | tf_op jit(solution)/shard_map/ppermute | solution.py:57
  28.0 5.3 %collective-permute-start.7 = (bf16[96,768]{1,0:T(8,128)(2,1)S(1)}, bf16[96,768]{1,0:T(8,128)(2,1)S(1)}, u32[]{:S(2)}, u32[]{:S(2)}) collective-permute-start(bf16[96,768]{1,0:T(8,128)(2,1)S(1)} %collective-permute-done.4), channel_id=1, source_target_pairs={{0,4},{2,6},{4,0},{6,2},{8,12},{10,14},{12,8},{14,10},{16,20},{18,... | collective-permute-start | bytes 442376 | tf_op jit(solution)/shard_map/ppermute | solution.py:57
  33.4 10.6 %collective-permute-start.10 = (bf16[768,768]{1,0:T(8,128)(2,1)S(1)}, bf16[768,768]{1,0:T(8,128)(2,1)}, u32[]{:S(2)}, u32[]{:S(2)}) collective-permute-start(bf16[768,768]{1,0:T(8,128)(2,1)S(1)} %bitcast.197), channel_id=1, source_target_pairs={{0,2},{2,0},{4,6},{6,4},{8,10},{10,8},{12,14},{14,12},{16,18},{18,... | collective-permute-start | bytes 3538952 | tf_op jit(solution)/shard_map/ppermute | solution.py:54
  33.6 14.9 %collective-permute-start.9 = (bf16[96,2432]{1,0:T(8,128)(2,1)S(1)}, bf16[96,2432]{1,0:T(8,128)(2,1)S(1)}, u32[]{:S(2)}, u32[]{:S(2)}) collective-permute-start(bf16[96,2432]{1,0:T(8,128)(2,1)S(1)} %bitcast.201), channel_id=1, source_target_pairs={{0,8},{2,10},{4,12},{6,14},{8,16},{10,18},{12,20},{14,22},{16,24},... | collective-permute-start | bytes 1400840 | tf_op jit(solution)/shard_map/ppermute | solution.py:60
  35.1 25.6 %collective-permute-start.12 = (bf16[96,2432]{1,0:T(8,128)(2,1)S(1)}, bf16[96,2432]{1,0:T(8,128)(2,1)}, u32[]{:S(2)}, u32[]{:S(2)}) collective-permute-start(bf16[96,2432]{1,0:T(8,128)(2,1)S(1)} %bitcast.202), channel_id=1, source_target_pairs={{0,4},{2,6},{4,0},{6,2},{8,12},{10,14},{12,8},{14,10},{16,20},{18,... | collective-permute-start | bytes 1400840 | tf_op jit(solution)/shard_map/ppermute | solution.py:57
  36.1 27.8 %collective-permute-start.15 = (bf16[768,768]{1,0:T(8,128)(2,1)S(1)}, bf16[768,768]{1,0:T(8,128)(2,1)S(1)}, u32[]{:S(2)}, u32[]{:S(2)}) collective-permute-start(bf16[768,768]{1,0:T(8,128)(2,1)S(1)} %bitcast.198), channel_id=1, source_target_pairs={{0,1},{1,0},{2,3},{3,2},{4,5},{5,4},{6,7},{7,6},{8,9},{9,8},{10,11... | collective-permute-start | bytes 3538952 | tf_op jit(solution)/shard_map/ppermute | solution.py:120
  48.6 14.1 %collective-permute-start.11 = (bf16[96,2432]{1,0:T(8,128)(2,1)S(1)}, bf16[96,2432]{1,0:T(8,128)(2,1)}, u32[]{:S(2)}, u32[]{:S(2)}) collective-permute-start(bf16[96,2432]{1,0:T(8,128)(2,1)S(1)} %collective-permute-done.9), channel_id=1, source_target_pairs={{0,8},{2,10},{4,12},{6,14},{8,16},{10,18},{12,20},{14,22},{16,24},... | collective-permute-start | bytes 1400840 | tf_op jit(solution)/shard_map/ppermute | solution.py:60
  48.6 14.1 %collective-permute-start.13 = (bf16[96,2432]{1,0:T(8,128)(2,1)S(1)}, bf16[96,2432]{1,0:T(8,128)(2,1)}, u32[]{:S(2)}, u32[]{:S(2)}) collective-permute-start(bf16[96,2432]{1,0:T(8,128)(2,1)S(1)} %collective-permute-done.9), channel_id=1, source_target_pairs={{0,4},{2,6},{4,0},{6,2},{8,12},{10,14},{12,8},{14,10},{16,20},{18,... | collective-permute-start | bytes 1400840 | tf_op jit(solution)/shard_map/ppermute | solution.py:57
  50.5 10.3 %collective-permute-start.14 = (bf16[128,768]{1,0:T(8,128)(2,1)}, bf16[128,768]{1,0:T(8,128)(2,1)}, u32[]{:S(2)}, u32[]{:S(2)}) collective-permute-start(bf16[128,768]{1,0:T(8,128)(2,1)} %get-tuple-element.159), channel_id=1, source_target_pairs={{0,2},{1,3},{2,0},{3,1},{4,6},{5,7},{6,4},{7,5},{8,10},{9,11},{10,... | collective-permute-start | bytes 589832 | tf_op jit(solution)/shard_map/ppermute | solution.py:120
  62.7 13.7 %collective-permute-start.16 = (bf16[96,2432]{1,0:T(8,128)(2,1)}, bf16[96,2432]{1,0:T(8,128)(2,1)S(1)}, u32[]{:S(2)}, u32[]{:S(2)}) collective-permute-start(bf16[96,2432]{1,0:T(8,128)(2,1)} %collective-permute-done.11), channel_id=1, source_target_pairs={{0,8},{2,10},{4,12},{6,14},{8,16},{10,18},{12,20},{14,22},{16,24},... | collective-permute-start | bytes 1400840 | tf_op jit(solution)/shard_map/ppermute | solution.py:60
  62.7 13.7 %collective-permute-start.17 = (bf16[96,2432]{1,0:T(8,128)(2,1)}, bf16[96,2432]{1,0:T(8,128)(2,1)S(1)}, u32[]{:S(2)}, u32[]{:S(2)}) collective-permute-start(bf16[96,2432]{1,0:T(8,128)(2,1)} %collective-permute-done.11), channel_id=1, source_target_pairs={{0,4},{2,6},{4,0},{6,2},{8,12},{10,14},{12,8},{14,10},{16,20},{18,... | collective-permute-start | bytes 1400840 | tf_op jit(solution)/shard_map/ppermute | solution.py:57
  63.9 8.5 %collective-permute-start.18 = (bf16[128,768]{1,0:T(8,128)(2,1)}, bf16[128,768]{1,0:T(8,128)(2,1)S(1)}, u32[]{:S(2)}, u32[]{:S(2)}) collective-permute-start(bf16[128,768]{1,0:T(8,128)(2,1)} %get-tuple-element.172), channel_id=1, source_target_pairs={{0,1},{1,0},{2,3},{3,2},{4,5},{5,4},{6,7},{7,6},{8,9},{9,8},{10,11... | collective-permute-start | bytes 589832 | tf_op jit(solution)/shard_map/ppermute | solution.py:120
  65.5 7.1 %collective-permute-start.19 = (bf16[128,768]{1,0:T(8,128)(2,1)}, bf16[128,768]{1,0:T(8,128)(2,1)S(1)}, u32[]{:S(2)}, u32[]{:S(2)}) collective-permute-start(bf16[128,768]{1,0:T(8,128)(2,1)} %get-tuple-element.172), channel_id=1, source_target_pairs={{0,2},{1,3},{2,0},{3,1},{4,6},{5,7},{6,4},{7,5},{8,10},{9,11},{10,... | collective-permute-start | bytes 589832 | tf_op jit(solution)/shard_map/ppermute | solution.py:120
  65.5 8.7 %collective-permute-start.20 = (bf16[128,768]{1,0:T(8,128)(2,1)}, bf16[128,768]{1,0:T(8,128)(2,1)S(1)}, u32[]{:S(2)}, u32[]{:S(2)}) collective-permute-start(bf16[128,768]{1,0:T(8,128)(2,1)} %get-tuple-element.172), channel_id=1, source_target_pairs={{0,3},{1,2},{2,1},{3,0},{4,7},{5,6},{6,5},{7,4},{8,11},{9,10},{10,... | collective-permute-start | bytes 589832 | tf_op jit(solution)/shard_map/ppermute | solution.py:120
  72.5 6.7 %collective-permute-start.23 = (bf16[768,768]{1,0:T(8,128)(2,1)S(1)}, bf16[768,768]{1,0:T(8,128)(2,1)S(1)}, u32[]{:S(2)}, u32[]{:S(2)}) collective-permute-start(bf16[768,768]{1,0:T(8,128)(2,1)S(1)} %collective-permute-done.15), channel_id=1, source_target_pairs={{0,2},{2,0},{4,6},{6,4},{8,10},{10,8},{12,14},{14,12},{16,18},{18,... | collective-permute-start | bytes 3538952 | tf_op jit(solution)/shard_map/ppermute | solution.py:54
  72.6 8.2 %collective-permute-start.22 = (bf16[128,384]{1,0:T(8,128)(2,1)S(1)}, bf16[128,384]{1,0:T(8,128)(2,1)S(1)}, u32[]{:S(2)}, u32[]{:S(2)}) collective-permute-start(bf16[128,384]{1,0:T(8,128)(2,1)S(1)} %copy-done.10), channel_id=1, source_target_pairs={{0,1},{1,0},{2,3},{3,2},{4,5},{5,4},{6,7},{7,6},{8,9},{9,8},{10,11... | collective-permute-start | bytes 294920 | tf_op jit(solution)/shard_map/ppermute | solution.py:120
  77.6 10.9 %collective-permute-start.21 = (bf16[96,2432]{1,0:T(8,128)(2,1)S(1)}, bf16[96,2432]{1,0:T(8,128)(2,1)S(1)}, u32[]{:S(2)}, u32[]{:S(2)}) collective-permute-start(bf16[96,2432]{1,0:T(8,128)(2,1)S(1)} %collective-permute-done.16), channel_id=1, source_target_pairs={{0,4},{2,6},{4,0},{6,2},{8,12},{10,14},{12,8},{14,10},{16,20},{18,... | collective-permute-start | bytes 1400840 | tf_op jit(solution)/shard_map/ppermute | solution.py:57
  88.5 4.7 %collective-permute-start.27 = (bf16[768,896]{1,0:T(8,128)(2,1)S(1)}, bf16[768,896]{1,0:T(8,128)(2,1)S(1)}, u32[]{:S(2)}, u32[]{:S(2)}) collective-permute-start(bf16[768,896]{1,0:T(8,128)(2,1)S(1)} %bitcast.189), channel_id=1, source_target_pairs={{0,2},{2,0},{4,6},{6,4},{8,10},{10,8},{12,14},{14,12},{16,18},{18,... | collective-permute-start | bytes 4128776 | tf_op jit(solution)/shard_map/ppermute | solution.py:54
  90.9 5.7 %collective-permute-start.24 = (bf16[64,768]{1,0:T(8,128)(2,1)S(1)}, bf16[64,768]{1,0:T(8,128)(2,1)S(1)}, u32[]{:S(2)}, u32[]{:S(2)}) collective-permute-start(bf16[64,768]{1,0:T(8,128)(2,1)S(1)} %get-tuple-element.297), channel_id=1, source_target_pairs={{0,1},{1,0},{2,3},{3,2},{4,5},{5,4},{6,7},{7,6},{8,9},{9,8},{10,11... | collective-permute-start | bytes 294920 | tf_op jit(solution)/shard_map/ppermute | solution.py:120
  92.7 5.1 %collective-permute-start.26 = (bf16[64,768]{1,0:T(8,128)(2,1)S(1)}, bf16[64,768]{1,0:T(8,128)(2,1)S(1)}, u32[]{:S(2)}, u32[]{:S(2)}) collective-permute-start(bf16[64,768]{1,0:T(8,128)(2,1)S(1)} %get-tuple-element.295), channel_id=1, source_target_pairs={{0,3},{1,2},{2,1},{3,0},{4,7},{5,6},{6,5},{7,4},{8,11},{9,10},{10,... | collective-permute-start | bytes 294920 | tf_op jit(solution)/shard_map/ppermute | solution.py:120
  98.8 5.9 %collective-permute-start.31 = (bf16[64,768]{1,0:T(8,128)(2,1)S(1)}, bf16[64,768]{1,0:T(8,128)(2,1)S(1)}, u32[]{:S(2)}, u32[]{:S(2)}) collective-permute-start(bf16[64,768]{1,0:T(8,128)(2,1)S(1)} %get-tuple-element.190), channel_id=1, source_target_pairs={{0,1},{1,0},{2,3},{3,2},{4,5},{5,4},{6,7},{7,6},{8,9},{9,8},{10,11... | collective-permute-start | bytes 294920 | tf_op jit(solution)/shard_map/ppermute | solution.py:120
  104.8 16.2 %collective-permute-start.38 = (bf16[128,768]{1,0:T(8,128)(2,1)S(1)}, bf16[128,768]{1,0:T(8,128)(2,1)S(1)}, u32[]{:S(2)}, u32[]{:S(2)}) collective-permute-start(bf16[128,768]{1,0:T(8,128)(2,1)S(1)} %pad_maximum_fusion.8), channel_id=1, source_target_pairs={{0,2},{2,0},{4,6},{6,4},{8,10},{10,8},{12,14},{14,12},{16,18},{18,... | collective-permute-start | bytes 589832 | tf_op jit(solution)/shard_map/ppermute | solution.py:54
  108.6 5.4 %collective-permute-start.34 = (f32[9,128]{1,0:T(8,128)S(1)}, f32[9,128]{1,0:T(8,128)S(1)}, u32[]{:S(2)}, u32[]{:S(2)}) collective-permute-start(f32[9,128]{1,0:T(8,128)S(1)} %add_add_fusion.1.refs_0_), channel_id=1, source_target_pairs={{0,20},{2,22},{4,16},{6,18},{8,28},{10,30},{12,24},{14,26},{16,4},... | collective-permute-start | bytes 13832 | tf_op jit(solution)/shard_map/ppermute | solution.py:115
  114.6 5.1 %collective-permute-start.35 = (bf16[64,768]{1,0:T(8,128)(2,1)S(1)}, bf16[64,768]{1,0:T(8,128)(2,1)S(1)}, u32[]{:S(2)}, u32[]{:S(2)}) collective-permute-start(bf16[64,768]{1,0:T(8,128)(2,1)S(1)} %get-tuple-element.201), channel_id=1, source_target_pairs={{0,1},{1,0},{2,3},{3,2},{4,5},{5,4},{6,7},{7,6},{8,9},{9,8},{10,11... | collective-permute-start | bytes 294920 | tf_op jit(solution)/shard_map/ppermute | solution.py:120
  115.9 5.1 %collective-permute-start.37 = (bf16[64,768]{1,0:T(8,128)(2,1)S(1)}, bf16[64,768]{1,0:T(8,128)(2,1)S(1)}, u32[]{:S(2)}, u32[]{:S(2)}) collective-permute-start(bf16[64,768]{1,0:T(8,128)(2,1)S(1)} %get-tuple-element.201), channel_id=1, source_target_pairs={{0,3},{1,2},{2,1},{3,0},{4,7},{5,6},{6,5},{7,4},{8,11},{9,10},{10,... | collective-permute-start | bytes 294920 | tf_op jit(solution)/shard_map/ppermute | solution.py:120
  125.3 20.6 %collective-permute-start.39 = (bf16[2,2,96,768]{3,2,1,0:T(8,128)(2,1)S(1)}, bf16[2,2,96,768]{3,2,1,0:T(8,128)(2,1)S(1)}, u32[]{:S(2)}, u32[]{:S(2)}) collective-permute-start(bf16[2,2,96,768]{3,2,1,0:T(8,128)(2,1)S(1)} %get-tuple-element.279), channel_id=1, source_target_pairs={{0,8},{2,10},{4,12},{6,14},{8,0},{10,2},{12,4},{14,6},{16,24},{18,... | collective-permute-start | bytes 1769480 | tf_op jit(solution)/shard_map/ppermute | solution.py:96
  126.5 7.1 %collective-permute-start.42 = (bf16[128,768]{1,0:T(8,128)(2,1)S(1)}, bf16[128,768]{1,0:T(8,128)(2,1)S(1)}, u32[]{:S(2)}, u32[]{:S(2)}) collective-permute-start(bf16[128,768]{1,0:T(8,128)(2,1)S(1)} %add_convert_fusion.7), channel_id=1, source_target_pairs={{0,1},{1,0},{2,3},{3,2},{4,5},{5,4},{6,7},{7,6},{8,9},{9,8},{10,11... | collective-permute-start | bytes 589832 | tf_op jit(solution)/shard_map/ppermute | solution.py:120
  129.2 19.3 %collective-permute-start.40 = (bf16[2,2,96,960]{3,2,1,0:T(8,128)(2,1)S(1)}, bf16[2,2,96,960]{3,2,1,0:T(8,128)(2,1)S(1)}, u32[]{:S(2)}, u32[]{:S(2)}) collective-permute-start(bf16[2,2,96,960]{3,2,1,0:T(8,128)(2,1)S(1)} %get-tuple-element.271), channel_id=1, source_target_pairs={{0,4},{2,6},{4,0},{6,2},{8,12},{10,14},{12,8},{14,10},{16,20},{18,... | collective-permute-start | bytes 2211848 | tf_op jit(solution)/shard_map/ppermute | solution.py:96
  135.1 10.8 %collective-permute-start.43 = (bf16[128,384]{1,0:T(8,128)(2,1)S(1)}, bf16[128,384]{1,0:T(8,128)(2,1)S(1)}, u32[]{:S(2)}, u32[]{:S(2)}) collective-permute-start(bf16[128,384]{1,0:T(8,128)(2,1)S(1)} %convolution_convert_fusion.4.d_att_ref), channel_id=1, source_target_pairs={{0,1},{1,0},{2,3},{3,2},{4,5},{5,4},{6,7},{7,6},{8,9},{9,8},{10,11... | collective-permute-start | bytes 294920 | tf_op jit(solution)/shard_map/ppermute | solution.py:120
  148.5 10.7 %collective-permute-start.45 = (bf16[768,768]{1,0:T(8,128)(2,1)}, bf16[768,768]{1,0:T(8,128)(2,1)}, u32[]{:S(2)}, u32[]{:S(2)}) collective-permute-start(bf16[768,768]{1,0:T(8,128)(2,1)} %get-tuple-element.216), channel_id=1, source_target_pairs={{0,2},{2,0},{4,6},{6,4},{8,10},{10,8},{12,14},{14,12},{16,18},{18,... | collective-permute-start | bytes 3538952 | tf_op jit(solution)/shard_map/ppermute | solution.py:54
  149.6 9.7 %collective-permute-start.46 = (bf16[2,96,768]{2,1,0:T(8,128)(2,1)}, bf16[2,96,768]{2,1,0:T(8,128)(2,1)S(1)}, u32[]{:S(2)}, u32[]{:S(2)}) collective-permute-start(bf16[2,96,768]{2,1,0:T(8,128)(2,1)} %get-tuple-element.287), channel_id=1, source_target_pairs={{0,4},{2,6},{4,0},{6,2},{8,12},{10,14},{12,8},{14,10},{16,20},{18,... | collective-permute-start | bytes 884744 | tf_op jit(solution)/shard_map/ppermute | solution.py:96
  150.6 6.3 %collective-permute-start.44 = (bf16[640,128]{1,0:T(8,128)(2,1)S(1)}, bf16[640,128]{1,0:T(8,128)(2,1)S(1)}, u32[]{:S(2)}, u32[]{:S(2)}) collective-permute-start(bf16[640,128]{1,0:T(8,128)(2,1)S(1)} %get-tuple-element.215), channel_id=1, source_target_pairs={{0,1},{1,0},{2,3},{3,2},{4,5},{5,4},{6,7},{7,6},{8,9},{9,8},{10,11... | collective-permute-start | bytes 491528 | tf_op jit(solution)/shard_map/ppermute | solution.py:120
  161.0 14.9 %collective-permute-start.49 = (bf16[2,2,96,768]{3,2,1,0:T(8,128)(2,1)S(1)}, bf16[2,2,96,768]{3,2,1,0:T(8,128)(2,1)S(1)}, u32[]{:S(2)}, u32[]{:S(2)}) collective-permute-start(bf16[2,2,96,768]{3,2,1,0:T(8,128)(2,1)S(1)} %get-tuple-element.277), channel_id=1, source_target_pairs={{0,4},{2,6},{4,0},{6,2},{8,12},{10,14},{12,8},{14,10},{16,20},{18,... | collective-permute-start | bytes 1769480 | tf_op jit(solution)/shard_map/ppermute | solution.py:96
  162.1 13.6 %collective-permute-start.48 = (bf16[2,96,960]{2,1,0:T(8,128)(2,1)S(1)}, bf16[2,96,960]{2,1,0:T(8,128)(2,1)S(1)}, u32[]{:S(2)}, u32[]{:S(2)}) collective-permute-start(bf16[2,96,960]{2,1,0:T(8,128)(2,1)S(1)} %get-tuple-element.281), channel_id=1, source_target_pairs={{0,8},{2,10},{4,12},{6,14},{8,0},{10,2},{12,4},{14,6},{16,24},{18,... | collective-permute-start | bytes 1105928 | tf_op jit(solution)/shard_map/ppermute | solution.py:96
  163.5 11.0 %collective-permute-start.47 = (bf16[96,768]{1,0:T(8,128)(2,1)S(1)}, bf16[96,768]{1,0:T(8,128)(2,1)S(1)}, u32[]{:S(2)}, u32[]{:S(2)}) collective-permute-start(bf16[96,768]{1,0:T(8,128)(2,1)S(1)} %get-tuple-element.303), channel_id=1, source_target_pairs={{0,16},{2,18},{4,20},{6,22},{8,24},{10,26},{12,28},{14,30},{16,0},... | collective-permute-start | bytes 442376 | tf_op jit(solution)/shard_map/ppermute | solution.py:96
  176.1 14.1 %collective-permute-start.51 = (bf16[2,96,768]{2,1,0:T(8,128)(2,1)S(1)}, bf16[2,96,768]{2,1,0:T(8,128)(2,1)S(1)}, u32[]{:S(2)}, u32[]{:S(2)}) collective-permute-start(bf16[2,96,768]{2,1,0:T(8,128)(2,1)S(1)} %get-tuple-element.285), channel_id=1, source_target_pairs={{0,8},{2,10},{4,12},{6,14},{8,0},{10,2},{12,4},{14,6},{16,24},{18,... | collective-permute-start | bytes 884744 | tf_op jit(solution)/shard_map/ppermute | solution.py:96
  177.5 8.3 %collective-permute-start.50 = (f32[48,768]{1,0:T(8,128)S(1)}, f32[48,768]{1,0:T(8,128)S(1)}, u32[]{:S(2)}, u32[]{:S(2)}) collective-permute-start(f32[48,768]{1,0:T(8,128)S(1)} %dynamic-slice_bitcast_fusion.18), channel_id=1, source_target_pairs={{0,2},{2,0},{4,6},{6,4},{8,10},{10,8},{12,14},{14,12},{16,18},{18,... | collective-permute-start | bytes 442376 | tf_op jit(solution)/shard_map/ppermute | solution.py:54
  177.8 12.5 %collective-permute-start.52 = (bf16[96,960]{1,0:T(8,128)(2,1)S(1)}, bf16[96,960]{1,0:T(8,128)(2,1)S(1)}, u32[]{:S(2)}, u32[]{:S(2)}) collective-permute-start(bf16[96,960]{1,0:T(8,128)(2,1)S(1)} %get-tuple-element.293), channel_id=1, source_target_pairs={{0,16},{2,18},{4,20},{6,22},{8,24},{10,26},{12,28},{14,30},{16,0},... | collective-permute-start | bytes 552968 | tf_op jit(solution)/shard_map/ppermute | solution.py:96
  186.0 13.6 %collective-permute-start.56 = (f32[2,48]{1,0:T(2,128)S(1)}, f32[2,48]{1,0:T(2,128)S(1)}, u32[]{:S(2)}, u32[]{:S(2)}) collective-permute-start(f32[2,48]{1,0:T(2,128)S(1)} %stack.19), channel_id=1, source_target_pairs={{0,1},{1,0},{2,3},{3,2},{4,5},{5,4},{6,7},{7,6},{8,9},{9,8},{10,11... | collective-permute-start | bytes 1160 | tf_op jit(solution)/shard_map/ppermute | solution.py:120
  190.3 7.6 %collective-permute-start.54 = (f32[48,960]{1,0:T(8,128)S(1)}, f32[48,960]{1,0:T(8,128)S(1)}, u32[]{:S(2)}, u32[]{:S(2)}) collective-permute-start(f32[48,960]{1,0:T(8,128)S(1)} %dynamic-slice_bitcast_fusion.12), channel_id=1, source_target_pairs={{0,2},{2,0},{4,6},{6,4},{8,10},{10,8},{12,14},{14,12},{16,18},{18,... | collective-permute-start | bytes 552968 | tf_op jit(solution)/shard_map/ppermute | solution.py:54
  190.5 9.9 %collective-permute-start.53 = (bf16[96,768]{1,0:T(8,128)(2,1)S(1)}, bf16[96,768]{1,0:T(8,128)(2,1)S(1)}, u32[]{:S(2)}, u32[]{:S(2)}) collective-permute-start(bf16[96,768]{1,0:T(8,128)(2,1)S(1)} %get-tuple-element.301), channel_id=1, source_target_pairs={{0,16},{2,18},{4,20},{6,22},{8,24},{10,26},{12,28},{14,30},{16,0},... | collective-permute-start | bytes 442376 | tf_op jit(solution)/shard_map/ppermute | solution.py:96
  198.1 4.6 %collective-permute-start.55 = (f32[48,384]{1,0:T(8,128)S(1)}, f32[48,384]{1,0:T(8,128)S(1)}, u32[]{:S(2)}, u32[]{:S(2)}) collective-permute-start(f32[48,384]{1,0:T(8,128)S(1)} %pad_maximum_fusion.10), channel_id=1, source_target_pairs={{0,1},{1,0},{2,3},{3,2},{4,5},{5,4},{6,7},{7,6},{8,9},{9,8},{10,11... | collective-permute-start | bytes 221192 | tf_op jit(solution)/shard_map/ppermute | solution.py:120
  (56 other events, 307.5 us)

commit v7 on v6

--- a/solution.py
+++ b/solution.py
@@ -429,10 +429,10 @@
     )(core, d_mid, d_att, unit, unit_end, mixed, probs, queries, attended)
 
 
-def lower_back_body(flag_ref, d_out_ref, active_ref, pooled_ref, d_embed_ref, out_ref):
-    hidden = active_ref.shape[1]
+def raise_back_body(flag_ref, second_ref, d_raised_ref, pooled_ref, d_embed_ref, out_ref):
+    hidden = d_raised_ref.shape[1]
     quarter = WIDTH // 4
-    out_ref[:, :hidden] = mm_tn(d_out_ref[...], active_ref[...]).astype(low)
+    out_ref[:, :hidden] = mm_tn(second_ref[...], d_raised_ref[...]).astype(low)
     here = d_embed_ref[:, :quarter]
     for index in range(1, 4):
         part = d_embed_ref[:, index * quarter : (index + 1) * quarter]
@@ -440,16 +440,16 @@
     out_ref[:, hidden:] = mm_tn(pooled_ref[...], here).astype(low)
 
 
-def lower_back(flag, d_out, active, pooled, d_embed):
+def raise_back(flag, second, d_raised, pooled, d_embed):
     vmem = pl.BlockSpec(memory_space=pltpu.VMEM)
     return pl.pallas_call(
-        lower_back_body,
-        out_shape=jax.ShapeDtypeStruct((WIDTH, active.shape[1] + WIDTH // 4), low),
+        raise_back_body,
+        out_shape=jax.ShapeDtypeStruct((WIDTH, d_raised.shape[1] + WIDTH // 4), low),
         in_specs=[pl.BlockSpec(memory_space=pltpu.SMEM)] + [vmem] * 4,
         out_specs=vmem,
-        name="lower_back",
+        name="raise_back",
         compiler_params=LIMIT,
-    )(flag, d_out, active, pooled, d_embed)
+    )(flag, second, d_raised, pooled, d_embed)
 
 
 def own_slots(index_ref, valid, main):
@@ -899,9 +899,9 @@
     d_out_low = d_pooled.astype(low)
     d_raised = (mm(d_out_low, w_lower) * slope).astype(low)
     d_second = mm_nt(d_raised, w_raise).astype(low)
-    g_raise = mm_tn(second_low, d_raised).astype(low)
-    d_out_late = after(d_out_low, g_raise, d_second)
-    g_lower = lower_back(2 * group_flag + core_flag, d_out_late, active, pooled_all, d_embed_all)
+    second_late = after(second_low, d_second)
+    g_raise = raise_back(2 * group_flag + core_flag, second_late, d_raised, pooled_all, d_embed_all)
+    g_lower = mm_tn(after(d_out_low, d_second), active).astype(low)
     if plane.fast:
         raise_stay, raise_in = plane.halve(g_raise.reshape(2, 2, 2, 2 * rows, -1), 1, 4)
         lower_stay, lower_in = plane.halve(g_lower.reshape(2, 2, 2, 2 * rows, -1), 2, 2)
@@ -919,9 +919,9 @@
     )
 
     def early_parts(raise_sum, lower_sum):
-        grad_down = jnp.concatenate([part[:, :hidden] for part in lower_sum], 1)
-        proj_own = jnp.concatenate([part[:, hidden:] for part in lower_sum], 1)
-        raised_sum = jnp.concatenate(raise_sum, 1)
+        grad_down = jnp.concatenate(lower_sum, 1)
+        proj_own = jnp.concatenate([part[:, hidden:] for part in raise_sum], 1)
+        raised_sum = jnp.concatenate([part[:, :hidden] for part in raise_sum], 1)
         gain_second = jnp.sum(raised_sum * w_up.astype(full), 1)
         early = jnp.stack([gain_second, jnp.broadcast_to(objective[0, 0], (rows,))])
         return proj_own, grad_down, raised_sum, early
@@ -933,8 +933,8 @@
         )
 
     if plane.fast:
-        raise_stay, raise_in, lower_stay, lower_in, small, d_queries, g_send, d_attended_far = joint(
-            raise_stay, raise_in, lower_stay, lower_in, small, d_queries, g_send, d_attended_far
+        raise_stay, raise_in, lower_stay, lower_in, d_queries, g_send, d_attended_far = joint(
+            raise_stay, raise_in, lower_stay, lower_in, d_queries, g_send, d_attended_far
         )
         small_far = swap_group(small)
         mix_in = plane.swap_core(g_send)

time: 213 us -> 211 us (level)
  waiting for transfers between devices: 62.2 us -> 55.4 us
  other arithmetic: 15.5 us -> 18.7 us
  starting transfers between devices: 53.5 us -> 56 us
    ppermute x9, waiting for transfers between devices: 10 us -> 6.39 us  [halve(): lax.ppermute(leave, 'dp', [(i, i ^ bit) for i in range(self.count)])]
    ppermute x9, starting transfers between devices: 7.92 us -> 10.2 us  [halve(): lax.ppermute(leave, 'dp', [(i, i ^ bit) for i in range(self.count)])]
    ppermute x20, waiting for transfers between devices: 19.2 us -> 17 us  [swap_near(): return lax.ppermute(x, ('dp', 'mp'), [(i, i ^ flip) for i in range(size)])]
  transfers between devices with their start and end apart: 60 -> 60, of which waited for: 29 -> 23; matrix products, arithmetic and copies ran while one was open for 14% -> 15% of each run, Pallas kernels for 24% -> 24%
where the time goes in v7:
time: 211 us
  starting transfers between devices  56 us (27%)
  waiting for transfers between devices  55.4 us (26%)
  Pallas kernels  53.4 us (25%)
  other arithmetic  18.7 us (9%)
  local copies, waits for them, and re-layouts  17 us (8%)
  matrix products  5.72 us (3%)
  between operations  4.43 us (2%)
    pallas_call x3, Pallas kernels, captions_back(): pl.pallas_call(functools.partial(captions_body, start, blocks), out_shape...  25.1 us
    ppermute x20, starting transfers between devices, swap_near(): return lax.ppermute(x, ('dp', 'mp'), [(i, i ^ flip) for i in range(size)])  17.7 us
    ppermute x20, waiting for transfers between devices, swap_near(): return lax.ppermute(x, ('dp', 'mp'), [(i, i ^ flip) for i in range(size)])  17 us
    ppermute x6, waiting for transfers between devices, shift_depth(): lax.ppermute(x, 'dp', [(i, (i + 4 * step) % self.count) for i in range(se...  13.2 us
    ppermute x8, waiting for transfers between devices, swap_side(): return lax.ppermute(x, 'dp', [(i, i ^ 2) for i in range(self.count)])  11.6 us
    ppermute x9, starting transfers between devices, halve(): lax.ppermute(leave, 'dp', [(i, i ^ bit) for i in range(self.count)])  10.2 us
    pallas_call x1, Pallas kernels, attend(): pl.pallas_call(attend_body, grid=(steps,), out_shape=shapes(((count * LEN...  9.93 us
    ppermute x8, starting transfers between devices, swap_side(): return lax.ppermute(x, 'dp', [(i, i ^ 2) for i in range(self.count)])  8.91 us
  transfers between devices with their start and end apart: 60, of which 23 were waited for; matrix products, arithmetic and copies ran while one was open for 15% of the time, Pallas kernels for 24%

profile of v7, /device:TPU:0, one launch (start us, length us, event | category | flops | bytes accessed | tf_op | source)
XLA Modules:
  0.0 210.6 jit_solution(6015873955982422470)
XLA Ops:
  0.7 2.1 pack.1
  4.4 3.0 %collective-permute-start.1 = (bf16[96,768]{1,0:T(8,128)(2,1)S(1)}, bf16[96,768]{1,0:T(8,128)(2,1)S(1)}, u32[]{:S(2)}, u32[]{:S(2)}) collective-permute-start(bf16[96,768]{1,0:T(8,128)(2,1)S(1)} %bitcast.219), channel_id=1, source_target_pairs={{0,8},{2,10},{4,12},{6,14},{8,16},{10,18},{12,20},{14,22},{16,24},... | collective-permute-start | bytes 442376 | tf_op jit(solution)/shard_map/ppermute | solution.py:60
  7.4 2.1 collective-permute-start.2
  9.5 1.6 collective-permute-start.3
  12.2 3.5 %all-to-all-start = ((bf16[16,8,768]{2,1,0:T(8,128)(2,1)}), bf16[16,8,768]{2,1,0:T(8,128)(2,1)S(1)}, u32[]{:S(2)}, u32[]{:S(2)}) async-start(bf16[16,8,768]{2,1,0:T(8,128)(2,1)} %fusion.1), calls=%async_computation | async-start | bytes 393216 | tf_op jit(solution)/shard_map/all_to_all | solution.py:722
  16.2 1.5 collective-permute-start.4
  17.7 1.5 collective-permute-start.5
  19.8 7.1 %collective-permute-done.4 = bf16[96,768]{1,0:T(8,128)(2,1)S(1)} collective-permute-done((bf16[96,768]{1,0:T(8,128)(2,1)S(1)}, bf16[96,768]{1,0:T(8,128)(2,1)S(1)}, u32[]{:S(2)}, u32[]{:S(2)}) %collective-permute-start.4) | collective-permute-done | bytes 147488 | tf_op jit(solution)/shard_map/ppermute | solution.py:60
  29.4 4.0 %collective-permute-done.7 = bf16[96,768]{1,0:T(8,128)(2,1)S(1)} collective-permute-done((bf16[96,768]{1,0:T(8,128)(2,1)S(1)}, bf16[96,768]{1,0:T(8,128)(2,1)S(1)}, u32[]{:S(2)}, u32[]{:S(2)}) %collective-permute-start.7) | collective-permute-done | bytes 147488 | tf_op jit(solution)/shard_map/ppermute | solution.py:57
  33.6 1.5 collective-permute-start.9
  36.1 1.5 collective-permute-start.15
  38.6 5.5 %norm_first.1 = (bf16[2048,768]{1,0:T(8,128)(2,1)}, f32[2048,128]{1,0:T(8,128)}, bf16[128,768]{1,0:T(8,128)(2,1)}, bf16[128,768]{1,0:T(8,128)(2,1)}) custom-call(s32[1]{0:T(128)} %bitcast.24.group_ref, bf16[2048,768]{1,0:T(8,128)(2,1)} %bitcast.198, s32[128,1]{1,0:T(8,128)} %copy.33.ends_ref), custom_call_target="tpu_custom_call" | custom-call | tf_op jit(solution)/shard_map/norm_first/pallas_call | solution.py:236
  44.1 2.9 %broadcast_select_fusion.2 = (bf16[768,768]{1,0:T(8,128)(2,1)}, bf16[768,768]{1,0:T(8,128)(2,1)}) fusion(bf16[768,768]{1,0:T(8,128)(2,1)} %collective-permute-done.10, pred[]{:T(512)S(6)} %eq.81, bf16[8,96,768]{2,1,0:T(8,128)(2,1)S(1)} %bitcast_dynamic-update-slice_fusion.15), kind=kLoop, calls=%fused_computation.14 | loop fusion | flops 1179648 | bytes 4718593 | tf_op jit(solution)/shard_map/jit(_where)/select_n | solution.py:41
  46.9 1.6 collective-permute-done.9
  50.8 9.9 %attend.1 = (bf16[2048,768]{1,0:T(8,128)(2,1)}, f32[768,512]{1,0:T(8,128)}, bf16[128,384]{1,0:T(8,128)(2,1)}, bf16[128,384]{1,0:T(8,128)(2,1)}, bf16[128,768]{1,0:T(8,128)(2,1)}) custom-call(bf16[2048,768]{1,0:T(8,128)(2,1)} %get-tuple-element.161.unit_ref, bf16[128,768]{1,0:T(8,128)(2,1)} %get-tuple-element.162.unit_end_ref, s32[128,1]{1,0:T(8,128)} %copy.33.ends_ref, ...), custom_call_target="tpu_custom_call" | custom-call | tf_op jit(solution)/shard_map/attend/pallas_call | solution.py:314
  60.7 2.0 collective-permute-done.11
  63.9 1.5 collective-permute-start.18
  72.6 1.6 collective-permute-start.22
  74.2 2.2 %collective-permute-done.16 = bf16[96,2432]{1,0:T(8,128)(2,1)S(1)} collective-permute-done((bf16[96,2432]{1,0:T(8,128)(2,1)}, bf16[96,2432]{1,0:T(8,128)(2,1)S(1)}, u32[]{:S(2)}, u32[]{:S(2)}) %collective-permute-start.16) | collective-permute-done | bytes 466976 | tf_op jit(solution)/shard_map/ppermute | solution.py:60
  76.4 1.2 fusion.29
  80.1 1.8 broadcast_select_fusion
  81.9 6.8 %collective-permute-done.21 = bf16[96,2432]{1,0:T(8,128)(2,1)S(1)} collective-permute-done((bf16[96,2432]{1,0:T(8,128)(2,1)S(1)}, bf16[96,2432]{1,0:T(8,128)(2,1)S(1)}, u32[]{:S(2)}, u32[]{:S(2)}) %collective-permute-start.21) | collective-permute-done | bytes 466976 | tf_op jit(solution)/shard_map/ppermute | solution.py:57
  89.0 1.7 multiply_convert_fusion
  91.2 1.6 collective-permute-start.24
  95.1 1.8 collective-permute-done.24.refs_1_
  99.2 1.6 collective-permute-start.31
  100.8 1.2 collective-permute-start.29
  102.6 1.8 collective-permute-done.29
  106.4 2.5 %collective-permute-start.33 = (f32[9,128]{1,0:T(8,128)S(1)}, f32[9,128]{1,0:T(8,128)S(1)}, u32[]{:S(2)}, u32[]{:S(2)}) collective-permute-start(f32[9,128]{1,0:T(8,128)S(1)} %add_add_fusion.1.refs_0_), channel_id=1, source_target_pairs={{0,16},{2,18},{4,20},{6,22},{8,24},{10,26},{12,28},{14,30},{16,0},... | collective-permute-start | bytes 13832 | tf_op jit(solution)/shard_map/ppermute | solution.py:115
  109.8 1.2 collective-permute-done.33.refs_2_
  111.0 3.4 %collective-permute-done.34.refs_3_ = f32[9,128]{1,0:T(8,128)S(1)} collective-permute-done((f32[9,128]{1,0:T(8,128)S(1)}, f32[9,128]{1,0:T(8,128)S(1)}, u32[]{:S(2)}, u32[]{:S(2)}) %collective-permute-start.34) | collective-permute-done | bytes 4640 | tf_op jit(solution)/shard_map/ppermute | solution.py:115
  114.9 1.3 collective-permute-start.35
  117.1 2.9 %collective-permute-done.35 = bf16[64,768]{1,0:T(8,128)(2,1)S(1)} collective-permute-done((bf16[64,768]{1,0:T(8,128)(2,1)S(1)}, bf16[64,768]{1,0:T(8,128)(2,1)S(1)}, u32[]{:S(2)}, u32[]{:S(2)}) %collective-permute-start.35) | collective-permute-done | bytes 98336 | tf_op jit(solution)/shard_map/ppermute | solution.py:120
  120.0 1.3 collective-permute-done.37
  126.6 1.5 collective-permute-start.42
  130.5 4.3 %collective-permute-done.40 = bf16[128,768]{1,0:T(8,128)(2,1)S(1)} collective-permute-done((bf16[128,768]{1,0:T(8,128)(2,1)S(1)}, bf16[128,768]{1,0:T(8,128)(2,1)S(1)}, u32[]{:S(2)}, u32[]{:S(2)}) %collective-permute-start.40) | collective-permute-done | bytes 196640 | tf_op jit(solution)/shard_map/ppermute | solution.py:120
  136.9 8.5 %attend_back.1 = (bf16[768,768]{1,0:T(8,128)(2,1)S(1)}, bf16[768,768]{1,0:T(8,128)(2,1)}, bf16[2048,768]{1,0:T(8,128)(2,1)S(1)}, bf16[128,384]{1,0:T(8,128)(2,1)S(1)}, bf16[640,128]{1,0:T(8,128)(2,1)S(1)}) custom-call(s32[1]{0:T(128)} %bitcast.core_ref, bf16[128,768]{1,0:T(8,128)(2,1)S(1)} %get-tuple-element.261.d_mid_ref, ...), custom_call_target="tpu_custom_call" | custom-call | tf_op jit(solution)/shard_map/attend_back/pallas_call | solution.py:399
  149.2 1.3 collective-permute-start.41
  150.7 4.4 %collective-permute-done.41.small_far_ref = bf16[640,128]{1,0:T(8,128)(2,1)S(1)} collective-permute-done((bf16[640,128]{1,0:T(8,128)(2,1)S(1)}, bf16[640,128]{1,0:T(8,128)(2,1)S(1)}, u32[]{:S(2)}, u32[]{:S(2)}) %collective-permute-start.41) | collective-permute-done | bytes 163872 | tf_op jit(solution)/shard_map/ppermute | solution.py:120
  155.1 4.5 %collective-permute-done.46 = bf16[2,96,960]{2,1,0:T(8,128)(2,1)} collective-permute-done((bf16[2,96,960]{2,1,0:T(8,128)(2,1)}, bf16[2,96,960]{2,1,0:T(8,128)(2,1)}, u32[]{:S(2)}, u32[]{:S(2)}) %collective-permute-start.46) | collective-permute-done | bytes 368672 | tf_op jit(solution)/shard_map/ppermute | solution.py:96
  159.6 1.6 add_convert_fusion
  165.8 10.6 %captions_back.3.refs_0_ = f32[2048,768]{1,0:T(8,128)} custom-call(s32[1]{0:T(128)} %bitcast.24.group_ref, s32[128,1]{1,0:T(8,128)} %copy.33.ends_ref, bf16[2048,768]{1,0:T(8,128)(2,1)} %get-tuple-element.161.unit_ref, f32[2048,128]{1,0:T(8,128)} %get-tuple-element.226.scale_ref, f32[128,768]{1,0:T(8,128)} %get-tuple-element.262.d_mid_ref, ...), custom_call_target="tpu_custom_call" | custom-call | tf_op jit(solution)/shard_map/captions_back/pallas_call | solution.py:644
  178.0 2.5 %collective-permute-start.52 = (bf16[96,768]{1,0:T(8,128)(2,1)S(1)}, bf16[96,768]{1,0:T(8,128)(2,1)S(1)}, u32[]{:S(2)}, u32[]{:S(2)}) collective-permute-start(bf16[96,768]{1,0:T(8,128)(2,1)S(1)} %get-tuple-element.305), channel_id=1, source_target_pairs={{0,16},{2,18},{4,20},{6,22},{8,24},{10,26},{12,28},{14,30},{16,0},... | collective-permute-start | bytes 442376 | tf_op jit(solution)/shard_map/ppermute | solution.py:96
  180.6 7.2 %captions_back.4.refs_0_ = f32[2048,768]{1,0:T(8,128)} custom-call(s32[1]{0:T(128)} %bitcast.24.group_ref, s32[128,1]{1,0:T(8,128)} %copy.33.ends_ref, bf16[2048,768]{1,0:T(8,128)(2,1)} %get-tuple-element.161.unit_ref, f32[2048,128]{1,0:T(8,128)} %get-tuple-element.226.scale_ref, ...), custom_call_target="tpu_custom_call", output_to_operand_aliasing={{}: (14, {})} | custom-call | tf_op jit(solution)/shard_map/captions_back/pallas_call | solution.py:644
  188.0 1.4 collective-permute-start.54
  191.1 7.2 %captions_back.5 = f32[2048,768]{1,0:T(8,128)} custom-call(s32[1]{0:T(128)} %bitcast.24.group_ref, s32[128,1]{1,0:T(8,128)} %copy.33.ends_ref, bf16[2048,768]{1,0:T(8,128)(2,1)} %get-tuple-element.161.unit_ref, f32[2048,128]{1,0:T(8,128)} %get-tuple-element.226.scale_ref, f32[128,768]{1,0:T(8,128)} %get-tuple-element.262.d_mid_ref, ...), custom_call_target="tpu_custom_call", output_to_operand_aliasing={{}: (14, {})} | custom-call | tf_op jit(solution)/shard_map/captions_back/pallas_call | solution.py:644
  199.1 1.8 collective-permute-done.53
  205.3 1.4 collective-permute-start.58
  (304 shorter events, 59.4 us)
Async XLA Ops:
  4.4 11.4 %collective-permute-start.1 = (bf16[96,768]{1,0:T(8,128)(2,1)S(1)}, bf16[96,768]{1,0:T(8,128)(2,1)S(1)}, u32[]{:S(2)}, u32[]{:S(2)}) collective-permute-start(bf16[96,768]{1,0:T(8,128)(2,1)S(1)} %bitcast.219), channel_id=1, source_target_pairs={{0,8},{2,10},{4,12},{6,14},{8,16},{10,18},{12,20},{14,22},{16,24},... | collective-permute-start | bytes 442376 | tf_op jit(solution)/shard_map/ppermute | solution.py:60
  7.4 8.8 %collective-permute-start.2 = (bf16[96,768]{1,0:T(8,128)(2,1)S(1)}, bf16[96,768]{1,0:T(8,128)(2,1)S(1)}, u32[]{:S(2)}, u32[]{:S(2)}) collective-permute-start(bf16[96,768]{1,0:T(8,128)(2,1)S(1)} %bitcast.220), channel_id=1, source_target_pairs={{0,24},{2,26},{4,28},{6,30},{8,0},{10,2},{12,4},{14,6},{16,8},{18,... | collective-permute-start | bytes 442376 | tf_op jit(solution)/shard_map/ppermute | solution.py:60
  9.5 6.7 %collective-permute-start.3 = (bf16[96,768]{1,0:T(8,128)(2,1)S(1)}, bf16[96,768]{1,0:T(8,128)(2,1)S(1)}, u32[]{:S(2)}, u32[]{:S(2)}) collective-permute-start(bf16[96,768]{1,0:T(8,128)(2,1)S(1)} %bitcast.221), channel_id=1, source_target_pairs={{0,4},{2,6},{4,0},{6,2},{8,12},{10,14},{12,8},{14,10},{16,20},{18,... | collective-permute-start | bytes 442376 | tf_op jit(solution)/shard_map/ppermute | solution.py:57
  12.2 15.5 %all-to-all-start = ((bf16[16,8,768]{2,1,0:T(8,128)(2,1)}), bf16[16,8,768]{2,1,0:T(8,128)(2,1)S(1)}, u32[]{:S(2)}, u32[]{:S(2)}) async-start(bf16[16,8,768]{2,1,0:T(8,128)(2,1)} %fusion.1), calls=%async_computation | async-start | bytes 393216 | tf_op jit(solution)/shard_map/all_to_all | solution.py:722
  16.2 10.7 %collective-permute-start.4 = (bf16[96,768]{1,0:T(8,128)(2,1)S(1)}, bf16[96,768]{1,0:T(8,128)(2,1)S(1)}, u32[]{:S(2)}, u32[]{:S(2)}) collective-permute-start(bf16[96,768]{1,0:T(8,128)(2,1)S(1)} %collective-permute-done.1), channel_id=1, source_target_pairs={{0,8},{2,10},{4,12},{6,14},{8,16},{10,18},{12,20},{14,22},{16,24},... | collective-permute-start | bytes 442376 | tf_op jit(solution)/shard_map/ppermute | solution.py:60
  17.7 9.2 %collective-permute-start.5 = (bf16[96,768]{1,0:T(8,128)(2,1)S(1)}, bf16[96,768]{1,0:T(8,128)(2,1)S(1)}, u32[]{:S(2)}, u32[]{:S(2)}) collective-permute-start(bf16[96,768]{1,0:T(8,128)(2,1)S(1)} %collective-permute-done.1), channel_id=1, source_target_pairs={{0,4},{2,6},{4,0},{6,2},{8,12},{10,14},{12,8},{14,10},{16,20},{18,... | collective-permute-start | bytes 442376 | tf_op jit(solution)/shard_map/ppermute | solution.py:57
  19.1 8.6 %collective-permute-start.6 = (bf16[96,768]{1,0:T(8,128)(2,1)S(1)}, bf16[96,768]{1,0:T(8,128)(2,1)S(1)}, u32[]{:S(2)}, u32[]{:S(2)}) collective-permute-start(bf16[96,768]{1,0:T(8,128)(2,1)S(1)} %collective-permute-done.2), channel_id=1, source_target_pairs={{0,4},{2,6},{4,0},{6,2},{8,12},{10,14},{12,8},{14,10},{16,20},{18,... | collective-permute-start | bytes 442376 | tf_op jit(solution)/shard_map/ppermute | solution.py:57
  28.0 5.3 %collective-permute-start.7 = (bf16[96,768]{1,0:T(8,128)(2,1)S(1)}, bf16[96,768]{1,0:T(8,128)(2,1)S(1)}, u32[]{:S(2)}, u32[]{:S(2)}) collective-permute-start(bf16[96,768]{1,0:T(8,128)(2,1)S(1)} %collective-permute-done.4), channel_id=1, source_target_pairs={{0,4},{2,6},{4,0},{6,2},{8,12},{10,14},{12,8},{14,10},{16,20},{18,... | collective-permute-start | bytes 442376 | tf_op jit(solution)/shard_map/ppermute | solution.py:57
  33.4 10.6 %collective-permute-start.10 = (bf16[768,768]{1,0:T(8,128)(2,1)S(1)}, bf16[768,768]{1,0:T(8,128)(2,1)}, u32[]{:S(2)}, u32[]{:S(2)}) collective-permute-start(bf16[768,768]{1,0:T(8,128)(2,1)S(1)} %bitcast.195), channel_id=1, source_target_pairs={{0,2},{2,0},{4,6},{6,4},{8,10},{10,8},{12,14},{14,12},{16,18},{18,... | collective-permute-start | bytes 3538952 | tf_op jit(solution)/shard_map/ppermute | solution.py:54
  33.6 14.9 %collective-permute-start.9 = (bf16[96,2432]{1,0:T(8,128)(2,1)S(1)}, bf16[96,2432]{1,0:T(8,128)(2,1)S(1)}, u32[]{:S(2)}, u32[]{:S(2)}) collective-permute-start(bf16[96,2432]{1,0:T(8,128)(2,1)S(1)} %bitcast.203), channel_id=1, source_target_pairs={{0,8},{2,10},{4,12},{6,14},{8,16},{10,18},{12,20},{14,22},{16,24},... | collective-permute-start | bytes 1400840 | tf_op jit(solution)/shard_map/ppermute | solution.py:60
  35.1 25.6 %collective-permute-start.12 = (bf16[96,2432]{1,0:T(8,128)(2,1)S(1)}, bf16[96,2432]{1,0:T(8,128)(2,1)}, u32[]{:S(2)}, u32[]{:S(2)}) collective-permute-start(bf16[96,2432]{1,0:T(8,128)(2,1)S(1)} %bitcast.204), channel_id=1, source_target_pairs={{0,4},{2,6},{4,0},{6,2},{8,12},{10,14},{12,8},{14,10},{16,20},{18,... | collective-permute-start | bytes 1400840 | tf_op jit(solution)/shard_map/ppermute | solution.py:57
  36.1 27.8 %collective-permute-start.15 = (bf16[768,768]{1,0:T(8,128)(2,1)S(1)}, bf16[768,768]{1,0:T(8,128)(2,1)S(1)}, u32[]{:S(2)}, u32[]{:S(2)}) collective-permute-start(bf16[768,768]{1,0:T(8,128)(2,1)S(1)} %bitcast.196), channel_id=1, source_target_pairs={{0,1},{1,0},{2,3},{3,2},{4,5},{5,4},{6,7},{7,6},{8,9},{9,8},{10,11... | collective-permute-start | bytes 3538952 | tf_op jit(solution)/shard_map/ppermute | solution.py:120
  48.6 14.1 %collective-permute-start.11 = (bf16[96,2432]{1,0:T(8,128)(2,1)S(1)}, bf16[96,2432]{1,0:T(8,128)(2,1)}, u32[]{:S(2)}, u32[]{:S(2)}) collective-permute-start(bf16[96,2432]{1,0:T(8,128)(2,1)S(1)} %collective-permute-done.9), channel_id=1, source_target_pairs={{0,8},{2,10},{4,12},{6,14},{8,16},{10,18},{12,20},{14,22},{16,24},... | collective-permute-start | bytes 1400840 | tf_op jit(solution)/shard_map/ppermute | solution.py:60
  48.6 14.1 %collective-permute-start.13 = (bf16[96,2432]{1,0:T(8,128)(2,1)S(1)}, bf16[96,2432]{1,0:T(8,128)(2,1)}, u32[]{:S(2)}, u32[]{:S(2)}) collective-permute-start(bf16[96,2432]{1,0:T(8,128)(2,1)S(1)} %collective-permute-done.9), channel_id=1, source_target_pairs={{0,4},{2,6},{4,0},{6,2},{8,12},{10,14},{12,8},{14,10},{16,20},{18,... | collective-permute-start | bytes 1400840 | tf_op jit(solution)/shard_map/ppermute | solution.py:57
  50.5 10.3 %collective-permute-start.14 = (bf16[128,768]{1,0:T(8,128)(2,1)}, bf16[128,768]{1,0:T(8,128)(2,1)}, u32[]{:S(2)}, u32[]{:S(2)}) collective-permute-start(bf16[128,768]{1,0:T(8,128)(2,1)} %get-tuple-element.159), channel_id=1, source_target_pairs={{0,2},{1,3},{2,0},{3,1},{4,6},{5,7},{6,4},{7,5},{8,10},{9,11},{10,... | collective-permute-start | bytes 589832 | tf_op jit(solution)/shard_map/ppermute | solution.py:120
  62.7 13.7 %collective-permute-start.16 = (bf16[96,2432]{1,0:T(8,128)(2,1)}, bf16[96,2432]{1,0:T(8,128)(2,1)S(1)}, u32[]{:S(2)}, u32[]{:S(2)}) collective-permute-start(bf16[96,2432]{1,0:T(8,128)(2,1)} %collective-permute-done.11), channel_id=1, source_target_pairs={{0,8},{2,10},{4,12},{6,14},{8,16},{10,18},{12,20},{14,22},{16,24},... | collective-permute-start | bytes 1400840 | tf_op jit(solution)/shard_map/ppermute | solution.py:60
  62.7 13.7 %collective-permute-start.17 = (bf16[96,2432]{1,0:T(8,128)(2,1)}, bf16[96,2432]{1,0:T(8,128)(2,1)S(1)}, u32[]{:S(2)}, u32[]{:S(2)}) collective-permute-start(bf16[96,2432]{1,0:T(8,128)(2,1)} %collective-permute-done.11), channel_id=1, source_target_pairs={{0,4},{2,6},{4,0},{6,2},{8,12},{10,14},{12,8},{14,10},{16,20},{18,... | collective-permute-start | bytes 1400840 | tf_op jit(solution)/shard_map/ppermute | solution.py:57
  63.9 8.5 %collective-permute-start.18 = (bf16[128,768]{1,0:T(8,128)(2,1)}, bf16[128,768]{1,0:T(8,128)(2,1)S(1)}, u32[]{:S(2)}, u32[]{:S(2)}) collective-permute-start(bf16[128,768]{1,0:T(8,128)(2,1)} %get-tuple-element.172), channel_id=1, source_target_pairs={{0,1},{1,0},{2,3},{3,2},{4,5},{5,4},{6,7},{7,6},{8,9},{9,8},{10,11... | collective-permute-start | bytes 589832 | tf_op jit(solution)/shard_map/ppermute | solution.py:120
  65.5 7.1 %collective-permute-start.19 = (bf16[128,768]{1,0:T(8,128)(2,1)}, bf16[128,768]{1,0:T(8,128)(2,1)S(1)}, u32[]{:S(2)}, u32[]{:S(2)}) collective-permute-start(bf16[128,768]{1,0:T(8,128)(2,1)} %get-tuple-element.172), channel_id=1, source_target_pairs={{0,2},{1,3},{2,0},{3,1},{4,6},{5,7},{6,4},{7,5},{8,10},{9,11},{10,... | collective-permute-start | bytes 589832 | tf_op jit(solution)/shard_map/ppermute | solution.py:120
  65.5 8.7 %collective-permute-start.20 = (bf16[128,768]{1,0:T(8,128)(2,1)}, bf16[128,768]{1,0:T(8,128)(2,1)S(1)}, u32[]{:S(2)}, u32[]{:S(2)}) collective-permute-start(bf16[128,768]{1,0:T(8,128)(2,1)} %get-tuple-element.172), channel_id=1, source_target_pairs={{0,3},{1,2},{2,1},{3,0},{4,7},{5,6},{6,5},{7,4},{8,11},{9,10},{10,... | collective-permute-start | bytes 589832 | tf_op jit(solution)/shard_map/ppermute | solution.py:120
  72.5 7.6 %collective-permute-start.23 = (bf16[768,768]{1,0:T(8,128)(2,1)S(1)}, bf16[768,768]{1,0:T(8,128)(2,1)S(1)}, u32[]{:S(2)}, u32[]{:S(2)}) collective-permute-start(bf16[768,768]{1,0:T(8,128)(2,1)S(1)} %collective-permute-done.15), channel_id=1, source_target_pairs={{0,2},{2,0},{4,6},{6,4},{8,10},{10,8},{12,14},{14,12},{16,18},{18,... | collective-permute-start | bytes 3538952 | tf_op jit(solution)/shard_map/ppermute | solution.py:54
  72.6 9.4 %collective-permute-start.22 = (bf16[128,384]{1,0:T(8,128)(2,1)S(1)}, bf16[128,384]{1,0:T(8,128)(2,1)S(1)}, u32[]{:S(2)}, u32[]{:S(2)}) collective-permute-start(bf16[128,384]{1,0:T(8,128)(2,1)S(1)} %copy-done.10), channel_id=1, source_target_pairs={{0,1},{1,0},{2,3},{3,2},{4,5},{5,4},{6,7},{7,6},{8,9},{9,8},{10,11... | collective-permute-start | bytes 294920 | tf_op jit(solution)/shard_map/ppermute | solution.py:120
  77.8 10.9 %collective-permute-start.21 = (bf16[96,2432]{1,0:T(8,128)(2,1)S(1)}, bf16[96,2432]{1,0:T(8,128)(2,1)S(1)}, u32[]{:S(2)}, u32[]{:S(2)}) collective-permute-start(bf16[96,2432]{1,0:T(8,128)(2,1)S(1)} %collective-permute-done.16), channel_id=1, source_target_pairs={{0,4},{2,6},{4,0},{6,2},{8,12},{10,14},{12,8},{14,10},{16,20},{18,... | collective-permute-start | bytes 1400840 | tf_op jit(solution)/shard_map/ppermute | solution.py:57
  88.8 4.8 %collective-permute-start.27 = (bf16[768,896]{1,0:T(8,128)(2,1)S(1)}, bf16[768,896]{1,0:T(8,128)(2,1)S(1)}, u32[]{:S(2)}, u32[]{:S(2)}) collective-permute-start(bf16[768,896]{1,0:T(8,128)(2,1)S(1)} %bitcast.191), channel_id=1, source_target_pairs={{0,2},{2,0},{4,6},{6,4},{8,10},{10,8},{12,14},{14,12},{16,18},{18,... | collective-permute-start | bytes 4128776 | tf_op jit(solution)/shard_map/ppermute | solution.py:54
  91.2 5.7 %collective-permute-start.24 = (bf16[64,768]{1,0:T(8,128)(2,1)S(1)}, bf16[64,768]{1,0:T(8,128)(2,1)S(1)}, u32[]{:S(2)}, u32[]{:S(2)}) collective-permute-start(bf16[64,768]{1,0:T(8,128)(2,1)S(1)} %get-tuple-element.299), channel_id=1, source_target_pairs={{0,1},{1,0},{2,3},{3,2},{4,5},{5,4},{6,7},{7,6},{8,9},{9,8},{10,11... | collective-permute-start | bytes 294920 | tf_op jit(solution)/shard_map/ppermute | solution.py:120
  93.0 5.1 %collective-permute-start.26 = (bf16[64,768]{1,0:T(8,128)(2,1)S(1)}, bf16[64,768]{1,0:T(8,128)(2,1)S(1)}, u32[]{:S(2)}, u32[]{:S(2)}) collective-permute-start(bf16[64,768]{1,0:T(8,128)(2,1)S(1)} %get-tuple-element.297), channel_id=1, source_target_pairs={{0,3},{1,2},{2,1},{3,0},{4,7},{5,6},{6,5},{7,4},{8,11},{9,10},{10,... | collective-permute-start | bytes 294920 | tf_op jit(solution)/shard_map/ppermute | solution.py:120
  99.2 5.9 %collective-permute-start.31 = (bf16[64,768]{1,0:T(8,128)(2,1)S(1)}, bf16[64,768]{1,0:T(8,128)(2,1)S(1)}, u32[]{:S(2)}, u32[]{:S(2)}) collective-permute-start(bf16[64,768]{1,0:T(8,128)(2,1)S(1)} %get-tuple-element.190), channel_id=1, source_target_pairs={{0,1},{1,0},{2,3},{3,2},{4,5},{5,4},{6,7},{7,6},{8,9},{9,8},{10,11... | collective-permute-start | bytes 294920 | tf_op jit(solution)/shard_map/ppermute | solution.py:120
  105.1 16.2 %collective-permute-start.38 = (bf16[128,768]{1,0:T(8,128)(2,1)S(1)}, bf16[128,768]{1,0:T(8,128)(2,1)}, u32[]{:S(2)}, u32[]{:S(2)}) collective-permute-start(bf16[128,768]{1,0:T(8,128)(2,1)S(1)} %pad_maximum_fusion.8), channel_id=1, source_target_pairs={{0,2},{2,0},{4,6},{6,4},{8,10},{10,8},{12,14},{14,12},{16,18},{18,... | collective-permute-start | bytes 589832 | tf_op jit(solution)/shard_map/ppermute | solution.py:54
  108.9 5.4 %collective-permute-start.34 = (f32[9,128]{1,0:T(8,128)S(1)}, f32[9,128]{1,0:T(8,128)S(1)}, u32[]{:S(2)}, u32[]{:S(2)}) collective-permute-start(f32[9,128]{1,0:T(8,128)S(1)} %add_add_fusion.1.refs_0_), channel_id=1, source_target_pairs={{0,20},{2,22},{4,16},{6,18},{8,28},{10,30},{12,24},{14,26},{16,4},... | collective-permute-start | bytes 13832 | tf_op jit(solution)/shard_map/ppermute | solution.py:115
  114.9 5.1 %collective-permute-start.35 = (bf16[64,768]{1,0:T(8,128)(2,1)S(1)}, bf16[64,768]{1,0:T(8,128)(2,1)S(1)}, u32[]{:S(2)}, u32[]{:S(2)}) collective-permute-start(bf16[64,768]{1,0:T(8,128)(2,1)S(1)} %get-tuple-element.201), channel_id=1, source_target_pairs={{0,1},{1,0},{2,3},{3,2},{4,5},{5,4},{6,7},{7,6},{8,9},{9,8},{10,11... | collective-permute-start | bytes 294920 | tf_op jit(solution)/shard_map/ppermute | solution.py:120
  116.2 5.1 %collective-permute-start.37 = (bf16[64,768]{1,0:T(8,128)(2,1)S(1)}, bf16[64,768]{1,0:T(8,128)(2,1)S(1)}, u32[]{:S(2)}, u32[]{:S(2)}) collective-permute-start(bf16[64,768]{1,0:T(8,128)(2,1)S(1)} %get-tuple-element.201), channel_id=1, source_target_pairs={{0,3},{1,2},{2,1},{3,0},{4,7},{5,6},{6,5},{7,4},{8,11},{9,10},{10,... | collective-permute-start | bytes 294920 | tf_op jit(solution)/shard_map/ppermute | solution.py:120
  126.6 19.9 %collective-permute-start.42 = (bf16[2,2,96,960]{3,2,1,0:T(8,128)(2,1)S(1)}, bf16[2,2,96,960]{3,2,1,0:T(8,128)(2,1)S(1)}, u32[]{:S(2)}, u32[]{:S(2)}) collective-permute-start(bf16[2,2,96,960]{3,2,1,0:T(8,128)(2,1)S(1)} %get-tuple-element.273), channel_id=1, source_target_pairs={{0,8},{2,10},{4,12},{6,14},{8,0},{10,2},{12,4},{14,6},{16,24},{18,... | collective-permute-start | bytes 2211848 | tf_op jit(solution)/shard_map/ppermute | solution.py:96
  128.1 6.6 %collective-permute-start.40 = (bf16[128,768]{1,0:T(8,128)(2,1)S(1)}, bf16[128,768]{1,0:T(8,128)(2,1)S(1)}, u32[]{:S(2)}, u32[]{:S(2)}) collective-permute-start(bf16[128,768]{1,0:T(8,128)(2,1)S(1)} %add_convert_fusion.7), channel_id=1, source_target_pairs={{0,1},{1,0},{2,3},{3,2},{4,5},{5,4},{6,7},{7,6},{8,9},{9,8},{10,11... | collective-permute-start | bytes 589832 | tf_op jit(solution)/shard_map/ppermute | solution.py:120
  129.4 17.0 %collective-permute-start.43 = (bf16[2,2,96,768]{3,2,1,0:T(8,128)(2,1)S(1)}, bf16[2,2,96,768]{3,2,1,0:T(8,128)(2,1)S(1)}, u32[]{:S(2)}, u32[]{:S(2)}) collective-permute-start(bf16[2,2,96,768]{3,2,1,0:T(8,128)(2,1)S(1)} %get-tuple-element.281), channel_id=1, source_target_pairs={{0,4},{2,6},{4,0},{6,2},{8,12},{10,14},{12,8},{14,10},{16,20},{18,... | collective-permute-start | bytes 1769480 | tf_op jit(solution)/shard_map/ppermute | solution.py:96
  136.2 10.2 %collective-permute-start.44 = (bf16[128,384]{1,0:T(8,128)(2,1)S(1)}, bf16[128,384]{1,0:T(8,128)(2,1)S(1)}, u32[]{:S(2)}, u32[]{:S(2)}) collective-permute-start(bf16[128,384]{1,0:T(8,128)(2,1)S(1)} %convolution_convert_fusion.4.d_att_ref), channel_id=1, source_target_pairs={{0,1},{1,0},{2,3},{3,2},{4,5},{5,4},{6,7},{7,6},{8,9},{9,8},{10,11... | collective-permute-start | bytes 294920 | tf_op jit(solution)/shard_map/ppermute | solution.py:120
  146.5 13.2 %collective-permute-start.45 = (bf16[768,768]{1,0:T(8,128)(2,1)}, bf16[768,768]{1,0:T(8,128)(2,1)}, u32[]{:S(2)}, u32[]{:S(2)}) collective-permute-start(bf16[768,768]{1,0:T(8,128)(2,1)} %get-tuple-element.216), channel_id=1, source_target_pairs={{0,2},{2,0},{4,6},{6,4},{8,10},{10,8},{12,14},{14,12},{16,18},{18,... | collective-permute-start | bytes 3538952 | tf_op jit(solution)/shard_map/ppermute | solution.py:54
  148.3 11.4 %collective-permute-start.46 = (bf16[2,96,960]{2,1,0:T(8,128)(2,1)}, bf16[2,96,960]{2,1,0:T(8,128)(2,1)}, u32[]{:S(2)}, u32[]{:S(2)}) collective-permute-start(bf16[2,96,960]{2,1,0:T(8,128)(2,1)} %get-tuple-element.283), channel_id=1, source_target_pairs={{0,4},{2,6},{4,0},{6,2},{8,12},{10,14},{12,8},{14,10},{16,20},{18,... | collective-permute-start | bytes 1105928 | tf_op jit(solution)/shard_map/ppermute | solution.py:96
  149.2 5.9 %collective-permute-start.41 = (bf16[640,128]{1,0:T(8,128)(2,1)S(1)}, bf16[640,128]{1,0:T(8,128)(2,1)S(1)}, u32[]{:S(2)}, u32[]{:S(2)}) collective-permute-start(bf16[640,128]{1,0:T(8,128)(2,1)S(1)} %get-tuple-element.210), channel_id=1, source_target_pairs={{0,1},{1,0},{2,3},{3,2},{4,5},{5,4},{6,7},{7,6},{8,9},{9,8},{10,11... | collective-permute-start | bytes 491528 | tf_op jit(solution)/shard_map/ppermute | solution.py:120
  161.3 15.1 %collective-permute-start.49 = (bf16[2,2,96,768]{3,2,1,0:T(8,128)(2,1)S(1)}, bf16[2,2,96,768]{3,2,1,0:T(8,128)(2,1)S(1)}, u32[]{:S(2)}, u32[]{:S(2)}) collective-permute-start(bf16[2,2,96,768]{3,2,1,0:T(8,128)(2,1)S(1)} %get-tuple-element.279), channel_id=1, source_target_pairs={{0,4},{2,6},{4,0},{6,2},{8,12},{10,14},{12,8},{14,10},{16,20},{18,... | collective-permute-start | bytes 1769480 | tf_op jit(solution)/shard_map/ppermute | solution.py:96
  163.1 13.3 %collective-permute-start.48 = (bf16[2,96,768]{2,1,0:T(8,128)(2,1)}, bf16[2,96,768]{2,1,0:T(8,128)(2,1)S(1)}, u32[]{:S(2)}, u32[]{:S(2)}) collective-permute-start(bf16[2,96,768]{2,1,0:T(8,128)(2,1)} %get-tuple-element.289), channel_id=1, source_target_pairs={{0,8},{2,10},{4,12},{6,14},{8,0},{10,2},{12,4},{14,6},{16,24},{18,... | collective-permute-start | bytes 884744 | tf_op jit(solution)/shard_map/ppermute | solution.py:96
  165.4 11.0 %collective-permute-start.47 = (bf16[96,960]{1,0:T(8,128)(2,1)S(1)}, bf16[96,960]{1,0:T(8,128)(2,1)S(1)}, u32[]{:S(2)}, u32[]{:S(2)}) collective-permute-start(bf16[96,960]{1,0:T(8,128)(2,1)S(1)} %get-tuple-element.295), channel_id=1, source_target_pairs={{0,16},{2,18},{4,20},{6,22},{8,24},{10,26},{12,28},{14,30},{16,0},... | collective-permute-start | bytes 552968 | tf_op jit(solution)/shard_map/ppermute | solution.py:96
  176.6 13.7 %collective-permute-start.51 = (bf16[2,96,768]{2,1,0:T(8,128)(2,1)S(1)}, bf16[2,96,768]{2,1,0:T(8,128)(2,1)S(1)}, u32[]{:S(2)}, u32[]{:S(2)}) collective-permute-start(bf16[2,96,768]{2,1,0:T(8,128)(2,1)S(1)} %get-tuple-element.287), channel_id=1, source_target_pairs={{0,8},{2,10},{4,12},{6,14},{8,0},{10,2},{12,4},{14,6},{16,24},{18,... | collective-permute-start | bytes 884744 | tf_op jit(solution)/shard_map/ppermute | solution.py:96
  177.8 10.0 %collective-permute-start.50 = (f32[48,960]{1,0:T(8,128)S(1)}, f32[48,960]{1,0:T(8,128)S(1)}, u32[]{:S(2)}, u32[]{:S(2)}) collective-permute-start(f32[48,960]{1,0:T(8,128)S(1)} %dynamic-slice_bitcast_fusion.12), channel_id=1, source_target_pairs={{0,2},{2,0},{4,6},{6,4},{8,10},{10,8},{12,14},{14,12},{16,18},{18,... | collective-permute-start | bytes 552968 | tf_op jit(solution)/shard_map/ppermute | solution.py:54
  178.0 12.3 %collective-permute-start.52 = (bf16[96,768]{1,0:T(8,128)(2,1)S(1)}, bf16[96,768]{1,0:T(8,128)(2,1)S(1)}, u32[]{:S(2)}, u32[]{:S(2)}) collective-permute-start(bf16[96,768]{1,0:T(8,128)(2,1)S(1)} %get-tuple-element.305), channel_id=1, source_target_pairs={{0,16},{2,18},{4,20},{6,22},{8,24},{10,26},{12,28},{14,30},{16,0},... | collective-permute-start | bytes 442376 | tf_op jit(solution)/shard_map/ppermute | solution.py:96
  188.0 11.1 %collective-permute-start.54 = (f32[48,384]{1,0:T(8,128)S(1)}, f32[48,384]{1,0:T(8,128)S(1)}, u32[]{:S(2)}, u32[]{:S(2)}) collective-permute-start(f32[48,384]{1,0:T(8,128)S(1)} %pad_maximum_fusion.10), channel_id=1, source_target_pairs={{0,1},{1,0},{2,3},{3,2},{4,5},{5,4},{6,7},{7,6},{8,9},{9,8},{10,11... | collective-permute-start | bytes 221192 | tf_op jit(solution)/shard_map/ppermute | solution.py:120
  189.5 9.5 %collective-permute-start.55 = (f32[2,48]{1,0:T(2,128)S(1)}, f32[2,48]{1,0:T(2,128)S(1)}, u32[]{:S(2)}, u32[]{:S(2)}) collective-permute-start(f32[2,48]{1,0:T(2,128)S(1)} %stack.19), channel_id=1, source_target_pairs={{0,1},{1,0},{2,3},{3,2},{4,5},{5,4},{6,7},{7,6},{8,9},{9,8},{10,11... | collective-permute-start | bytes 1160 | tf_op jit(solution)/shard_map/ppermute | solution.py:120
  190.4 7.9 %collective-permute-start.56 = (f32[48,768]{1,0:T(8,128)S(1)}, f32[48,768]{1,0:T(8,128)S(1)}, u32[]{:S(2)}, u32[]{:S(2)}) collective-permute-start(f32[48,768]{1,0:T(8,128)S(1)} %dynamic-slice_bitcast_fusion.16), channel_id=1, source_target_pairs={{0,2},{2,0},{4,6},{6,4},{8,10},{10,8},{12,14},{14,12},{16,18},{18,... | collective-permute-start | bytes 442376 | tf_op jit(solution)/shard_map/ppermute | solution.py:54
  190.6 10.4 %collective-permute-start.53 = (bf16[96,768]{1,0:T(8,128)(2,1)S(1)}, bf16[96,768]{1,0:T(8,128)(2,1)S(1)}, u32[]{:S(2)}, u32[]{:S(2)}) collective-permute-start(bf16[96,768]{1,0:T(8,128)(2,1)S(1)} %get-tuple-element.303), channel_id=1, source_target_pairs={{0,16},{2,18},{4,20},{6,22},{8,24},{10,26},{12,28},{14,30},{16,0},... | collective-permute-start | bytes 442376 | tf_op jit(solution)/shard_map/ppermute | solution.py:96
  (53 other events, 294.7 us)

commit v8 on v7

--- a/solution.py
+++ b/solution.py
@@ -161,7 +161,7 @@
     return raised * cumulative, slope
 
 
-LIMIT = pltpu.CompilerParams(vmem_limit_bytes=18 * 1024 * 1024)
+LIMIT = pltpu.CompilerParams(vmem_limit_bytes=14 * 1024 * 1024)
 
 
 def whole_block(shape):

time: 211 us -> 209 us (level)
  local copies, waits for them, and re-layouts: 17 us -> 14.2 us
  waiting for transfers between devices: 55.4 us -> 57.7 us
    dynamic_update_slice x24, local copies, waits for them, and re-layouts: 6.29 us -> 2.57 us  [place(): lax.dynamic_update_slice(whole, block[None, :, start:end], (at, 0, 0))]
    unnamed x85 -> x93, local copies, waits for them, and re-layouts: 3.69 us -> 4.59 us
  transfers between devices with their start and end apart: 60 -> 60, of which waited for: 23 -> 25; matrix products, arithmetic and copies ran while one was open for 15% -> 13% of each run, Pallas kernels for 24% -> 24%
where the time goes in v8:
time: 209 us
  waiting for transfers between devices  57.7 us (28%)
  starting transfers between devices  56.7 us (27%)
  Pallas kernels  53.3 us (26%)
  other arithmetic  16.8 us (8%)
  local copies, waits for them, and re-layouts  14.2 us (7%)
  matrix products  5.67 us (3%)
  between operations  4.38 us (2%)
    pallas_call x3, Pallas kernels, captions_back(): pl.pallas_call(functools.partial(captions_body, start, blocks), out_shape...  25.1 us
    ppermute x20, waiting for transfers between devices, swap_near(): return lax.ppermute(x, ('dp', 'mp'), [(i, i ^ flip) for i in range(size)])  19 us
    ppermute x20, starting transfers between devices, swap_near(): return lax.ppermute(x, ('dp', 'mp'), [(i, i ^ flip) for i in range(size)])  18.3 us
    ppermute x6, waiting for transfers between devices, shift_depth(): lax.ppermute(x, 'dp', [(i, (i + 4 * step) % self.count) for i in range(se...  14.8 us
    ppermute x9, starting transfers between devices, halve(): lax.ppermute(leave, 'dp', [(i, i ^ bit) for i in range(self.count)])  10.5 us
    ppermute x8, waiting for transfers between devices, swap_side(): return lax.ppermute(x, 'dp', [(i, i ^ 2) for i in range(self.count)])  10.4 us
    pallas_call x1, Pallas kernels, attend(): pl.pallas_call(attend_body, grid=(steps,), out_shape=shapes(((count * LEN...  9.93 us
    ppermute x8, starting transfers between devices, swap_side(): return lax.ppermute(x, 'dp', [(i, i ^ 2) for i in range(self.count)])  8.91 us
  transfers between devices with their start and end apart: 60, of which 25 were waited for; matrix products, arithmetic and copies ran while one was open for 13% of the time, Pallas kernels for 24%

profile of v8, /device:TPU:0, one launch (start us, length us, event | category | flops | bytes accessed | tf_op | source)
XLA Modules:
  0.0 208.7 jit_solution(8280013511764756211)
XLA Ops:
  0.7 2.1 pack.1
  4.4 3.0 %collective-permute-start.1 = (bf16[96,768]{1,0:T(8,128)(2,1)S(1)}, bf16[96,768]{1,0:T(8,128)(2,1)S(1)}, u32[]{:S(2)}, u32[]{:S(2)}) collective-permute-start(bf16[96,768]{1,0:T(8,128)(2,1)S(1)} %bitcast.219), channel_id=1, source_target_pairs={{0,8},{2,10},{4,12},{6,14},{8,16},{10,18},{12,20},{14,22},{16,24},... | collective-permute-start | bytes 442376 | tf_op jit(solution)/shard_map/ppermute | solution.py:60
  7.4 2.1 %collective-permute-start.2 = (bf16[96,768]{1,0:T(8,128)(2,1)S(1)}, bf16[96,768]{1,0:T(8,128)(2,1)S(1)}, u32[]{:S(2)}, u32[]{:S(2)}) collective-permute-start(bf16[96,768]{1,0:T(8,128)(2,1)S(1)} %bitcast.220), channel_id=1, source_target_pairs={{0,24},{2,26},{4,28},{6,30},{8,0},{10,2},{12,4},{14,6},{16,8},{18,... | collective-permute-start | bytes 442376 | tf_op jit(solution)/shard_map/ppermute | solution.py:60
  9.5 1.6 collective-permute-start.3
  12.2 3.5 %all-to-all-start = ((bf16[16,8,768]{2,1,0:T(8,128)(2,1)}), bf16[16,8,768]{2,1,0:T(8,128)(2,1)S(1)}, u32[]{:S(2)}, u32[]{:S(2)}) async-start(bf16[16,8,768]{2,1,0:T(8,128)(2,1)} %fusion.1), calls=%async_computation | async-start | bytes 393216 | tf_op jit(solution)/shard_map/all_to_all | solution.py:722
  16.2 1.5 collective-permute-start.4
  17.7 1.5 collective-permute-start.5
  19.8 7.1 %collective-permute-done.4 = bf16[96,768]{1,0:T(8,128)(2,1)S(1)} collective-permute-done((bf16[96,768]{1,0:T(8,128)(2,1)S(1)}, bf16[96,768]{1,0:T(8,128)(2,1)S(1)}, u32[]{:S(2)}, u32[]{:S(2)}) %collective-permute-start.4) | collective-permute-done | bytes 147488 | tf_op jit(solution)/shard_map/ppermute | solution.py:60
  29.4 4.0 %collective-permute-done.7 = bf16[96,768]{1,0:T(8,128)(2,1)S(1)} collective-permute-done((bf16[96,768]{1,0:T(8,128)(2,1)S(1)}, bf16[96,768]{1,0:T(8,128)(2,1)S(1)}, u32[]{:S(2)}, u32[]{:S(2)}) %collective-permute-start.7) | collective-permute-done | bytes 147488 | tf_op jit(solution)/shard_map/ppermute | solution.py:57
  33.6 1.5 collective-permute-start.9
  36.1 1.5 collective-permute-start.15
  38.6 5.5 %norm_first.1 = (bf16[2048,768]{1,0:T(8,128)(2,1)}, f32[2048,128]{1,0:T(8,128)}, bf16[128,768]{1,0:T(8,128)(2,1)}, bf16[128,768]{1,0:T(8,128)(2,1)}) custom-call(s32[1]{0:T(128)} %bitcast.24.group_ref, bf16[2048,768]{1,0:T(8,128)(2,1)} %bitcast.198, s32[128,1]{1,0:T(8,128)} %copy.33.ends_ref), custom_call_target="tpu_custom_call" | custom-call | tf_op jit(solution)/shard_map/norm_first/pallas_call | solution.py:236
  44.0 1.8 broadcast_select_fusion.2
  45.9 2.7 %collective-permute-done.9 = bf16[96,2432]{1,0:T(8,128)(2,1)S(1)} collective-permute-done((bf16[96,2432]{1,0:T(8,128)(2,1)S(1)}, bf16[96,2432]{1,0:T(8,128)(2,1)S(1)}, u32[]{:S(2)}, u32[]{:S(2)}) %collective-permute-start.9) | collective-permute-done | bytes 466976 | tf_op jit(solution)/shard_map/ppermute | solution.py:60
  50.8 9.9 %attend.1 = (bf16[2048,768]{1,0:T(8,128)(2,1)}, f32[768,512]{1,0:T(8,128)}, bf16[128,384]{1,0:T(8,128)(2,1)}, bf16[128,384]{1,0:T(8,128)(2,1)}, bf16[128,768]{1,0:T(8,128)(2,1)}) custom-call(bf16[2048,768]{1,0:T(8,128)(2,1)} %get-tuple-element.161.unit_ref, bf16[128,768]{1,0:T(8,128)(2,1)} %get-tuple-element.162.unit_end_ref, s32[128,1]{1,0:T(8,128)} %copy.33.ends_ref, ...), custom_call_target="tpu_custom_call" | custom-call | tf_op jit(solution)/shard_map/attend/pallas_call | solution.py:314
  60.7 1.9 collective-permute-done.11
  64.4 1.5 collective-permute-start.18
  69.2 2.7 %collective-permute-done.18 = bf16[128,768]{1,0:T(8,128)(2,1)S(1)} collective-permute-done((bf16[128,768]{1,0:T(8,128)(2,1)}, bf16[128,768]{1,0:T(8,128)(2,1)S(1)}, u32[]{:S(2)}, u32[]{:S(2)}) %collective-permute-start.18) | collective-permute-done | bytes 196640 | tf_op jit(solution)/shard_map/ppermute | solution.py:120
  71.9 2.0 collective-permute-start.22
  74.0 2.8 %collective-permute-done.16 = bf16[96,2432]{1,0:T(8,128)(2,1)S(1)} collective-permute-done((bf16[96,2432]{1,0:T(8,128)(2,1)S(1)}, bf16[96,2432]{1,0:T(8,128)(2,1)S(1)}, u32[]{:S(2)}, u32[]{:S(2)}) %collective-permute-start.16) | collective-permute-done | bytes 466976 | tf_op jit(solution)/shard_map/ppermute | solution.py:60
  79.6 2.9 %broadcast_select_fusion = (bf16[768,768]{1,0:T(8,128)(2,1)}, bf16[768,768]{1,0:T(8,128)(2,1)}) fusion(bf16[768,768]{1,0:T(8,128)(2,1)S(1)} %collective-permute-done.23, bf16[768,768]{1,0:T(8,128)(2,1)} %collective-permute-done.15, pred[]{:T(512)S(6)} %eq.81), kind=kLoop, calls=%fused_computation.12 | loop fusion | flops 1179648 | bytes 4718593 | tf_op jit(solution)/shard_map/jit(_where)/select_n | solution.py:41
  82.5 5.6 %collective-permute-done.21 = bf16[96,2432]{1,0:T(8,128)(2,1)S(1)} collective-permute-done((bf16[96,2432]{1,0:T(8,128)(2,1)S(1)}, bf16[96,2432]{1,0:T(8,128)(2,1)S(1)}, u32[]{:S(2)}, u32[]{:S(2)}) %collective-permute-start.21) | collective-permute-done | bytes 466976 | tf_op jit(solution)/shard_map/ppermute | solution.py:57
  88.3 1.6 multiply_convert_fusion
  90.5 1.6 collective-permute-start.24
  94.4 1.8 collective-permute-done.24.refs_1_
  98.4 1.6 collective-permute-start.31
  100.0 1.4 collective-permute-start.29
  101.9 1.8 collective-permute-done.29
  105.8 2.7 %collective-permute-start.33 = (f32[9,128]{1,0:T(8,128)S(1)}, f32[9,128]{1,0:T(8,128)S(1)}, u32[]{:S(2)}, u32[]{:S(2)}) collective-permute-start(f32[9,128]{1,0:T(8,128)S(1)} %add_add_fusion.1.refs_0_), channel_id=1, source_target_pairs={{0,16},{2,18},{4,20},{6,22},{8,24},{10,26},{12,28},{14,30},{16,0},... | collective-permute-start | bytes 13832 | tf_op jit(solution)/shard_map/ppermute | solution.py:115
  110.4 3.6 %collective-permute-done.34.refs_3_ = f32[9,128]{1,0:T(8,128)S(1)} collective-permute-done((f32[9,128]{1,0:T(8,128)S(1)}, f32[9,128]{1,0:T(8,128)S(1)}, u32[]{:S(2)}, u32[]{:S(2)}) %collective-permute-start.34) | collective-permute-done | bytes 4640 | tf_op jit(solution)/shard_map/ppermute | solution.py:115
  114.5 1.2 collective-permute-start.35
  116.7 3.0 %collective-permute-done.35 = bf16[64,768]{1,0:T(8,128)(2,1)S(1)} collective-permute-done((bf16[64,768]{1,0:T(8,128)(2,1)S(1)}, bf16[64,768]{1,0:T(8,128)(2,1)S(1)}, u32[]{:S(2)}, u32[]{:S(2)}) %collective-permute-start.35) | collective-permute-done | bytes 98336 | tf_op jit(solution)/shard_map/ppermute | solution.py:120
  126.2 1.4 collective-permute-start.42
  130.8 3.4 %collective-permute-done.40 = bf16[128,768]{1,0:T(8,128)(2,1)S(1)} collective-permute-done((bf16[128,768]{1,0:T(8,128)(2,1)S(1)}, bf16[128,768]{1,0:T(8,128)(2,1)S(1)}, u32[]{:S(2)}, u32[]{:S(2)}) %collective-permute-start.40) | collective-permute-done | bytes 196640 | tf_op jit(solution)/shard_map/ppermute | solution.py:120
  136.4 8.3 %attend_back.1 = (bf16[768,768]{1,0:T(8,128)(2,1)S(1)}, bf16[768,768]{1,0:T(8,128)(2,1)}, bf16[2048,768]{1,0:T(8,128)(2,1)S(1)}, bf16[128,384]{1,0:T(8,128)(2,1)S(1)}, bf16[640,128]{1,0:T(8,128)(2,1)S(1)}) custom-call(s32[1]{0:T(128)} %bitcast.core_ref, bf16[128,768]{1,0:T(8,128)(2,1)S(1)} %get-tuple-element.261.d_mid_ref, ...), custom_call_target="tpu_custom_call" | custom-call | tf_op jit(solution)/shard_map/attend_back/pallas_call | solution.py:399
  144.7 1.6 copy-done.3
  148.8 1.3 collective-permute-start.41
  150.3 4.8 %collective-permute-done.41.small_far_ref = bf16[640,128]{1,0:T(8,128)(2,1)S(1)} collective-permute-done((bf16[640,128]{1,0:T(8,128)(2,1)S(1)}, bf16[640,128]{1,0:T(8,128)(2,1)S(1)}, u32[]{:S(2)}, u32[]{:S(2)}) %collective-permute-start.41) | collective-permute-done | bytes 163872 | tf_op jit(solution)/shard_map/ppermute | solution.py:120
  155.1 4.1 %collective-permute-done.46 = bf16[2,96,960]{2,1,0:T(8,128)(2,1)S(1)} collective-permute-done((bf16[2,96,960]{2,1,0:T(8,128)(2,1)S(1)}, bf16[2,96,960]{2,1,0:T(8,128)(2,1)S(1)}, u32[]{:S(2)}, u32[]{:S(2)}) %collective-permute-start.46) | collective-permute-done | bytes 368672 | tf_op jit(solution)/shard_map/ppermute | solution.py:96
  159.2 1.6 add_convert_fusion
  162.1 1.2 collective-permute-start.48
  163.8 10.6 %captions_back.3.refs_0_ = f32[2048,768]{1,0:T(8,128)} custom-call(s32[1]{0:T(128)} %bitcast.24.group_ref, s32[128,1]{1,0:T(8,128)} %copy.33.ends_ref, bf16[2048,768]{1,0:T(8,128)(2,1)} %get-tuple-element.161.unit_ref, f32[2048,128]{1,0:T(8,128)} %get-tuple-element.226.scale_ref, f32[128,768]{1,0:T(8,128)} %get-tuple-element.262.d_mid_ref, ...), custom_call_target="tpu_custom_call" | custom-call | tf_op jit(solution)/shard_map/captions_back/pallas_call | solution.py:644
  176.1 1.2 collective-permute-start.51
  178.7 7.2 %captions_back.4.refs_0_ = f32[2048,768]{1,0:T(8,128)} custom-call(s32[1]{0:T(128)} %bitcast.24.group_ref, s32[128,1]{1,0:T(8,128)} %copy.33.ends_ref, bf16[2048,768]{1,0:T(8,128)(2,1)} %get-tuple-element.161.unit_ref, f32[2048,128]{1,0:T(8,128)} %get-tuple-element.226.scale_ref, ...), custom_call_target="tpu_custom_call", output_to_operand_aliasing={{}: (14, {})} | custom-call | tf_op jit(solution)/shard_map/captions_back/pallas_call | solution.py:644
  186.1 1.3 collective-permute-start.54
  188.7 2.0 collective-permute-start.53
  190.6 7.2 %captions_back.5 = f32[2048,768]{1,0:T(8,128)} custom-call(s32[1]{0:T(128)} %bitcast.24.group_ref, s32[128,1]{1,0:T(8,128)} %copy.33.ends_ref, bf16[2048,768]{1,0:T(8,128)(2,1)} %get-tuple-element.161.unit_ref, f32[2048,128]{1,0:T(8,128)} %get-tuple-element.226.scale_ref, f32[128,768]{1,0:T(8,128)} %get-tuple-element.262.d_mid_ref, ...), custom_call_target="tpu_custom_call", output_to_operand_aliasing={{}: (14, {})} | custom-call | tf_op jit(solution)/shard_map/captions_back/pallas_call | solution.py:644
  203.4 1.4 collective-permute-start.58
  (312 shorter events, 56.6 us)
Async XLA Ops:
  4.4 11.4 %collective-permute-start.1 = (bf16[96,768]{1,0:T(8,128)(2,1)S(1)}, bf16[96,768]{1,0:T(8,128)(2,1)S(1)}, u32[]{:S(2)}, u32[]{:S(2)}) collective-permute-start(bf16[96,768]{1,0:T(8,128)(2,1)S(1)} %bitcast.219), channel_id=1, source_target_pairs={{0,8},{2,10},{4,12},{6,14},{8,16},{10,18},{12,20},{14,22},{16,24},... | collective-permute-start | bytes 442376 | tf_op jit(solution)/shard_map/ppermute | solution.py:60
  7.4 8.8 %collective-permute-start.2 = (bf16[96,768]{1,0:T(8,128)(2,1)S(1)}, bf16[96,768]{1,0:T(8,128)(2,1)S(1)}, u32[]{:S(2)}, u32[]{:S(2)}) collective-permute-start(bf16[96,768]{1,0:T(8,128)(2,1)S(1)} %bitcast.220), channel_id=1, source_target_pairs={{0,24},{2,26},{4,28},{6,30},{8,0},{10,2},{12,4},{14,6},{16,8},{18,... | collective-permute-start | bytes 442376 | tf_op jit(solution)/shard_map/ppermute | solution.py:60
  9.5 6.7 %collective-permute-start.3 = (bf16[96,768]{1,0:T(8,128)(2,1)S(1)}, bf16[96,768]{1,0:T(8,128)(2,1)S(1)}, u32[]{:S(2)}, u32[]{:S(2)}) collective-permute-start(bf16[96,768]{1,0:T(8,128)(2,1)S(1)} %bitcast.221), channel_id=1, source_target_pairs={{0,4},{2,6},{4,0},{6,2},{8,12},{10,14},{12,8},{14,10},{16,20},{18,... | collective-permute-start | bytes 442376 | tf_op jit(solution)/shard_map/ppermute | solution.py:57
  12.2 15.5 %all-to-all-start = ((bf16[16,8,768]{2,1,0:T(8,128)(2,1)}), bf16[16,8,768]{2,1,0:T(8,128)(2,1)S(1)}, u32[]{:S(2)}, u32[]{:S(2)}) async-start(bf16[16,8,768]{2,1,0:T(8,128)(2,1)} %fusion.1), calls=%async_computation | async-start | bytes 393216 | tf_op jit(solution)/shard_map/all_to_all | solution.py:722
  16.2 10.7 %collective-permute-start.4 = (bf16[96,768]{1,0:T(8,128)(2,1)S(1)}, bf16[96,768]{1,0:T(8,128)(2,1)S(1)}, u32[]{:S(2)}, u32[]{:S(2)}) collective-permute-start(bf16[96,768]{1,0:T(8,128)(2,1)S(1)} %collective-permute-done.1), channel_id=1, source_target_pairs={{0,8},{2,10},{4,12},{6,14},{8,16},{10,18},{12,20},{14,22},{16,24},... | collective-permute-start | bytes 442376 | tf_op jit(solution)/shard_map/ppermute | solution.py:60
  17.7 9.2 %collective-permute-start.5 = (bf16[96,768]{1,0:T(8,128)(2,1)S(1)}, bf16[96,768]{1,0:T(8,128)(2,1)S(1)}, u32[]{:S(2)}, u32[]{:S(2)}) collective-permute-start(bf16[96,768]{1,0:T(8,128)(2,1)S(1)} %collective-permute-done.1), channel_id=1, source_target_pairs={{0,4},{2,6},{4,0},{6,2},{8,12},{10,14},{12,8},{14,10},{16,20},{18,... | collective-permute-start | bytes 442376 | tf_op jit(solution)/shard_map/ppermute | solution.py:57
  19.1 8.6 %collective-permute-start.6 = (bf16[96,768]{1,0:T(8,128)(2,1)S(1)}, bf16[96,768]{1,0:T(8,128)(2,1)S(1)}, u32[]{:S(2)}, u32[]{:S(2)}) collective-permute-start(bf16[96,768]{1,0:T(8,128)(2,1)S(1)} %collective-permute-done.2), channel_id=1, source_target_pairs={{0,4},{2,6},{4,0},{6,2},{8,12},{10,14},{12,8},{14,10},{16,20},{18,... | collective-permute-start | bytes 442376 | tf_op jit(solution)/shard_map/ppermute | solution.py:57
  28.0 5.3 %collective-permute-start.7 = (bf16[96,768]{1,0:T(8,128)(2,1)S(1)}, bf16[96,768]{1,0:T(8,128)(2,1)S(1)}, u32[]{:S(2)}, u32[]{:S(2)}) collective-permute-start(bf16[96,768]{1,0:T(8,128)(2,1)S(1)} %collective-permute-done.4), channel_id=1, source_target_pairs={{0,4},{2,6},{4,0},{6,2},{8,12},{10,14},{12,8},{14,10},{16,20},{18,... | collective-permute-start | bytes 442376 | tf_op jit(solution)/shard_map/ppermute | solution.py:57
  33.4 10.6 %collective-permute-start.10 = (bf16[768,768]{1,0:T(8,128)(2,1)S(1)}, bf16[768,768]{1,0:T(8,128)(2,1)S(1)}, u32[]{:S(2)}, u32[]{:S(2)}) collective-permute-start(bf16[768,768]{1,0:T(8,128)(2,1)S(1)} %bitcast.195), channel_id=1, source_target_pairs={{0,2},{2,0},{4,6},{6,4},{8,10},{10,8},{12,14},{14,12},{16,18},{18,... | collective-permute-start | bytes 3538952 | tf_op jit(solution)/shard_map/ppermute | solution.py:54
  33.6 14.9 %collective-permute-start.9 = (bf16[96,2432]{1,0:T(8,128)(2,1)S(1)}, bf16[96,2432]{1,0:T(8,128)(2,1)S(1)}, u32[]{:S(2)}, u32[]{:S(2)}) collective-permute-start(bf16[96,2432]{1,0:T(8,128)(2,1)S(1)} %bitcast.203), channel_id=1, source_target_pairs={{0,8},{2,10},{4,12},{6,14},{8,16},{10,18},{12,20},{14,22},{16,24},... | collective-permute-start | bytes 1400840 | tf_op jit(solution)/shard_map/ppermute | solution.py:60
  35.1 25.6 %collective-permute-start.12 = (bf16[96,2432]{1,0:T(8,128)(2,1)S(1)}, bf16[96,2432]{1,0:T(8,128)(2,1)}, u32[]{:S(2)}, u32[]{:S(2)}) collective-permute-start(bf16[96,2432]{1,0:T(8,128)(2,1)S(1)} %bitcast.204), channel_id=1, source_target_pairs={{0,4},{2,6},{4,0},{6,2},{8,12},{10,14},{12,8},{14,10},{16,20},{18,... | collective-permute-start | bytes 1400840 | tf_op jit(solution)/shard_map/ppermute | solution.py:57
  36.1 28.2 %collective-permute-start.15 = (bf16[768,768]{1,0:T(8,128)(2,1)S(1)}, bf16[768,768]{1,0:T(8,128)(2,1)}, u32[]{:S(2)}, u32[]{:S(2)}) collective-permute-start(bf16[768,768]{1,0:T(8,128)(2,1)S(1)} %bitcast.196), channel_id=1, source_target_pairs={{0,1},{1,0},{2,3},{3,2},{4,5},{5,4},{6,7},{7,6},{8,9},{9,8},{10,11... | collective-permute-start | bytes 3538952 | tf_op jit(solution)/shard_map/ppermute | solution.py:120
  48.6 14.0 %collective-permute-start.11 = (bf16[96,2432]{1,0:T(8,128)(2,1)S(1)}, bf16[96,2432]{1,0:T(8,128)(2,1)S(1)}, u32[]{:S(2)}, u32[]{:S(2)}) collective-permute-start(bf16[96,2432]{1,0:T(8,128)(2,1)S(1)} %collective-permute-done.9), channel_id=1, source_target_pairs={{0,8},{2,10},{4,12},{6,14},{8,16},{10,18},{12,20},{14,22},{16,24},... | collective-permute-start | bytes 1400840 | tf_op jit(solution)/shard_map/ppermute | solution.py:60
  48.6 14.0 %collective-permute-start.13 = (bf16[96,2432]{1,0:T(8,128)(2,1)S(1)}, bf16[96,2432]{1,0:T(8,128)(2,1)S(1)}, u32[]{:S(2)}, u32[]{:S(2)}) collective-permute-start(bf16[96,2432]{1,0:T(8,128)(2,1)S(1)} %collective-permute-done.9), channel_id=1, source_target_pairs={{0,4},{2,6},{4,0},{6,2},{8,12},{10,14},{12,8},{14,10},{16,20},{18,... | collective-permute-start | bytes 1400840 | tf_op jit(solution)/shard_map/ppermute | solution.py:57
  50.5 10.3 %collective-permute-start.14 = (bf16[128,768]{1,0:T(8,128)(2,1)}, bf16[128,768]{1,0:T(8,128)(2,1)S(1)}, u32[]{:S(2)}, u32[]{:S(2)}) collective-permute-start(bf16[128,768]{1,0:T(8,128)(2,1)} %get-tuple-element.159), channel_id=1, source_target_pairs={{0,2},{1,3},{2,0},{3,1},{4,6},{5,7},{6,4},{7,5},{8,10},{9,11},{10,... | collective-permute-start | bytes 589832 | tf_op jit(solution)/shard_map/ppermute | solution.py:120
  63.4 13.3 %collective-permute-start.16 = (bf16[96,2432]{1,0:T(8,128)(2,1)S(1)}, bf16[96,2432]{1,0:T(8,128)(2,1)S(1)}, u32[]{:S(2)}, u32[]{:S(2)}) collective-permute-start(bf16[96,2432]{1,0:T(8,128)(2,1)S(1)} %collective-permute-done.11), channel_id=1, source_target_pairs={{0,8},{2,10},{4,12},{6,14},{8,16},{10,18},{12,20},{14,22},{16,24},... | collective-permute-start | bytes 1400840 | tf_op jit(solution)/shard_map/ppermute | solution.py:60
  63.4 13.3 %collective-permute-start.17 = (bf16[96,2432]{1,0:T(8,128)(2,1)S(1)}, bf16[96,2432]{1,0:T(8,128)(2,1)S(1)}, u32[]{:S(2)}, u32[]{:S(2)}) collective-permute-start(bf16[96,2432]{1,0:T(8,128)(2,1)S(1)} %collective-permute-done.11), channel_id=1, source_target_pairs={{0,4},{2,6},{4,0},{6,2},{8,12},{10,14},{12,8},{14,10},{16,20},{18,... | collective-permute-start | bytes 1400840 | tf_op jit(solution)/shard_map/ppermute | solution.py:57
  64.4 7.6 %collective-permute-start.18 = (bf16[128,768]{1,0:T(8,128)(2,1)}, bf16[128,768]{1,0:T(8,128)(2,1)S(1)}, u32[]{:S(2)}, u32[]{:S(2)}) collective-permute-start(bf16[128,768]{1,0:T(8,128)(2,1)} %get-tuple-element.172), channel_id=1, source_target_pairs={{0,1},{1,0},{2,3},{3,2},{4,5},{5,4},{6,7},{7,6},{8,9},{9,8},{10,11... | collective-permute-start | bytes 589832 | tf_op jit(solution)/shard_map/ppermute | solution.py:120
  65.9 6.1 %collective-permute-start.19 = (bf16[128,768]{1,0:T(8,128)(2,1)}, bf16[128,768]{1,0:T(8,128)(2,1)S(1)}, u32[]{:S(2)}, u32[]{:S(2)}) collective-permute-start(bf16[128,768]{1,0:T(8,128)(2,1)} %get-tuple-element.172), channel_id=1, source_target_pairs={{0,2},{1,3},{2,0},{3,1},{4,6},{5,7},{6,4},{7,5},{8,10},{9,11},{10,... | collective-permute-start | bytes 589832 | tf_op jit(solution)/shard_map/ppermute | solution.py:120
  65.9 8.1 %collective-permute-start.20 = (bf16[128,768]{1,0:T(8,128)(2,1)}, bf16[128,768]{1,0:T(8,128)(2,1)S(1)}, u32[]{:S(2)}, u32[]{:S(2)}) collective-permute-start(bf16[128,768]{1,0:T(8,128)(2,1)} %get-tuple-element.172), channel_id=1, source_target_pairs={{0,3},{1,2},{2,1},{3,0},{4,7},{5,6},{6,5},{7,4},{8,11},{9,10},{10,... | collective-permute-start | bytes 589832 | tf_op jit(solution)/shard_map/ppermute | solution.py:120
  71.9 7.6 %collective-permute-start.23 = (bf16[768,768]{1,0:T(8,128)(2,1)}, bf16[768,768]{1,0:T(8,128)(2,1)S(1)}, u32[]{:S(2)}, u32[]{:S(2)}) collective-permute-start(bf16[768,768]{1,0:T(8,128)(2,1)} %collective-permute-done.15), channel_id=1, source_target_pairs={{0,2},{2,0},{4,6},{6,4},{8,10},{10,8},{12,14},{14,12},{16,18},{18,... | collective-permute-start | bytes 3538952 | tf_op jit(solution)/shard_map/ppermute | solution.py:54
  71.9 10.5 %collective-permute-start.22 = (bf16[128,384]{1,0:T(8,128)(2,1)S(1)}, bf16[128,384]{1,0:T(8,128)(2,1)S(1)}, u32[]{:S(2)}, u32[]{:S(2)}) collective-permute-start(bf16[128,384]{1,0:T(8,128)(2,1)S(1)} %copy-done.10), channel_id=1, source_target_pairs={{0,1},{1,0},{2,3},{3,2},{4,5},{5,4},{6,7},{7,6},{8,9},{9,8},{10,11... | collective-permute-start | bytes 294920 | tf_op jit(solution)/shard_map/ppermute | solution.py:120
  77.3 10.8 %collective-permute-start.21 = (bf16[96,2432]{1,0:T(8,128)(2,1)S(1)}, bf16[96,2432]{1,0:T(8,128)(2,1)S(1)}, u32[]{:S(2)}, u32[]{:S(2)}) collective-permute-start(bf16[96,2432]{1,0:T(8,128)(2,1)S(1)} %collective-permute-done.16), channel_id=1, source_target_pairs={{0,4},{2,6},{4,0},{6,2},{8,12},{10,14},{12,8},{14,10},{16,20},{18,... | collective-permute-start | bytes 1400840 | tf_op jit(solution)/shard_map/ppermute | solution.py:57
  88.1 4.7 %collective-permute-start.27 = (bf16[768,896]{1,0:T(8,128)(2,1)S(1)}, bf16[768,896]{1,0:T(8,128)(2,1)S(1)}, u32[]{:S(2)}, u32[]{:S(2)}) collective-permute-start(bf16[768,896]{1,0:T(8,128)(2,1)S(1)} %bitcast.191), channel_id=1, source_target_pairs={{0,2},{2,0},{4,6},{6,4},{8,10},{10,8},{12,14},{14,12},{16,18},{18,... | collective-permute-start | bytes 4128776 | tf_op jit(solution)/shard_map/ppermute | solution.py:54
  90.5 5.7 %collective-permute-start.24 = (bf16[64,768]{1,0:T(8,128)(2,1)S(1)}, bf16[64,768]{1,0:T(8,128)(2,1)S(1)}, u32[]{:S(2)}, u32[]{:S(2)}) collective-permute-start(bf16[64,768]{1,0:T(8,128)(2,1)S(1)} %get-tuple-element.299), channel_id=1, source_target_pairs={{0,1},{1,0},{2,3},{3,2},{4,5},{5,4},{6,7},{7,6},{8,9},{9,8},{10,11... | collective-permute-start | bytes 294920 | tf_op jit(solution)/shard_map/ppermute | solution.py:120
  92.3 5.1 %collective-permute-start.26 = (bf16[64,768]{1,0:T(8,128)(2,1)S(1)}, bf16[64,768]{1,0:T(8,128)(2,1)S(1)}, u32[]{:S(2)}, u32[]{:S(2)}) collective-permute-start(bf16[64,768]{1,0:T(8,128)(2,1)S(1)} %get-tuple-element.297), channel_id=1, source_target_pairs={{0,3},{1,2},{2,1},{3,0},{4,7},{5,6},{6,5},{7,4},{8,11},{9,10},{10,... | collective-permute-start | bytes 294920 | tf_op jit(solution)/shard_map/ppermute | solution.py:120
  98.4 6.1 %collective-permute-start.31 = (bf16[64,768]{1,0:T(8,128)(2,1)S(1)}, bf16[64,768]{1,0:T(8,128)(2,1)S(1)}, u32[]{:S(2)}, u32[]{:S(2)}) collective-permute-start(bf16[64,768]{1,0:T(8,128)(2,1)S(1)} %get-tuple-element.190), channel_id=1, source_target_pairs={{0,1},{1,0},{2,3},{3,2},{4,5},{5,4},{6,7},{7,6},{8,9},{9,8},{10,11... | collective-permute-start | bytes 294920 | tf_op jit(solution)/shard_map/ppermute | solution.py:120
  104.6 16.2 %collective-permute-start.38 = (bf16[128,768]{1,0:T(8,128)(2,1)S(1)}, bf16[128,768]{1,0:T(8,128)(2,1)}, u32[]{:S(2)}, u32[]{:S(2)}) collective-permute-start(bf16[128,768]{1,0:T(8,128)(2,1)S(1)} %pad_maximum_fusion.8), channel_id=1, source_target_pairs={{0,2},{2,0},{4,6},{6,4},{8,10},{10,8},{12,14},{14,12},{16,18},{18,... | collective-permute-start | bytes 589832 | tf_op jit(solution)/shard_map/ppermute | solution.py:54
  108.5 5.4 %collective-permute-start.34 = (f32[9,128]{1,0:T(8,128)S(1)}, f32[9,128]{1,0:T(8,128)S(1)}, u32[]{:S(2)}, u32[]{:S(2)}) collective-permute-start(f32[9,128]{1,0:T(8,128)S(1)} %add_add_fusion.1.refs_0_), channel_id=1, source_target_pairs={{0,20},{2,22},{4,16},{6,18},{8,28},{10,30},{12,24},{14,26},{16,4},... | collective-permute-start | bytes 13832 | tf_op jit(solution)/shard_map/ppermute | solution.py:115
  114.5 5.2 %collective-permute-start.35 = (bf16[64,768]{1,0:T(8,128)(2,1)S(1)}, bf16[64,768]{1,0:T(8,128)(2,1)S(1)}, u32[]{:S(2)}, u32[]{:S(2)}) collective-permute-start(bf16[64,768]{1,0:T(8,128)(2,1)S(1)} %get-tuple-element.201), channel_id=1, source_target_pairs={{0,1},{1,0},{2,3},{3,2},{4,5},{5,4},{6,7},{7,6},{8,9},{9,8},{10,11... | collective-permute-start | bytes 294920 | tf_op jit(solution)/shard_map/ppermute | solution.py:120
  115.7 5.1 %collective-permute-start.37 = (bf16[64,768]{1,0:T(8,128)(2,1)S(1)}, bf16[64,768]{1,0:T(8,128)(2,1)S(1)}, u32[]{:S(2)}, u32[]{:S(2)}) collective-permute-start(bf16[64,768]{1,0:T(8,128)(2,1)S(1)} %get-tuple-element.201), channel_id=1, source_target_pairs={{0,3},{1,2},{2,1},{3,0},{4,7},{5,6},{6,5},{7,4},{8,11},{9,10},{10,... | collective-permute-start | bytes 294920 | tf_op jit(solution)/shard_map/ppermute | solution.py:120
  126.2 20.2 %collective-permute-start.42 = (bf16[2,2,96,960]{3,2,1,0:T(8,128)(2,1)S(1)}, bf16[2,2,96,960]{3,2,1,0:T(8,128)(2,1)S(1)}, u32[]{:S(2)}, u32[]{:S(2)}) collective-permute-start(bf16[2,2,96,960]{3,2,1,0:T(8,128)(2,1)S(1)} %get-tuple-element.273), channel_id=1, source_target_pairs={{0,8},{2,10},{4,12},{6,14},{8,0},{10,2},{12,4},{14,6},{16,24},{18,... | collective-permute-start | bytes 2211848 | tf_op jit(solution)/shard_map/ppermute | solution.py:96
  127.6 6.6 %collective-permute-start.40 = (bf16[128,768]{1,0:T(8,128)(2,1)S(1)}, bf16[128,768]{1,0:T(8,128)(2,1)S(1)}, u32[]{:S(2)}, u32[]{:S(2)}) collective-permute-start(bf16[128,768]{1,0:T(8,128)(2,1)S(1)} %add_convert_fusion.7), channel_id=1, source_target_pairs={{0,1},{1,0},{2,3},{3,2},{4,5},{5,4},{6,7},{7,6},{8,9},{9,8},{10,11... | collective-permute-start | bytes 589832 | tf_op jit(solution)/shard_map/ppermute | solution.py:120
  129.7 16.6 %collective-permute-start.43 = (bf16[2,2,96,768]{3,2,1,0:T(8,128)(2,1)S(1)}, bf16[2,2,96,768]{3,2,1,0:T(8,128)(2,1)S(1)}, u32[]{:S(2)}, u32[]{:S(2)}) collective-permute-start(bf16[2,2,96,768]{3,2,1,0:T(8,128)(2,1)S(1)} %get-tuple-element.281), channel_id=1, source_target_pairs={{0,4},{2,6},{4,0},{6,2},{8,12},{10,14},{12,8},{14,10},{16,20},{18,... | collective-permute-start | bytes 1769480 | tf_op jit(solution)/shard_map/ppermute | solution.py:96
  135.7 10.7 %collective-permute-start.44 = (bf16[128,384]{1,0:T(8,128)(2,1)S(1)}, bf16[128,384]{1,0:T(8,128)(2,1)S(1)}, u32[]{:S(2)}, u32[]{:S(2)}) collective-permute-start(bf16[128,384]{1,0:T(8,128)(2,1)S(1)} %convolution_convert_fusion.4.d_att_ref), channel_id=1, source_target_pairs={{0,1},{1,0},{2,3},{3,2},{4,5},{5,4},{6,7},{7,6},{8,9},{9,8},{10,11... | collective-permute-start | bytes 294920 | tf_op jit(solution)/shard_map/ppermute | solution.py:120
  146.4 12.8 %collective-permute-start.45 = (bf16[768,768]{1,0:T(8,128)(2,1)}, bf16[768,768]{1,0:T(8,128)(2,1)}, u32[]{:S(2)}, u32[]{:S(2)}) collective-permute-start(bf16[768,768]{1,0:T(8,128)(2,1)} %get-tuple-element.216), channel_id=1, source_target_pairs={{0,2},{2,0},{4,6},{6,4},{8,10},{10,8},{12,14},{14,12},{16,18},{18,... | collective-permute-start | bytes 3538952 | tf_op jit(solution)/shard_map/ppermute | solution.py:54
  147.6 11.6 %collective-permute-start.46 = (bf16[2,96,960]{2,1,0:T(8,128)(2,1)S(1)}, bf16[2,96,960]{2,1,0:T(8,128)(2,1)S(1)}, u32[]{:S(2)}, u32[]{:S(2)}) collective-permute-start(bf16[2,96,960]{2,1,0:T(8,128)(2,1)S(1)} %get-tuple-element.283), channel_id=1, source_target_pairs={{0,4},{2,6},{4,0},{6,2},{8,12},{10,14},{12,8},{14,10},{16,20},{18,... | collective-permute-start | bytes 1105928 | tf_op jit(solution)/shard_map/ppermute | solution.py:96
  148.8 6.3 %collective-permute-start.41 = (bf16[640,128]{1,0:T(8,128)(2,1)S(1)}, bf16[640,128]{1,0:T(8,128)(2,1)S(1)}, u32[]{:S(2)}, u32[]{:S(2)}) collective-permute-start(bf16[640,128]{1,0:T(8,128)(2,1)S(1)} %get-tuple-element.210), channel_id=1, source_target_pairs={{0,1},{1,0},{2,3},{3,2},{4,5},{5,4},{6,7},{7,6},{8,9},{9,8},{10,11... | collective-permute-start | bytes 491528 | tf_op jit(solution)/shard_map/ppermute | solution.py:120
  160.9 14.9 %collective-permute-start.49 = (bf16[2,2,96,768]{3,2,1,0:T(8,128)(2,1)S(1)}, bf16[2,2,96,768]{3,2,1,0:T(8,128)(2,1)S(1)}, u32[]{:S(2)}, u32[]{:S(2)}) collective-permute-start(bf16[2,2,96,768]{3,2,1,0:T(8,128)(2,1)S(1)} %get-tuple-element.279), channel_id=1, source_target_pairs={{0,4},{2,6},{4,0},{6,2},{8,12},{10,14},{12,8},{14,10},{16,20},{18,... | collective-permute-start | bytes 1769480 | tf_op jit(solution)/shard_map/ppermute | solution.py:96
  162.1 12.6 %collective-permute-start.48 = (bf16[2,96,768]{2,1,0:T(8,128)(2,1)S(1)}, bf16[2,96,768]{2,1,0:T(8,128)(2,1)S(1)}, u32[]{:S(2)}, u32[]{:S(2)}) collective-permute-start(bf16[2,96,768]{2,1,0:T(8,128)(2,1)S(1)} %get-tuple-element.289), channel_id=1, source_target_pairs={{0,8},{2,10},{4,12},{6,14},{8,0},{10,2},{12,4},{14,6},{16,24},{18,... | collective-permute-start | bytes 884744 | tf_op jit(solution)/shard_map/ppermute | solution.py:96
  163.5 11.1 %collective-permute-start.47 = (bf16[96,960]{1,0:T(8,128)(2,1)S(1)}, bf16[96,960]{1,0:T(8,128)(2,1)S(1)}, u32[]{:S(2)}, u32[]{:S(2)}) collective-permute-start(bf16[96,960]{1,0:T(8,128)(2,1)S(1)} %get-tuple-element.295), channel_id=1, source_target_pairs={{0,16},{2,18},{4,20},{6,22},{8,24},{10,26},{12,28},{14,30},{16,0},... | collective-permute-start | bytes 552968 | tf_op jit(solution)/shard_map/ppermute | solution.py:96
  176.1 12.3 %collective-permute-start.51 = (bf16[2,96,768]{2,1,0:T(8,128)(2,1)S(1)}, bf16[2,96,768]{2,1,0:T(8,128)(2,1)S(1)}, u32[]{:S(2)}, u32[]{:S(2)}) collective-permute-start(bf16[2,96,768]{2,1,0:T(8,128)(2,1)S(1)} %get-tuple-element.287), channel_id=1, source_target_pairs={{0,8},{2,10},{4,12},{6,14},{8,0},{10,2},{12,4},{14,6},{16,24},{18,... | collective-permute-start | bytes 884744 | tf_op jit(solution)/shard_map/ppermute | solution.py:96
  177.4 8.5 %collective-permute-start.50 = (f32[48,960]{1,0:T(8,128)S(1)}, f32[48,960]{1,0:T(8,128)S(1)}, u32[]{:S(2)}, u32[]{:S(2)}) collective-permute-start(f32[48,960]{1,0:T(8,128)S(1)} %dynamic-slice_bitcast_fusion.12), channel_id=1, source_target_pairs={{0,2},{2,0},{4,6},{6,4},{8,10},{10,8},{12,14},{14,12},{16,18},{18,... | collective-permute-start | bytes 552968 | tf_op jit(solution)/shard_map/ppermute | solution.py:54
  177.6 10.8 %collective-permute-start.52 = (bf16[96,768]{1,0:T(8,128)(2,1)S(1)}, bf16[96,768]{1,0:T(8,128)(2,1)S(1)}, u32[]{:S(2)}, u32[]{:S(2)}) collective-permute-start(bf16[96,768]{1,0:T(8,128)(2,1)S(1)} %get-tuple-element.305), channel_id=1, source_target_pairs={{0,16},{2,18},{4,20},{6,22},{8,24},{10,26},{12,28},{14,30},{16,0},... | collective-permute-start | bytes 442376 | tf_op jit(solution)/shard_map/ppermute | solution.py:96
  186.1 12.6 %collective-permute-start.54 = (f32[48,384]{1,0:T(8,128)S(1)}, f32[48,384]{1,0:T(8,128)S(1)}, u32[]{:S(2)}, u32[]{:S(2)}) collective-permute-start(f32[48,384]{1,0:T(8,128)S(1)} %pad_maximum_fusion.10), channel_id=1, source_target_pairs={{0,1},{1,0},{2,3},{3,2},{4,5},{5,4},{6,7},{7,6},{8,9},{9,8},{10,11... | collective-permute-start | bytes 221192 | tf_op jit(solution)/shard_map/ppermute | solution.py:120
  187.6 11.0 %collective-permute-start.55 = (f32[2,48]{1,0:T(2,128)S(1)}, f32[2,48]{1,0:T(2,128)S(1)}, u32[]{:S(2)}, u32[]{:S(2)}) collective-permute-start(f32[2,48]{1,0:T(2,128)S(1)} %stack.19), channel_id=1, source_target_pairs={{0,1},{1,0},{2,3},{3,2},{4,5},{5,4},{6,7},{7,6},{8,9},{9,8},{10,11... | collective-permute-start | bytes 1160 | tf_op jit(solution)/shard_map/ppermute | solution.py:120
  188.5 9.4 %collective-permute-start.56 = (f32[48,768]{1,0:T(8,128)S(1)}, f32[48,768]{1,0:T(8,128)S(1)}, u32[]{:S(2)}, u32[]{:S(2)}) collective-permute-start(f32[48,768]{1,0:T(8,128)S(1)} %dynamic-slice_bitcast_fusion.16), channel_id=1, source_target_pairs={{0,2},{2,0},{4,6},{6,4},{8,10},{10,8},{12,14},{14,12},{16,18},{18,... | collective-permute-start | bytes 442376 | tf_op jit(solution)/shard_map/ppermute | solution.py:54
  188.7 10.4 %collective-permute-start.53 = (bf16[96,768]{1,0:T(8,128)(2,1)S(1)}, bf16[96,768]{1,0:T(8,128)(2,1)S(1)}, u32[]{:S(2)}, u32[]{:S(2)}) collective-permute-start(bf16[96,768]{1,0:T(8,128)(2,1)S(1)} %get-tuple-element.303), channel_id=1, source_target_pairs={{0,16},{2,18},{4,20},{6,22},{8,24},{10,26},{12,28},{14,30},{16,0},... | collective-permute-start | bytes 442376 | tf_op jit(solution)/shard_map/ppermute | solution.py:96
  (57 other events, 301.3 us)
